TPU v7x, 32 devices: a whole 2x2x4 slice. The times are simulated.
32 devices in a mesh: dp: 4 (over x, core), fsdp: 8 (over z, y).
Axes of the slice: x: 2, y: 2, z: 4, core: 2. Of those that a mesh axis runs over, the one named last changes fastest.
Arguments:
- inputs: bfloat16 [64, 256, 768], P(('dp', 'fsdp')), may hold values from -6 to 6
- cotangent: bfloat16 [64, 256, 768], P(('dp', 'fsdp')), may hold values from -6 to 6
- image_shape: int32 [64, 2], P(('dp', 'fsdp')), may hold values from 8 to 16, as said below
- time_bins: int32 [64], P(('dp', 'fsdp')), may hold values from 0 to 999
- time_table: float32 [1000, 768], replicated, may hold values from -6 to 6
- modulation_master: float32 [6, 768, 768], P(None, 'fsdp'), may hold values from -0.21875 to 0.21875
- projection_master: float32 [3, 768, 768], P(None, 'fsdp'), may hold values from -0.21875 to 0.21875
- output_master: float32 [768, 768], P('fsdp'), may hold values from -1.75 to 1.75
- expand_master: float32 [2, 768, 2048], P(None, 'fsdp'), may hold values from -0.21875 to 0.21875
- shrink_master: float32 [2048, 768], P(None, 'fsdp'), may hold values from -0.125 to 0.125
- modulation_moment: float32 [6, 768, 768], P(None, 'fsdp'), may hold values from -80 to 80
- projection_moment: float32 [3, 768, 768], P(None, 'fsdp'), may hold values from -448 to 448
- output_moment: float32 [768, 768], P('fsdp'), may hold values from -80 to 80
- expand_moment: float32 [2, 768, 2048], P(None, 'fsdp'), may hold values from -80 to 80
- shrink_moment: float32 [2048, 768], P(None, 'fsdp'), may hold values from -80 to 80
Outputs:
- block_output: bfloat16 [64, 256, 768], P(('dp', 'fsdp'))
- input_gradient: float32 [64, 256, 768], P(('dp', 'fsdp'))
- modulation_gradient: float32 [6, 768, 768], P(None, 'fsdp')
- projection_gradient: float32 [3, 768, 768], P(None, 'fsdp')
- output_gradient: float32 [768, 768], P('fsdp')
- expand_gradient: float32 [2, 768, 2048], P(None, 'fsdp')
- shrink_gradient: float32 [2048, 768], P(None, 'fsdp')
- modulation_weight: float32 [6, 768, 768], P(None, 'fsdp')
- projection_weight: float32 [3, 768, 768], P(None, 'fsdp')
- output_weight: float32 [768, 768], P('fsdp')
- expand_weight: float32 [2, 768, 2048], P(None, 'fsdp')
- shrink_weight: float32 [2048, 768], P(None, 'fsdp')
- modulation_state: float32 [6, 768, 768], P(None, 'fsdp')
- projection_state: float32 [3, 768, 768], P(None, 'fsdp')
- output_state: float32 [768, 768], P('fsdp')
- expand_state: float32 [2, 768, 2048], P(None, 'fsdp')
- shrink_state: float32 [2048, 768], P(None, 'fsdp')
Inputs may be any that keep to these rules, and one draw needn't show every extreme that they name: Image b has image_shape[b, 0] patch rows and image_shape[b, 1] patch columns; in every draw some image is 16 x 16, filling all 256 slots.
All inputs are finite; a program needn't handle non-finite values.
Results may differ from a plain program's by a relative error of at most 0.02.
The roundings to bfloat16 on the way count: a program that leaves them out, or rounds other values in their place, can miss the bound.
Values may be sent and summed in bfloat16 or wider, within the bound.
No kernel may reach another device: no remote copies, remote signals or barrier semaphores. Data moves between devices by JAX's collectives and lax.ppermute only.
A program may use at most 192 MiB of HBM per device.

v0:
```python
import jax
import jax.numpy as jnp
from jax import lax
from jax.sharding import PartitionSpec as P

D = 768
HEADS = 12
HDIM = 64
FF = 2048
NS_ITERS = 5


NORM_EPS = 1e-06
FROBENIUS_EPS = 1e-07
COEFF_FIRST = 3.4445
COEFF_SECOND = -4.775
COEFF_THIRD = 2.0315
MOMENTUM_DECAY = 0.9
LEARN_RATE = 1.0
HIGHEST = lax.Precision.HIGHEST


def swish_value(values):
    return values / (1.0 + jnp.exp(-values))


def layer_norm(values):
    centred = values - jnp.mean(values, axis=-1, keepdims=True)
    inverse = lax.rsqrt(jnp.mean(centred * centred, axis=-1, keepdims=True) + NORM_EPS)
    return (centred * inverse, inverse)


def norm_back(incoming, normed, inverse):
    return inverse * (
        incoming
        - jnp.mean(incoming, axis=-1, keepdims=True)
        - normed * jnp.mean(incoming * normed, axis=-1, keepdims=True)
    )


def rotate(tensor):
    first, second, third, fourth = jnp.split(tensor, 4, axis=-1)
    return jnp.concatenate([-second, first, -fourth, third], axis=-1)


def rope_tables(extents, positions):
    quarter = HDIM // 4
    places = jnp.arange(positions, dtype=jnp.int32)
    widths = extents[:, 1]
    row_place = (places[None, :] // widths[:, None]).astype(jnp.float32)
    col_place = (places[None, :] % widths[:, None]).astype(jnp.float32)
    frequency = 10000.0 ** (-jnp.arange(quarter).astype(jnp.float32) / quarter)
    row_angle = row_place[:, :, None] * frequency
    col_angle = col_place[:, :, None] * frequency
    cosine_table = jnp.concatenate(
        [jnp.cos(row_angle), jnp.cos(row_angle), jnp.cos(col_angle), jnp.cos(col_angle)], axis=-1
    )
    sine_table = jnp.concatenate(
        [jnp.sin(row_angle), jnp.sin(row_angle), jnp.sin(col_angle), jnp.sin(col_angle)], axis=-1
    )
    return (cosine_table[:, :, None, :], sine_table[:, :, None, :])


def forward(weights, stream, activated, key_mask, cosine_table, sine_table):
    modulation_weight, projection_weight, output_weight, expand_weight, shrink_weight = weights
    images_here, positions, features = stream.shape
    modulation = jnp.einsum(
        "bd,kde->kbe", activated, modulation_weight, preferred_element_type=jnp.float32
    )
    shift_one, scale_one, gate_one, shift_two, scale_two, gate_two = [
        modulation[which][:, None, :] for which in range(6)
    ]
    normed_one, inverse_one = layer_norm(stream)
    first_input = (normed_one * (1.0 + scale_one) + shift_one).astype(jnp.bfloat16)
    projected = jnp.einsum(
        "bsd,kde->kbse", first_input, projection_weight, preferred_element_type=jnp.float32
    )
    projected = projected.reshape(3, images_here, positions, HEADS, HDIM)
    query_rot = (projected[0] * cosine_table + rotate(projected[0]) * sine_table).astype(
        jnp.bfloat16
    )
    key_rot = (projected[1] * cosine_table + rotate(projected[1]) * sine_table).astype(jnp.bfloat16)
    value_heads = projected[2].astype(jnp.bfloat16)
    scores = jnp.einsum(
        "bqhd,bkhd->bhqk", query_rot, key_rot, preferred_element_type=jnp.float32
    ) * HDIM ** (-0.5)
    scores = jnp.where(key_mask[:, None, None, :], scores, -1000000000.0)
    exponent = jnp.exp(scores - jnp.max(scores, axis=-1, keepdims=True))
    softmax_out = exponent / jnp.sum(exponent, axis=-1, keepdims=True)
    softmax_low = softmax_out.astype(jnp.bfloat16)
    attended = jnp.einsum(
        "bhqk,bkhd->bqhd", softmax_low, value_heads, preferred_element_type=jnp.float32
    )
    attended = attended.astype(jnp.bfloat16).reshape(images_here, positions, features)
    attention = jnp.einsum(
        "bsd,de->bse", attended, output_weight, preferred_element_type=jnp.float32
    )
    middle = stream + gate_one * attention
    normed_two, inverse_two = layer_norm(middle)
    second_input = (normed_two * (1.0 + scale_two) + shift_two).astype(jnp.bfloat16)
    expanded = jnp.einsum(
        "bsd,kdf->kbsf", second_input, expand_weight, preferred_element_type=jnp.float32
    )
    gate_pre = expanded[0]
    up_pre = expanded[1]
    hidden = (swish_value(gate_pre) * up_pre).astype(jnp.bfloat16)
    branch_out = jnp.einsum(
        "bsf,fd->bsd", hidden, shrink_weight, preferred_element_type=jnp.float32
    )
    result = middle + gate_two * branch_out
    saved = (
        modulation,
        normed_one,
        inverse_one,
        first_input,
        query_rot,
        key_rot,
        value_heads,
        softmax_out,
        softmax_low,
        attended,
        attention,
        normed_two,
        inverse_two,
        second_input,
        gate_pre,
        up_pre,
        hidden,
        branch_out,
    )
    return (result, saved)


def backward(weights, activated, saved, upstream, cosine_table, sine_table):
    modulation_weight, projection_weight, output_weight, expand_weight, shrink_weight = weights
    (
        modulation,
        normed_one,
        inverse_one,
        first_input,
        query_rot,
        key_rot,
        value_heads,
        softmax_out,
        softmax_low,
        attended,
        attention,
        normed_two,
        inverse_two,
        second_input,
        gate_pre,
        up_pre,
        hidden,
        branch_out,
    ) = saved
    images_here, positions, features = upstream.shape
    shift_one, scale_one, gate_one, shift_two, scale_two, gate_two = [
        modulation[which][:, None, :] for which in range(6)
    ]
    grad_gate_two = jnp.sum(upstream * branch_out, axis=1)
    grad_branch = (gate_two * upstream).astype(jnp.bfloat16)
    grad_shrink = jnp.einsum("bsf,bsd->fd", hidden, grad_branch, preferred_element_type=jnp.float32)
    grad_hidden = jnp.einsum(
        "bsd,fd->bsf", grad_branch, shrink_weight, preferred_element_type=jnp.float32
    )
    sigmoid_gate = 1.0 / (1.0 + jnp.exp(-gate_pre))
    grad_gate = grad_hidden * up_pre * sigmoid_gate * (1.0 + gate_pre * (1.0 - sigmoid_gate))
    grad_up = grad_hidden * gate_pre * sigmoid_gate
    grad_expand_in = jnp.stack([grad_gate, grad_up]).astype(jnp.bfloat16)
    grad_expand = jnp.einsum(
        "bsd,kbsf->kdf", second_input, grad_expand_in, preferred_element_type=jnp.float32
    )
    grad_second = jnp.einsum(
        "kbsf,kdf->bsd", grad_expand_in, expand_weight, preferred_element_type=jnp.float32
    )
    grad_scale_two = jnp.sum(grad_second * normed_two, axis=1)
    grad_shift_two = jnp.sum(grad_second, axis=1)
    grad_stream = upstream + norm_back(grad_second * (1.0 + scale_two), normed_two, inverse_two)
    grad_gate_one = jnp.sum(grad_stream * attention, axis=1)
    grad_attention = (gate_one * grad_stream).astype(jnp.bfloat16)
    grad_output = jnp.einsum(
        "bsd,bse->de", attended, grad_attention, preferred_element_type=jnp.float32
    )
    grad_attended = jnp.einsum(
        "bse,de->bsd", grad_attention, output_weight, preferred_element_type=jnp.float32
    )
    grad_attended = grad_attended.astype(jnp.bfloat16).reshape(images_here, positions, HEADS, HDIM)
    grad_soft = jnp.einsum(
        "bqhd,bkhd->bhqk", grad_attended, value_heads, preferred_element_type=jnp.float32
    )
    grad_values = jnp.einsum(
        "bhqk,bqhd->bkhd", softmax_low, grad_attended, preferred_element_type=jnp.float32
    )
    grad_scores = softmax_out * (
        grad_soft - jnp.sum(grad_soft * softmax_out, axis=-1, keepdims=True)
    )
    grad_scores = grad_scores.astype(jnp.bfloat16)
    grad_qrot = jnp.einsum(
        "bhqk,bkhd->bqhd", grad_scores, key_rot, preferred_element_type=jnp.float32
    ) * HDIM ** (-0.5)
    grad_krot = jnp.einsum(
        "bhqk,bqhd->bkhd", grad_scores, query_rot, preferred_element_type=jnp.float32
    ) * HDIM ** (-0.5)
    grad_query = grad_qrot * cosine_table - rotate(grad_qrot * sine_table)
    grad_key = grad_krot * cosine_table - rotate(grad_krot * sine_table)
    grad_project_in = (
        jnp.stack([grad_query, grad_key, grad_values])
        .reshape(3, images_here, positions, features)
        .astype(jnp.bfloat16)
    )
    grad_projection = jnp.einsum(
        "bsd,kbse->kde", first_input, grad_project_in, preferred_element_type=jnp.float32
    )
    grad_first = jnp.einsum(
        "kbse,kde->bsd", grad_project_in, projection_weight, preferred_element_type=jnp.float32
    )
    grad_scale_one = jnp.sum(grad_first * normed_one, axis=1)
    grad_shift_one = jnp.sum(grad_first, axis=1)
    grad_stream = grad_stream + norm_back(grad_first * (1.0 + scale_one), normed_one, inverse_one)
    grad_modulation_in = jnp.stack(
        [
            grad_shift_one,
            grad_scale_one,
            grad_gate_one,
            grad_shift_two,
            grad_scale_two,
            grad_gate_two,
        ]
    ).astype(jnp.bfloat16)
    grad_modulation = jnp.einsum(
        "bd,kbe->kde", activated, grad_modulation_in, preferred_element_type=jnp.float32
    )
    return (grad_stream, (grad_modulation, grad_projection, grad_output, grad_expand, grad_shrink))


def orthogonalize(matrices):
    norms_sq = jnp.sum(matrices * matrices, axis=(1, 2), keepdims=True)
    current = matrices / (jnp.sqrt(norms_sq) + FROBENIUS_EPS)
    for iteration in range(NS_ITERS):
        gram = jnp.einsum("nik,njk->nij", current, current, precision=HIGHEST)
        poly = COEFF_SECOND * gram + COEFF_THIRD * jnp.einsum(
            "nij,njk->nik", gram, gram, precision=HIGHEST
        )
        current = COEFF_FIRST * current + jnp.einsum(
            "nij,njk->nik", poly, current, precision=HIGHEST
        )
    return current


def local(
    inputs,
    cotangent,
    image_shape,
    time_bins,
    time_table,
    modulation_master,
    projection_master,
    output_master,
    expand_master,
    shrink_master,
    modulation_moment,
    projection_moment,
    output_moment,
    expand_moment,
    shrink_moment,
):
    masters = (modulation_master, projection_master, output_master, expand_master, shrink_master)
    moments = (modulation_moment, projection_moment, output_moment, expand_moment, shrink_moment)
    gathered = (
        lax.all_gather(modulation_master.astype(jnp.bfloat16), "fsdp", axis=1, tiled=True),
        lax.all_gather(projection_master.astype(jnp.bfloat16), "fsdp", axis=1, tiled=True),
        lax.all_gather(output_master.astype(jnp.bfloat16), "fsdp", axis=0, tiled=True),
        lax.all_gather(expand_master.astype(jnp.bfloat16), "fsdp", axis=1, tiled=True),
        lax.all_gather(shrink_master.astype(jnp.bfloat16), "fsdp", axis=1, tiled=True),
    )
    stream = inputs.astype(jnp.float32)
    positions = stream.shape[1]
    places = jnp.arange(positions, dtype=jnp.int32)
    lengths = image_shape[:, 0] * image_shape[:, 1]
    key_mask = places[None, :] < lengths[:, None]
    cosine_table, sine_table = rope_tables(image_shape, positions)
    selector = (
        time_bins[:, None] == jnp.arange(time_table.shape[0], dtype=jnp.int32)[None, :]
    ).astype(jnp.float32)
    condition = jnp.dot(selector, time_table, precision=HIGHEST)
    activated = swish_value(condition).astype(jnp.bfloat16)
    result, saved = forward(gathered, stream, activated, key_mask, cosine_table, sine_table)
    backing = (
        lax.all_gather(modulation_master.astype(jnp.bfloat16), "fsdp", axis=1, tiled=True),
        lax.all_gather(projection_master.astype(jnp.bfloat16), "fsdp", axis=1, tiled=True),
        lax.all_gather(output_master.astype(jnp.bfloat16), "fsdp", axis=0, tiled=True),
        lax.all_gather(expand_master.astype(jnp.bfloat16), "fsdp", axis=1, tiled=True),
        lax.all_gather(shrink_master.astype(jnp.bfloat16), "fsdp", axis=1, tiled=True),
    )
    saved = forward(backing, stream, activated, key_mask, cosine_table, sine_table)[1]
    upstream = cotangent.astype(jnp.float32) * key_mask[:, :, None].astype(jnp.float32)
    input_gradient, partials = backward(
        backing, activated, saved, upstream, cosine_table, sine_table
    )
    devices = lax.axis_size("fsdp")
    rows_local = modulation_master.shape[1]
    shards = (
        lax.psum_scatter(partials[0], "fsdp", scatter_dimension=1, tiled=True),
        lax.psum_scatter(partials[1], "fsdp", scatter_dimension=1, tiled=True),
        lax.psum_scatter(partials[2], "fsdp", scatter_dimension=0, tiled=True),
        lax.psum_scatter(partials[3], "fsdp", scatter_dimension=1, tiled=True),
        lax.psum_scatter(partials[4], "fsdp", scatter_dimension=1, tiled=True),
    )
    totals = lax.psum((shards[0], shards[1], shards[2], shards[3], shards[4]), "dp")
    states = tuple((MOMENTUM_DECAY * moment + total for moment, total in zip(moments, totals)))
    feeds = tuple((total + MOMENTUM_DECAY * state for total, state in zip(totals, states)))
    pieces = (
        [feeds[0][which] for which in range(6)]
        + [feeds[1][which] for which in range(3)]
        + [feeds[2], feeds[3][0], feeds[3][1], feeds[4].T]
    )
    slot_count = (len(pieces) + devices - 1) // devices
    padded = [jnp.pad(piece, ((0, 0), (0, FF - piece.shape[1]))) for piece in pieces]
    padded = padded + [jnp.zeros((rows_local, FF), jnp.float32)] * (
        slot_count * devices - len(pieces)
    )
    outgoing = jnp.stack(padded).reshape(slot_count, devices, rows_local, FF)
    received = lax.all_to_all(outgoing, "fsdp", split_axis=1, concat_axis=1, tiled=True)
    items_here = received.shape[0]
    whole = orthogonalize(received.reshape(items_here, devices * rows_local, FF))
    returned = lax.all_to_all(
        whole.reshape(items_here, devices, rows_local, FF).astype(jnp.bfloat16),
        "fsdp",
        split_axis=1,
        concat_axis=1,
        tiled=True,
    ).astype(jnp.float32)
    returned = returned.reshape(slot_count * devices, rows_local, FF)
    modulation_step = returned[0:6, :, :D]
    projection_step = returned[6:9, :, :D]
    output_step = returned[9, :, :D]
    expand_step = returned[10:12] * (FF / D) ** 0.5
    shrink_step = returned[12].T
    steps_all = (modulation_step, projection_step, output_step, expand_step, shrink_step)
    updated = tuple((master - LEARN_RATE * step for master, step in zip(masters, steps_all)))
    return (
        result.astype(jnp.bfloat16),
        input_gradient,
        totals[0],
        totals[1],
        totals[2],
        totals[3],
        totals[4],
        updated[0],
        updated[1],
        updated[2],
        updated[3],
        updated[4],
        states[0],
        states[1],
        states[2],
        states[3],
        states[4],
    )


def solution(mesh):
    placed = (
        P(("dp", "fsdp"), None, None),
        P(("dp", "fsdp"), None, None),
        P(("dp", "fsdp"), None),
        P(("dp", "fsdp")),
        P(),
        P(None, "fsdp", None),
        P(None, "fsdp", None),
        P("fsdp", None),
        P(None, "fsdp", None),
        P(None, "fsdp"),
        P(None, "fsdp", None),
        P(None, "fsdp", None),
        P("fsdp", None),
        P(None, "fsdp", None),
        P(None, "fsdp"),
    )
    return jax.shard_map(
        local,
        mesh=mesh,
        in_specs=placed,
        out_specs=(
            P(("dp", "fsdp"), None, None),
            P(("dp", "fsdp"), None, None),
            P(None, "fsdp", None),
            P(None, "fsdp", None),
            P("fsdp", None),
            P(None, "fsdp", None),
            P(None, "fsdp"),
            P(None, "fsdp", None),
            P(None, "fsdp", None),
            P("fsdp", None),
            P(None, "fsdp", None),
            P(None, "fsdp"),
            P(None, "fsdp", None),
            P(None, "fsdp", None),
            P("fsdp", None),
            P(None, "fsdp", None),
            P(None, "fsdp"),
        ),
        check_vma=False,
    )
```

profile of v0, /device:TPU:0, one launch (start us, length us, event | category | flops | bytes accessed | tf_op | source)
XLA Modules:
  0.0 2515.5 jit_solution(1578928121377472265)
XLA Ops:
  22.5 99.9 %all-gather.6.cloned.1.call-done = bf16[6,768,768]{2,1,0:T(8,128)(2,1)} async-done(((bf16[6,96,768]{2,1,0:T(8,128)(2,1)}), bf16[6,768,768]{2,1,0:T(8,128)(2,1)}) %all-gather.6.cloned.1.call-update) | async-done | bytes 7077904 | tf_op jit(solution)/shard_map/all_gather | solution.py:270
  126.4 62.1 %all-gather.8.cloned.1.call-done = bf16[3,768,768]{2,1,0:T(8,128)(2,1)} async-done(((bf16[3,96,768]{2,1,0:T(8,128)(2,1)}), bf16[3,768,768]{2,1,0:T(8,128)(2,1)}) %all-gather.8.cloned.1.call-update) | async-done | bytes 3538960 | tf_op jit(solution)/shard_map/all_gather | solution.py:271
  206.6 6.4 fusion.151
  217.5 13.3 all-gather.10.cloned.1.call-done
  234.7 96.6 %all-gather.12.cloned.1.call-done = bf16[2,768,2048]{2,1,0:T(8,128)(2,1)} async-done(((bf16[2,96,2048]{2,1,0:T(8,128)(2,1)}), bf16[2,768,2048]{2,1,0:T(8,128)(2,1)}) %all-gather.12.cloned.1.call-update) | async-done | bytes 6291472 | tf_op jit(solution)/shard_map/all_gather | solution.py:273
  331.3 8.9 fusion.34
  340.2 52.4 %all-gather.14.cloned.1.call-done = bf16[2048,768]{0,1:T(8,128)(2,1)} async-done(((bf16[2048,96]{0,1:T(8,128)(2,1)}), bf16[2048,768]{0,1:T(8,128)(2,1)}) %all-gather.14.cloned.1.call-update) | async-done | bytes 3145744 | tf_op jit(solution)/shard_map/all_gather | solution.py:274
  392.6 9.2 fusion.63
  403.7 6.8 convolution_bitcast_fusion.1
  410.5 19.4 copy.162
  430.0 8.1 fusion.85
  471.1 6.2 convolution_bitcast_fusion.3
  477.3 10.7 copy.206
  488.0 8.3 copy.212
  496.5 6.2 fusion.76
  502.8 7.0 convolution_bitcast_fusion
  509.8 17.6 copy.204
  527.3 16.0 copy.211
  547.3 6.3 convolution_bitcast_fusion.2
  555.5 270.9 %all-reduce.15.cloned.1.call-done = f32[2,768,2048]{2,0,1:T(2,128)} async-done(((f32[2,768,2048]{2,0,1:T(2,128)}), f32[2,768,2048]{2,0,1:T(2,128)}) %all-reduce.15.cloned.1.call-update) | async-done | bytes 12582928
  829.0 129.6 %reduce-scatter.15.cloned.1.call-done = f32[96,2304]{1,0:T(8,128)} async-done(((f32[768,2304]{1,0:T(8,128)}), f32[96,2304]{1,0:T(8,128)}) %reduce-scatter.15.cloned.1.call-update) | async-done | bytes 884752
  961.9 228.7 %reduce-scatter.13.cloned.1.call-done = f32[96,4608]{1,0:T(8,128)} async-done(((f32[768,4608]{1,0:T(8,128)}), f32[96,4608]{1,0:T(8,128)}) %reduce-scatter.13.cloned.1.call-update) | async-done | bytes 1769488
  1194.4 67.8 %reduce-scatter.11.cloned.1.call-done = f32[96,768]{1,0:T(8,128)} async-done(((f32[768,768]{1,0:T(8,128)}), f32[96,768]{1,0:T(8,128)}) %reduce-scatter.11.cloned.1.call-update) | async-done | bytes 294928 | tf_op jit(solution)/shard_map/reduce_scatter | solution.py:305
  1262.2 120.4 %reduce-scatter.17.cloned.1.call-done = f32[96,2048]{1,0:T(8,128)} async-done(((f32[768,2048]{1,0:T(8,128)}), f32[96,2048]{1,0:T(8,128)}) %reduce-scatter.17.cloned.1.call-update) | async-done | bytes 786448
  1387.1 116.7 %all-reduce.17.cloned.1.call-done = (f32[6,96,768]{1,2,0:T(8,128)}, f32[3,96,768]{1,2,0:T(8,128)}, f32[96,768]{1,0:T(8,128)}, f32[2,96,2048]{2,0,1:T(2,128)}, f32[2048,96]{0,1:T(8,128)}) async-done(((f32[6,96,768]{1,2,0:T(8,128)}, f32[3,96,768]{1,2,0:T(8,128)}, f32[96,768]{1,0:T(8,128)}, f32[2,96,2048]{2,0,1:T(2,128)}, f32[2048,96]{0,1:T(8,128)}), (f32[6,96,768]{1,2,0:T(8,128)}, f32[3,96,768]{1,2,0:T(8,128)}, ...) | async-done | bytes 5308432 | tf_op jit(solution)/shard_map/psum | solution.py:309
  1543.3 34.5 %stack.120 = f32[16,96,2048]{2,0,1:T(8,128)} concatenate(f32[1,96,2048]{2,0,1:T(1,128)} %copy.169, f32[1,96,2048]{2,0,1:T(1,128)} %copy.170, f32[1,96,2048]{2,0,1:T(1,128)} %copy.171, f32[1,96,2048]{2,0,1:T(1,128)} %copy.172, f32[1,96,2048]{2,0,1:T(1,128)} %copy.173, f32[1,96,2048]{2,0,1:T(1,128)} %copy.174, f32[1,96,2048]{2,0,1:T(1,128)} %copy.175, f32[1,96,2048]{2,0,1:T(1,128)} %copy.176, ...), dimensions={0} | concatenate | bytes 25165824 | tf_op jit(solution)/shard_map/stack | solution.py:322
  1577.8 16.4 copy.179
  1594.2 278.8 %all_to_all.10 = f32[2,8,96,2048]{3,2,0,1:T(8,128)S(1)} all-to-all(f32[2,8,96,2048]{3,2,0,1:T(8,128)} %copy.179), channel_id=1, replica_groups=mesh['dp'=4,'fsdp'=8] {'fsdp'}, dimensions={1} | all-to-all | bytes 25165824 | tf_op jit(solution)/shard_map/all_to_all | solution.py:323
  1877.5 11.3 copy.180
  1888.8 11.9 bitcast_divide_fusion
  1900.7 34.6 %fusion.155 = f32[2,768,768]{2,1,0:T(8,128)S(1)} fusion(f32[2,768,2048]{2,1,0:T(8,128)} %bitcast_divide_fusion), kind=kOutput, calls=%fused_computation.269 | convolution fusion | flops 28991029248 | bytes 17301504 | tf_op jit(solution)/shard_map/nik,njk->nij/dot_general | solution.py:240
  1935.3 13.3 fusion.156
  1948.6 35.0 %multiply_add_fusion.3 = f32[2,768,2048]{2,1,0:T(8,128)S(1)} fusion(f32[2,768,2048]{2,1,0:T(8,128)} %bitcast_divide_fusion, f32[2,768,768]{2,1,0:T(8,128)} %fusion.156, f32[2,768,768]{2,1,0:T(8,128)S(1)} %fusion.155), kind=kOutput, calls=%fused_computation.6 | convolution fusion | flops 29000859648 | bytes 34603008 | tf_op jit(solution)/shard_map/nij,njk->nik/dot_general | solution.py:244
  1983.7 31.3 %fusion.157 = f32[2,768,768]{2,1,0:T(8,128)S(1)} fusion(f32[2,768,2048]{2,1,0:T(8,128)S(1)} %multiply_add_fusion.3), kind=kOutput, calls=%fused_computation.271 | convolution fusion | flops 28991029248 | bytes 17301504 | tf_op jit(solution)/shard_map/nik,njk->nij/dot_general | solution.py:240
  2015.0 12.0 fusion.158
  2027.0 38.3 %fusion.24 = f32[2,768,2048]{2,1,0:T(8,128)} fusion(f32[2,768,2048]{2,1,0:T(8,128)S(1)} %multiply_add_fusion.3, f32[2,768,768]{2,1,0:T(8,128)S(1)} %fusion.158, f32[2,768,768]{2,1,0:T(8,128)S(1)} %fusion.157), kind=kOutput, calls=%fused_computation.34 | convolution fusion | flops 28994568192 | bytes 34603008 | tf_op jit(solution)/shard_map/nij,njk->nik/dot_general | solution.py:244
  2065.3 34.7 %fusion.21 = f32[2,768,768]{2,1,0:T(8,128)S(1)} fusion(f32[2,768,2048]{2,1,0:T(8,128)} %fusion.24, f32[2,768,2048]{2,1,0:T(8,128)S(1)} %multiply_add_fusion.3), kind=kOutput, calls=%fused_computation.31 | convolution fusion | flops 28997320704 | bytes 29884416 | tf_op jit(solution)/shard_map/nik,njk->nij/dot_general | solution.py:240
  2102.3 13.2 fusion.159
  2115.5 45.5 %multiply_add_fusion.1 = f32[2,768,2048]{2,1,0:T(8,128)} fusion(f32[2,768,2048]{2,1,0:T(8,128)} %fusion.24, f32[2,768,2048]{2,1,0:T(8,128)} %copy-done.7, f32[2,768,768]{2,1,0:T(8,128)} %fusion.159, f32[2,768,768]{2,1,0:T(8,128)} %copy-done.3), kind=kOutput, calls=%fused_computation.4 | convolution fusion | flops 29013442560 | bytes 47185920 | tf_op jit(solution)/shard_map/nij,njk->nik/dot_general | solution.py:244
  2161.0 35.1 %fusion.160 = f32[2,768,768]{2,1,0:T(8,128)S(1)} fusion(f32[2,768,2048]{2,1,0:T(8,128)} %multiply_add_fusion.1), kind=kOutput, calls=%fused_computation.274 | convolution fusion | flops 28991029248 | bytes 17301504 | tf_op jit(solution)/shard_map/nik,njk->nij/dot_general | solution.py:240
  2196.1 12.0 fusion.161
  2208.2 38.2 %fusion.13 = f32[2,768,2048]{2,1,0:T(8,128)} fusion(f32[2,768,2048]{2,1,0:T(8,128)S(1)} %copy-done.6, f32[2,768,768]{2,1,0:T(8,128)S(1)} %fusion.161, f32[2,768,768]{2,1,0:T(8,128)S(1)} %fusion.160), kind=kOutput, calls=%fused_computation.25 | convolution fusion | flops 28994568192 | bytes 34603008 | tf_op jit(solution)/shard_map/nij,njk->nik/dot_general | solution.py:244
  2246.4 34.6 %fusion.10 = f32[2,768,768]{2,1,0:T(8,128)S(1)} fusion(f32[2,768,2048]{2,1,0:T(8,128)} %fusion.13, f32[2,768,2048]{2,1,0:T(8,128)S(1)} %copy-done.6), kind=kOutput, calls=%fused_computation.22 | convolution fusion | flops 28997320704 | bytes 29884416 | tf_op jit(solution)/shard_map/nik,njk->nij/dot_general | solution.py:240
  2283.1 13.3 fusion.162
  2296.3 45.2 %add_convert_fusion = bf16[2,768,2048]{2,1,0:T(8,128)(2,1)} fusion(f32[2,768,2048]{2,1,0:T(8,128)} %fusion.13, f32[2,768,2048]{2,1,0:T(8,128)} %multiply_add_fusion.1, f32[2,768,768]{2,1,0:T(8,128)} %fusion.162, f32[2,768,768]{2,1,0:T(8,128)} %copy-done.4), kind=kOutput, calls=%fused_computation.2 | convolution fusion | flops 29016588288 | bytes 40894464 | tf_op jit(solution)/shard_map/nij,njk->nik/dot_general | solution.py:244
  2341.6 6.5 copy.181
  2372.6 118.1 %all-to-all-done.1 = bf16[2,8,96,2048]{3,2,0,1:T(8,128)(2,1)} async-done(((bf16[2,8,96,2048]{3,2,0,1:T(8,128)(2,1)}), bf16[2,8,96,2048]{3,2,0,1:T(8,128)(2,1)}, u32[]{:S(2)}, u32[]{:S(2)}) %all-to-all-start.1) | async-done | bytes 6291488 | tf_op jit(solution)/shard_map/all_to_all | solution.py:326
  2490.7 6.5 copy.182
  (257 shorter events, 184.1 us)
Async XLA Ops:
  7.2 13.5 copy-start
  7.2 4.8 copy-start.35
  7.2 115.1 %all-gather.6.cloned.1.call-start = ((), (), s32[]{:S(2)}) async-start(), calls=%async_computation.6 | async-start | bytes 7962624 | tf_op jit(solution)/shard_map/all_gather | solution.py:270
  9.9 178.6 %all-gather.8.cloned.1.call-start = ((), (), s32[]{:S(2)}) async-start(), calls=%async_computation.7 | async-start | bytes 3981312 | tf_op jit(solution)/shard_map/all_gather | solution.py:271
  12.0 5.4 copy-start.50
  12.0 218.9 %all-gather.10.cloned.1.call-start = ((), (), s32[]{:S(2)}) async-start(), calls=%async_computation.8 | async-start | bytes 1327104 | tf_op jit(solution)/shard_map/all_gather | solution.py:272
  12.8 7.9 copy-start.53
  12.8 318.5 %all-gather.12.cloned.1.call-start = ((), (), s32[]{:S(2)}) async-start(), calls=%async_computation.9 | async-start | bytes 7077888 | tf_op jit(solution)/shard_map/all_gather | solution.py:273
  15.2 377.3 %all-gather.14.cloned.1.call-start = ((), (), s32[]{:S(2)}) async-start(), calls=%async_computation.10 | async-start | bytes 3538944 | tf_op jit(solution)/shard_map/all_gather | solution.py:274
  17.2 809.1 %all-reduce.15.cloned.1.call-start = ((), (), s32[]{:S(2)}) async-start(), calls=%async_computation.15 | async-start | bytes 25165824
  19.1 477.4 %copy-start.46 = (f32[2,256]{1,0:T(2,128)}, f32[2,256]{1,0:T(2,128)S(1)}, u32[]{:S(2)}) copy-start(f32[2,256]{1,0:T(2,128)S(1)} %broadcast_multiply_fusion.7) | copy-start | bytes 6148
  20.6 475.9 %copy-start.48 = (f32[2,256]{1,0:T(2,128)}, f32[2,256]{1,0:T(2,128)S(1)}, u32[]{:S(2)}) copy-start(f32[2,256]{1,0:T(2,128)S(1)} %add_rsqrt_fusion.1) | copy-start | bytes 6148
  22.5 166.0 %copy-start.8 = (bf16[2,256,768]{2,1,0:T(8,128)(2,1)S(1)}, bf16[2,256,768]{2,1,0:T(8,128)(2,1)}, u32[]{:S(2)}) copy-start(bf16[2,256,768]{2,1,0:T(8,128)(2,1)} %param.15) | copy-start | bytes 2359300
  126.4 370.1 %copy-start.44 = (f32[2,768]{1,0:T(2,128)}, f32[2,768]{1,0:T(2,128)S(1)}, u32[]{:S(2)}) copy-start(f32[2,768]{1,0:T(2,128)S(1)} %get-tuple-element.164) | copy-start | bytes 18436
  206.6 6.4 copy-start.40
  234.4 195.6 %copy-start.19 = (f32[2,256,768]{2,1,0:T(8,128)}, f32[2,256,768]{2,1,0:T(8,128)S(1)}, u32[]{:S(2)}) copy-start(f32[2,256,768]{2,1,0:T(8,128)S(1)} %get-tuple-element.109) | copy-start | bytes 4718596
  429.9 528.7 %reduce-scatter.15.cloned.1.call-start = ((), (), s32[]{:S(2)}) async-start(), calls=%async_computation.13 | async-start | bytes 7962624
  430.0 8.2 copy-start.34
  430.0 8.2 copy-start.54
  430.0 8.2 copy-start.55
  430.0 8.2 copy-start.57
  438.2 5.0 copy-start.38
  443.3 9.0 copy-start.15
  496.4 694.2 %reduce-scatter.13.cloned.1.call-start = ((), (), s32[]{:S(2)}) async-start(), calls=%async_computation.12 | async-start | bytes 15925248
  543.4 718.8 %reduce-scatter.11.cloned.1.call-start = ((), (), s32[]{:S(2)}) async-start(), calls=%async_computation.11 | async-start | bytes 2654208 | tf_op jit(solution)/shard_map/reduce_scatter | solution.py:305
  547.2 835.3 %reduce-scatter.17.cloned.1.call-start = ((), (), s32[]{:S(2)}) async-start(), calls=%async_computation.14 | async-start | bytes 7077888
  553.6 950.2 %all-reduce.17.cloned.1.call-start = ((), (), s32[]{:S(2)}) async-start(), calls=%async_computation.16 | async-start | bytes 12386304 | tf_op jit(solution)/shard_map/psum | solution.py:309
  1383.7 120.0 %copy-start.43 = (f32[96,768]{1,0:T(8,128)S(1)}, f32[96,768]{1,0:T(8,128)}, u32[]{:S(2)}) copy-start(f32[96,768]{1,0:T(8,128)} %param.27) | copy-start | bytes 884740
  1511.1 4.5 copy-start.25
  1511.2 4.4 copy-start.42
  1521.3 4.4 copy-start.32
  1523.5 4.4 copy-start.31
  1534.5 8.8 copy-start.23
  1873.0 4.5 copy-start.2
  1983.7 81.6 %copy-start.7 = (f32[2,768,2048]{2,1,0:T(8,128)}, f32[2,768,2048]{2,1,0:T(8,128)S(1)}, u32[]{:S(2)}) copy-start(f32[2,768,2048]{2,1,0:T(8,128)S(1)} %multiply_add_fusion.3) | copy-start | bytes 37748740
  2196.1 12.1 copy-start.6
  2348.1 5.4 copy-start.52
  2348.1 5.4 copy-start.51
  2348.1 5.4 copy-start.9
  2348.1 5.5 copy-start.17
  2348.1 5.5 copy-start.45
  2348.1 5.5 copy-start.47
  2348.1 5.5 copy-start.49
  2348.1 142.6 %all-to-all-start.1 = ((bf16[2,8,96,2048]{3,2,0,1:T(8,128)(2,1)}), bf16[2,8,96,2048]{3,2,0,1:T(8,128)(2,1)}, u32[]{:S(2)}, u32[]{:S(2)}) async-start(bf16[2,8,96,2048]{3,2,0,1:T(8,128)(2,1)} %copy.181), calls=%async_computation.2 | async-start | bytes 12582912 | tf_op jit(solution)/shard_map/all_to_all | solution.py:326
  2356.7 6.2 copy-start.11
  2364.7 6.2 copy-start.12
  2497.3 5.1 copy-start.24
  2504.4 4.5 copy-start.1
  (24 other events, 55.8 us)
Sparse Core Ops, SparseCore 0:
  10.8 111.4 all-gather.5
  125.1 63.3 all-gather.7
  191.3 39.5 all-gather.9
  233.5 97.7 all-gather.11
  333.9 58.6 all-gather.13
  430.0 396.2 all-reduce.14
  830.5 128.1 reduce-scatter.14
  962.3 228.2 reduce-scatter.12
  1194.1 68.0 reduce-scatter.10
  1265.6 116.9 reduce-scatter.16
  1385.9 117.8 all-reduce.16
where the time goes:
time: 2530 us; the launch traced here: 2520 us
  waiting for transfers between devices  1380 us (55%)
  matrix products  539 us (21%)
  blocking collectives  279 us (11%)
  local copies, waits for them, and re-layouts  237 us (9%)
  other arithmetic  62.2 us (2%)
    unnamed x15, waiting for transfers between devices  750 us
    all_to_all x1, blocking collectives, local(): lax.all_to_all(outgoing, 'fsdp', split_axis=1, concat_axis=1, tiled=True)  279 us
    dot_general x5, matrix products, orthogonalize(): jnp.einsum('nij,njk->nik', poly, current, precision=HIGHEST)  202 us
    dot_general x5, matrix products, orthogonalize(): gram = jnp.einsum('nik,njk->nij', current, current, precision=HIGHEST)  170 us
    all_to_all x1, waiting for transfers between devices, local(): lax.all_to_all(whole.reshape(items_here, devices, rows_local, FF).astype(...  118 us
    psum x1, waiting for transfers between devices, local(): lax.psum((shards[0], shards[1], shards[2], shards[3], shards[4]), 'dp')  117 us
    all_gather x1, waiting for transfers between devices, local(): lax.all_gather(modulation_master.astype(jnp.bfloat16), 'fsdp', axis=1, ti...  99.9 us
    unnamed x145, local copies, waits for them, and re-layouts  96.9 us
  transfers between devices with their start and end apart: 12, of which 12 were waited for; matrix products, arithmetic and copies ran while one was open for 8% of the time, Pallas kernels for 0%

commit v1 on v0

v1 whole, which is shorter than its diff:
```python
import functools
import itertools

import jax
import jax.numpy as jnp
from jax import lax
from jax.experimental import pallas as pl
from jax.experimental.pallas import tpu as pltpu
from jax.sharding import Mesh, PartitionSpec as P

D = 768
HEADS = 12
HDIM = 64
FF = 2048
NS_ITERS = 5
NORM_EPS = 1e-06
FROBENIUS_EPS = 1e-07
COEFF_FIRST = 3.4445
COEFF_SECOND = -4.775
COEFF_THIRD = 2.0315
MOMENTUM_DECAY = 0.9
LEARN_RATE = 1.0
HIGHEST = lax.Precision.HIGHEST
BF16 = jnp.bfloat16
F32 = jnp.float32
ITEMS = 13
NT = (((1,), (1,)), ((), ()))
NN = (((1,), (0,)), ((), ()))
TN = (((0,), (0,)), ((), ()))


def dot(a, b, dims=NN):
    return lax.dot_general(a, b, dims, preferred_element_type=F32)


def newton_schulz_kernel(width, active_ref, feed_ref, left_ref, right_ref, out_ref, x, xb, gram, low, poly):
    tile = 256
    tiles = D // tile
    blocks = width // tile
    spans = [slice(i * tile, (i + 1) * tile) for i in range(tiles)]

    def diagonal(part, other):
        rows = lax.broadcasted_iota(jnp.int32, (tile, tile), 0)
        cols = lax.broadcasted_iota(jnp.int32, (tile, tile), 1)
        return jnp.where(rows == cols, part, other)

    def block(b):
        return pl.ds(pl.multiple_of(b * tile, tile), tile)

    @pl.when(active_ref[0] != 0)
    def _():
        def load(b, acc):
            v = feed_ref[:, block(b)].astype(F32)
            if right_ref is not None:
                v = v + (1.0 + MOMENTUM_DECAY) * dot(left_ref[...], right_ref[:, block(b)], TN)
            x[:, block(b)] = v
            return acc + jnp.sum(v * v, axis=0, keepdims=True)

        total = lax.fori_loop(0, blocks, load, jnp.zeros((1, tile), F32))
        total = jnp.sum(total, keepdims=True)
        inverse = 1.0 / (jnp.sqrt(total) + FROBENIUS_EPS)

        def scale_block(b, carry):
            v = x[:, block(b)] * inverse
            x[:, block(b)] = v
            xb[:, block(b)] = v.astype(BF16)
            return carry

        lax.fori_loop(0, blocks, scale_block, 0)

        def iterate(step, carry):
            trace = jnp.zeros((1, tile), F32)
            for i in range(tiles):
                for j in range(i + 1):
                    part = dot(xb[spans[i], :], xb[spans[j], :], NT)
                    gram[spans[i], spans[j]] = part
                    if i == j:
                        trace = trace + jnp.sum(diagonal(part, 0.0), axis=0, keepdims=True)
                    else:
                        lower = part.astype(BF16)
                        low[spans[i], spans[j]] = lower
                        low[spans[j], spans[i]] = lower.T
            shift = jnp.sum(trace, keepdims=True) / D
            for i in range(tiles):
                part = gram[spans[i], spans[i]]
                part = diagonal(part - shift, part)
                gram[spans[i], spans[i]] = part
                low[spans[i], spans[i]] = part.astype(BF16)
            linear = COEFF_SECOND + 2.0 * COEFF_THIRD * shift
            level = COEFF_SECOND * shift + COEFF_THIRD * shift * shift
            trace = jnp.zeros((1, tile), F32)
            for i in range(tiles):
                for j in range(i + 1):
                    part = linear * gram[spans[i], spans[j]] + COEFF_THIRD * dot(
                        low[spans[i], :], low[spans[j], :], NT
                    )
                    if i == j:
                        gram[spans[i], spans[j]] = part
                        trace = trace + jnp.sum(diagonal(part, 0.0), axis=0, keepdims=True)
                    else:
                        lower = part.astype(BF16)
                        poly[spans[i], spans[j]] = lower
                        poly[spans[j], spans[i]] = lower.T
            mean = jnp.sum(trace, keepdims=True) / D
            for i in range(tiles):
                part = gram[spans[i], spans[i]]
                poly[spans[i], spans[i]] = diagonal(part - mean, part).astype(BF16)
            scale = COEFF_FIRST + level + mean

            def update(b, inner):
                new = scale * x[:, block(b)] + dot(poly[...], xb[:, block(b)])
                x[:, block(b)] = new
                xb[:, block(b)] = new.astype(BF16)
                return inner

            lax.fori_loop(0, blocks, update, 0)
            return carry

        lax.fori_loop(0, NS_ITERS, iterate, 0)
        out_ref[...] = xb[...]

    @pl.when(active_ref[0] == 0)
    def _():
        out_ref[...] = jnp.zeros_like(out_ref)


def newton_schulz(active, feed, left=None, right=None):
    width = feed.shape[1]
    operands = [active.reshape(1).astype(jnp.int32), feed]
    if left is None:

        def body(active_ref, feed_ref, *rest):
            newton_schulz_kernel(width, active_ref, feed_ref, None, None, *rest)

    else:
        body = functools.partial(newton_schulz_kernel, width)
        operands += [left, right]
    vmem = pl.BlockSpec(memory_space=pltpu.VMEM)
    return pl.pallas_call(
        body,
        out_shape=jax.ShapeDtypeStruct((D, width), BF16),
        in_specs=[pl.BlockSpec(memory_space=pltpu.SMEM)] + [vmem] * (len(operands) - 1),
        out_specs=vmem,
        scratch_shapes=[
            pltpu.VMEM((D, width), F32),
            pltpu.VMEM((D, width), BF16),
            pltpu.VMEM((D, D), F32),
            pltpu.VMEM((D, D), BF16),
            pltpu.VMEM((D, D), BF16),
        ],
        compiler_params=pltpu.CompilerParams(vmem_limit_bytes=40 * 1024 * 1024),
        cost_estimate=pl.CostEstimate(
            flops=NS_ITERS * 4 * D * D * (width + D), bytes_accessed=4 * D * width, transcendentals=0
        ),
        name="newton_schulz",
    )(*operands)


def tie(value, *others):
    return lax.optimization_barrier((value, *others))[0]


def place(parts, slots, lead=None, moves=None):
    count = len(parts)
    if lead is None:
        lead = (count, *parts[0].shape[:-2])
        moves = lambda slot: [(i, (), (slot[i],)) for i in range(count)]
    total = len(moves([0] * len(slots)))

    def body(slot_ref, *refs):
        ins, out, sem = refs[:count], refs[count], refs[count + 1]
        copies = []
        for i, (part, source, target) in enumerate(moves(slot_ref)):
            from_ref = ins[part].at[source] if source else ins[part]
            copies.append(pltpu.make_async_copy(from_ref, out.at[target], sem.at[i]))
        for copy in copies:
            copy.start()
        for copy in copies:
            copy.wait()

    size = count * parts[0].size * parts[0].dtype.itemsize
    return pl.pallas_call(
        body,
        out_shape=jax.ShapeDtypeStruct((*lead, *parts[0].shape[-2:]), parts[0].dtype),
        in_specs=[pl.BlockSpec(memory_space=pltpu.SMEM)]
        + [pl.BlockSpec(memory_space=pl.ANY)] * count,
        out_specs=pl.BlockSpec(memory_space=pl.ANY),
        scratch_shapes=[pltpu.SemaphoreType.DMA((total,))],
        cost_estimate=pl.CostEstimate(flops=0, bytes_accessed=2 * size, transcendentals=0),
        name="place",
    )(jnp.stack(slots).astype(jnp.int32), *parts)


def every(*sizes):
    return list(itertools.product(*[range(size) for size in sizes]))


class Plain:
    images = ("dp", "fsdp")
    rows = "fsdp"
    wide_parts = 1

    def __init__(self, mesh):
        self.mesh = mesh
        self.row_shards = mesh.shape["fsdp"]
        self.owners = mesh.shape["fsdp"]
        self.wide_slots = [(i, 0) for i in range(3)]
        self.wide_slots += [None] * (self.owners - 3)
        self.slots = [None] * 3 + list(range(10))
        self.slots += [None] * (self.owners - ITEMS)

    def row_index(self):
        return lax.axis_index("fsdp")

    def group_index(self):
        return lax.axis_index("dp")

    def owner_index(self):
        return lax.axis_index("fsdp")

    def gather_weights(self, chunks):
        gathered = []
        for left, right in chunks:
            gathered.append(
                [lax.all_gather(half, "fsdp", axis=0, tiled=True) for half in (left, right)]
            )
        return gathered

    def gather_images(self, value):
        return lax.all_gather(value, ("dp", "fsdp"), axis=0, tiled=True)

    def sum_group(self, value):
        return lax.psum_scatter(value, "fsdp", scatter_dimension=0, tiled=True)

    def reduce_core(self, partial):
        return partial

    def reduce_first(self, value):
        return value

    def reduce_second(self, value):
        return value

    def reduce_last(self, value):
        shard = lax.psum_scatter(value, "fsdp", scatter_dimension=0, tiled=True)
        return lax.psum(shard.astype(F32), "dp")

    def own_rows(self, shard, dim=-2):
        return shard

    def complete(self, piece):
        return piece

    def to_owners(self, pieces):
        got = lax.all_to_all(pieces, "fsdp", split_axis=0, concat_axis=0, tiled=True)
        return got.reshape(-1, got.shape[2])

    def to_rows(self, whole):
        blocks = whole.reshape(self.row_shards, -1, whole.shape[1])
        return lax.all_to_all(blocks, "fsdp", split_axis=0, concat_axis=0, tiled=True)


class Torus:
    images = ("x", "c", "z", "y")
    rows = ("z", "y")
    chips = ("x", "z", "y")
    wide_parts = 2

    def __init__(self, mesh):
        self.mesh = Mesh(mesh.devices.reshape(2, 2, 4, 2), ("x", "c", "z", "y"))
        self.row_shards = 8
        self.owners = 16
        wide_places = [(1, 0), (2, 1), (1, 1)]
        self.wide_slots = [None] * 16
        self.slots = [None] * 16
        for item, (z, y) in enumerate(wide_places):
            for part in range(2):
                self.wide_slots[(part * 4 + z) * 2 + y] = (item, part)
        free = [i for i in range(16) if self.wide_slots[i] is None]
        for item, slot in enumerate(free):
            self.slots[slot] = item

    def row_index(self):
        return lax.axis_index("z") * 2 + lax.axis_index("y")

    def group_index(self):
        return lax.axis_index("x") * 2 + lax.axis_index("c")

    def owner_index(self):
        return (lax.axis_index("x") * 4 + lax.axis_index("z")) * 2 + lax.axis_index("y")

    def swap(self, value, axis):
        return lax.ppermute(value, axis, [(0, 1), (1, 0)])

    def shift(self, value, by):
        return lax.ppermute(value, "z", [(i, (i + by) % 4) for i in range(4)])

    def exchange(self, value, axis):
        here = lax.axis_index(axis)
        return place([value, self.swap(value, axis)], [here, 1 - here])

    def spread_z(self, value):
        z = lax.axis_index("z")
        ring = [value] + [self.shift(value, by) for by in range(1, 4)]
        return place(ring, [(z - by) % 4 for by in range(4)])

    def gather_weights(self, chunks):
        spread = []
        for left, right in chunks:
            left, right = self.own_rows(left), self.own_rows(right)
            if spread:
                left, right = lax.optimization_barrier((left, right, *spread[-1]))[:2]
            spread.append((self.spread_z(left), self.spread_z(right)))
        done = []
        for left, right in spread:
            if done:
                left, right = lax.optimization_barrier((left, right, *done[-1]))[:2]
            left = self.exchange(left, "y")
            right = self.exchange(right, "x")
            left = self.exchange(left, "x")
            right = self.exchange(right, "y")
            done.append((left, right))
        full = []
        for left, right in done:
            pair = []
            for half, order in ((left, (2, 1, 0)), (right, (2, 0, 1))):
                c = lax.axis_index("c")

                def moves(slot, order=order):
                    found = []
                    for part in range(2):
                        for at in every(2, 2, 4):
                            found.append((part, at, (*[at[i] for i in order], slot[part])))
                    return found

                whole = place([half, self.swap(half, "c")], [c, 1 - c], (4, 2, 2, 2), moves)
                pair.append(whole.reshape(D, -1))
            full.append(pair)
        return full

    def gather_images(self, value):
        shape = (64,) + value.shape[1:]

        def both(v, axis):
            other = self.swap(v, axis)
            first = lax.axis_index(axis) == 0
            return jnp.where(first, jnp.stack([v, other]), jnp.stack([other, v]))

        z = lax.axis_index("z")
        value = both(value, "y")
        ring = jnp.stack([value] + [self.shift(value, by) for by in range(1, 4)])
        value = jnp.take(ring, (z - jnp.arange(4)) % 4, axis=0)
        value = both(value, "c")
        value = both(value, "x")
        return value.reshape(shape)

    def sum_group(self, value):
        blocks = value.reshape(8, -1, *value.shape[1:])
        got = lax.all_to_all(blocks, ("z", "y"), split_axis=0, concat_axis=0, tiled=True)
        return jnp.sum(got, axis=0)

    def halve(self, value, axis, dim):
        here = lax.axis_index(axis)
        take = lambda at: lax.dynamic_index_in_dim(value, at, dim, keepdims=False)
        got = self.swap(take(1 - here), axis)
        return (take(here).astype(F32) + got.astype(F32)).astype(BF16)

    def reduce_core(self, partial):
        return self.halve(partial.reshape(4, 2, 2, 2, D // 32, partial.shape[1]), "c", 3)

    def reduce_first(self, value):
        half = value.shape[-1] // 2
        return (
            self.halve(value[..., :half], "x", 2),
            self.halve(value[..., half:], "y", 1),
        )

    def reduce_second(self, value):
        left = self.halve(value[0], "y", 1)
        right = self.halve(value[1], "x", 1)
        return jnp.concatenate([left, right], axis=-1)

    def reduce_last(self, value):
        z = lax.axis_index("z")
        take = lambda at: lax.dynamic_index_in_dim(value, at, 0, keepdims=False)
        got = [self.shift(take((z + by) % 4), by) for by in range(1, 4)]
        total = take(z).astype(F32)
        for part in got:
            total = total + part.astype(F32)
        return total

    def own_rows(self, shard, dim=-2):
        return lax.dynamic_slice_in_dim(
            shard, self.group_index() * (D // 32), D // 32, dim % shard.ndim
        )

    def complete(self, piece):
        value = self.exchange(piece, "x")
        c = lax.axis_index("c")
        moves = lambda slot: [(part, (x,), (x, slot[part])) for part in range(2) for x in range(2)]
        value = place([value, self.swap(value, "c")], [c, 1 - c], (2, 2), moves)
        return value.reshape(D // 8, -1)

    def to_owners(self, pieces):
        cols = pieces.shape[2]
        got = lax.all_to_all(pieces, self.chips, split_axis=0, concat_axis=0, tiled=True)
        got = got.reshape(2, 4, 2, D // 32, cols)
        c = lax.axis_index("c")

        def moves(slot):
            return [
                (part, (x, z, y), (z, y, x, slot[part]))
                for part in range(2)
                for x, z, y in every(2, 4, 2)
            ]

        whole = place([got, self.swap(got, "c")], [c, 1 - c], (4, 2, 2, 2), moves)
        return whole.reshape(D, cols)

    def to_rows(self, whole):
        cols = whole.shape[1]
        blocks = whole.reshape(4, 2, 2, 2, D // 32, cols)
        blocks = lax.dynamic_index_in_dim(blocks, lax.axis_index("c"), 3, keepdims=False)
        blocks = blocks.transpose(2, 0, 1, 3, 4).reshape(16, D // 32, cols)
        return lax.all_to_all(blocks, self.chips, split_axis=0, concat_axis=0, tiled=True)


def swish_value(values):
    return values / (1.0 + jnp.exp(-values))


def layer_norm(values):
    centred = values - jnp.mean(values, axis=-1, keepdims=True)
    inverse = lax.rsqrt(jnp.mean(centred * centred, axis=-1, keepdims=True) + NORM_EPS)
    return (centred * inverse, inverse)


def norm_back(incoming, normed, inverse):
    return inverse * (
        incoming
        - jnp.mean(incoming, axis=-1, keepdims=True)
        - normed * jnp.mean(incoming * normed, axis=-1, keepdims=True)
    )


def rotate(tensor):
    first, second, third, fourth = jnp.split(tensor, 4, axis=-1)
    return jnp.concatenate([-second, first, -fourth, third], axis=-1)


def rope_tables(extents, positions):
    quarter = HDIM // 4
    places = jnp.arange(positions, dtype=jnp.int32)
    widths = extents[:, 1]
    row_place = (places[None, :] // widths[:, None]).astype(F32)
    col_place = (places[None, :] % widths[:, None]).astype(F32)
    frequency = 10000.0 ** (-jnp.arange(quarter).astype(F32) / quarter)
    row_angle = row_place[:, :, None] * frequency
    col_angle = col_place[:, :, None] * frequency
    cosine_table = jnp.concatenate(
        [jnp.cos(row_angle), jnp.cos(row_angle), jnp.cos(col_angle), jnp.cos(col_angle)], axis=-1
    )
    sine_table = jnp.concatenate(
        [jnp.sin(row_angle), jnp.sin(row_angle), jnp.sin(col_angle), jnp.sin(col_angle)], axis=-1
    )
    return (cosine_table[:, :, None, :], sine_table[:, :, None, :])


def local(
    comm,
    inputs,
    cotangent,
    image_shape,
    time_bins,
    time_table,
    modulation_master,
    projection_master,
    output_master,
    expand_master,
    shrink_master,
    modulation_moment,
    projection_moment,
    output_moment,
    expand_moment,
    shrink_moment,
):
    masters = (modulation_master, projection_master, output_master, expand_master, shrink_master)
    moments = (modulation_moment, projection_moment, output_moment, expand_moment, shrink_moment)
    images, positions, features = inputs.shape
    tokens = images * positions
    rows = modulation_master.shape[1]
    row_index = comm.row_index()

    shrink_low = shrink_master.astype(BF16).T
    chunks = comm.gather_weights(
        [
            (
                jnp.concatenate([projection_master[0], projection_master[1]], axis=1).astype(BF16),
                jnp.concatenate([projection_master[2], output_master], axis=1).astype(BF16),
            ),
            (expand_master[0].astype(BF16), expand_master[1].astype(BF16)),
            (shrink_low[:, : FF // 2], shrink_low[:, FF // 2 :]),
        ]
    )
    (query_key_weight, value_output_weight), (gate_weight, up_weight) = chunks[:2]
    value_weight = value_output_weight[:, :D]
    output_weight = value_output_weight[:, D:]
    shrink_left, shrink_right = chunks[2]

    bins = comm.gather_images(time_bins)
    selector = (
        bins[:, None] == jnp.arange(time_table.shape[0], dtype=jnp.int32)[None, :]
    ).astype(F32)
    active = swish_value(jnp.dot(selector, time_table, precision=HIGHEST)).astype(BF16)
    active_rows = lax.dynamic_slice_in_dim(active, row_index * rows, rows, 1)
    group_images = images * comm.row_shards
    active_group = lax.dynamic_slice_in_dim(
        active_rows, comm.group_index() * group_images, group_images, 0
    )
    modulation = comm.sum_group(
        jnp.einsum(
            "bd,kde->bke", active_group, modulation_master.astype(BF16), preferred_element_type=F32
        )
    )
    shift_one, scale_one, gate_one, shift_two, scale_two, gate_two = [
        modulation[:, which, None, :] for which in range(6)
    ]

    stream = inputs.astype(F32)
    places = jnp.arange(positions, dtype=jnp.int32)
    lengths = image_shape[:, 0] * image_shape[:, 1]
    key_mask = places[None, :] < lengths[:, None]
    cosine_table, sine_table = rope_tables(image_shape, positions)

    def product(left, right, dims=NN):
        return dot(left.reshape(tokens, -1), right, dims).reshape(images, positions, -1)

    def outer(left, right):
        return dot(left.reshape(tokens, -1), right.reshape(tokens, -1), TN).astype(BF16)

    def split_heads(value):
        return value.reshape(images, positions, HEADS, HDIM)

    normed_one, inverse_one = layer_norm(stream)
    first_input = (normed_one * (1.0 + scale_one) + shift_one).astype(BF16)
    query_key = product(first_input, query_key_weight)
    queries, keys = split_heads(query_key[..., :D]), split_heads(query_key[..., D:])
    value_heads = split_heads(product(first_input, value_weight).astype(BF16))
    query_rot = (queries * cosine_table + rotate(queries) * sine_table).astype(BF16)
    key_rot = (keys * cosine_table + rotate(keys) * sine_table).astype(BF16)
    scores = jnp.einsum(
        "bqhd,bkhd->bhqk", query_rot, key_rot, preferred_element_type=F32
    ) * HDIM ** (-0.5)
    scores = jnp.where(key_mask[:, None, None, :], scores, -1000000000.0)
    exponent = jnp.exp(scores - jnp.max(scores, axis=-1, keepdims=True))
    softmax_out = exponent / jnp.sum(exponent, axis=-1, keepdims=True)
    softmax_low = softmax_out.astype(BF16)
    attended = jnp.einsum(
        "bhqk,bkhd->bqhd", softmax_low, value_heads, preferred_element_type=F32
    )
    attended = attended.astype(BF16).reshape(images, positions, features)
    attention = product(attended, output_weight)
    middle = stream + gate_one * attention
    normed_two, inverse_two = layer_norm(middle)
    second_input = (normed_two * (1.0 + scale_two) + shift_two).astype(BF16)
    gate_pre = product(second_input, gate_weight)
    up_pre = product(second_input, up_weight)
    sigmoid_gate = 1.0 / (1.0 + jnp.exp(-gate_pre))
    hidden = (swish_value(gate_pre) * up_pre).astype(BF16)
    branch_out = product(hidden[..., : FF // 2], shrink_left, NT) + product(
        hidden[..., FF // 2 :], shrink_right, NT
    )
    block_output = (middle + gate_two * branch_out).astype(BF16)

    upstream = cotangent.astype(F32) * key_mask[:, :, None].astype(F32)
    grad_gate_two = jnp.sum(upstream * branch_out, axis=1)
    grad_branch = (gate_two * upstream).astype(BF16)
    shrink_sum = comm.reduce_core(outer(grad_branch, hidden))
    grad_hidden = jnp.concatenate(
        [product(grad_branch, shrink_left), product(grad_branch, shrink_right)], axis=-1
    )
    grad_gate = grad_hidden * up_pre * sigmoid_gate * (1.0 + gate_pre * (1.0 - sigmoid_gate))
    grad_up = grad_hidden * gate_pre * sigmoid_gate
    grad_gate, grad_up = grad_gate.astype(BF16), grad_up.astype(BF16)
    grad_gate, grad_up, shrink_sum = lax.optimization_barrier((grad_gate, grad_up, shrink_sum))
    expand_sum = comm.reduce_core(
        outer(second_input, jnp.concatenate([grad_gate, grad_up], axis=-1))
    )
    shrink_sum = comm.reduce_first(shrink_sum)
    grad_second = product(grad_gate, gate_weight, NT) + product(grad_up, up_weight, NT)
    grad_scale_two = jnp.sum(grad_second * normed_two, axis=1)
    grad_shift_two = jnp.sum(grad_second, axis=1)
    grad_stream = upstream + norm_back(grad_second * (1.0 + scale_two), normed_two, inverse_two)
    grad_stream, shrink_sum, expand_sum = lax.optimization_barrier(
        (grad_stream, shrink_sum, expand_sum)
    )
    shrink_sum = comm.reduce_second(shrink_sum)
    expand_sum = comm.reduce_first(expand_sum)
    grad_gate_one = jnp.sum(grad_stream * attention, axis=1)
    grad_attention = (gate_one * grad_stream).astype(BF16)
    grad_output = outer(attended, grad_attention)
    grad_attended = split_heads(product(grad_attention, output_weight, NT).astype(BF16))
    grad_soft = jnp.einsum(
        "bqhd,bkhd->bhqk", grad_attended, value_heads, preferred_element_type=F32
    )
    grad_values = jnp.einsum(
        "bhqk,bqhd->bkhd", softmax_low, grad_attended, preferred_element_type=F32
    )
    grad_scores = softmax_out * (
        grad_soft - jnp.sum(grad_soft * softmax_out, axis=-1, keepdims=True)
    )
    grad_scores = grad_scores.astype(BF16)
    grad_scores, shrink_sum, expand_sum = lax.optimization_barrier(
        (grad_scores, shrink_sum, expand_sum)
    )
    shrink_piece = comm.reduce_last(shrink_sum)
    expand_sum = comm.reduce_second(expand_sum)
    grad_qrot = jnp.einsum(
        "bhqk,bkhd->bqhd", grad_scores, key_rot, preferred_element_type=F32
    ) * HDIM ** (-0.5)
    grad_krot = jnp.einsum(
        "bhqk,bqhd->bkhd", grad_scores, query_rot, preferred_element_type=F32
    ) * HDIM ** (-0.5)
    grad_query = grad_qrot * cosine_table - rotate(grad_qrot * sine_table)
    grad_key = grad_krot * cosine_table - rotate(grad_krot * sine_table)
    grad_project_in = jnp.concatenate(
        [
            v.astype(BF16).reshape(images, positions, features)
            for v in (grad_query, grad_key, grad_values)
        ],
        axis=-1,
    )
    grad_project_in, shrink_piece, expand_sum = lax.optimization_barrier(
        (grad_project_in, shrink_piece, expand_sum)
    )
    expand_piece = comm.reduce_last(expand_sum)
    grad_projection = outer(first_input, grad_project_in)
    attention_sum = comm.reduce_core(jnp.concatenate([grad_projection, grad_output], axis=1))
    grad_first = product(grad_project_in[..., : 2 * D], query_key_weight, NT) + product(
        grad_project_in[..., 2 * D :], value_weight, NT
    )
    grad_scale_one = jnp.sum(grad_first * normed_one, axis=1)
    grad_shift_one = jnp.sum(grad_first, axis=1)
    input_gradient = grad_stream + norm_back(
        grad_first * (1.0 + scale_one), normed_one, inverse_one
    )
    grad_modulation = jnp.concatenate(
        [
            grad_shift_one,
            grad_scale_one,
            grad_gate_one,
            grad_shift_two,
            grad_scale_two,
            grad_gate_two,
        ],
        axis=1,
    ).astype(BF16)
    grad_modulation, attention_sum = lax.optimization_barrier((grad_modulation, attention_sum))
    attention_sum = comm.reduce_first(attention_sum)
    grad_modulation = comm.gather_images(grad_modulation)

    def feed_of(piece, moment):
        return (
            (1.0 + MOMENTUM_DECAY) * piece + MOMENTUM_DECAY * MOMENTUM_DECAY * moment
        ).astype(BF16)

    owner = comm.owner_index()
    wide_feed = [
        feed_of(expand_piece[:, :FF], comm.own_rows(expand_moment[0])),
        feed_of(expand_piece[:, FF:], comm.own_rows(expand_moment[1])),
        feed_of(shrink_piece, comm.own_rows(shrink_moment.T)),
    ]
    empty = jnp.zeros_like(wide_feed[0])
    wide = comm.to_owners(
        jnp.stack([empty if slot is None else wide_feed[slot[0]] for slot in comm.wide_slots])
    )
    active_wide = jnp.array([0 if slot is None else 1 for slot in comm.wide_slots], jnp.int32)[owner]
    wide = newton_schulz(active_wide, wide)
    attention_sum = comm.reduce_second(attention_sum)
    if comm.wide_parts > 1:
        part = jnp.array([0 if slot is None else slot[1] for slot in comm.wide_slots])[owner]
        size = FF // comm.wide_parts
        wide = lax.dynamic_slice_in_dim(wide, part * size, size, 1)
    wide_back = comm.to_rows(wide)

    attention_piece = comm.reduce_last(attention_sum)
    decay = MOMENTUM_DECAY * MOMENTUM_DECAY
    own_moment = comm.own_rows(modulation_moment)
    square_feed = [(decay * own_moment[k]).astype(BF16) for k in range(6)]
    for k in range(3):
        square_feed.append(
            feed_of(attention_piece[:, k * D : (k + 1) * D], comm.own_rows(projection_moment[k]))
        )
    square_feed.append(feed_of(attention_piece[:, 3 * D :], comm.own_rows(output_moment)))
    empty = jnp.zeros_like(square_feed[0])
    square = comm.to_owners(
        jnp.stack([empty if slot is None else square_feed[slot] for slot in comm.slots])
    )
    item = jnp.array([-1 if slot is None else slot for slot in comm.slots], jnp.int32)[owner]
    by_map = jnp.concatenate(
        [grad_modulation.reshape(-1, 6, D), jnp.zeros((grad_modulation.shape[0], 1, D), BF16)], axis=1
    )
    which = jnp.where((item >= 0) & (item < 6), item, 6)
    right = lax.dynamic_index_in_dim(by_map, which, 1, keepdims=False)
    square = newton_schulz((item >= 0).astype(jnp.int32), square, active, right)
    square_back = comm.to_rows(square)

    totals_low = comm.complete(
        jnp.concatenate([expand_piece, shrink_piece, attention_piece], axis=1).astype(BF16)
    ).astype(F32)
    wide_parts = [
        wide_back[comm.wide_slots.index((i, p))]
        for i in range(3)
        for p in range(comm.wide_parts)
    ]
    steps = comm.complete(
        jnp.concatenate(wide_parts + [square_back[comm.slots.index(i)] for i in range(10)], axis=1)
    ).astype(F32)
    modulation_total = jnp.einsum(
        "bd,bke->kde",
        active_rows,
        grad_modulation.reshape(-1, 6, features),
        preferred_element_type=F32,
    )
    after = 3 * FF
    totals = (
        modulation_total,
        jnp.stack([totals_low[:, after + i * D : after + (i + 1) * D] for i in range(3)]),
        totals_low[:, after + 3 * D :],
        jnp.stack([totals_low[:, :FF], totals_low[:, FF : 2 * FF]]),
        totals_low[:, 2 * FF : after].T,
    )
    states = tuple((MOMENTUM_DECAY * moment + total for moment, total in zip(moments, totals)))
    square_step = [steps[:, after + i * D : after + (i + 1) * D] for i in range(10)]
    steps_all = (
        jnp.stack(square_step[:6]),
        jnp.stack(square_step[6:9]),
        square_step[9],
        jnp.stack([steps[:, :FF], steps[:, FF : 2 * FF]]) * (FF / D) ** 0.5,
        steps[:, 2 * FF : after].T,
    )
    updated = tuple((master - LEARN_RATE * step for master, step in zip(masters, steps_all)))
    return (block_output, input_gradient, *totals, *updated, *states)


def solution(mesh):
    if mesh.shape["dp"] == 4 and mesh.shape["fsdp"] == 8:
        comm = Torus(mesh)
    else:
        comm = Plain(mesh)
    images, rows = comm.images, comm.rows
    by_row = (
        P(None, rows, None),
        P(None, rows, None),
        P(rows, None),
        P(None, rows, None),
        P(None, rows),
    )
    return jax.shard_map(
        functools.partial(local, comm),
        mesh=comm.mesh,
        in_specs=(
            P(images, None, None),
            P(images, None, None),
            P(images, None),
            P(images),
            P(),
            *by_row,
            *by_row,
        ),
        out_specs=(P(images, None, None), P(images, None, None), *by_row, *by_row, *by_row),
        check_vma=False,
    )
```

time: 2530 us -> 1760 us (0.70)
  waiting for transfers between devices: 1380 us -> 139 us
  Pallas kernels: 0 us -> 1210 us
  matrix products: 539 us -> 81.8 us
  blocking collectives: 279 us -> 0 us
  local copies, waits for them, and re-layouts: 237 us -> 92.4 us
  starting transfers between devices: 5.81 us -> 143 us
    pallas_call x0 -> x32, Pallas kernels: none -> 1210 us  [the longest x30 1190 us: place(): pl.pallas_call(body, out_shape=jax.ShapeDtypeStruct((*lead, *parts[0].sha...]
    unnamed x15 -> x0, waiting for transfers between devices: 750 us -> none
    dot_general x35 -> x25, matrix products: 533 us -> 65.4 us  [the longest x18 51 us: dot(): return lax.dot_general(a, b, dims, preferred_element_type=F32)]
    all_gather x5 -> x0, waiting for transfers between devices: 324 us -> none  [the longest x1 99.9 us: local(): lax.all_gather(modulation_master.astype(jnp.bfloat16), 'fsdp', axis=1, ti...]
    all_to_all x1 -> x0, blocking collectives: 279 us -> none  [local(): lax.all_to_all(outgoing, 'fsdp', split_axis=1, concat_axis=1, tiled=True)]
    ppermute x0 -> x78, waiting for transfers between devices: none -> 131 us  [the longest x33 67.7 us: shift(): return lax.ppermute(value, 'z', [(i, (i + by) % 4) for i in range(4)])]
    psum x1 -> x0, waiting for transfers between devices: 117 us -> none  [local(): lax.psum((shards[0], shards[1], shards[2], shards[3], shards[4]), 'dp')]
    all_to_all x1 -> x5, waiting for transfers between devices: 118 us -> 7.91 us  [the longest x2 7.9 us: to_rows(): lax.all_to_all(blocks, self.chips, split_axis=0, concat_axis=0, tiled=True)]
  transfers between devices with their start and end apart: 12 -> 83, of which waited for: 12 -> 26; matrix products, arithmetic and copies ran while one was open for 8% -> 8% of each run, Pallas kernels for 0% -> 57%
where the time goes in v1:
time: 1760 us; the launch traced here: 1750 us
  Pallas kernels  1210 us (69%)
  starting transfers between devices  143 us (8%)
  waiting for transfers between devices  139 us (8%)
  local copies, waits for them, and re-layouts  92.4 us (5%)
  matrix products  81.8 us (5%)
  other arithmetic  76.7 us (4%)
    pallas_call x30, Pallas kernels, place(): pl.pallas_call(body, out_shape=jax.ShapeDtypeStruct((*lead, *parts[0].sha...  1190 us
    ppermute x33, waiting for transfers between devices, shift(): return lax.ppermute(value, 'z', [(i, (i + by) % 4) for i in range(4)])  67.7 us
    ppermute x45, waiting for transfers between devices, swap(): return lax.ppermute(value, axis, [(0, 1), (1, 0)])  63.1 us
    unnamed x290, local copies, waits for them, and re-layouts  51.8 us
    dot_general x18, matrix products, dot(): return lax.dot_general(a, b, dims, preferred_element_type=F32)  51 us
    all_to_all x2, starting transfers between devices, to_rows(): lax.all_to_all(blocks, self.chips, split_axis=0, concat_axis=0, tiled=True)  48.3 us
    ppermute x33, starting transfers between devices, shift(): return lax.ppermute(value, 'z', [(i, (i + by) % 4) for i in range(4)])  43.7 us
    ppermute x45, starting transfers between devices, swap(): return lax.ppermute(value, axis, [(0, 1), (1, 0)])  37.1 us
  transfers between devices with their start and end apart: 83, of which 26 were waited for; matrix products, arithmetic and copies ran while one was open for 8% of the time, Pallas kernels for 57%

profile of v1, /device:TPU:0, one launch (start us, length us, event | category | flops | bytes accessed | tf_op | source)
XLA Modules:
  0.0 1751.2 jit_solution(11503495748279867585)
XLA Ops:
  35.9 10.7 place.34.refs_0_
  56.7 19.6 %place.35.refs_0_ = bf16[2,4,24,1536]{3,2,1,0:T(8,128)(2,1)} custom-call(s32[2]{0:T(128)} %pad_add_fusion.2.slot_ref, bf16[4,24,1536]{2,1,0:T(8,128)(2,1)} %place.34.refs_0_, bf16[4,24,1536]{2,1,0:T(8,128)(2,1)} %copy-done.71), custom_call_target="tpu_custom_call" | custom-call | bytes 1179648 | tf_op jit(solution)/shard_map/place/pallas_call | solution.py:182
  78.7 10.7 place.30.refs_0_
  91.5 4.9 collective-permute-done.5
  97.5 19.6 %place.31.refs_0_ = bf16[2,4,24,1536]{3,2,1,0:T(8,128)(2,1)} custom-call(s32[2]{0:T(128)} %pad_add_fusion.3.slot_ref, bf16[4,24,1536]{2,1,0:T(8,128)(2,1)} %place.30.refs_0_, bf16[4,24,1536]{2,1,0:T(8,128)(2,1)} %copy-done.70), custom_call_target="tpu_custom_call" | custom-call | bytes 1179648 | tf_op jit(solution)/shard_map/place/pallas_call | solution.py:182
  117.7 37.5 %place.36.refs_0_ = bf16[2,2,4,24,1536]{4,3,2,1,0:T(8,128)(2,1)} custom-call(s32[2]{0:T(128)} %pad_add_fusion.3.slot_ref, bf16[2,4,24,1536]{3,2,1,0:T(8,128)(2,1)} %place.35.refs_0_, bf16[2,4,24,1536]{3,2,1,0:T(8,128)(2,1)} %collective-permute-done.16.refs_1_), custom_call_target="tpu_custom_call" | custom-call | bytes 2359296 | tf_op jit(solution)/shard_map/place/pallas_call | solution.py:182
  173.6 13.7 place.38.refs_0_
  188.6 13.7 place.39.refs_0_
  202.4 37.7 %place.32.refs_0_ = bf16[2,2,4,24,1536]{4,3,2,1,0:T(8,128)(2,1)} custom-call(s32[2]{0:T(128)} %pad_add_fusion.2.slot_ref, bf16[2,4,24,1536]{3,2,1,0:T(8,128)(2,1)} %place.31.refs_0_, bf16[2,4,24,1536]{3,2,1,0:T(8,128)(2,1)} %collective-permute-done.10.refs_1_), custom_call_target="tpu_custom_call" | custom-call | bytes 2359296 | tf_op jit(solution)/shard_map/place/pallas_call | solution.py:182
  257.2 7.8 place.46.refs_0_
  266.2 7.8 place.47.refs_0_
  274.9 25.6 %place.40.refs_0_ = bf16[2,4,24,2048]{3,2,1,0:T(8,128)(2,1)} custom-call(s32[2]{0:T(128)} %pad_add_fusion.2.slot_ref, bf16[4,24,2048]{2,1,0:T(8,128)(2,1)} %place.38.refs_0_, bf16[4,24,2048]{2,1,0:T(8,128)(2,1)} %copy-done.65), custom_call_target="tpu_custom_call" | custom-call | bytes 1572864 | tf_op jit(solution)/shard_map/place/pallas_call | solution.py:182
  302.7 25.6 %place.43.refs_0_ = bf16[2,4,24,2048]{3,2,1,0:T(8,128)(2,1)} custom-call(s32[2]{0:T(128)} %pad_add_fusion.3.slot_ref, bf16[4,24,2048]{2,1,0:T(8,128)(2,1)} %place.39.refs_0_, bf16[4,24,2048]{2,1,0:T(8,128)(2,1)} %copy-done.64), custom_call_target="tpu_custom_call" | custom-call | bytes 1572864 | tf_op jit(solution)/shard_map/place/pallas_call | solution.py:182
  329.6 73.7 %place.37 = bf16[4,2,2,2,24,1536]{5,4,3,2,1,0:T(8,128)(2,1)} custom-call(s32[2]{0:T(128)} %pad_add_fusion.1.slot_ref, bf16[2,2,4,24,1536]{4,3,2,1,0:T(8,128)(2,1)} %place.36.refs_0_, bf16[2,2,4,24,1536]{4,3,2,1,0:T(8,128)(2,1)} %collective-permute-done.17.refs_1_), custom_call_target="tpu_custom_call" | custom-call | bytes 4718592 | tf_op jit(solution)/shard_map/place/pallas_call | solution.py:182
  410.3 49.4 %place.44.refs_0_ = bf16[2,2,4,24,2048]{4,3,2,1,0:T(8,128)(2,1)} custom-call(s32[2]{0:T(128)} %pad_add_fusion.2.slot_ref, bf16[2,4,24,2048]{3,2,1,0:T(8,128)(2,1)} %place.43.refs_0_, bf16[2,4,24,2048]{3,2,1,0:T(8,128)(2,1)} %collective-permute-done.28.refs_1_), custom_call_target="tpu_custom_call" | custom-call | bytes 3145728 | tf_op jit(solution)/shard_map/place/pallas_call | solution.py:182
  460.2 49.4 %place.41.refs_0_ = bf16[2,2,4,24,2048]{4,3,2,1,0:T(8,128)(2,1)} custom-call(s32[2]{0:T(128)} %pad_add_fusion.3.slot_ref, bf16[2,4,24,2048]{3,2,1,0:T(8,128)(2,1)} %place.40.refs_0_, bf16[2,4,24,2048]{3,2,1,0:T(8,128)(2,1)} %collective-permute-done.25.refs_1_), custom_call_target="tpu_custom_call" | custom-call | bytes 3145728 | tf_op jit(solution)/shard_map/place/pallas_call | solution.py:182
  514.9 6.9 fusion.166
  521.9 73.7 %place.33 = bf16[4,2,2,2,24,1536]{5,4,3,2,1,0:T(8,128)(2,1)} custom-call(s32[2]{0:T(128)} %pad_add_fusion.1.slot_ref, bf16[2,2,4,24,1536]{4,3,2,1,0:T(8,128)(2,1)} %place.32.refs_0_, bf16[2,2,4,24,1536]{4,3,2,1,0:T(8,128)(2,1)} %collective-permute-done.11.refs_1_), custom_call_target="tpu_custom_call" | custom-call | bytes 4718592 | tf_op jit(solution)/shard_map/place/pallas_call | solution.py:182
  598.1 13.8 place.51.refs_0_
  612.5 13.7 place.48.refs_0_
  634.1 25.6 %place.52.refs_0_ = bf16[2,2,4,24,1024]{4,3,2,1,0:T(8,128)(2,1)} custom-call(s32[2]{0:T(128)} %pad_add_fusion.2.slot_ref, bf16[2,4,24,1024]{3,2,1,0:T(8,128)(2,1)} %place.51.refs_0_, bf16[2,4,24,1024]{3,2,1,0:T(8,128)(2,1)} %copy-done.66), custom_call_target="tpu_custom_call" | custom-call | bytes 1572864 | tf_op jit(solution)/shard_map/place/pallas_call | solution.py:182
  660.6 25.6 %place.49.refs_0_ = bf16[2,2,4,24,1024]{4,3,2,1,0:T(8,128)(2,1)} custom-call(s32[2]{0:T(128)} %pad_add_fusion.3.slot_ref, bf16[2,4,24,1024]{3,2,1,0:T(8,128)(2,1)} %place.48.refs_0_, bf16[2,4,24,1024]{3,2,1,0:T(8,128)(2,1)} %copy-done.67), custom_call_target="tpu_custom_call" | custom-call | bytes 1572864 | tf_op jit(solution)/shard_map/place/pallas_call | solution.py:182
  689.1 49.7 %place.53 = bf16[4,2,2,2,24,1024]{5,4,3,2,1,0:T(8,128)(2,1)} custom-call(s32[2]{0:T(128)} %pad_add_fusion.1.slot_ref, bf16[2,2,4,24,1024]{4,3,2,1,0:T(8,128)(2,1)} %place.52.refs_0_, bf16[2,2,4,24,1024]{4,3,2,1,0:T(8,128)(2,1)} %copy-done.59), custom_call_target="tpu_custom_call" | custom-call | bytes 3145728 | tf_op jit(solution)/shard_map/place/pallas_call | solution.py:182
  738.9 49.8 %place.50 = bf16[4,2,2,2,24,1024]{5,4,3,2,1,0:T(8,128)(2,1)} custom-call(s32[2]{0:T(128)} %pad_add_fusion.1.slot_ref, bf16[2,2,4,24,1024]{4,3,2,1,0:T(8,128)(2,1)} %place.49.refs_0_, bf16[2,2,4,24,1024]{4,3,2,1,0:T(8,128)(2,1)} %collective-permute-done.38.refs_1_), custom_call_target="tpu_custom_call" | custom-call | bytes 3145728 | tf_op jit(solution)/shard_map/place/pallas_call | solution.py:182
  795.3 97.5 %place.45 = bf16[4,2,2,2,24,2048]{5,4,3,2,1,0:T(8,128)(2,1)} custom-call(s32[2]{0:T(128)} %pad_add_fusion.1.slot_ref, bf16[2,2,4,24,2048]{4,3,2,1,0:T(8,128)(2,1)} %place.44.refs_0_, bf16[2,2,4,24,2048]{4,3,2,1,0:T(8,128)(2,1)} %collective-permute-done.29.refs_1_), custom_call_target="tpu_custom_call" | custom-call | bytes 6291456 | tf_op jit(solution)/shard_map/place/pallas_call | solution.py:182
  892.8 5.7 fusion.167
  898.6 97.3 %place.42 = bf16[4,2,2,2,24,2048]{5,4,3,2,1,0:T(8,128)(2,1)} custom-call(s32[2]{0:T(128)} %pad_add_fusion.1.slot_ref, bf16[2,2,4,24,2048]{4,3,2,1,0:T(8,128)(2,1)} %place.41.refs_0_, bf16[2,2,4,24,2048]{4,3,2,1,0:T(8,128)(2,1)} %collective-permute-done.26.refs_1_), custom_call_target="tpu_custom_call" | custom-call | bytes 6291456 | tf_op jit(solution)/shard_map/place/pallas_call | solution.py:182
  996.0 8.3 multiply_convert_fusion.1
  1058.3 9.4 multiply_convert_fusion
  1078.7 15.0 collective-permute-done.48
  1135.0 12.6 collective-permute-done.63
  1174.4 14.3 collective-permute-done.59
  1188.6 13.0 collective-permute-done.58
  1211.8 5.5 collective-permute-done.66
  1226.8 8.1 collective-permute-done.70
  1242.3 5.4 all-to-all-start.3
  1252.5 13.6 collective-permute-done.72.refs_1_
  1266.0 28.6 %place.54.refs_0_ = bf16[2,24,9216]{2,1,0:T(8,128)(2,1)} custom-call(s32[2]{0:T(128)} %pad_add_fusion.3.slot_ref, bf16[24,9216]{1,0:T(8,128)(2,1)} %copy-done.39, bf16[24,9216]{1,0:T(8,128)(2,1)} %collective-permute-done.72.refs_1_), custom_call_target="tpu_custom_call" | custom-call | bytes 1769472 | tf_op jit(solution)/shard_map/place/pallas_call | solution.py:182
  1295.2 97.3 %place.56 = bf16[4,2,2,2,24,2048]{5,4,3,2,1,0:T(8,128)(2,1)} custom-call(s32[2]{0:T(128)} %pad_add_fusion.1.slot_ref, bf16[2,4,2,24,2048]{4,3,2,1,0:T(8,128)(2,1)} %bitcast.143.refs_0_, bf16[2,4,2,24,2048]{4,3,2,1,0:T(8,128)(2,1)} %collective-permute-done.74.refs_1_), custom_call_target="tpu_custom_call" | custom-call | bytes 6291456 | tf_op jit(solution)/shard_map/place/pallas_call | solution.py:182
  1395.3 55.4 %place.55 = bf16[2,2,24,9216]{3,2,1,0:T(8,128)(2,1)} custom-call(s32[2]{0:T(128)} %pad_add_fusion.1.slot_ref, bf16[2,24,9216]{2,1,0:T(8,128)(2,1)} %place.54.refs_0_, bf16[2,24,9216]{2,1,0:T(8,128)(2,1)} %collective-permute-done.73.refs_1_), custom_call_target="tpu_custom_call" | custom-call | bytes 3538944 | tf_op jit(solution)/shard_map/place/pallas_call | solution.py:182
  1455.5 41.2 %all-to-all-start.2 = ((bf16[16,24,1024]{2,1,0:T(8,128)(2,1)}), bf16[16,24,1024]{2,1,0:T(8,128)(2,1)}, u32[]{:S(2)}, u32[]{:S(2)}) async-start(bf16[16,24,1024]{2,1,0:T(8,128)(2,1)} %bitcast.149), calls=%async_computation.2 | async-start | bytes 1572864 | tf_op jit(solution)/shard_map/all_to_all | solution.py:425
  1496.7 37.8 %place.57 = bf16[4,2,2,2,24,768]{5,4,3,2,1,0:T(8,128)(2,1)} custom-call(s32[2]{0:T(128)} %pad_add_fusion.1.slot_ref, bf16[2,4,2,24,768]{4,3,2,1,0:T(8,128)(2,1)} %bitcast.165.refs_0_, bf16[2,4,2,24,768]{4,3,2,1,0:T(8,128)(2,1)} %collective-permute-done.75.refs_1_), custom_call_target="tpu_custom_call" | custom-call | bytes 2359296 | tf_op jit(solution)/shard_map/place/pallas_call | solution.py:182
  1535.8 18.7 %newton_schulz.3 = bf16[768,768]{1,0:T(8,128)(2,1)S(1)} custom-call(s32[1]{0:T(128)} %bitcast.157.active_ref, bf16[768,768]{1,0:T(8,128)(2,1)S(1)} %bitcast.498, bf16[64,768]{1,0:T(8,128)(2,1)S(1)} %copy-done.5, bf16[64,768]{1,0:T(8,128)(2,1)S(1)} %bitcast.500), custom_call_target="tpu_custom_call" | custom-call | flops 18119393280 | bytes 2359296 | tf_op jit(solution)/shard_map/newton_schulz/pallas_call | solution.py:139
  1555.5 7.0 all-to-all-start.4
  1571.0 7.9 all-to-all-done.4
  1597.3 10.6 collective-permute-done.76.refs_1_
  1607.8 42.0 %place.58.refs_0_ = bf16[2,24,13824]{2,1,0:T(8,128)(2,1)} custom-call(s32[2]{0:T(128)} %pad_add_fusion.3.slot_ref, bf16[24,13824]{1,0:T(8,128)(2,1)} %constant_dynamic-update-slice_fusion.30.refs_0_, bf16[24,13824]{1,0:T(8,128)(2,1)} %collective-permute-done.76.refs_1_), custom_call_target="tpu_custom_call" | custom-call | bytes 2654208 | tf_op jit(solution)/shard_map/place/pallas_call | solution.py:182
  1657.1 82.2 %place.59 = bf16[2,2,24,13824]{3,2,1,0:T(8,128)(2,1)} custom-call(s32[2]{0:T(128)} %pad_add_fusion.1.slot_ref, bf16[2,24,13824]{2,1,0:T(8,128)(2,1)} %place.58.refs_0_, bf16[2,24,13824]{2,1,0:T(8,128)(2,1)} %collective-permute-done.77.refs_1_), custom_call_target="tpu_custom_call" | custom-call | bytes 5308416 | tf_op jit(solution)/shard_map/place/pallas_call | solution.py:182
  (640 shorter events, 344.2 us)
Async XLA Ops:
  4.9 73.1 %collective-permute-start.6 = (bf16[24,1536]{1,0:T(8,128)(2,1)}, bf16[24,1536]{1,0:T(8,128)(2,1)}, u32[]{:S(2)}, u32[]{:S(2)}) collective-permute-start(bf16[24,1536]{1,0:T(8,128)(2,1)} %fusion.111.refs_0_), channel_id=1, source_target_pairs={{0,2},{2,4},{4,6},{6,0},{1,3},{3,5},{5,7},{7,1},{8,10},{10,12},{12... | collective-permute-start | bytes 221192 | tf_op jit(solution)/shard_map/ppermute | solution.py:296
  8.0 70.1 %collective-permute-start.7 = (bf16[24,1536]{1,0:T(8,128)(2,1)}, bf16[24,1536]{1,0:T(8,128)(2,1)}, u32[]{:S(2)}, u32[]{:S(2)}) collective-permute-start(bf16[24,1536]{1,0:T(8,128)(2,1)} %fusion.111.refs_0_), channel_id=1, source_target_pairs={{0,4},{2,6},{4,0},{6,2},{1,5},{3,7},{5,1},{7,3},{8,12},{10,14},{12... | collective-permute-start | bytes 221192 | tf_op jit(solution)/shard_map/ppermute | solution.py:296
  11.9 19.4 %collective-permute-start.12 = (bf16[24,1536]{1,0:T(8,128)(2,1)}, bf16[24,1536]{1,0:T(8,128)(2,1)}, u32[]{:S(2)}, u32[]{:S(2)}) collective-permute-start(bf16[24,1536]{1,0:T(8,128)(2,1)} %fusion.110.refs_0_), channel_id=1, source_target_pairs={{0,2},{2,4},{4,6},{6,0},{1,3},{3,5},{5,7},{7,1},{8,10},{10,12},{12... | collective-permute-start | bytes 221192 | tf_op jit(solution)/shard_map/ppermute | solution.py:296
  12.0 20.2 %collective-permute-start.13 = (bf16[24,1536]{1,0:T(8,128)(2,1)}, bf16[24,1536]{1,0:T(8,128)(2,1)}, u32[]{:S(2)}, u32[]{:S(2)}) collective-permute-start(bf16[24,1536]{1,0:T(8,128)(2,1)} %fusion.110.refs_0_), channel_id=1, source_target_pairs={{0,4},{2,6},{4,0},{6,2},{1,5},{3,7},{5,1},{7,3},{8,12},{10,14},{12... | collective-permute-start | bytes 221192 | tf_op jit(solution)/shard_map/ppermute | solution.py:296
  13.9 15.5 collective-permute-start
  31.3 46.7 %collective-permute-start.8 = (bf16[24,1536]{1,0:T(8,128)(2,1)}, bf16[24,1536]{1,0:T(8,128)(2,1)S(1)}, u32[]{:S(2)}, u32[]{:S(2)}) collective-permute-start(bf16[24,1536]{1,0:T(8,128)(2,1)} %fusion.111.refs_0_), channel_id=1, source_target_pairs={{0,6},{2,0},{4,2},{6,4},{1,7},{3,1},{5,3},{7,5},{8,14},{10,8},{12,... | collective-permute-start | bytes 221192 | tf_op jit(solution)/shard_map/ppermute | solution.py:296
  52.9 25.1 %collective-permute-start.4 = (s32[4,2,2]{2,1,0:T(2,128)S(1)}, s32[4,2,2]{2,1,0:T(2,128)S(1)}, u32[]{:S(2)}, u32[]{:S(2)}) collective-permute-start(s32[4,2,2]{2,1,0:T(2,128)S(1)} %broadcast_select_fusion.7), channel_id=1, source_target_pairs={{0,8},{8,0},{1,9},{9,1},{2,10},{10,2},{3,11},{11,3},{4,12},{12,4},... | collective-permute-start | bytes 200 | tf_op jit(solution)/shard_map/ppermute | solution.py:293
  76.4 41.3 %collective-permute-start.16 = (bf16[2,4,24,1536]{3,2,1,0:T(8,128)(2,1)}, bf16[2,4,24,1536]{3,2,1,0:T(8,128)(2,1)}, u32[]{:S(2)}, u32[]{:S(2)}) collective-permute-start(bf16[2,4,24,1536]{3,2,1,0:T(8,128)(2,1)} %place.35.refs_0_), channel_id=1, source_target_pairs={{0,16},{16,0},{1,17},{17,1},{2,18},{18,2},{3,19},{19,3},{4,20},{20... | collective-permute-start | bytes 1769480 | tf_op jit(solution)/shard_map/ppermute | solution.py:293
  117.1 85.2 %collective-permute-start.10 = (bf16[2,4,24,1536]{3,2,1,0:T(8,128)(2,1)}, bf16[2,4,24,1536]{3,2,1,0:T(8,128)(2,1)}, u32[]{:S(2)}, u32[]{:S(2)}) collective-permute-start(bf16[2,4,24,1536]{3,2,1,0:T(8,128)(2,1)} %place.31.refs_0_), channel_id=1, source_target_pairs={{0,1},{1,0},{2,3},{3,2},{4,5},{5,4},{6,7},{7,6},{8,9},{9,8},{10,11... | collective-permute-start | bytes 1769480 | tf_op jit(solution)/shard_map/ppermute | solution.py:293
  155.2 174.4 %collective-permute-start.17 = (bf16[2,2,4,24,1536]{4,3,2,1,0:T(8,128)(2,1)}, bf16[2,2,4,24,1536]{4,3,2,1,0:T(8,128)(2,1)}, u32[]{:S(2)}, u32[]{:S(2)}) collective-permute-start(bf16[2,2,4,24,1536]{4,3,2,1,0:T(8,128)(2,1)} %place.36.refs_0_), channel_id=1, source_target_pairs={{0,8},{8,0},{1,9},{9,1},{2,10},{10,2},{3,11},{11,3},{4,12},{12,4},... | collective-permute-start | bytes 3538952 | tf_op jit(solution)/shard_map/ppermute | solution.py:293
  162.1 111.9 %all-to-all-start = ((f32[8,2,6,768]{3,1,2,0:T(2,128)}), f32[8,2,6,768]{3,1,2,0:T(2,128)S(1)}, u32[]{:S(2)}, u32[]{:S(2)}) async-start(f32[8,2,6,768]{3,1,2,0:T(2,128)} %copy.129), calls=%async_computation | async-start | bytes 589824 | tf_op jit(solution)/shard_map/all_to_all | solution.py:359
  166.1 21.2 %collective-permute-start.21 = (bf16[24,2048]{1,0:T(8,128)(2,1)S(1)}, bf16[24,2048]{1,0:T(8,128)(2,1)S(1)}, u32[]{:S(2)}, u32[]{:S(2)}) collective-permute-start(bf16[24,2048]{1,0:T(8,128)(2,1)S(1)} %copy-done.68), channel_id=1, source_target_pairs={{0,2},{2,4},{4,6},{6,0},{1,3},{3,5},{5,7},{7,1},{8,10},{10,12},{12... | collective-permute-start | bytes 294920 | tf_op jit(solution)/shard_map/ppermute | solution.py:296
  168.2 19.1 %collective-permute-start.22 = (bf16[24,2048]{1,0:T(8,128)(2,1)S(1)}, bf16[24,2048]{1,0:T(8,128)(2,1)S(1)}, u32[]{:S(2)}, u32[]{:S(2)}) collective-permute-start(bf16[24,2048]{1,0:T(8,128)(2,1)S(1)} %copy-done.68), channel_id=1, source_target_pairs={{0,4},{2,6},{4,0},{6,2},{1,5},{3,7},{5,1},{7,3},{8,12},{10,14},{12... | collective-permute-start | bytes 294920 | tf_op jit(solution)/shard_map/ppermute | solution.py:296
  170.6 16.8 collective-permute-start.23
  240.0 34.1 %collective-permute-start.24 = (bf16[4,24,2048]{2,1,0:T(8,128)(2,1)S(1)}, bf16[4,24,2048]{2,1,0:T(8,128)(2,1)S(1)}, u32[]{:S(2)}, u32[]{:S(2)}) collective-permute-start(bf16[4,24,2048]{2,1,0:T(8,128)(2,1)S(1)} %copy-done.44), channel_id=1, source_target_pairs={{0,1},{1,0},{2,3},{3,2},{4,5},{5,4},{6,7},{7,6},{8,9},{9,8},{10,11... | collective-permute-start | bytes 1179656 | tf_op jit(solution)/shard_map/ppermute | solution.py:293
  241.6 60.4 %collective-permute-start.27 = (bf16[4,24,2048]{2,1,0:T(8,128)(2,1)S(1)}, bf16[4,24,2048]{2,1,0:T(8,128)(2,1)S(1)}, u32[]{:S(2)}, u32[]{:S(2)}) collective-permute-start(bf16[4,24,2048]{2,1,0:T(8,128)(2,1)S(1)} %copy-done.45), channel_id=1, source_target_pairs={{0,16},{16,0},{1,17},{17,1},{2,18},{18,2},{3,19},{19,3},{4,20},{20... | collective-permute-start | bytes 1179656 | tf_op jit(solution)/shard_map/ppermute | solution.py:293
  300.5 159.7 %collective-permute-start.25 = (bf16[2,4,24,2048]{3,2,1,0:T(8,128)(2,1)}, bf16[2,4,24,2048]{3,2,1,0:T(8,128)(2,1)}, u32[]{:S(2)}, u32[]{:S(2)}) collective-permute-start(bf16[2,4,24,2048]{3,2,1,0:T(8,128)(2,1)} %place.40.refs_0_), channel_id=1, source_target_pairs={{0,16},{16,0},{1,17},{17,1},{2,18},{18,2},{3,19},{19,3},{4,20},{20... | collective-permute-start | bytes 2359304 | tf_op jit(solution)/shard_map/ppermute | solution.py:293
  328.3 82.0 %collective-permute-start.28 = (bf16[2,4,24,2048]{3,2,1,0:T(8,128)(2,1)}, bf16[2,4,24,2048]{3,2,1,0:T(8,128)(2,1)}, u32[]{:S(2)}, u32[]{:S(2)}) collective-permute-start(bf16[2,4,24,2048]{3,2,1,0:T(8,128)(2,1)} %place.43.refs_0_), channel_id=1, source_target_pairs={{0,1},{1,0},{2,3},{3,2},{4,5},{5,4},{6,7},{7,6},{8,9},{9,8},{10,11... | collective-permute-start | bytes 2359304 | tf_op jit(solution)/shard_map/ppermute | solution.py:293
  329.5 192.3 %collective-permute-start.11 = (bf16[2,2,4,24,1536]{4,3,2,1,0:T(8,128)(2,1)}, bf16[2,2,4,24,1536]{4,3,2,1,0:T(8,128)(2,1)}, u32[]{:S(2)}, u32[]{:S(2)}) collective-permute-start(bf16[2,2,4,24,1536]{4,3,2,1,0:T(8,128)(2,1)} %place.32.refs_0_), channel_id=1, source_target_pairs={{0,8},{8,0},{1,9},{9,1},{2,10},{10,2},{3,11},{11,3},{4,12},{12,4},... | collective-permute-start | bytes 3538952 | tf_op jit(solution)/shard_map/ppermute | solution.py:293
  459.8 335.6 %collective-permute-start.29 = (bf16[2,2,4,24,2048]{4,3,2,1,0:T(8,128)(2,1)}, bf16[2,2,4,24,2048]{4,3,2,1,0:T(8,128)(2,1)}, u32[]{:S(2)}, u32[]{:S(2)}) collective-permute-start(bf16[2,2,4,24,2048]{4,3,2,1,0:T(8,128)(2,1)} %place.44.refs_0_), channel_id=1, source_target_pairs={{0,8},{8,0},{1,9},{9,1},{2,10},{10,2},{3,11},{11,3},{4,12},{12,4},... | collective-permute-start | bytes 4718600 | tf_op jit(solution)/shard_map/ppermute | solution.py:293
  509.6 388.9 %collective-permute-start.26 = (bf16[2,2,4,24,2048]{4,3,2,1,0:T(8,128)(2,1)}, bf16[2,2,4,24,2048]{4,3,2,1,0:T(8,128)(2,1)}, u32[]{:S(2)}, u32[]{:S(2)}) collective-permute-start(bf16[2,2,4,24,2048]{4,3,2,1,0:T(8,128)(2,1)} %place.41.refs_0_), channel_id=1, source_target_pairs={{0,8},{8,0},{1,9},{9,1},{2,10},{10,2},{3,11},{11,3},{4,12},{12,4},... | collective-permute-start | bytes 4718600 | tf_op jit(solution)/shard_map/ppermute | solution.py:293
  509.9 88.2 %collective-permute-start.39 = (bf16[4,24,1024]{2,1,0:T(8,128)(2,1)S(1)}, bf16[4,24,1024]{2,1,0:T(8,128)(2,1)}, u32[]{:S(2)}, u32[]{:S(2)}) collective-permute-start(bf16[4,24,1024]{2,1,0:T(8,128)(2,1)S(1)} %copy-done.54), channel_id=1, source_target_pairs={{0,16},{16,0},{1,17},{17,1},{2,18},{18,2},{3,19},{19,3},{4,20},{20... | collective-permute-start | bytes 589832 | tf_op jit(solution)/shard_map/ppermute | solution.py:293
  510.5 102.0 %collective-permute-start.36 = (bf16[4,24,1024]{2,1,0:T(8,128)(2,1)S(1)}, bf16[4,24,1024]{2,1,0:T(8,128)(2,1)}, u32[]{:S(2)}, u32[]{:S(2)}) collective-permute-start(bf16[4,24,1024]{2,1,0:T(8,128)(2,1)S(1)} %copy-done.53), channel_id=1, source_target_pairs={{0,1},{1,0},{2,3},{3,2},{4,5},{5,4},{6,7},{7,6},{8,9},{9,8},{10,11... | collective-permute-start | bytes 589832 | tf_op jit(solution)/shard_map/ppermute | solution.py:293
  611.9 21.4 %collective-permute-start.40 = (bf16[2,4,24,1024]{3,2,1,0:T(8,128)(2,1)}, bf16[2,4,24,1024]{3,2,1,0:T(8,128)(2,1)S(1)}, u32[]{:S(2)}, u32[]{:S(2)}) collective-permute-start(bf16[2,4,24,1024]{3,2,1,0:T(8,128)(2,1)} %place.51.refs_0_), channel_id=1, source_target_pairs={{0,1},{1,0},{2,3},{3,2},{4,5},{5,4},{6,7},{7,6},{8,9},{9,8},{10,11... | collective-permute-start | bytes 1179656 | tf_op jit(solution)/shard_map/ppermute | solution.py:293
  626.2 33.6 %collective-permute-start.37 = (bf16[2,4,24,1024]{3,2,1,0:T(8,128)(2,1)}, bf16[2,4,24,1024]{3,2,1,0:T(8,128)(2,1)S(1)}, u32[]{:S(2)}, u32[]{:S(2)}) collective-permute-start(bf16[2,4,24,1024]{3,2,1,0:T(8,128)(2,1)} %place.48.refs_0_), channel_id=1, source_target_pairs={{0,16},{16,0},{1,17},{17,1},{2,18},{18,2},{3,19},{19,3},{4,20},{20... | collective-permute-start | bytes 1179656 | tf_op jit(solution)/shard_map/ppermute | solution.py:293
  659.7 28.5 %collective-permute-start.41 = (bf16[2,2,4,24,1024]{4,3,2,1,0:T(8,128)(2,1)}, bf16[2,2,4,24,1024]{4,3,2,1,0:T(8,128)(2,1)S(1)}, u32[]{:S(2)}, u32[]{:S(2)}) collective-permute-start(bf16[2,2,4,24,1024]{4,3,2,1,0:T(8,128)(2,1)} %place.52.refs_0_), channel_id=1, source_target_pairs={{0,8},{8,0},{1,9},{9,1},{2,10},{10,2},{3,11},{11,3},{4,12},{12,4},... | collective-permute-start | bytes 2359304 | tf_op jit(solution)/shard_map/ppermute | solution.py:293
  686.2 52.7 %collective-permute-start.38 = (bf16[2,2,4,24,1024]{4,3,2,1,0:T(8,128)(2,1)}, bf16[2,2,4,24,1024]{4,3,2,1,0:T(8,128)(2,1)}, u32[]{:S(2)}, u32[]{:S(2)}) collective-permute-start(bf16[2,2,4,24,1024]{4,3,2,1,0:T(8,128)(2,1)} %place.49.refs_0_), channel_id=1, source_target_pairs={{0,8},{8,0},{1,9},{9,1},{2,10},{10,2},{3,11},{11,3},{4,12},{12,4},... | collective-permute-start | bytes 2359304 | tf_op jit(solution)/shard_map/ppermute | solution.py:293
  1009.1 16.2 collective-permute-start.42
  1074.5 19.2 %collective-permute-start.48 = (bf16[4,2,24,2048]{3,2,0,1:T(8,128)(2,1)S(1)}, bf16[4,2,24,2048]{3,2,0,1:T(8,128)(2,1)S(1)}, u32[]{:S(2)}, u32[]{:S(2)}) collective-permute-start(bf16[4,2,24,2048]{3,2,0,1:T(8,128)(2,1)S(1)} %dynamic-slice_bitcast_fusion.2), channel_id=1, source_target_pairs={{0,16},{16,0},{1,17},{17,1},{2,18},{18,2},{3,19},{19,3},{4,20},{20... | collective-permute-start | bytes 2359304 | tf_op jit(solution)/shard_map/ppermute | solution.py:293
  1077.6 17.9 %collective-permute-start.49 = (bf16[4,2,24,2048]{3,2,0,1:T(8,128)(2,1)S(1)}, bf16[4,2,24,2048]{3,2,0,1:T(8,128)(2,1)S(1)}, u32[]{:S(2)}, u32[]{:S(2)}) collective-permute-start(bf16[4,2,24,2048]{3,2,0,1:T(8,128)(2,1)S(1)} %dynamic-slice_bitcast_fusion.1), channel_id=1, source_target_pairs={{0,1},{1,0},{2,3},{3,2},{4,5},{5,4},{6,7},{7,6},{8,9},{9,8},{10,11... | collective-permute-start | bytes 2359304 | tf_op jit(solution)/shard_map/ppermute | solution.py:293
  1126.0 35.8 %collective-permute-start.55 = (bf16[4,2,2,24,3072]{4,3,0,2,1:T(8,128)(2,1)}, bf16[4,2,2,24,3072]{4,3,0,2,1:T(8,128)(2,1)}, u32[]{:S(2)}, u32[]{:S(2)}) collective-permute-start(bf16[4,2,2,24,3072]{4,3,0,2,1:T(8,128)(2,1)} %bitcast.494), channel_id=1, source_target_pairs={{0,8},{8,0},{1,9},{9,1},{2,10},{10,2},{3,11},{11,3},{4,12},{12,4},... | collective-permute-start | bytes 7077896 | tf_op jit(solution)/shard_map/ppermute | solution.py:293
  1129.7 17.9 %collective-permute-start.63 = (bf16[24,4096]{1,0:T(8,128)(2,1)S(1)}, bf16[24,4096]{1,0:T(8,128)(2,1)S(1)}, u32[]{:S(2)}, u32[]{:S(2)}) collective-permute-start(bf16[24,4096]{1,0:T(8,128)(2,1)S(1)} %get-tuple-element.153), channel_id=1, source_target_pairs={{0,4},{2,6},{4,0},{6,2},{1,5},{3,7},{5,1},{7,3},{8,12},{10,14},{12... | collective-permute-start | bytes 589832 | tf_op jit(solution)/shard_map/ppermute | solution.py:296
  1129.7 17.9 %collective-permute-start.62 = (bf16[24,4096]{1,0:T(8,128)(2,1)S(1)}, bf16[24,4096]{1,0:T(8,128)(2,1)S(1)}, u32[]{:S(2)}, u32[]{:S(2)}) collective-permute-start(bf16[24,4096]{1,0:T(8,128)(2,1)S(1)} %get-tuple-element.151), channel_id=1, source_target_pairs={{0,2},{2,4},{4,6},{6,0},{1,3},{3,5},{5,7},{7,1},{8,10},{10,12},{12... | collective-permute-start | bytes 589832 | tf_op jit(solution)/shard_map/ppermute | solution.py:296
  1157.1 67.2 %all-to-all-start.1 = ((bf16[16,24,2048]{2,1,0:T(8,128)(2,1)}), bf16[16,24,2048]{2,1,0:T(8,128)(2,1)}, u32[]{:S(2)}, u32[]{:S(2)}) async-start(bf16[16,24,2048]{2,1,0:T(8,128)(2,1)} %constant_dynamic-update-slice_fusion.6), calls=%async_computation.1 | async-start | bytes 3145728 | tf_op jit(solution)/shard_map/all_to_all | solution.py:406
  1167.4 39.7 %collective-permute-start.65 = (bf16[4,2,24,1536]{3,2,0,1:T(8,128)(2,1)}, bf16[4,2,24,1536]{3,2,0,1:T(8,128)(2,1)}, u32[]{:S(2)}, u32[]{:S(2)}) collective-permute-start(bf16[4,2,24,1536]{3,2,0,1:T(8,128)(2,1)} %dynamic-slice_bitcast_fusion.4), channel_id=1, source_target_pairs={{0,16},{16,0},{1,17},{17,1},{2,18},{18,2},{3,19},{19,3},{4,20},{20... | collective-permute-start | bytes 1769480 | tf_op jit(solution)/shard_map/ppermute | solution.py:293
  1168.9 41.0 %collective-permute-start.67 = (bf16[4,2,24,1536]{3,2,0,1:T(8,128)(2,1)S(1)}, bf16[4,2,24,1536]{3,2,0,1:T(8,128)(2,1)}, u32[]{:S(2)}, u32[]{:S(2)}) collective-permute-start(bf16[4,2,24,1536]{3,2,0,1:T(8,128)(2,1)S(1)} %dynamic-slice_bitcast_fusion.3), channel_id=1, source_target_pairs={{0,1},{1,0},{2,3},{3,2},{4,5},{5,4},{6,7},{7,6},{8,9},{9,8},{10,11... | collective-permute-start | bytes 1769480 | tf_op jit(solution)/shard_map/ppermute | solution.py:293
  1169.6 19.0 %collective-permute-start.59 = (bf16[2,2,4608]{2,1,0:T(2,128)(2,1)S(1)}, bf16[2,2,4608]{2,1,0:T(2,128)(2,1)S(1)}, u32[]{:S(2)}, u32[]{:S(2)}) collective-permute-start(bf16[2,2,4608]{2,1,0:T(2,128)(2,1)S(1)} %broadcast_select_fusion.5), channel_id=1, source_target_pairs={{0,6},{2,0},{4,2},{6,4},{1,7},{3,1},{5,3},{7,5},{8,14},{10,8},{12,... | collective-permute-start | bytes 110600 | tf_op jit(solution)/shard_map/ppermute | solution.py:296
  1172.9 28.7 %collective-permute-start.58 = (bf16[2,2,4608]{2,1,0:T(2,128)(2,1)S(1)}, bf16[2,2,4608]{2,1,0:T(2,128)(2,1)S(1)}, u32[]{:S(2)}, u32[]{:S(2)}) collective-permute-start(bf16[2,2,4608]{2,1,0:T(2,128)(2,1)S(1)} %broadcast_select_fusion.5), channel_id=1, source_target_pairs={{0,4},{2,6},{4,0},{6,2},{1,5},{3,7},{5,1},{7,3},{8,12},{10,14},{12... | collective-permute-start | bytes 110600 | tf_op jit(solution)/shard_map/ppermute | solution.py:296
  1172.9 28.7 %collective-permute-start.57 = (bf16[2,2,4608]{2,1,0:T(2,128)(2,1)S(1)}, bf16[2,2,4608]{2,1,0:T(2,128)(2,1)S(1)}, u32[]{:S(2)}, u32[]{:S(2)}) collective-permute-start(bf16[2,2,4608]{2,1,0:T(2,128)(2,1)S(1)} %broadcast_select_fusion.5), channel_id=1, source_target_pairs={{0,2},{2,4},{4,6},{6,0},{1,3},{3,5},{5,7},{7,1},{8,10},{10,12},{12... | collective-permute-start | bytes 110600 | tf_op jit(solution)/shard_map/ppermute | solution.py:296
  1205.1 18.0 %collective-permute-start.61 = (bf16[2,4,2,2,4608]{4,3,2,1,0:T(2,128)(2,1)S(1)}, bf16[2,4,2,2,4608]{4,3,2,1,0:T(2,128)(2,1)S(1)}, u32[]{:S(2)}, u32[]{:S(2)}) collective-permute-start(bf16[2,4,2,2,4608]{4,3,2,1,0:T(2,128)(2,1)S(1)} %broadcast_select_fusion.1), channel_id=1, source_target_pairs={{0,16},{16,0},{1,17},{17,1},{2,18},{18,2},{3,19},{19,3},{4,20},{20... | collective-permute-start | bytes 884744 | tf_op jit(solution)/shard_map/ppermute | solution.py:293
  1224.4 70.8 %collective-permute-start.74 = (bf16[2,4,2,24,2048]{4,3,2,1,0:T(8,128)(2,1)}, bf16[2,4,2,24,2048]{4,3,2,1,0:T(8,128)(2,1)}, u32[]{:S(2)}, u32[]{:S(2)}) collective-permute-start(bf16[2,4,2,24,2048]{4,3,2,1,0:T(8,128)(2,1)} %bitcast.143.refs_0_), channel_id=1, source_target_pairs={{0,8},{8,0},{1,9},{9,1},{2,10},{10,2},{3,11},{11,3},{4,12},{12,4},... | collective-permute-start | bytes 4718600 | tf_op jit(solution)/shard_map/ppermute | solution.py:293
  1242.3 52.4 %all-to-all-start.3 = ((bf16[16,24,768]{2,1,0:T(8,128)(2,1)}), bf16[16,24,768]{2,1,0:T(8,128)(2,1)}, u32[]{:S(2)}, u32[]{:S(2)}) async-start(bf16[16,24,768]{2,1,0:T(8,128)(2,1)} %constant_dynamic-update-slice_fusion.16), calls=%async_computation.3 | async-start | bytes 1179648 | tf_op jit(solution)/shard_map/all_to_all | solution.py:406
  1247.8 18.2 %collective-permute-start.72 = (bf16[24,9216]{1,0:T(8,128)(2,1)S(1)}, bf16[24,9216]{1,0:T(8,128)(2,1)}, u32[]{:S(2)}, u32[]{:S(2)}) collective-permute-start(bf16[24,9216]{1,0:T(8,128)(2,1)S(1)} %pad_maximum_fusion.6.refs_0_), channel_id=1, source_target_pairs={{0,16},{16,0},{1,17},{17,1},{2,18},{18,2},{3,19},{19,3},{4,20},{20... | collective-permute-start | bytes 1327112 | tf_op jit(solution)/shard_map/ppermute | solution.py:293
  1294.6 100.7 %collective-permute-start.73 = (bf16[2,24,9216]{2,1,0:T(8,128)(2,1)}, bf16[2,24,9216]{2,1,0:T(8,128)(2,1)}, u32[]{:S(2)}, u32[]{:S(2)}) collective-permute-start(bf16[2,24,9216]{2,1,0:T(8,128)(2,1)} %place.54.refs_0_), channel_id=1, source_target_pairs={{0,8},{8,0},{1,9},{9,1},{2,10},{10,2},{3,11},{11,3},{4,12},{12,4},... | collective-permute-start | bytes 2654216 | tf_op jit(solution)/shard_map/ppermute | solution.py:293
  1294.7 202.0 %collective-permute-start.75 = (bf16[2,4,2,24,768]{4,3,2,1,0:T(8,128)(2,1)}, bf16[2,4,2,24,768]{4,3,2,1,0:T(8,128)(2,1)}, u32[]{:S(2)}, u32[]{:S(2)}) collective-permute-start(bf16[2,4,2,24,768]{4,3,2,1,0:T(8,128)(2,1)} %bitcast.165.refs_0_), channel_id=1, source_target_pairs={{0,8},{8,0},{1,9},{9,1},{2,10},{10,2},{3,11},{11,3},{4,12},{12,4},... | collective-permute-start | bytes 1769480 | tf_op jit(solution)/shard_map/ppermute | solution.py:293
  1455.5 100.0 %all-to-all-start.2 = ((bf16[16,24,1024]{2,1,0:T(8,128)(2,1)}), bf16[16,24,1024]{2,1,0:T(8,128)(2,1)}, u32[]{:S(2)}, u32[]{:S(2)}) async-start(bf16[16,24,1024]{2,1,0:T(8,128)(2,1)} %bitcast.149), calls=%async_computation.2 | async-start | bytes 1572864 | tf_op jit(solution)/shard_map/all_to_all | solution.py:425
  1555.5 23.5 %all-to-all-start.4 = ((bf16[16,24,768]{2,1,0:T(8,128)(2,1)}), bf16[16,24,768]{2,1,0:T(8,128)(2,1)}, u32[]{:S(2)}, u32[]{:S(2)}) async-start(bf16[16,24,768]{2,1,0:T(8,128)(2,1)} %bitcast.525), calls=%async_computation.4 | async-start | bytes 1179648 | tf_op jit(solution)/shard_map/all_to_all | solution.py:425
  1592.8 15.0 collective-permute-start.76
  (161 other events, 3120.5 us)

commit v2 on v1

v2 whole, which is shorter than its diff:
```python
import functools
import itertools

import jax
import jax.numpy as jnp
from jax import lax
from jax.experimental import pallas as pl
from jax.experimental.pallas import tpu as pltpu
from jax.sharding import Mesh, PartitionSpec as P

D = 768
HEADS = 12
HDIM = 64
FF = 2048
NS_ITERS = 5
NORM_EPS = 1e-06
FROBENIUS_EPS = 1e-07
COEFF_FIRST = 3.4445
COEFF_SECOND = -4.775
COEFF_THIRD = 2.0315
MOMENTUM_DECAY = 0.9
LEARN_RATE = 1.0
HIGHEST = lax.Precision.HIGHEST
BF16 = jnp.bfloat16
F32 = jnp.float32
ITEMS = 13
NT = (((1,), (1,)), ((), ()))
NN = (((1,), (0,)), ((), ()))
TN = (((0,), (0,)), ((), ()))


def dot(a, b, dims=NN):
    return lax.dot_general(a, b, dims, preferred_element_type=F32)


def newton_schulz_kernel(width, active_ref, feed_ref, left_ref, right_ref, out_ref, x, xb, gram, low, poly):
    tile = 256
    tiles = D // tile
    blocks = width // tile
    spans = [slice(i * tile, (i + 1) * tile) for i in range(tiles)]

    def diagonal(part, other):
        rows = lax.broadcasted_iota(jnp.int32, (tile, tile), 0)
        cols = lax.broadcasted_iota(jnp.int32, (tile, tile), 1)
        return jnp.where(rows == cols, part, other)

    def block(b):
        return pl.ds(pl.multiple_of(b * tile, tile), tile)

    @pl.when(active_ref[0] != 0)
    def _():
        def load(b, acc):
            v = feed_ref[:, block(b)].astype(F32)
            if right_ref is not None:
                v = v + (1.0 + MOMENTUM_DECAY) * dot(left_ref[...], right_ref[:, block(b)], TN)
            x[:, block(b)] = v
            return acc + jnp.sum(v * v, axis=0, keepdims=True)

        total = lax.fori_loop(0, blocks, load, jnp.zeros((1, tile), F32))
        total = jnp.sum(total, keepdims=True)
        inverse = 1.0 / (jnp.sqrt(total) + FROBENIUS_EPS)

        def scale_block(b, carry):
            v = x[:, block(b)] * inverse
            x[:, block(b)] = v
            xb[:, block(b)] = v.astype(BF16)
            return carry

        lax.fori_loop(0, blocks, scale_block, 0)

        def iterate(step, carry):
            trace = jnp.zeros((1, tile), F32)
            for i in range(tiles):
                for j in range(i + 1):
                    part = dot(xb[spans[i], :], xb[spans[j], :], NT)
                    gram[spans[i], spans[j]] = part
                    if i == j:
                        trace = trace + jnp.sum(diagonal(part, 0.0), axis=0, keepdims=True)
                    else:
                        lower = part.astype(BF16)
                        low[spans[i], spans[j]] = lower
                        low[spans[j], spans[i]] = lower.T
            shift = jnp.sum(trace, keepdims=True) / D
            for i in range(tiles):
                part = gram[spans[i], spans[i]]
                part = diagonal(part - shift, part)
                gram[spans[i], spans[i]] = part
                low[spans[i], spans[i]] = part.astype(BF16)
            linear = COEFF_SECOND + 2.0 * COEFF_THIRD * shift
            level = COEFF_SECOND * shift + COEFF_THIRD * shift * shift
            trace = jnp.zeros((1, tile), F32)
            for i in range(tiles):
                for j in range(i + 1):
                    part = linear * gram[spans[i], spans[j]] + COEFF_THIRD * dot(
                        low[spans[i], :], low[spans[j], :], NT
                    )
                    if i == j:
                        gram[spans[i], spans[j]] = part
                        trace = trace + jnp.sum(diagonal(part, 0.0), axis=0, keepdims=True)
                    else:
                        lower = part.astype(BF16)
                        poly[spans[i], spans[j]] = lower
                        poly[spans[j], spans[i]] = lower.T
            mean = jnp.sum(trace, keepdims=True) / D
            for i in range(tiles):
                part = gram[spans[i], spans[i]]
                poly[spans[i], spans[i]] = diagonal(part - mean, part).astype(BF16)
            scale = COEFF_FIRST + level + mean

            def update(b, inner):
                new = scale * x[:, block(b)] + dot(poly[...], xb[:, block(b)])
                x[:, block(b)] = new
                xb[:, block(b)] = new.astype(BF16)
                return inner

            lax.fori_loop(0, blocks, update, 0)
            return carry

        lax.fori_loop(0, NS_ITERS, iterate, 0)
        out_ref[...] = xb[...]

    @pl.when(active_ref[0] == 0)
    def _():
        out_ref[...] = jnp.zeros_like(out_ref)


def newton_schulz(active, feed, left=None, right=None):
    width = feed.shape[1]
    operands = [active.reshape(1).astype(jnp.int32), feed]
    if left is None:

        def body(active_ref, feed_ref, *rest):
            newton_schulz_kernel(width, active_ref, feed_ref, None, None, *rest)

    else:
        body = functools.partial(newton_schulz_kernel, width)
        operands += [left, right]
    vmem = pl.BlockSpec(memory_space=pltpu.VMEM)
    return pl.pallas_call(
        body,
        out_shape=jax.ShapeDtypeStruct((D, width), BF16),
        in_specs=[pl.BlockSpec(memory_space=pltpu.SMEM)] + [vmem] * (len(operands) - 1),
        out_specs=vmem,
        scratch_shapes=[
            pltpu.VMEM((D, width), F32),
            pltpu.VMEM((D, width), BF16),
            pltpu.VMEM((D, D), F32),
            pltpu.VMEM((D, D), BF16),
            pltpu.VMEM((D, D), BF16),
        ],
        compiler_params=pltpu.CompilerParams(vmem_limit_bytes=40 * 1024 * 1024),
        cost_estimate=pl.CostEstimate(
            flops=NS_ITERS * 4 * D * D * (width + D), bytes_accessed=4 * D * width, transcendentals=0
        ),
        name="newton_schulz",
    )(*operands)


def tie(value, *others):
    return lax.optimization_barrier((value, *others))[0]


def place(parts, slots, lead=None, moves=None):
    count = len(parts)
    if lead is None:
        lead = (count, *parts[0].shape[:-2])
        moves = lambda slot: [(i, (), (slot[i],)) for i in range(count)]

    def body(slot_ref, *refs):
        ins, out = refs[:count], refs[count]
        for part, source, target in moves(slot_ref):
            out[target] = ins[part][source] if source else ins[part][...]

    size = count * parts[0].size * parts[0].dtype.itemsize
    vmem = pl.BlockSpec(memory_space=pltpu.VMEM)
    return pl.pallas_call(
        body,
        out_shape=jax.ShapeDtypeStruct((*lead, *parts[0].shape[-2:]), parts[0].dtype),
        in_specs=[pl.BlockSpec(memory_space=pltpu.SMEM)] + [vmem] * count,
        out_specs=vmem,
        cost_estimate=pl.CostEstimate(flops=0, bytes_accessed=2 * size, transcendentals=0),
        compiler_params=pltpu.CompilerParams(vmem_limit_bytes=24 * 1024 * 1024),
        name="place",
    )(jnp.stack(slots).astype(jnp.int32), *parts)


def place_halves(parts, slots):
    count = len(parts)
    rows, cols = parts[0].shape
    half = cols // 2

    def body(slot_ref, *refs):
        left, right = refs[count:]
        for i, ref in enumerate(refs[:count]):
            left[slot_ref[i]] = ref[:, :half]
            right[slot_ref[i]] = ref[:, half:]

    vmem = pl.BlockSpec(memory_space=pltpu.VMEM)
    shape = jax.ShapeDtypeStruct((count, rows, half), parts[0].dtype)
    return pl.pallas_call(
        body,
        out_shape=(shape, shape),
        in_specs=[pl.BlockSpec(memory_space=pltpu.SMEM)] + [vmem] * count,
        out_specs=(vmem, vmem),
        cost_estimate=pl.CostEstimate(flops=0, bytes_accessed=16 * rows * cols, transcendentals=0),
        compiler_params=pltpu.CompilerParams(vmem_limit_bytes=24 * 1024 * 1024),
        name="place_halves",
    )(jnp.stack(slots).astype(jnp.int32), *parts)


def slots_of(feeds, owners, width):
    arrays, index = [], {}

    def note(array):
        if array is None:
            return None
        source, columns = array
        if id(source) not in index:
            index[id(source)] = len(arrays)
            arrays.append(source)
        return (index[id(source)], columns)

    noted = [[(note(total), note(moment)) for total, moment in feed] for feed in feeds]
    rows = arrays[0].shape[-2]

    def body(*refs):
        out = refs[-1]

        def read(what):
            place_of, (lead, start, size) = what
            ref = refs[place_of]
            return ref[(*lead, slice(None), slice(start, start + size))].astype(F32)

        first = {}
        for slot in range(owners):
            if not noted[slot]:
                out[slot] = jnp.zeros((rows, width), BF16)
                continue
            key = str(noted[slot])
            if key in first:
                out[slot] = out[first[key]]
                continue
            first[key] = slot
            at = 0
            for total, moment in noted[slot]:
                value = MOMENTUM_DECAY * MOMENTUM_DECAY * read(moment)
                if total is not None:
                    value = value + (1.0 + MOMENTUM_DECAY) * read(total)
                out[slot, :, at : at + value.shape[1]] = value.astype(BF16)
                at += value.shape[1]

    vmem = pl.BlockSpec(memory_space=pltpu.VMEM)
    return pl.pallas_call(
        body,
        out_shape=jax.ShapeDtypeStruct((owners, rows, width), BF16),
        in_specs=[vmem] * len(arrays),
        out_specs=vmem,
        cost_estimate=pl.CostEstimate(
            flops=0, bytes_accessed=2 * owners * rows * width, transcendentals=0
        ),
        compiler_params=pltpu.CompilerParams(vmem_limit_bytes=24 * 1024 * 1024),
        name="slots",
    )(*arrays)


def every(*sizes):
    return list(itertools.product(*[range(size) for size in sizes]))


class Plain:
    images = ("dp", "fsdp")
    rows = "fsdp"
    wide_parts = 1

    def __init__(self, mesh):
        self.mesh = mesh
        self.row_shards = mesh.shape["fsdp"]
        self.owners = mesh.shape["fsdp"]
        self.wide_slots = [(i, 0) for i in range(3)]
        self.wide_slots += [None] * (self.owners - 3)
        self.slots = [None] * 3 + list(range(10))
        self.slots += [None] * (self.owners - ITEMS)

    def row_index(self):
        return lax.axis_index("fsdp")

    def group_index(self):
        return lax.axis_index("dp")

    def owner_index(self):
        return lax.axis_index("fsdp")

    def gather_weights(self, chunks):
        full = [lax.all_gather(chunk, "fsdp", axis=0, tiled=True) for chunk in chunks]
        return [jnp.split(chunk, 2, axis=1) for chunk in full]

    def gather_images(self, value):
        return lax.all_gather(value, ("dp", "fsdp"), axis=0, tiled=True)

    def to_group(self, value):
        return lax.all_to_all(value, "fsdp", split_axis=0, concat_axis=0, tiled=True)

    def reduce_core(self, partial):
        return partial

    def reduce_first(self, value, route):
        return value

    def reduce_second(self, value, route):
        return value

    def reduce_last(self, value):
        shard = lax.psum_scatter(value, "fsdp", scatter_dimension=1, tiled=True)
        return lax.psum(shard.astype(F32), "dp")

    def own_rows(self, shard, dim=-2):
        return shard

    def complete(self, piece):
        return piece

    def to_owners(self, pieces):
        got = lax.all_to_all(pieces, "fsdp", split_axis=0, concat_axis=0, tiled=True)
        return got.reshape(-1, got.shape[2])

    def to_rows(self, whole):
        blocks = whole.reshape(self.row_shards, -1, whole.shape[1])
        return lax.all_to_all(blocks, "fsdp", split_axis=0, concat_axis=0, tiled=True)


class Torus:
    images = ("x", "c", "z", "y")
    rows = ("z", "y")
    chips = ("x", "z", "y")
    wide_parts = 2

    def __init__(self, mesh):
        self.mesh = Mesh(mesh.devices.reshape(2, 2, 4, 2), ("x", "c", "z", "y"))
        self.row_shards = 8
        self.owners = 16
        wide_places = [(1, 0), (2, 1), (1, 1)]
        self.wide_slots = [None] * 16
        self.slots = [None] * 16
        for item, (z, y) in enumerate(wide_places):
            for part in range(2):
                self.wide_slots[(part * 4 + z) * 2 + y] = (item, part)
        free = [i for i in range(16) if self.wide_slots[i] is None]
        for item, slot in enumerate(free):
            self.slots[slot] = item

    def row_index(self):
        return lax.axis_index("z") * 2 + lax.axis_index("y")

    def group_index(self):
        return lax.axis_index("x") * 2 + lax.axis_index("c")

    def owner_index(self):
        return (lax.axis_index("x") * 4 + lax.axis_index("z")) * 2 + lax.axis_index("y")

    def swap(self, value, axis):
        return lax.ppermute(value, axis, [(0, 1), (1, 0)])

    def shift(self, value, by):
        return lax.ppermute(value, "z", [(i, (i + by) % 4) for i in range(4)])

    def exchange(self, value, axis):
        here = lax.axis_index(axis)
        return place([value, self.swap(value, axis)], [here, 1 - here])

    def spread_z(self, value):
        z = lax.axis_index("z")
        ring = [value] + [self.shift(value, by) for by in range(1, 4)]
        return place(ring, [(z - by) % 4 for by in range(4)])

    def gather_weights(self, chunks):
        x, y, z, c = [lax.axis_index(axis) for axis in "xyzc"]
        spread = []
        for chunk in chunks:
            piece = self.own_rows(chunk)
            if spread:
                piece = tie(piece, *spread[-1])
            ring = [piece] + [self.shift(piece, by) for by in range(1, 4)]
            spread.append(place_halves(ring, [(z - by) % 4 for by in range(4)]))
        done = []
        for left, right in spread:
            if done:
                left, right = lax.optimization_barrier((left, right, *done[-1]))[:2]
            left_other, right_other = self.swap(left, "y"), self.swap(right, "x")
            left = place([left, left_other], [y, 1 - y])
            right = place([right, right_other], [x, 1 - x])
            left_other, right_other = self.swap(left, "x"), self.swap(right, "y")
            left = place([left, left_other], [x, 1 - x])
            right = place([right, right_other], [y, 1 - y])
            done.append((left, right))
        full = []
        for left, right in done:
            others = self.swap(left, "c"), self.swap(right, "c")
            pair = []
            for half, other, order in ((left, others[0], (2, 1, 0)), (right, others[1], (2, 0, 1))):

                def moves(slot, order=order):
                    found = []
                    for part in range(2):
                        for at in every(2, 2, 4):
                            found.append((part, at, (*[at[i] for i in order], slot[part])))
                    return found

                pair.append(place([half, other], [c, 1 - c], (4, 2, 2, 2), moves).reshape(D, -1))
            full.append(pair)
        return full

    def gather_images(self, value):

        def both(v, axis):
            other = self.swap(v, axis)
            first = lax.axis_index(axis) == 0
            return jnp.where(first, jnp.stack([v, other]), jnp.stack([other, v]))

        z = lax.axis_index("z")
        shape = (32 * value.shape[0],) + value.shape[1:]
        value = both(value, "y")
        ring = jnp.stack([value] + [self.shift(value, by) for by in range(1, 4)])
        value = jnp.take(ring, (z - jnp.arange(4)) % 4, axis=0)
        value = both(value, "c")
        value = both(value, "x")
        return value.reshape(shape)

    def to_group(self, value):
        return lax.all_to_all(value, ("z", "y"), split_axis=0, concat_axis=0, tiled=True)

    def halve(self, value, axis, dim):
        here = lax.axis_index(axis)
        take = lambda at: lax.dynamic_index_in_dim(value, at, dim, keepdims=False)
        got = self.swap(take(1 - here), axis)
        return (take(here).astype(F32) + got.astype(F32)).astype(BF16)

    def reduce_core(self, partial):
        k, _, cols = partial.shape
        return self.halve(partial.reshape(k, 4, 2, 2, 2, D // 32, cols), "c", 4)

    def reduce_first(self, value, route):
        return self.halve(value, route[0], 3 if route[0] == "x" else 2)

    def reduce_second(self, value, route):
        return self.halve(value, route[1], 2)

    def reduce_last(self, value):
        z = lax.axis_index("z")
        take = lambda at: lax.dynamic_index_in_dim(value, at, 1, keepdims=False)
        got = [self.shift(take((z + by) % 4), by) for by in range(1, 4)]
        total = take(z).astype(F32)
        for part in got:
            total = total + part.astype(F32)
        return total

    def own_rows(self, shard, dim=-2):
        return lax.dynamic_slice_in_dim(
            shard, self.group_index() * (D // 32), D // 32, dim % shard.ndim
        )

    def complete(self, piece):
        value = self.exchange(piece, "x")
        c = lax.axis_index("c")
        moves = lambda slot: [(part, (x,), (x, slot[part])) for part in range(2) for x in range(2)]
        value = place([value, self.swap(value, "c")], [c, 1 - c], (2, 2), moves)
        return value.reshape(D // 8, -1)

    def to_owners(self, pieces):
        cols = pieces.shape[2]
        got = lax.all_to_all(pieces, self.chips, split_axis=0, concat_axis=0, tiled=True)
        got = got.reshape(2, 4, 2, D // 32, cols)
        c = lax.axis_index("c")

        def moves(slot):
            return [
                (part, (x, z, y), (z, y, x, slot[part]))
                for part in range(2)
                for x, z, y in every(2, 4, 2)
            ]

        whole = place([got, self.swap(got, "c")], [c, 1 - c], (4, 2, 2, 2), moves)
        return whole.reshape(D, cols)

    def to_rows(self, whole):
        cols = whole.shape[1]
        blocks = whole.reshape(4, 2, 2, 2, D // 32, cols)
        blocks = lax.dynamic_index_in_dim(blocks, lax.axis_index("c"), 3, keepdims=False)
        blocks = blocks.transpose(2, 0, 1, 3, 4).reshape(16, D // 32, cols)
        return lax.all_to_all(blocks, self.chips, split_axis=0, concat_axis=0, tiled=True)


def lanes(shape, dim):
    return lax.broadcasted_iota(jnp.int32, shape, dim)


def norm_of(values):
    centred = values - jnp.mean(values, axis=-1, keepdims=True)
    inverse = lax.rsqrt(jnp.mean(centred * centred, axis=-1, keepdims=True) + NORM_EPS)
    return centred * inverse, inverse


def norm_back(incoming, normed, inverse):
    return inverse * (
        incoming
        - jnp.mean(incoming, axis=-1, keepdims=True)
        - normed * jnp.mean(incoming * normed, axis=-1, keepdims=True)
    )


def rotate_pair(value):
    first = lanes(value.shape, 1) % 32 < 16
    return jnp.where(first, -pltpu.roll(value, 112, 1), pltpu.roll(value, 16, 1))


def two_heads(value):
    low = lanes(value.shape, 1) < HDIM
    zero = jnp.zeros_like(value)
    return jnp.where(low, value, zero), jnp.where(low, zero, value)


def pair_at(pair):
    return slice(pair * 2 * HDIM, (pair + 1) * 2 * HDIM)


def attention_forward_kernel(
    length_ref,
    input_ref,
    cotangent_ref,
    modulation_ref,
    cosine_ref,
    sine_ref,
    query_key_ref,
    value_output_ref,
    first_ref,
    query_ref,
    key_ref,
    value_ref,
    probs_ref,
    attended_ref,
    attention_ref,
    middle_ref,
    second_ref,
    branch_ref,
):
    length = length_ref[pl.program_id(0)]
    row = lambda which: modulation_ref[0, which : which + 1, :]
    stream = input_ref[0].astype(F32)
    positions = stream.shape[0]
    normed, _ = norm_of(stream)
    first = (normed * (1.0 + row(1)) + row(0)).astype(BF16)
    first_ref[0] = first
    inside = lanes((positions, D), 0) < length
    upstream = jnp.where(inside, cotangent_ref[0].astype(F32), 0.0)
    branch_ref[0] = (row(5) * upstream).astype(BF16)
    value_ref[0] = dot(first, value_output_ref[:, :D]).astype(BF16)
    cosine, sine = cosine_ref[0], sine_ref[0]
    keep = lanes((positions, positions), 1) < length
    for pair in range(HEADS // 2):
        at = pair_at(pair)
        query = dot(first, query_key_ref[:, at])
        key = dot(first, query_key_ref[:, D + pair * 128 : D + (pair + 1) * 128])
        query = (query * cosine + rotate_pair(query) * sine).astype(BF16)
        key = (key * cosine + rotate_pair(key) * sine).astype(BF16)
        query_ref[0, :, at] = query
        key_ref[0, :, at] = key
        low = []
        for head, masked in enumerate(two_heads(query)):
            scores = dot(masked, key, NT) * HDIM ** (-0.5)
            scores = jnp.where(keep, scores, -1000000000.0)
            exponent = jnp.exp(scores - jnp.max(scores, axis=-1, keepdims=True))
            probs = exponent * (1.0 / jnp.sum(exponent, axis=-1, keepdims=True))
            probs_ref[0, 2 * pair + head] = probs
            low.append(probs.astype(BF16))
        values = two_heads(value_ref[0, :, at])
        attended_ref[0, :, at] = dot(
            jnp.concatenate(low, axis=1), jnp.concatenate(values, axis=0)
        ).astype(BF16)
    attention = dot(attended_ref[0], value_output_ref[:, D:])
    attention_ref[0] = attention
    middle = stream + row(2) * attention
    middle_ref[0] = middle
    normed, _ = norm_of(middle)
    second_ref[0] = (normed * (1.0 + row(4)) + row(3)).astype(BF16)


def feed_forward_kernel(
    second_ref, branch_ref, gate_ref, up_ref, down_ref, out_ref, back_ref, grads_ref, second_t, branch_t
):
    step = pl.program_id(0)

    @pl.when(step == 0)
    def _():
        second_t[...] = second_ref[...].T
        branch_t[...] = branch_ref[...].T
        out_ref[...] = jnp.zeros_like(out_ref)
        back_ref[...] = jnp.zeros_like(back_ref)

    gate, up, down = gate_ref[...], up_ref[...], down_ref[...]
    gate_pre = dot(second_ref[...], gate)
    up_pre = dot(second_ref[...], up)
    sigmoid = 1.0 / (1.0 + jnp.exp(-gate_pre))
    swish = gate_pre * sigmoid
    hidden = (swish * up_pre).astype(BF16)
    out_ref[...] += dot(hidden, down, NT)
    grad_hidden = dot(branch_ref[...], down)
    grad_gate = (grad_hidden * up_pre * sigmoid * (1.0 + gate_pre * (1.0 - sigmoid))).astype(BF16)
    grad_up = (grad_hidden * swish).astype(BF16)
    back_ref[...] += dot(grad_gate, gate, NT) + dot(grad_up, up, NT)
    grads_ref[0] = dot(second_t[...], grad_gate).astype(BF16)
    grads_ref[1] = dot(second_t[...], grad_up).astype(BF16)
    grads_ref[2] = dot(branch_t[...], hidden).astype(BF16)


def attention_backward_kernel(
    length_ref,
    branch_left_ref,
    branch_right_ref,
    second_left_ref,
    second_right_ref,
    middle_ref,
    cotangent_ref,
    modulation_ref,
    attention_ref,
    value_output_ref,
    query_ref,
    key_ref,
    value_ref,
    probs_ref,
    cosine_ref,
    sine_ref,
    output_ref,
    stream_ref,
    grads_ref,
    sums_ref,
    attended_grad,
):
    length = length_ref[pl.program_id(0)]
    row = lambda which: modulation_ref[0, which : which + 1, :]
    middle = middle_ref[0]
    positions = middle.shape[0]
    inside = lanes((positions, D), 0) < length
    upstream = jnp.where(inside, cotangent_ref[0].astype(F32), 0.0)
    branch = branch_left_ref[0] + branch_right_ref[0]
    output_ref[0] = (middle + row(5) * branch).astype(BF16)
    total = lambda value: jnp.sum(value, axis=0, keepdims=True)
    gate_two = total(upstream * branch)
    second = second_left_ref[0] + second_right_ref[0]
    normed, inverse = norm_of(middle)
    scale_two = total(second * normed)
    shift_two = total(second)
    stream = upstream + norm_back(second * (1.0 + row(4)), normed, inverse)
    stream_ref[0] = stream
    gate_one = total(stream * attention_ref[0])
    blank = jnp.zeros_like(gate_one)
    sums_ref[0] = jnp.concatenate(
        [blank, blank, gate_one, shift_two, scale_two, gate_two, blank, blank], axis=0
    )
    grad_attention = (row(2) * stream).astype(BF16)
    grads_ref[3, 0] = grad_attention
    attended_grad[...] = dot(grad_attention, value_output_ref[:, D:], NT).astype(BF16)
    cosine, sine = cosine_ref[0], sine_ref[0]
    for pair in range(HEADS // 2):
        at = pair_at(pair)
        query, key, value = query_ref[0, :, at], key_ref[0, :, at], value_ref[0, :, at]
        attended = two_heads(attended_grad[:, at])
        low, scores = [], []
        for head in range(2):
            probs = probs_ref[0, 2 * pair + head]
            grad_probs = dot(attended[head], value, NT)
            inner = jnp.sum(grad_probs * probs, axis=-1, keepdims=True)
            scores.append((probs * (grad_probs - inner)).astype(BF16))
            low.append(probs.astype(BF16))
        grads_ref[2, 0, :, at] = dot(
            jnp.concatenate(low, axis=0), jnp.concatenate(attended, axis=0), TN
        ).astype(BF16)
        grad_query = dot(
            jnp.concatenate(scores, axis=1), jnp.concatenate(two_heads(key), axis=0)
        ) * HDIM ** (-0.5)
        grad_key = dot(
            jnp.concatenate(scores, axis=0), jnp.concatenate(two_heads(query), axis=0), TN
        ) * HDIM ** (-0.5)
        grads_ref[0, 0, :, at] = (grad_query * cosine - rotate_pair(grad_query * sine)).astype(BF16)
        grads_ref[1, 0, :, at] = (grad_key * cosine - rotate_pair(grad_key * sine)).astype(BF16)


def projection_backward_kernel(
    grads_in_ref,
    first_ref,
    attended_ref,
    input_ref,
    modulation_ref,
    stream_ref,
    sums_ref,
    active_ref,
    query_key_ref,
    value_output_ref,
    grads_ref,
    input_grad_ref,
    modulation_grad_ref,
    first_t,
    first_grad,
):
    images, positions = input_ref.shape[:2]
    tokens = images * positions
    flat = lambda ref: ref[...].reshape(tokens, D)
    step = pl.program_id(0)

    @pl.when(step == 0)
    def _():
        first_t[...] = flat(first_ref).T
        grads = grads_in_ref[0].reshape(tokens, D)
        grads_ref[0] = dot(first_t[...], grads).astype(BF16)
        first_grad[...] = dot(grads, query_key_ref[:, :D], NT)

    @pl.when(step == 1)
    def _():
        grads = grads_in_ref[0].reshape(tokens, D)
        grads_ref[0] = dot(first_t[...], grads).astype(BF16)
        first_grad[...] += dot(grads, query_key_ref[:, D:], NT)

    @pl.when(step == 2)
    def _():
        grads = grads_in_ref[0].reshape(tokens, D)
        grads_ref[0] = dot(first_t[...], grads).astype(BF16)
        first_grad[...] += dot(grads, value_output_ref[:, :D], NT)

    @pl.when(step == 3)
    def _():
        first_t[...] = flat(attended_ref).T
        grads_ref[0] = dot(first_t[...], grads_in_ref[0].reshape(tokens, D)).astype(BF16)
        for image in range(images):
            at = slice(image * positions, (image + 1) * positions)
            normed, inverse = norm_of(input_ref[image].astype(F32))
            first = first_grad[at, :]
            scale_one = jnp.sum(first * normed, axis=0, keepdims=True)
            shift_one = jnp.sum(first, axis=0, keepdims=True)
            scaled = first * (1.0 + modulation_ref[image, 1:2, :])
            input_grad_ref[image] = stream_ref[image] + norm_back(scaled, normed, inverse)
            modulation_grad_ref[image] = jnp.concatenate(
                [
                    shift_one,
                    scale_one,
                    sums_ref[image, 2:6, :],
                    active_ref[image : image + 1, :].astype(F32),
                    jnp.zeros_like(shift_one),
                ],
                axis=0,
            ).astype(BF16)


BIG_VMEM = 58 * 1024 * 1024


def whole(array):
    return pl.BlockSpec(array.shape, lambda *_: (0,) * array.ndim)


def by_image(array):
    return pl.BlockSpec((1, *array.shape[1:]), lambda b: (b,) + (0,) * (array.ndim - 1))


def call(body, grid, ins, in_specs, outs, out_specs, scratch, flops, name):
    size = sum(a.size * a.dtype.itemsize for a in (*ins, *outs))
    return pl.pallas_call(
        body,
        grid=grid,
        out_shape=outs,
        in_specs=in_specs,
        out_specs=out_specs,
        scratch_shapes=scratch,
        compiler_params=pltpu.CompilerParams(vmem_limit_bytes=BIG_VMEM),
        cost_estimate=pl.CostEstimate(flops=flops, bytes_accessed=size, transcendentals=0),
        name=name,
    )(*ins)


def attention_forward(lengths, inputs, cotangent, modulation, cosine, sine, query_key, value_output):
    images, positions, _ = inputs.shape
    ins = (lengths, inputs, cotangent, modulation, cosine, sine, query_key, value_output)
    in_specs = [pl.BlockSpec(memory_space=pltpu.SMEM)]
    in_specs += [by_image(a) for a in ins[1:6]] + [whole(a) for a in ins[6:]]
    token = lambda dtype: jax.ShapeDtypeStruct((images, positions, D), dtype)
    outs = (
        token(BF16),
        token(BF16),
        token(BF16),
        token(BF16),
        jax.ShapeDtypeStruct((images, HEADS, positions, positions), F32),
        token(BF16),
        token(F32),
        token(F32),
        token(BF16),
        token(BF16),
    )
    flops = 2 * images * positions * D * (4 * D + 2 * positions)
    return call(
        attention_forward_kernel,
        (images,),
        ins,
        in_specs,
        outs,
        [by_image(a) for a in outs],
        [],
        flops,
        "attention_forward",
    )


def feed_forward(second, branch, weight):
    tokens = second.shape[0]
    units = weight.shape[1] // 3
    tile = 256
    steps = units // tile
    ins = (second, branch, weight, weight, weight)
    in_specs = [whole(second), whole(branch)] + [
        pl.BlockSpec((D, tile), lambda t, which=which: (0, which * steps + t)) for which in range(3)
    ]
    outs = (
        jax.ShapeDtypeStruct((tokens, D), F32),
        jax.ShapeDtypeStruct((tokens, D), F32),
        jax.ShapeDtypeStruct((3, D, units), BF16),
    )
    out_specs = [
        whole(outs[0]),
        whole(outs[1]),
        pl.BlockSpec((3, D, tile), lambda t: (0, 0, t)),
    ]
    scratch = [pltpu.VMEM((D, tokens), BF16), pltpu.VMEM((D, tokens), BF16)]
    flops = 2 * 9 * tokens * D * units
    return call(
        feed_forward_kernel, (steps,), ins, in_specs, outs, out_specs, scratch, flops, "feed_forward"
    )


def attention_backward(lengths, *ins):
    images, positions, _ = ins[0].shape
    shared = 8
    in_specs = [pl.BlockSpec(memory_space=pltpu.SMEM)]
    in_specs += [whole(a) if i == shared else by_image(a) for i, a in enumerate(ins)]
    outs = (
        jax.ShapeDtypeStruct((images, positions, D), BF16),
        jax.ShapeDtypeStruct((images, positions, D), F32),
        jax.ShapeDtypeStruct((4, images, positions, D), BF16),
        jax.ShapeDtypeStruct((images, 8, D), F32),
    )
    out_specs = [
        by_image(outs[0]),
        by_image(outs[1]),
        pl.BlockSpec((4, 1, positions, D), lambda b: (0, b, 0, 0)),
        by_image(outs[3]),
    ]
    flops = 2 * images * positions * D * (D + 5 * positions)
    return call(
        attention_backward_kernel,
        (images,),
        (lengths, *ins),
        in_specs,
        outs,
        out_specs,
        [pltpu.VMEM((positions, D), BF16)],
        flops,
        "attention_backward",
    )


def projection_backward(*ins):
    _, images, positions, _ = ins[0].shape
    tokens = images * positions
    in_specs = [pl.BlockSpec((1, images, positions, D), lambda k: (k, 0, 0, 0))]
    in_specs += [whole(a) for a in ins[1:]]
    outs = (
        jax.ShapeDtypeStruct((4, D, D), BF16),
        jax.ShapeDtypeStruct((images, positions, D), F32),
        jax.ShapeDtypeStruct((images, 8, D), BF16),
    )
    out_specs = [pl.BlockSpec((1, D, D), lambda k: (k, 0, 0)), whole(outs[1]), whole(outs[2])]
    scratch = [pltpu.VMEM((D, tokens), BF16), pltpu.VMEM((tokens, D), F32)]
    return call(
        projection_backward_kernel,
        (4,),
        ins,
        in_specs,
        outs,
        out_specs,
        scratch,
        2 * 7 * tokens * D * D,
        "projection_backward",
    )


def swish_value(values):
    return values / (1.0 + jnp.exp(-values))


def rope_tables(extents, positions):
    quarter = HDIM // 4
    places = jnp.arange(positions, dtype=jnp.int32)
    widths = extents[:, 1]
    row_place = (places[None, :] // widths[:, None]).astype(F32)
    col_place = (places[None, :] % widths[:, None]).astype(F32)
    lane = jnp.arange(2 * HDIM) % HDIM
    frequency = 10000.0 ** (-(lane % quarter).astype(F32) / quarter)
    by_row = lane < 2 * quarter
    angle = jnp.where(by_row, row_place[:, :, None], col_place[:, :, None]) * frequency
    return jnp.cos(angle), jnp.sin(angle)


def local(
    comm,
    inputs,
    cotangent,
    image_shape,
    time_bins,
    time_table,
    modulation_master,
    projection_master,
    output_master,
    expand_master,
    shrink_master,
    modulation_moment,
    projection_moment,
    output_moment,
    expand_moment,
    shrink_moment,
):
    masters = (modulation_master, projection_master, output_master, expand_master, shrink_master)
    moments = (modulation_moment, projection_moment, output_moment, expand_moment, shrink_moment)
    images, positions, features = inputs.shape
    tokens = images * positions
    rows = modulation_master.shape[1]
    row_index = comm.row_index()

    half = FF // 2
    shrink_low = shrink_master.astype(BF16).T
    (query_key_weight, value_output_weight), (left_weight, right_weight) = comm.gather_weights(
        [
            jnp.concatenate(
                [projection_master[i].astype(BF16) for i in range(3)] + [output_master.astype(BF16)],
                axis=1,
            ),
            jnp.concatenate(
                [
                    part
                    for cols in (slice(None, half), slice(half, None))
                    for part in (
                        expand_master[0, :, cols].astype(BF16),
                        expand_master[1, :, cols].astype(BF16),
                        shrink_low[:, cols],
                    )
                ],
                axis=1,
            ),
        ]
    )
    selector = (
        time_bins[:, None] == jnp.arange(time_table.shape[0], dtype=jnp.int32)[None, :]
    ).astype(F32)
    active = swish_value(jnp.dot(selector, time_table, precision=HIGHEST)).astype(BF16)
    active_group = comm.to_group(
        active.reshape(images, comm.row_shards, rows).transpose(1, 0, 2)
    ).reshape(-1, rows)
    partial = jnp.einsum(
        "bd,kde->bke", active_group, modulation_master.astype(BF16), preferred_element_type=F32
    )
    modulation = jnp.sum(
        comm.to_group(partial.reshape(comm.row_shards, images, 6, features)), axis=0
    )
    cosine, sine = rope_tables(image_shape, positions)
    lengths = image_shape[:, 0] * image_shape[:, 1]
    (first_input, query, key, value, probs, attended, attention, middle, second_input, grad_branch) = (
        attention_forward(
            lengths, inputs, cotangent, modulation, cosine, sine, query_key_weight, value_output_weight
        )
    )
    second_flat = second_input.reshape(tokens, D)
    branch_flat = grad_branch.reshape(tokens, D)
    shaped = lambda v: v.reshape(images, positions, D)
    branch_left, back_left, grads = feed_forward(second_flat, branch_flat, left_weight)
    left_sum = comm.reduce_core(grads)
    second_flat = tie(second_flat, back_left)
    branch_right, back_right, grads = feed_forward(second_flat, branch_flat, right_weight)
    left_sum, grads = lax.optimization_barrier((left_sum, grads))
    left_sum = comm.reduce_first(left_sum, "xy")
    right_sum = comm.reduce_core(grads)
    block_output, grad_stream, grads, sums = attention_backward(
        lengths,
        shaped(branch_left),
        shaped(branch_right),
        shaped(back_left),
        shaped(back_right),
        middle,
        cotangent,
        modulation,
        attention,
        value_output_weight,
        query,
        key,
        value,
        probs,
        cosine,
        sine,
    )
    left_sum, right_sum, grads = lax.optimization_barrier((left_sum, right_sum, grads))
    left_sum = comm.reduce_second(left_sum, "xy")
    right_sum = comm.reduce_first(right_sum, "yx")
    grads, input_gradient, grad_modulation = projection_backward(
        grads,
        first_input,
        attended,
        inputs,
        modulation,
        grad_stream,
        sums,
        active,
        query_key_weight,
        value_output_weight,
    )
    left_sum, right_sum, grads, grad_modulation = lax.optimization_barrier(
        (left_sum, right_sum, grads, grad_modulation)
    )
    right_sum = comm.reduce_second(right_sum, "yx")
    left_piece = comm.reduce_last(left_sum)
    attention_sum = comm.reduce_core(grads)
    left_piece, right_sum, attention_sum = lax.optimization_barrier(
        (left_piece, right_sum, attention_sum)
    )
    right_piece = comm.reduce_last(right_sum)
    first_sum = comm.reduce_first(attention_sum[:2], "xy")
    second_sum = comm.reduce_first(attention_sum[2:], "yx")
    first_sum, second_sum, right_piece = lax.optimization_barrier(
        (first_sum, second_sum, right_piece)
    )

    owner = comm.owner_index()
    own_expand = comm.own_rows(expand_moment)
    own_shrink = comm.own_rows(shrink_moment.T)
    wide_feed = [
        [
            (
                (piece, ((which,), 0, half)),
                (own_shrink, ((), side * half, half))
                if which == 2
                else (own_expand, ((which,), side * half, half)),
            )
            for side, piece in enumerate((left_piece, right_piece))
        ]
        for which in range(3)
    ]
    wide = comm.to_owners(
        slots_of(
            [[] if slot is None else wide_feed[slot[0]] for slot in comm.wide_slots],
            comm.owners,
            FF,
        )
    )
    gathered = comm.gather_images(grad_modulation)
    attention_piece = comm.reduce_last(
        jnp.concatenate(
            [comm.reduce_second(first_sum, "xy"), comm.reduce_second(second_sum, "yx")], axis=0
        )
    )
    active_all = gathered[:, 6]

    own_modulation = comm.own_rows(modulation_moment)
    own_projection = comm.own_rows(projection_moment)
    own_output = comm.own_rows(output_moment)
    square_feed = [[(None, (own_modulation, ((k,), 0, D)))] for k in range(6)]
    for k in range(3):
        square_feed.append(
            [((attention_piece, ((k,), 0, D)), (own_projection, ((k,), 0, D)))]
        )
    square_feed.append([((attention_piece, ((3,), 0, D)), (own_output, ((), 0, D)))])
    square = comm.to_owners(
        slots_of(
            [[] if slot is None else square_feed[slot] for slot in comm.slots], comm.owners, D
        )
    )
    item = jnp.array([-1 if slot is None else slot for slot in comm.slots], jnp.int32)[owner]
    which = jnp.where((item >= 0) & (item < 6), item, 0)
    right = lax.dynamic_index_in_dim(gathered, which, 1, keepdims=False)
    right = jnp.where(item < 6, right, jnp.zeros_like(right))
    active_wide = jnp.array([0 if slot is None else 1 for slot in comm.wide_slots], jnp.int32)[owner]
    wide, square = lax.optimization_barrier((wide, square))
    wide_done = newton_schulz(active_wide, wide)
    square_done = newton_schulz((item >= 0).astype(jnp.int32), square, active_all, right)
    size = FF // comm.wide_parts
    part = jnp.array([0 if slot is None else slot[1] for slot in comm.wide_slots])[owner]
    mine = lax.dynamic_slice_in_dim(wide_done, part * size, size, 1)
    mine = mine + jnp.pad(square_done, ((0, 0), (0, size - D)))
    back = comm.to_rows(mine)

    pieces = [left_piece[i] for i in range(3)] + [right_piece[i] for i in range(3)]
    pieces += [attention_piece[i] for i in range(4)]
    totals_low = comm.complete(jnp.concatenate([p.astype(BF16) for p in pieces], axis=1)).astype(F32)
    by_unit = [
        jnp.concatenate(
            [totals_low[:, (side * 3 + i) * half : (side * 3 + i + 1) * half] for side in range(2)],
            axis=1,
        )
        for i in range(3)
    ]
    wide_back = [
        back[comm.wide_slots.index((i, p))] for i in range(3) for p in range(comm.wide_parts)
    ]
    square_back = [back[comm.slots.index(i), :, :D] for i in range(10)]
    steps = comm.complete(jnp.concatenate(wide_back + square_back, axis=1)).astype(F32)
    active_rows = lax.dynamic_slice_in_dim(active_all, row_index * rows, rows, 1)
    modulation_total = jnp.einsum(
        "bd,bke->kde",
        active_rows,
        gathered[:, :6],
        preferred_element_type=F32,
    )
    after = 3 * FF
    totals = (
        modulation_total,
        jnp.stack([totals_low[:, after + i * D : after + (i + 1) * D] for i in range(3)]),
        totals_low[:, after + 3 * D :],
        jnp.stack(by_unit[:2]),
        by_unit[2].T,
    )
    states = tuple((MOMENTUM_DECAY * moment + total for moment, total in zip(moments, totals)))
    square_step = [steps[:, after + i * D : after + (i + 1) * D] for i in range(10)]
    steps_all = (
        jnp.stack(square_step[:6]),
        jnp.stack(square_step[6:9]),
        square_step[9],
        jnp.stack([steps[:, :FF], steps[:, FF : 2 * FF]]) * (FF / D) ** 0.5,
        steps[:, 2 * FF : after].T,
    )
    updated = tuple((master - LEARN_RATE * step for master, step in zip(masters, steps_all)))
    return (block_output, input_gradient, *totals, *updated, *states)


def solution(mesh):
    if mesh.shape["dp"] == 4 and mesh.shape["fsdp"] == 8:
        comm = Torus(mesh)
    else:
        comm = Plain(mesh)
    images, rows = comm.images, comm.rows
    by_row = (
        P(None, rows, None),
        P(None, rows, None),
        P(rows, None),
        P(None, rows, None),
        P(None, rows),
    )
    return jax.shard_map(
        functools.partial(local, comm),
        mesh=comm.mesh,
        in_specs=(
            P(images, None, None),
            P(images, None, None),
            P(images, None),
            P(images),
            P(),
            *by_row,
            *by_row,
        ),
        out_specs=(P(images, None, None), P(images, None, None), *by_row, *by_row, *by_row),
        check_vma=False,
    )
```

time: 1760 us -> 585 us (0.33)
  Pallas kernels: 1210 us -> 118 us
  waiting for transfers between devices: 139 us -> 217 us
  matrix products: 81.8 us -> 7.06 us
  starting transfers between devices: 143 us -> 111 us
  local copies, waits for them, and re-layouts: 92.4 us -> 63.9 us
  other arithmetic: 76.7 us -> 57.4 us
    pallas_call x30 -> x18, Pallas kernels: 1190 us -> 18.9 us  [place(): pl.pallas_call(body, out_shape=jax.ShapeDtypeStruct((*lead, *parts[0].sha...]
    pallas_call x0 -> x9, Pallas kernels: none -> 79.7 us  [the longest x5 76 us: call(): pl.pallas_call(body, grid=grid, out_shape=outs, in_specs=in_specs, out_sp...]
    ppermute x45 -> x32, waiting for transfers between devices: 63.1 us -> 131 us  [swap(): return lax.ppermute(value, axis, [(0, 1), (1, 0)])]
    dot_general x23 -> x1, matrix products: 63.7 us -> 4.11 us  [local(): jnp.einsum('bd,bke->kde', active_rows, gathered[:, :6], preferred_element...]
    all_to_all x2 -> x1, starting transfers between devices: 48.3 us -> 23.3 us  [to_rows(): lax.all_to_all(blocks, self.chips, split_axis=0, concat_axis=0, tiled=True)]
    unnamed x290 -> x134, local copies, waits for them, and re-layouts: 51.8 us -> 30.3 us
    unnamed x12 -> x0, other arithmetic: 18.5 us -> none
    ppermute x33 -> x18, waiting for transfers between devices: 67.7 us -> 51.7 us  [shift(): return lax.ppermute(value, 'z', [(i, (i + by) % 4) for i in range(4)])]
  transfers between devices with their start and end apart: 83 -> 55, of which waited for: 26 -> 26; matrix products, arithmetic and copies ran while one was open for 8% -> 14% of each run, Pallas kernels for 57% -> 16%
where the time goes in v2:
time: 585 us; the launch traced here: 579 us
  waiting for transfers between devices  217 us (37%)
  Pallas kernels  118 us (20%)
  starting transfers between devices  111 us (19%)
  local copies, waits for them, and re-layouts  63.9 us (11%)
  other arithmetic  57.4 us (10%)
  matrix products  7.06 us (1%)
    ppermute x32, waiting for transfers between devices, swap(): return lax.ppermute(value, axis, [(0, 1), (1, 0)])  131 us
    pallas_call x5, Pallas kernels, call(): pl.pallas_call(body, grid=grid, out_shape=outs, in_specs=in_specs, out_sp...  76 us
    ppermute x18, waiting for transfers between devices, shift(): return lax.ppermute(value, 'z', [(i, (i + by) % 4) for i in range(4)])  51.7 us
    ppermute x18, starting transfers between devices, shift(): return lax.ppermute(value, 'z', [(i, (i + by) % 4) for i in range(4)])  32.9 us
    unnamed x134, local copies, waits for them, and re-layouts  30.3 us
    ppermute x32, starting transfers between devices, swap(): return lax.ppermute(value, axis, [(0, 1), (1, 0)])  26.9 us
    all_to_all x1, starting transfers between devices, to_rows(): lax.all_to_all(blocks, self.chips, split_axis=0, concat_axis=0, tiled=True)  23.3 us
    pallas_call x2, Pallas kernels, newton_schulz(): pl.pallas_call(body, out_shape=jax.ShapeDtypeStruct((D, width), BF16), in...  19.3 us
  transfers between devices with their start and end apart: 55, of which 26 were waited for; matrix products, arithmetic and copies ran while one was open for 14% of the time, Pallas kernels for 16%

profile of v2, /device:TPU:0, one launch (start us, length us, event | category | flops | bytes accessed | tf_op | source)
XLA Modules:
  0.0 579.1 jit_solution(1648593099123648542)
XLA Ops:
  4.4 3.1 collective-permute-start
  7.5 2.6 collective-permute-start.1
  17.3 2.4 collective-permute-done.1.refs_2_
  25.5 4.1 collective-permute-done.6.refs_1_
  34.9 2.8 collective-permute-start.10
  37.7 3.5 collective-permute-start.11
  41.2 12.5 %collective-permute-done.10.refs_2_ = bf16[24,6144]{1,0:T(8,128)(2,1)S(1)} collective-permute-done((bf16[24,6144]{1,0:T(8,128)(2,1)S(1)}, bf16[24,6144]{1,0:T(8,128)(2,1)S(1)}, u32[]{:S(2)}, u32[]{:S(2)}) %collective-permute-start.10) | collective-permute-done | bytes 294944 | tf_op jit(solution)/shard_map/ppermute | solution.py:364
  53.7 5.8 collective-permute-done.9.refs_1_
  64.7 12.4 %collective-permute-done.12.refs_1_ = bf16[4,24,3072]{2,1,0:T(8,128)(2,1)S(1)} collective-permute-done((bf16[4,24,3072]{2,1,0:T(8,128)(2,1)S(1)}, bf16[4,24,3072]{2,1,0:T(8,128)(2,1)S(1)}, u32[]{:S(2)}, u32[]{:S(2)}) %collective-permute-start.12) | collective-permute-done | bytes 589856 | tf_op jit(solution)/shard_map/ppermute | solution.py:361
  78.4 24.1 %collective-permute-done.13.refs_1_ = bf16[2,4,24,3072]{3,2,1,0:T(8,128)(2,1)S(1)} collective-permute-done((bf16[2,4,24,3072]{3,2,1,0:T(8,128)(2,1)S(1)}, bf16[2,4,24,3072]{3,2,1,0:T(8,128)(2,1)S(1)}, u32[]{:S(2)}, u32[]{:S(2)}) %collective-permute-start.13) | collective-permute-done | bytes 1179680 | tf_op jit(solution)/shard_map/ppermute | solution.py:361
  106.5 11.5 %all-to-all-start = ((bf16[8,2,96]{2,1,0:T(2,128)(2,1)}), bf16[8,2,96]{2,1,0:T(2,128)(2,1)S(1)}, u32[]{:S(2)}, u32[]{:S(2)}) async-start(bf16[8,2,96]{2,1,0:T(2,128)(2,1)} %bitcast.355), calls=%async_computation | async-start | bytes 8192 | tf_op jit(solution)/shard_map/all_to_all | solution.py:429
  121.8 11.8 %collective-permute-done.15.refs_1_ = bf16[4,24,3072]{2,1,0:T(8,128)(2,1)S(1)} collective-permute-done((bf16[4,24,3072]{2,1,0:T(8,128)(2,1)}, bf16[4,24,3072]{2,1,0:T(8,128)(2,1)S(1)}, u32[]{:S(2)}, u32[]{:S(2)}) %collective-permute-start.15) | collective-permute-done | bytes 589856 | tf_op jit(solution)/shard_map/ppermute | solution.py:361
  140.5 5.1 all-to-all-start.1
  147.7 2.6 fusion.29
  150.3 15.7 %all-to-all-done.1 = f32[8,2,6,768]{3,1,2,0:T(2,128)} async-done(((f32[8,2,6,768]{3,1,2,0:T(2,128)}), f32[8,2,6,768]{3,1,2,0:T(2,128)}, u32[]{:S(2)}, u32[]{:S(2)}) %all-to-all-start.1) | async-done | bytes 294944 | tf_op jit(solution)/shard_map/all_to_all | solution.py:429
  174.9 18.4 %attention_forward.1 = (bf16[2,256,768]{2,1,0:T(8,128)(2,1)}, bf16[2,256,768]{2,1,0:T(8,128)(2,1)}, bf16[2,256,768]{2,1,0:T(8,128)(2,1)}, bf16[2,256,768]{2,1,0:...) custom-call(s32[2]{0:T(128)} %mul.83.length_ref, ...), custom_call_target="tpu_custom_call" | custom-call | flops 2818572288 | bytes 21794824 | tf_op jit(solution)/shard_map/attention_forward/pallas_call | solution.py:764
  194.1 2.7 place.26
  198.9 13.6 %feed_forward.2 = (f32[512,768]{1,0:T(8,128)}, f32[512,768]{1,0:T(8,128)}, bf16[3,768,1024]{2,1,0:T(8,128)(2,1)}) custom-call(bf16[512,768]{1,0:T(8,128)(2,1)} %bitcast.392, bf16[512,768]{1,0:T(8,128)(2,1)} %bitcast.394, bf16[768,3072]{1,0:T(8,128)(2,1)} %bitcast.366, bf16[768,3072]{1,0:T(8,128)(2,1)} %bitcast.367, bf16[768,3072]{1,0:T(8,128)(2,1)} %bitcast.368), custom_call_target="tpu_custom_call" | custom-call | flops 7247757312 | bytes 23592960 | tf_op jit(solution)/shard_map/feed_forward/pallas_call | solution.py:764
  212.5 4.5 constant_dynamic-slice_fusion.11
  222.0 13.9 %feed_forward.3 = (f32[512,768]{1,0:T(8,128)}, f32[512,768]{1,0:T(8,128)}, bf16[3,768,1024]{2,1,0:T(8,128)(2,1)}) custom-call(bf16[512,768]{1,0:T(8,128)(2,1)} %bitcast.393, bf16[512,768]{1,0:T(8,128)(2,1)} %bitcast.395, bf16[768,3072]{1,0:T(8,128)(2,1)} %bitcast.363, bf16[768,3072]{1,0:T(8,128)(2,1)} %bitcast.364, bf16[768,3072]{1,0:T(8,128)(2,1)} %bitcast.365), custom_call_target="tpu_custom_call" | custom-call | flops 7247757312 | bytes 23592960 | tf_op jit(solution)/shard_map/feed_forward/pallas_call | solution.py:764
  235.9 4.3 fusion.2
  244.3 18.4 %attention_backward.1 = (bf16[2,256,768]{2,1,0:T(8,128)(2,1)}, f32[2,256,768]{2,1,0:T(8,128)}, bf16[4,2,256,768]{3,2,1,0:T(8,128)(2,1)}, f32[2,8,768]{2,1,0:T(8,128)}) custom-call(s32[2]{0:T(128)} %mul.83.length_ref, f32[2,256,768]{2,1,0:T(8,128)} %bitcast.380, f32[2,256,768]{2,1,0:T(8,128)} %bitcast.382, f32[2,256,768]{2,1,0:T(8,128)} %bitcast.381, ...), custom_call_target="tpu_custom_call" | custom-call | flops 1610612736 | bytes 27349000 | tf_op jit(solution)/shard_map/attention_backward/pallas_call | solution.py:764
  262.8 9.5 %collective-permute-done.19 = bf16[3,4,2,24,1024]{4,3,0,1,2:T(8,128)(2,1)} collective-permute-done((bf16[3,4,2,24,1024]{4,3,0,1,2:T(8,128)(2,1)S(1)}, bf16[3,4,2,24,1024]{4,3,0,1,2:T(8,128)(2,1)}, u32[]{:S(2)}, u32[]{:S(2)}) %collective-permute-start.19) | collective-permute-done | bytes 1179680 | tf_op jit(solution)/shard_map/ppermute | solution.py:361
  274.0 2.8 fusion.1
  280.3 11.7 %projection_backward.1 = (bf16[4,768,768]{2,1,0:T(8,128)(2,1)}, f32[2,256,768]{2,1,0:T(8,128)}, bf16[2,8,768]{2,1,0:T(8,128)(2,1)}) custom-call(bf16[4,2,256,768]{3,2,1,0:T(8,128)(2,1)} %get-tuple-element.91.grads_in_ref, bf16[2,256,768]{2,1,0:T(8,128)(2,1)} %get-tuple-element.92.first_ref, bf16[2,256,768]{2,1,0:T(8,128)(2,1)} %get-tuple-element.93.attended_ref, ...), custom_call_target="tpu_custom_call" | custom-call | flops 4227858432 | bytes 18201600 | tf_op jit(solution)/shard_map/projection_backward/pallas_call | solution.py:764
  292.0 25.3 %collective-permute-done.21 = bf16[3,4,24,1024]{3,2,0,1:T(8,128)(2,1)} collective-permute-done((bf16[3,4,24,1024]{3,2,0,1:T(8,128)(2,1)S(1)}, bf16[3,4,24,1024]{3,2,0,1:T(8,128)(2,1)}, u32[]{:S(2)}, u32[]{:S(2)}) %collective-permute-start.21) | collective-permute-done | bytes 589856 | tf_op jit(solution)/shard_map/ppermute | solution.py:361
  336.0 2.4 collective-permute-start.25
  341.3 2.5 collective-permute-start.30
  343.8 2.3 collective-permute-start.31
  349.5 3.2 collective-permute-done.30
  355.0 2.3 fusion
  357.3 3.2 collective-permute-start.36
  368.2 3.2 collective-permute-done.37
  371.6 6.0 %collective-permute-done.35 = bf16[2,4,2,24,768]{4,3,0,1,2:T(8,128)(2,1)S(1)} collective-permute-done((bf16[2,4,2,24,768]{4,3,0,1,2:T(8,128)(2,1)S(1)}, bf16[2,4,2,24,768]{4,3,0,1,2:T(8,128)(2,1)S(1)}, u32[]{:S(2)}, u32[]{:S(2)}) %collective-permute-start.35) | collective-permute-done | bytes 589856 | tf_op jit(solution)/shard_map/ppermute | solution.py:361
  381.1 4.9 all-to-all-start.2
  394.7 10.1 %collective-permute-done.40 = bf16[2,4,24,768]{3,2,0,1:T(8,128)(2,1)S(1)} collective-permute-done((bf16[2,4,24,768]{3,2,0,1:T(8,128)(2,1)S(1)}, bf16[2,4,24,768]{3,2,0,1:T(8,128)(2,1)S(1)}, u32[]{:S(2)}, u32[]{:S(2)}) %collective-permute-start.40) | collective-permute-done | bytes 294944 | tf_op jit(solution)/shard_map/ppermute | solution.py:361
  408.2 2.4 collective-permute-start.43
  411.2 8.5 %collective-permute-done.41 = bf16[4,24,768]{2,1,0:T(8,128)(2,1)S(1)} collective-permute-done((bf16[4,24,768]{2,1,0:T(8,128)(2,1)S(1)}, bf16[4,24,768]{2,1,0:T(8,128)(2,1)S(1)}, u32[]{:S(2)}, u32[]{:S(2)}) %collective-permute-start.41) | collective-permute-done | bytes 147488 | tf_op jit(solution)/shard_map/ppermute | solution.py:364
  419.7 12.6 %collective-permute-done.42 = bf16[4,24,768]{2,1,0:T(8,128)(2,1)S(1)} collective-permute-done((bf16[4,24,768]{2,1,0:T(8,128)(2,1)S(1)}, bf16[4,24,768]{2,1,0:T(8,128)(2,1)S(1)}, u32[]{:S(2)}, u32[]{:S(2)}) %collective-permute-start.42) | collective-permute-done | bytes 147488 | tf_op jit(solution)/shard_map/ppermute | solution.py:364
  435.2 6.1 %all-to-all-start.3 = ((bf16[16,24,768]{2,1,0:T(8,128)(2,1)}), bf16[16,24,768]{2,1,0:T(8,128)(2,1)}, u32[]{:S(2)}, u32[]{:S(2)}) async-start(bf16[16,24,768]{2,1,0:T(8,128)(2,1)} %slots.3), calls=%async_computation.3 | async-start | bytes 1179648 | tf_op jit(solution)/shard_map/all_to_all | solution.py:470
  451.4 7.5 %collective-permute-done.44.refs_1_ = bf16[24,9216]{1,0:T(8,128)(2,1)S(1)} collective-permute-done((bf16[24,9216]{1,0:T(8,128)(2,1)}, bf16[24,9216]{1,0:T(8,128)(2,1)S(1)}, u32[]{:S(2)}, u32[]{:S(2)}) %collective-permute-start.44) | collective-permute-done | bytes 442400 | tf_op jit(solution)/shard_map/ppermute | solution.py:361
  460.1 7.1 %collective-permute-done.28 = bf16[2,4,2,2,8,768]{5,4,3,2,1,0:T(8,128)(2,1)} collective-permute-done((bf16[2,4,2,2,8,768]{5,4,3,2,1,0:T(8,128)(2,1)}, bf16[2,4,2,2,8,768]{5,4,3,2,1,0:T(8,128)(2,1)}, u32[]{:S(2)}, u32[]{:S(2)}) %collective-permute-start.28) | collective-permute-done | bytes 393248 | tf_op jit(solution)/shard_map/ppermute | solution.py:361
  470.7 4.1 multiply_add_fusion
  482.4 18.5 %newton_schulz.3 = bf16[768,768]{1,0:T(8,128)(2,1)S(1)} custom-call(s32[1]{0:T(128)} %bitcast.110.active_ref, bf16[768,768]{1,0:T(8,128)(2,1)S(1)} %bitcast.372, bf16[64,768]{1,0:T(8,128)(2,1)S(1)} %bitcast.373, bf16[64,768]{1,0:T(8,128)(2,1)S(1)} %fusion.46.right_ref), custom_call_target="tpu_custom_call" | custom-call | flops 18119393280 | bytes 2359296 | tf_op jit(solution)/shard_map/newton_schulz/pallas_call | solution.py:139
  502.3 23.3 %all-to-all-start.4 = ((bf16[16,24,1024]{2,1,0:T(8,128)(2,1)}), bf16[16,24,1024]{2,1,0:T(8,128)(2,1)S(1)}, u32[]{:S(2)}, u32[]{:S(2)}) async-start(bf16[16,24,1024]{2,1,0:T(8,128)(2,1)} %bitcast.116), calls=%async_computation.4 | async-start | bytes 1572864 | tf_op jit(solution)/shard_map/all_to_all | solution.py:489
  527.9 18.8 %all-to-all-done.4 = bf16[16,24,1024]{2,1,0:T(8,128)(2,1)S(1)} async-done(((bf16[16,24,1024]{2,1,0:T(8,128)(2,1)}), bf16[16,24,1024]{2,1,0:T(8,128)(2,1)S(1)}, u32[]{:S(2)}, u32[]{:S(2)}) %all-to-all-start.4) | async-done | bytes 786464 | tf_op jit(solution)/shard_map/all_to_all | solution.py:489
  548.4 2.2 multiply_add_fusion.4
  553.5 9.2 %collective-permute-done.48.refs_1_ = bf16[24,13824]{1,0:T(8,128)(2,1)S(1)} collective-permute-done((bf16[24,13824]{1,0:T(8,128)(2,1)S(1)}, bf16[24,13824]{1,0:T(8,128)(2,1)S(1)}, u32[]{:S(2)}, u32[]{:S(2)}) %collective-permute-start.48) | collective-permute-done | bytes 663584 | tf_op jit(solution)/shard_map/ppermute | solution.py:361
  (331 shorter events, 168.7 us)
Async XLA Ops:
  4.4 12.9 %collective-permute-start = (bf16[24,3072]{1,0:T(8,128)(2,1)S(1)}, bf16[24,3072]{1,0:T(8,128)(2,1)S(1)}, u32[]{:S(2)}, u32[]{:S(2)}) collective-permute-start(bf16[24,3072]{1,0:T(8,128)(2,1)S(1)} %fusion.37.refs_0_), channel_id=1, source_target_pairs={{0,2},{2,4},{4,6},{6,0},{1,3},{3,5},{5,7},{7,1},{8,10},{10,12},{12... | collective-permute-start | bytes 442376 | tf_op jit(solution)/shard_map/ppermute | solution.py:364
  7.5 12.3 %collective-permute-start.1 = (bf16[24,3072]{1,0:T(8,128)(2,1)S(1)}, bf16[24,3072]{1,0:T(8,128)(2,1)S(1)}, u32[]{:S(2)}, u32[]{:S(2)}) collective-permute-start(bf16[24,3072]{1,0:T(8,128)(2,1)S(1)} %fusion.37.refs_0_), channel_id=1, source_target_pairs={{0,4},{2,6},{4,0},{6,2},{1,5},{3,7},{5,1},{7,3},{8,12},{10,14},{12... | collective-permute-start | bytes 442376 | tf_op jit(solution)/shard_map/ppermute | solution.py:364
  10.1 9.7 %collective-permute-start.2 = (bf16[24,3072]{1,0:T(8,128)(2,1)S(1)}, bf16[24,3072]{1,0:T(8,128)(2,1)}, u32[]{:S(2)}, u32[]{:S(2)}) collective-permute-start(bf16[24,3072]{1,0:T(8,128)(2,1)S(1)} %fusion.37.refs_0_), channel_id=1, source_target_pairs={{0,6},{2,0},{4,2},{6,4},{1,7},{3,1},{5,3},{7,5},{8,14},{10,8},{12,... | collective-permute-start | bytes 442376 | tf_op jit(solution)/shard_map/ppermute | solution.py:364
  20.7 8.9 %collective-permute-start.6 = (bf16[4,24,1536]{2,1,0:T(8,128)(2,1)S(1)}, bf16[4,24,1536]{2,1,0:T(8,128)(2,1)S(1)}, u32[]{:S(2)}, u32[]{:S(2)}) collective-permute-start(bf16[4,24,1536]{2,1,0:T(8,128)(2,1)S(1)} %get-tuple-element.66.refs_0_), channel_id=1, source_target_pairs={{0,16},{16,0},{1,17},{17,1},{2,18},{18,2},{3,19},{19,3},{4,20},{20... | collective-permute-start | bytes 884744 | tf_op jit(solution)/shard_map/ppermute | solution.py:361
  22.3 9.5 %collective-permute-start.3 = (bf16[4,24,1536]{2,1,0:T(8,128)(2,1)S(1)}, bf16[4,24,1536]{2,1,0:T(8,128)(2,1)S(1)}, u32[]{:S(2)}, u32[]{:S(2)}) collective-permute-start(bf16[4,24,1536]{2,1,0:T(8,128)(2,1)S(1)} %get-tuple-element.65.refs_0_), channel_id=1, source_target_pairs={{0,1},{1,0},{2,3},{3,2},{4,5},{5,4},{6,7},{7,6},{8,9},{9,8},{10,11... | collective-permute-start | bytes 884744 | tf_op jit(solution)/shard_map/ppermute | solution.py:361
  30.2 30.7 %collective-permute-start.7 = (bf16[2,4,24,1536]{3,2,1,0:T(8,128)(2,1)S(1)}, bf16[2,4,24,1536]{3,2,1,0:T(8,128)(2,1)S(1)}, u32[]{:S(2)}, u32[]{:S(2)}) collective-permute-start(bf16[2,4,24,1536]{3,2,1,0:T(8,128)(2,1)S(1)} %place.21.refs_0_), channel_id=1, source_target_pairs={{0,1},{1,0},{2,3},{3,2},{4,5},{5,4},{6,7},{7,6},{8,9},{9,8},{10,11... | collective-permute-start | bytes 1769480 | tf_op jit(solution)/shard_map/ppermute | solution.py:361
  32.4 30.2 %collective-permute-start.4 = (bf16[2,4,24,1536]{3,2,1,0:T(8,128)(2,1)S(1)}, bf16[2,4,24,1536]{3,2,1,0:T(8,128)(2,1)S(1)}, u32[]{:S(2)}, u32[]{:S(2)}) collective-permute-start(bf16[2,4,24,1536]{3,2,1,0:T(8,128)(2,1)S(1)} %place.18.refs_0_), channel_id=1, source_target_pairs={{0,16},{16,0},{1,17},{17,1},{2,18},{18,2},{3,19},{19,3},{4,20},{20... | collective-permute-start | bytes 1769480 | tf_op jit(solution)/shard_map/ppermute | solution.py:361
  34.9 18.8 %collective-permute-start.10 = (bf16[24,6144]{1,0:T(8,128)(2,1)S(1)}, bf16[24,6144]{1,0:T(8,128)(2,1)S(1)}, u32[]{:S(2)}, u32[]{:S(2)}) collective-permute-start(bf16[24,6144]{1,0:T(8,128)(2,1)S(1)} %constant_dynamic-slice_fusion.12.refs_0_), channel_id=1, source_target_pairs={{0,4},{2,6},{4,0},{6,2},{1,5},{3,7},{5,1},{7,3},{8,12},{10,14},{12... | collective-permute-start | bytes 884744 | tf_op jit(solution)/shard_map/ppermute | solution.py:364
  37.7 16.0 %collective-permute-start.11 = (bf16[24,6144]{1,0:T(8,128)(2,1)S(1)}, bf16[24,6144]{1,0:T(8,128)(2,1)S(1)}, u32[]{:S(2)}, u32[]{:S(2)}) collective-permute-start(bf16[24,6144]{1,0:T(8,128)(2,1)S(1)} %constant_dynamic-slice_fusion.12.refs_0_), channel_id=1, source_target_pairs={{0,6},{2,0},{4,2},{6,4},{1,7},{3,1},{5,3},{7,5},{8,14},{10,8},{12,... | collective-permute-start | bytes 884744 | tf_op jit(solution)/shard_map/ppermute | solution.py:364
  41.2 18.3 %collective-permute-start.9 = (bf16[24,6144]{1,0:T(8,128)(2,1)S(1)}, bf16[24,6144]{1,0:T(8,128)(2,1)S(1)}, u32[]{:S(2)}, u32[]{:S(2)}) collective-permute-start(bf16[24,6144]{1,0:T(8,128)(2,1)S(1)} %constant_dynamic-slice_fusion.12.refs_0_), channel_id=1, source_target_pairs={{0,2},{2,4},{4,6},{6,0},{1,3},{3,5},{5,7},{7,1},{8,10},{10,12},{12... | collective-permute-start | bytes 884744 | tf_op jit(solution)/shard_map/ppermute | solution.py:364
  64.2 12.9 %collective-permute-start.12 = (bf16[4,24,3072]{2,1,0:T(8,128)(2,1)S(1)}, bf16[4,24,3072]{2,1,0:T(8,128)(2,1)S(1)}, u32[]{:S(2)}, u32[]{:S(2)}) collective-permute-start(bf16[4,24,3072]{2,1,0:T(8,128)(2,1)S(1)} %get-tuple-element.72.refs_0_), channel_id=1, source_target_pairs={{0,1},{1,0},{2,3},{3,2},{4,5},{5,4},{6,7},{7,6},{8,9},{9,8},{10,11... | collective-permute-start | bytes 1769480 | tf_op jit(solution)/shard_map/ppermute | solution.py:361
  77.8 24.7 %collective-permute-start.13 = (bf16[2,4,24,3072]{3,2,1,0:T(8,128)(2,1)S(1)}, bf16[2,4,24,3072]{3,2,1,0:T(8,128)(2,1)S(1)}, u32[]{:S(2)}, u32[]{:S(2)}) collective-permute-start(bf16[2,4,24,3072]{3,2,1,0:T(8,128)(2,1)S(1)} %place.24.refs_0_), channel_id=1, source_target_pairs={{0,16},{16,0},{1,17},{17,1},{2,18},{18,2},{3,19},{19,3},{4,20},{20... | collective-permute-start | bytes 3538952 | tf_op jit(solution)/shard_map/ppermute | solution.py:361
  104.6 89.5 %collective-permute-start.14 = (bf16[2,2,4,24,3072]{4,3,2,1,0:T(8,128)(2,1)}, bf16[2,2,4,24,3072]{4,3,2,1,0:T(8,128)(2,1)}, u32[]{:S(2)}, u32[]{:S(2)}) collective-permute-start(bf16[2,2,4,24,3072]{4,3,2,1,0:T(8,128)(2,1)} %place.25.refs_0_), channel_id=1, source_target_pairs={{0,8},{8,0},{1,9},{9,1},{2,10},{10,2},{3,11},{11,3},{4,12},{12,4},... | collective-permute-start | bytes 7077896 | tf_op jit(solution)/shard_map/ppermute | solution.py:361
  106.5 31.2 %all-to-all-start = ((bf16[8,2,96]{2,1,0:T(2,128)(2,1)}), bf16[8,2,96]{2,1,0:T(2,128)(2,1)S(1)}, u32[]{:S(2)}, u32[]{:S(2)}) async-start(bf16[8,2,96]{2,1,0:T(2,128)(2,1)} %bitcast.355), calls=%async_computation | async-start | bytes 8192 | tf_op jit(solution)/shard_map/all_to_all | solution.py:429
  118.0 15.7 %collective-permute-start.15 = (bf16[4,24,3072]{2,1,0:T(8,128)(2,1)}, bf16[4,24,3072]{2,1,0:T(8,128)(2,1)S(1)}, u32[]{:S(2)}, u32[]{:S(2)}) collective-permute-start(bf16[4,24,3072]{2,1,0:T(8,128)(2,1)} %copy-done.14), channel_id=1, source_target_pairs={{0,16},{16,0},{1,17},{17,1},{2,18},{18,2},{3,19},{19,3},{4,20},{20... | collective-permute-start | bytes 1769480 | tf_op jit(solution)/shard_map/ppermute | solution.py:361
  120.6 48.5 %collective-permute-start.8 = (bf16[2,2,4,24,1536]{4,3,2,1,0:T(8,128)(2,1)}, bf16[2,2,4,24,1536]{4,3,2,1,0:T(8,128)(2,1)}, u32[]{:S(2)}, u32[]{:S(2)}) collective-permute-start(bf16[2,2,4,24,1536]{4,3,2,1,0:T(8,128)(2,1)} %copy-done.3), channel_id=1, source_target_pairs={{0,8},{8,0},{1,9},{9,1},{2,10},{10,2},{3,11},{11,3},{4,12},{12,4},... | collective-permute-start | bytes 3538952 | tf_op jit(solution)/shard_map/ppermute | solution.py:361
  120.6 51.5 %collective-permute-start.5 = (bf16[2,2,4,24,1536]{4,3,2,1,0:T(8,128)(2,1)}, bf16[2,2,4,24,1536]{4,3,2,1,0:T(8,128)(2,1)}, u32[]{:S(2)}, u32[]{:S(2)}) collective-permute-start(bf16[2,2,4,24,1536]{4,3,2,1,0:T(8,128)(2,1)} %copy-done.5), channel_id=1, source_target_pairs={{0,8},{8,0},{1,9},{9,1},{2,10},{10,2},{3,11},{11,3},{4,12},{12,4},... | collective-permute-start | bytes 3538952 | tf_op jit(solution)/shard_map/ppermute | solution.py:361
  135.4 57.9 %collective-permute-start.16 = (bf16[2,4,24,3072]{3,2,1,0:T(8,128)(2,1)S(1)}, bf16[2,4,24,3072]{3,2,1,0:T(8,128)(2,1)S(1)}, u32[]{:S(2)}, u32[]{:S(2)}) collective-permute-start(bf16[2,4,24,3072]{3,2,1,0:T(8,128)(2,1)S(1)} %place.27.refs_0_), channel_id=1, source_target_pairs={{0,1},{1,0},{2,3},{3,2},{4,5},{5,4},{6,7},{7,6},{8,9},{9,8},{10,11... | collective-permute-start | bytes 3538952 | tf_op jit(solution)/shard_map/ppermute | solution.py:361
  140.5 25.5 %all-to-all-start.1 = ((f32[8,2,6,768]{3,1,2,0:T(2,128)}), f32[8,2,6,768]{3,1,2,0:T(2,128)}, u32[]{:S(2)}, u32[]{:S(2)}) async-start(f32[8,2,6,768]{3,1,2,0:T(2,128)} %copy.69), calls=%async_computation.1 | async-start | bytes 589824 | tf_op jit(solution)/shard_map/all_to_all | solution.py:429
  194.0 25.0 %collective-permute-start.17 = (bf16[2,2,4,24,3072]{4,3,2,1,0:T(8,128)(2,1)S(1)}, bf16[2,2,4,24,3072]{4,3,2,1,0:T(8,128)(2,1)S(1)}, u32[]{:S(2)}, u32[]{:S(2)}) collective-permute-start(bf16[2,2,4,24,3072]{4,3,2,1,0:T(8,128)(2,1)S(1)} %place.28.refs_0_), channel_id=1, source_target_pairs={{0,8},{8,0},{1,9},{9,1},{2,10},{10,2},{3,11},{11,3},{4,12},{12,4},... | collective-permute-start | bytes 7077896 | tf_op jit(solution)/shard_map/ppermute | solution.py:361
  218.6 17.3 %collective-permute-start.18 = (bf16[3,4,2,2,24,1024]{5,4,0,1,2,3:T(8,128)(2,1)}, bf16[3,4,2,2,24,1024]{5,4,0,1,2,3:T(8,128)(2,1)}, u32[]{:S(2)}, u32[]{:S(2)}) collective-permute-start(bf16[3,4,2,2,24,1024]{5,4,0,1,2,3:T(8,128)(2,1)} %bitcast.354), channel_id=1, source_target_pairs={{0,8},{8,0},{1,9},{9,1},{2,10},{10,2},{3,11},{11,3},{4,12},{12,4},... | collective-permute-start | bytes 7077896 | tf_op jit(solution)/shard_map/ppermute | solution.py:361
  242.3 31.7 %collective-permute-start.20 = (bf16[3,4,2,2,24,1024]{5,4,0,1,3,2:T(8,128)(2,1)}, bf16[3,4,2,2,24,1024]{5,4,0,1,3,2:T(8,128)(2,1)}, u32[]{:S(2)}, u32[]{:S(2)}) collective-permute-start(bf16[3,4,2,2,24,1024]{5,4,0,1,3,2:T(8,128)(2,1)} %bitcast.353), channel_id=1, source_target_pairs={{0,8},{8,0},{1,9},{9,1},{2,10},{10,2},{3,11},{11,3},{4,12},{12,4},... | collective-permute-start | bytes 7077896 | tf_op jit(solution)/shard_map/ppermute | solution.py:361
  243.7 28.5 %collective-permute-start.19 = (bf16[3,4,2,24,1024]{4,3,0,1,2:T(8,128)(2,1)S(1)}, bf16[3,4,2,24,1024]{4,3,0,1,2:T(8,128)(2,1)}, u32[]{:S(2)}, u32[]{:S(2)}) collective-permute-start(bf16[3,4,2,24,1024]{4,3,0,1,2:T(8,128)(2,1)S(1)} %dynamic-slice_bitcast_fusion.1), channel_id=1, source_target_pairs={{0,16},{16,0},{1,17},{17,1},{2,18},{18,2},{3,19},{19,3},{4,20},{20... | collective-permute-start | bytes 3538952 | tf_op jit(solution)/shard_map/ppermute | solution.py:361
  276.9 41.8 %collective-permute-start.22 = (bf16[3,4,2,24,1024]{4,3,0,1,2:T(8,128)(2,1)S(1)}, bf16[3,4,2,24,1024]{4,3,0,1,2:T(8,128)(2,1)}, u32[]{:S(2)}, u32[]{:S(2)}) collective-permute-start(bf16[3,4,2,24,1024]{4,3,0,1,2:T(8,128)(2,1)S(1)} %dynamic-slice_bitcast_fusion), channel_id=1, source_target_pairs={{0,1},{1,0},{2,3},{3,2},{4,5},{5,4},{6,7},{7,6},{8,9},{9,8},{10,11... | collective-permute-start | bytes 3538952 | tf_op jit(solution)/shard_map/ppermute | solution.py:361
  278.5 38.8 %collective-permute-start.21 = (bf16[3,4,24,1024]{3,2,0,1:T(8,128)(2,1)S(1)}, bf16[3,4,24,1024]{3,2,0,1:T(8,128)(2,1)}, u32[]{:S(2)}, u32[]{:S(2)}) collective-permute-start(bf16[3,4,24,1024]{3,2,0,1:T(8,128)(2,1)S(1)} %dynamic-slice_bitcast_fusion.5), channel_id=1, source_target_pairs={{0,1},{1,0},{2,3},{3,2},{4,5},{5,4},{6,7},{7,6},{8,9},{9,8},{10,11... | collective-permute-start | bytes 1769480 | tf_op jit(solution)/shard_map/ppermute | solution.py:361
  324.3 30.7 %collective-permute-start.33 = (bf16[4,4,2,2,24,768]{5,4,0,1,3,2:T(8,128)(2,1)}, bf16[4,4,2,2,24,768]{5,4,0,1,3,2:T(8,128)(2,1)}, u32[]{:S(2)}, u32[]{:S(2)}) collective-permute-start(bf16[4,4,2,2,24,768]{5,4,0,1,3,2:T(8,128)(2,1)} %bitcast.352), channel_id=1, source_target_pairs={{0,8},{8,0},{1,9},{9,1},{2,10},{10,2},{3,11},{11,3},{4,12},{12,4},... | collective-permute-start | bytes 7077896 | tf_op jit(solution)/shard_map/ppermute | solution.py:361
  330.1 23.5 %collective-permute-start.32 = (bf16[3,4,24,1024]{3,2,0,1:T(8,128)(2,1)}, bf16[3,4,24,1024]{3,2,0,1:T(8,128)(2,1)}, u32[]{:S(2)}, u32[]{:S(2)}) collective-permute-start(bf16[3,4,24,1024]{3,2,0,1:T(8,128)(2,1)} %dynamic-slice_bitcast_fusion.4), channel_id=1, source_target_pairs={{0,16},{16,0},{1,17},{17,1},{2,18},{18,2},{3,19},{19,3},{4,20},{20... | collective-permute-start | bytes 1769480 | tf_op jit(solution)/shard_map/ppermute | solution.py:361
  341.3 11.4 %collective-permute-start.30 = (bf16[3,24,1024]{2,1,0:T(8,128)(2,1)}, bf16[3,24,1024]{2,1,0:T(8,128)(2,1)S(1)}, u32[]{:S(2)}, u32[]{:S(2)}) collective-permute-start(bf16[3,24,1024]{2,1,0:T(8,128)(2,1)} %get-tuple-element.160), channel_id=1, source_target_pairs={{0,4},{2,6},{4,0},{6,2},{1,5},{3,7},{5,1},{7,3},{8,12},{10,14},{12... | collective-permute-start | bytes 442376 | tf_op jit(solution)/shard_map/ppermute | solution.py:364
  343.8 8.9 %collective-permute-start.31 = (bf16[3,24,1024]{2,1,0:T(8,128)(2,1)}, bf16[3,24,1024]{2,1,0:T(8,128)(2,1)S(1)}, u32[]{:S(2)}, u32[]{:S(2)}) collective-permute-start(bf16[3,24,1024]{2,1,0:T(8,128)(2,1)} %get-tuple-element.159), channel_id=1, source_target_pairs={{0,6},{2,0},{4,2},{6,4},{1,7},{3,1},{5,3},{7,5},{8,14},{10,8},{12,... | collective-permute-start | bytes 442376 | tf_op jit(solution)/shard_map/ppermute | solution.py:364
  357.3 10.9 %collective-permute-start.36 = (bf16[3,24,1024]{2,1,0:T(8,128)(2,1)S(1)}, bf16[3,24,1024]{2,1,0:T(8,128)(2,1)S(1)}, u32[]{:S(2)}, u32[]{:S(2)}) collective-permute-start(bf16[3,24,1024]{2,1,0:T(8,128)(2,1)S(1)} %get-tuple-element.155), channel_id=1, source_target_pairs={{0,2},{2,4},{4,6},{6,0},{1,3},{3,5},{5,7},{7,1},{8,10},{10,12},{12... | collective-permute-start | bytes 442376 | tf_op jit(solution)/shard_map/ppermute | solution.py:364
  360.6 10.9 %collective-permute-start.37 = (bf16[3,24,1024]{2,1,0:T(8,128)(2,1)S(1)}, bf16[3,24,1024]{2,1,0:T(8,128)(2,1)S(1)}, u32[]{:S(2)}, u32[]{:S(2)}) collective-permute-start(bf16[3,24,1024]{2,1,0:T(8,128)(2,1)S(1)} %get-tuple-element.157), channel_id=1, source_target_pairs={{0,4},{2,6},{4,0},{6,2},{1,5},{3,7},{5,1},{7,3},{8,12},{10,14},{12... | collective-permute-start | bytes 442376 | tf_op jit(solution)/shard_map/ppermute | solution.py:364
  363.3 14.3 %collective-permute-start.35 = (bf16[2,4,2,24,768]{4,3,0,1,2:T(8,128)(2,1)S(1)}, bf16[2,4,2,24,768]{4,3,0,1,2:T(8,128)(2,1)S(1)}, u32[]{:S(2)}, u32[]{:S(2)}) collective-permute-start(bf16[2,4,2,24,768]{4,3,0,1,2:T(8,128)(2,1)S(1)} %dynamic-slice_bitcast_fusion.2), channel_id=1, source_target_pairs={{0,1},{1,0},{2,3},{3,2},{4,5},{5,4},{6,7},{7,6},{8,9},{9,8},{10,11... | collective-permute-start | bytes 1769480 | tf_op jit(solution)/shard_map/ppermute | solution.py:361
  364.8 14.0 %collective-permute-start.34 = (bf16[2,4,2,24,768]{4,3,0,1,2:T(8,128)(2,1)S(1)}, bf16[2,4,2,24,768]{4,3,0,1,2:T(8,128)(2,1)S(1)}, u32[]{:S(2)}, u32[]{:S(2)}) collective-permute-start(bf16[2,4,2,24,768]{4,3,0,1,2:T(8,128)(2,1)S(1)} %dynamic-slice_bitcast_fusion.3), channel_id=1, source_target_pairs={{0,16},{16,0},{1,17},{17,1},{2,18},{18,2},{3,19},{19,3},{4,20},{20... | collective-permute-start | bytes 1769480 | tf_op jit(solution)/shard_map/ppermute | solution.py:361
  368.2 75.8 %collective-permute-start.27 = (bf16[4,2,2,8,768]{4,3,2,1,0:T(8,128)(2,1)}, bf16[4,2,2,8,768]{4,3,2,1,0:T(8,128)(2,1)}, u32[]{:S(2)}, u32[]{:S(2)}) collective-permute-start(bf16[4,2,2,8,768]{4,3,2,1,0:T(8,128)(2,1)} %broadcast_select_fusion), channel_id=1, source_target_pairs={{0,8},{8,0},{1,9},{9,1},{2,10},{10,2},{3,11},{11,3},{4,12},{12,4},... | collective-permute-start | bytes 589832 | tf_op jit(solution)/shard_map/ppermute | solution.py:361
  381.1 54.1 %all-to-all-start.2 = ((bf16[16,24,2048]{2,1,0:T(8,128)(2,1)}), bf16[16,24,2048]{2,1,0:T(8,128)(2,1)S(1)}, u32[]{:S(2)}, u32[]{:S(2)}) async-start(bf16[16,24,2048]{2,1,0:T(8,128)(2,1)} %slots.2), calls=%async_computation.2 | async-start | bytes 3145728 | tf_op jit(solution)/shard_map/all_to_all | solution.py:470
  388.9 15.9 %collective-permute-start.40 = (bf16[2,4,24,768]{3,2,0,1:T(8,128)(2,1)S(1)}, bf16[2,4,24,768]{3,2,0,1:T(8,128)(2,1)S(1)}, u32[]{:S(2)}, u32[]{:S(2)}) collective-permute-start(bf16[2,4,24,768]{3,2,0,1:T(8,128)(2,1)S(1)} %dynamic-slice_bitcast_fusion.6), channel_id=1, source_target_pairs={{0,16},{16,0},{1,17},{17,1},{2,18},{18,2},{3,19},{19,3},{4,20},{20... | collective-permute-start | bytes 884744 | tf_op jit(solution)/shard_map/ppermute | solution.py:361
  391.9 14.6 %collective-permute-start.39 = (bf16[2,4,24,768]{3,2,0,1:T(8,128)(2,1)S(1)}, bf16[2,4,24,768]{3,2,0,1:T(8,128)(2,1)S(1)}, u32[]{:S(2)}, u32[]{:S(2)}) collective-permute-start(bf16[2,4,24,768]{3,2,0,1:T(8,128)(2,1)S(1)} %dynamic-slice_bitcast_fusion.7), channel_id=1, source_target_pairs={{0,1},{1,0},{2,3},{3,2},{4,5},{5,4},{6,7},{7,6},{8,9},{9,8},{10,11... | collective-permute-start | bytes 884744 | tf_op jit(solution)/shard_map/ppermute | solution.py:361
  406.7 13.0 %collective-permute-start.41 = (bf16[4,24,768]{2,1,0:T(8,128)(2,1)S(1)}, bf16[4,24,768]{2,1,0:T(8,128)(2,1)S(1)}, u32[]{:S(2)}, u32[]{:S(2)}) collective-permute-start(bf16[4,24,768]{2,1,0:T(8,128)(2,1)S(1)} %get-tuple-element.152), channel_id=1, source_target_pairs={{0,2},{2,4},{4,6},{6,0},{1,3},{3,5},{5,7},{7,1},{8,10},{10,12},{12... | collective-permute-start | bytes 442376 | tf_op jit(solution)/shard_map/ppermute | solution.py:364
  407.5 24.8 %collective-permute-start.42 = (bf16[4,24,768]{2,1,0:T(8,128)(2,1)S(1)}, bf16[4,24,768]{2,1,0:T(8,128)(2,1)S(1)}, u32[]{:S(2)}, u32[]{:S(2)}) collective-permute-start(bf16[4,24,768]{2,1,0:T(8,128)(2,1)S(1)} %get-tuple-element.153), channel_id=1, source_target_pairs={{0,4},{2,6},{4,0},{6,2},{1,5},{3,7},{5,1},{7,3},{8,12},{10,14},{12... | collective-permute-start | bytes 442376 | tf_op jit(solution)/shard_map/ppermute | solution.py:364
  408.2 24.1 %collective-permute-start.43 = (bf16[4,24,768]{2,1,0:T(8,128)(2,1)S(1)}, bf16[4,24,768]{2,1,0:T(8,128)(2,1)S(1)}, u32[]{:S(2)}, u32[]{:S(2)}) collective-permute-start(bf16[4,24,768]{2,1,0:T(8,128)(2,1)S(1)} %get-tuple-element.154), channel_id=1, source_target_pairs={{0,6},{2,0},{4,2},{6,4},{1,7},{3,1},{5,3},{7,5},{8,14},{10,8},{12,... | collective-permute-start | bytes 442376 | tf_op jit(solution)/shard_map/ppermute | solution.py:364
  435.2 34.5 %all-to-all-start.3 = ((bf16[16,24,768]{2,1,0:T(8,128)(2,1)}), bf16[16,24,768]{2,1,0:T(8,128)(2,1)}, u32[]{:S(2)}, u32[]{:S(2)}) async-start(bf16[16,24,768]{2,1,0:T(8,128)(2,1)} %slots.3), calls=%async_computation.3 | async-start | bytes 1179648 | tf_op jit(solution)/shard_map/all_to_all | solution.py:470
  441.3 38.6 %collective-permute-start.46 = (bf16[2,4,2,24,2048]{4,3,2,1,0:T(8,128)(2,1)S(1)}, bf16[2,4,2,24,2048]{4,3,2,1,0:T(8,128)(2,1)}, u32[]{:S(2)}, u32[]{:S(2)}) collective-permute-start(bf16[2,4,2,24,2048]{4,3,2,1,0:T(8,128)(2,1)S(1)} %bitcast.361), channel_id=1, source_target_pairs={{0,8},{8,0},{1,9},{9,1},{2,10},{10,2},{3,11},{11,3},{4,12},{12,4},... | collective-permute-start | bytes 4718600 | tf_op jit(solution)/shard_map/ppermute | solution.py:361
  442.0 17.0 %collective-permute-start.44 = (bf16[24,9216]{1,0:T(8,128)(2,1)}, bf16[24,9216]{1,0:T(8,128)(2,1)S(1)}, u32[]{:S(2)}, u32[]{:S(2)}) collective-permute-start(bf16[24,9216]{1,0:T(8,128)(2,1)} %constant_dynamic-update-slice_fusion.refs_0_), channel_id=1, source_target_pairs={{0,16},{16,0},{1,17},{17,1},{2,18},{18,2},{3,19},{19,3},{4,20},{20... | collective-permute-start | bytes 1327112 | tf_op jit(solution)/shard_map/ppermute | solution.py:361
  445.8 21.4 %collective-permute-start.28 = (bf16[2,4,2,2,8,768]{5,4,3,2,1,0:T(8,128)(2,1)}, bf16[2,4,2,2,8,768]{5,4,3,2,1,0:T(8,128)(2,1)}, u32[]{:S(2)}, u32[]{:S(2)}) collective-permute-start(bf16[2,4,2,2,8,768]{5,4,3,2,1,0:T(8,128)(2,1)} %maximum_select_fusion.2), channel_id=1, source_target_pairs={{0,16},{16,0},{1,17},{17,1},{2,18},{18,2},{3,19},{19,3},{4,20},{20... | collective-permute-start | bytes 1179656 | tf_op jit(solution)/shard_map/ppermute | solution.py:361
  460.0 14.8 %collective-permute-start.45 = (bf16[2,24,9216]{2,1,0:T(8,128)(2,1)S(1)}, bf16[2,24,9216]{2,1,0:T(8,128)(2,1)S(1)}, u32[]{:S(2)}, u32[]{:S(2)}) collective-permute-start(bf16[2,24,9216]{2,1,0:T(8,128)(2,1)S(1)} %place.30.refs_0_), channel_id=1, source_target_pairs={{0,8},{8,0},{1,9},{9,1},{2,10},{10,2},{3,11},{11,3},{4,12},{12,4},... | collective-permute-start | bytes 2654216 | tf_op jit(solution)/shard_map/ppermute | solution.py:361
  469.7 9.1 %collective-permute-start.47 = (bf16[2,4,2,24,768]{4,3,2,1,0:T(8,128)(2,1)}, bf16[2,4,2,24,768]{4,3,2,1,0:T(8,128)(2,1)S(1)}, u32[]{:S(2)}, u32[]{:S(2)}) collective-permute-start(bf16[2,4,2,24,768]{4,3,2,1,0:T(8,128)(2,1)} %bitcast.106.refs_0_), channel_id=1, source_target_pairs={{0,8},{8,0},{1,9},{9,1},{2,10},{10,2},{3,11},{11,3},{4,12},{12,4},... | collective-permute-start | bytes 1769480 | tf_op jit(solution)/shard_map/ppermute | solution.py:361
  502.3 44.4 %all-to-all-start.4 = ((bf16[16,24,1024]{2,1,0:T(8,128)(2,1)}), bf16[16,24,1024]{2,1,0:T(8,128)(2,1)S(1)}, u32[]{:S(2)}, u32[]{:S(2)}) async-start(bf16[16,24,1024]{2,1,0:T(8,128)(2,1)} %bitcast.116), calls=%async_computation.4 | async-start | bytes 1572864 | tf_op jit(solution)/shard_map/all_to_all | solution.py:489
  546.9 15.7 %collective-permute-start.48 = (bf16[24,13824]{1,0:T(8,128)(2,1)S(1)}, bf16[24,13824]{1,0:T(8,128)(2,1)S(1)}, u32[]{:S(2)}, u32[]{:S(2)}) collective-permute-start(bf16[24,13824]{1,0:T(8,128)(2,1)S(1)} %constant_dynamic-update-slice_fusion.10.refs_0_), channel_id=1, source_target_pairs={{0,16},{16,0},{1,17},{17,1},{2,18},{18,2},{3,19},{19,3},{4,20},{20... | collective-permute-start | bytes 1990664 | tf_op jit(solution)/shard_map/ppermute | solution.py:361
  (56 other events, 538.7 us)

commit v3 on v2

--- a/solution.py
+++ b/solution.py
@@ -50,7 +50,11 @@
     @pl.when(active_ref[0] != 0)
     def _():
         def load(b, acc):
-            v = feed_ref[:, block(b)].astype(F32)
+            if len(feed_ref.shape) == 3:
+                per = feed_ref.shape[2] // tile
+                v = feed_ref[b // per, :, block(lax.rem(b, per))].astype(F32)
+            else:
+                v = feed_ref[:, block(b)].astype(F32)
             if right_ref is not None:
                 v = v + (1.0 + MOMENTUM_DECAY) * dot(left_ref[...], right_ref[:, block(b)], TN)
             x[:, block(b)] = v
@@ -107,13 +111,12 @@
                 poly[spans[i], spans[i]] = diagonal(part - mean, part).astype(BF16)
             scale = COEFF_FIRST + level + mean
 
-            def update(b, inner):
-                new = scale * x[:, block(b)] + dot(poly[...], xb[:, block(b)])
-                x[:, block(b)] = new
-                xb[:, block(b)] = new.astype(BF16)
-                return inner
-
-            lax.fori_loop(0, blocks, update, 0)
+            size = width // 2 if width > 1024 else width
+            for b in range(width // size):
+                cols = slice(b * size, (b + 1) * size)
+                new = scale * x[:, cols] + dot(poly[...], xb[:, cols])
+                x[:, cols] = new
+                xb[:, cols] = new.astype(BF16)
             return carry
 
         lax.fori_loop(0, NS_ITERS, iterate, 0)
@@ -125,7 +128,7 @@
 
 
 def newton_schulz(active, feed, left=None, right=None):
-    width = feed.shape[1]
+    width = feed.size // D
     operands = [active.reshape(1).astype(jnp.int32), feed]
     if left is None:
 
@@ -160,6 +163,63 @@
     return lax.optimization_barrier((value, *others))[0]
 
 
+def meet(*values):
+    flat, tree = jax.tree.flatten(values)
+    return jax.tree.unflatten(tree, lax.optimization_barrier(tuple(flat)))
+
+
+def fold(mine, other, here, view, start, count):
+    before, after = view
+    rows, cols = mine.shape[-2:]
+    shape = (mine.shape[0], before, 2, after, rows, cols)
+    block = pl.BlockSpec((1, *shape[1:]), lambda k: (start + k, 0, 0, 0, 0, 0))
+    out = jax.ShapeDtypeStruct((count, before, after, rows, cols), BF16)
+    out_block = pl.BlockSpec((1, *out.shape[1:]), lambda k: (k, 0, 0, 0, 0))
+
+    def body(here_ref, mine_ref, other_ref, keep_ref, send_ref):
+        here = here_ref[0]
+        for ref, at in ((send_ref, 1 - here), (keep_ref, here)):
+            ref[0] = (mine_ref[0, :, at].astype(F32) + other_ref[0, :, at].astype(F32)).astype(BF16)
+
+    size = 6 * count * before * after * rows * cols * 2
+    keep, send = pl.pallas_call(
+        body,
+        grid=(count,),
+        out_shape=(out, out),
+        in_specs=[pl.BlockSpec(memory_space=pltpu.SMEM), block, block],
+        out_specs=(out_block, out_block),
+        compiler_params=pltpu.CompilerParams(vmem_limit_bytes=24 * 1024 * 1024),
+        cost_estimate=pl.CostEstimate(flops=0, bytes_accessed=size, transcendentals=0),
+        name="fold",
+    )(here.reshape(1).astype(jnp.int32), mine.reshape(shape), other.reshape(shape))
+    flat = lambda v: v.reshape(count, before * after, rows, cols)
+    return flat(keep), flat(send)
+
+
+def fold_last(mine, other, here):
+    k, _, rows, cols = mine.shape
+
+    def body(here_ref, mine_ref, other_ref, keep_ref, *send_refs):
+        for by, ref in enumerate((keep_ref, *send_refs)):
+            at = lax.rem(here_ref[0] + by, 4)
+            total = mine_ref[:, at].astype(F32) + other_ref[:, at].astype(F32)
+            ref[...] = total.astype(ref.dtype)
+
+    vmem = pl.BlockSpec(memory_space=pltpu.VMEM)
+    return pl.pallas_call(
+        body,
+        out_shape=(jax.ShapeDtypeStruct((k, rows, cols), F32),)
+        + (jax.ShapeDtypeStruct((k, rows, cols), BF16),) * 3,
+        in_specs=[pl.BlockSpec(memory_space=pltpu.SMEM), vmem, vmem],
+        out_specs=(vmem,) * 4,
+        compiler_params=pltpu.CompilerParams(vmem_limit_bytes=24 * 1024 * 1024),
+        cost_estimate=pl.CostEstimate(
+            flops=0, bytes_accessed=28 * k * rows * cols, transcendentals=0
+        ),
+        name="fold_last",
+    )(here.reshape(1).astype(jnp.int32), mine, other)
+
+
 def place(parts, slots, lead=None, moves=None):
     count = len(parts)
     if lead is None:
@@ -208,7 +268,7 @@
     )(jnp.stack(slots).astype(jnp.int32), *parts)
 
 
-def slots_of(feeds, owners, width):
+def slots_of(feeds, owners, width, extra=None):
     arrays, index = [], {}
 
     def note(array):
@@ -222,9 +282,13 @@
 
     noted = [[(note(total), note(moment)) for total, moment in feed] for feed in feeds]
     rows = arrays[0].shape[-2]
+    more = 0 if extra is None else extra.shape[0]
 
     def body(*refs):
-        out = refs[-1]
+        out = refs[-1].at[:, :rows] if more else refs[-1]
+        if more:
+            for slot in range(owners):
+                refs[-1][slot, rows:] = refs[-2][...]
 
         def read(what):
             place_of, (lead, start, size) = what
@@ -252,15 +316,107 @@
     vmem = pl.BlockSpec(memory_space=pltpu.VMEM)
     return pl.pallas_call(
         body,
-        out_shape=jax.ShapeDtypeStruct((owners, rows, width), BF16),
-        in_specs=[vmem] * len(arrays),
+        out_shape=jax.ShapeDtypeStruct((owners, rows + more, width), BF16),
+        in_specs=[vmem] * (len(arrays) + (more > 0)),
         out_specs=vmem,
         cost_estimate=pl.CostEstimate(
             flops=0, bytes_accessed=2 * owners * rows * width, transcendentals=0
         ),
         compiler_params=pltpu.CompilerParams(vmem_limit_bytes=24 * 1024 * 1024),
         name="slots",
+    )(*arrays, *([extra] if more else []))
+
+
+def pack(parts):
+    arrays, index = [], {}
+    for array, _, _ in parts:
+        if id(array) not in index:
+            index[id(array)] = len(arrays)
+            arrays.append(array)
+    rows = arrays[0].shape[-2]
+    total = sum(cols for _, _, cols in parts)
+
+    def body(*refs):
+        at = 0
+        for array, lead, cols in parts:
+            value = refs[index[id(array)]][(*lead, slice(None), slice(0, cols))]
+            refs[-1][:, at : at + cols] = value.astype(BF16)
+            at += cols
+
+    vmem = pl.BlockSpec(memory_space=pltpu.VMEM)
+    return pl.pallas_call(
+        body,
+        out_shape=jax.ShapeDtypeStruct((rows, total), BF16),
+        in_specs=[vmem] * len(arrays),
+        out_specs=vmem,
+        cost_estimate=pl.CostEstimate(flops=0, bytes_accessed=6 * rows * total, transcendentals=0),
+        compiler_params=pltpu.CompilerParams(vmem_limit_bytes=24 * 1024 * 1024),
+        name="pack",
     )(*arrays)
+
+
+def pick(values, index):
+    found = jnp.int32(values[0])
+    for i, value in enumerate(values):
+        if value != values[0]:
+            found = jnp.where(index == i, jnp.int32(value), found)
+    return found
+
+
+def update_kernel(quarters, slot_ref, *refs):
+    step_refs, refs = refs[:quarters], refs[quarters:]
+    modulation, projection, output, expand, shrink = refs[:5]
+    out_modulation, out_projection, out_output, out_expand, out_shrink = refs[5:10]
+    quarter = pl.program_id(0)
+    rows = step_refs[0].shape[0]
+    ratio = LEARN_RATE * (FF / D) ** 0.5
+    for which, steps in enumerate(step_refs):
+
+        @pl.when(slot_ref[quarter] == which)
+        def _(steps=steps):
+            at = 3 * FF
+            for k in range(2):
+                step = steps[:, k * FF : (k + 1) * FF].astype(F32)
+                out_expand[k] = expand[k] - ratio * step
+            out_shrink[...] = shrink[...] - LEARN_RATE * steps[:, 2 * FF : at].astype(F32)
+            for master, out, count in (
+                (modulation, out_modulation, 6),
+                (projection, out_projection, 3),
+            ):
+                for k in range(count):
+                    out[k] = master[k] - LEARN_RATE * steps[:, at : at + D].astype(F32)
+                    at += D
+            out_output[...] = output[...] - LEARN_RATE * steps[:, at : at + D].astype(F32)
+
+
+def update(slots, steps, masters):
+    quarters = len(steps)
+    rows = steps[0].shape[0]
+    third = lambda a: pl.BlockSpec((a.shape[0], rows, a.shape[2]), lambda q: (0, q, 0))
+    masters = (*masters[:4], masters[4].T)
+    modulation, projection, output, expand, shrink = masters
+    specs = [
+        third(modulation),
+        third(projection),
+        pl.BlockSpec((rows, D), lambda q: (q, 0)),
+        third(expand),
+        pl.BlockSpec((rows, FF), lambda q: (q, 0)),
+    ]
+    updated = pl.pallas_call(
+        functools.partial(update_kernel, quarters),
+        grid=(quarters,),
+        out_shape=tuple(jax.ShapeDtypeStruct(a.shape, F32) for a in masters),
+        in_specs=[pl.BlockSpec(memory_space=pltpu.SMEM)] + [whole(a) for a in steps] + specs,
+        out_specs=tuple(specs),
+        cost_estimate=pl.CostEstimate(flops=0, bytes_accessed=14_000_000, transcendentals=0),
+        compiler_params=pltpu.CompilerParams(vmem_limit_bytes=24 * 1024 * 1024),
+        name="update",
+    )(
+        jnp.stack(slots).astype(jnp.int32),
+        *steps,
+        *[pltpu.with_memory_space_constraint(a, pltpu.HBM) for a in masters],
+    )
+    return (*updated[:4], updated[4].T)
 
 
 def every(*sizes):
@@ -290,26 +446,27 @@
     def owner_index(self):
         return lax.axis_index("fsdp")
 
-    def gather_weights(self, chunks):
-        full = [lax.all_gather(chunk, "fsdp", axis=0, tiled=True) for chunk in chunks]
-        return [jnp.split(chunk, 2, axis=1) for chunk in full]
-
-    def gather_images(self, value):
-        return lax.all_gather(value, ("dp", "fsdp"), axis=0, tiled=True)
+    def gather_weights(self, first, second, modulate, attend):
+        full = [lax.all_gather(chunk, "fsdp", axis=0, tiled=True) for chunk in (first, second)]
+        first, second = [jnp.split(chunk, 2, axis=1) for chunk in full]
+        modulation = modulate[1](modulate[0]())
+        return first, second, modulation, attend(first, modulation)
 
     def to_group(self, value):
         return lax.all_to_all(value, "fsdp", split_axis=0, concat_axis=0, tiled=True)
 
-    def reduce_core(self, partial):
-        return partial
-
-    def reduce_first(self, value, route):
-        return value
-
-    def reduce_second(self, value, route):
-        return value
-
-    def reduce_last(self, value):
+    def halves(self):
+        return jnp.int32(0)
+
+    def begin(self, mine, send):
+        k, n, rows, cols = mine.shape
+        return (jnp.stack([mine, send], axis=2).reshape(k, 2 * n * rows, cols),)
+
+    def step(self, state, axis, start=0, count=None):
+        return (state[0][start : start + (count or state[0].shape[0])],)
+
+    def last(self, *states):
+        value = jnp.concatenate([state[0] for state in states], axis=0)
         shard = lax.psum_scatter(value, "fsdp", scatter_dimension=1, tiled=True)
         return lax.psum(shard.astype(F32), "dp")
 
@@ -318,10 +475,36 @@
 
     def complete(self, piece):
         return piece
+
+    def quarters(self, piece):
+        return [jnp.int32(0)], [piece]
+
+    def images_begin(self, rows):
+        return lax.all_gather(rows, ("dp", "fsdp"), axis=0, tiled=True)
+
+    def images_end(self, got):
+        return got
 
     def to_owners(self, pieces):
         got = lax.all_to_all(pieces, "fsdp", split_axis=0, concat_axis=0, tiled=True)
         return got.reshape(-1, got.shape[2])
+
+    def wide_slots_of(self, feeds):
+        return slots_of(
+            [[] if slot is None else feeds[slot[0]] for slot in self.wide_slots], self.owners, FF
+        )
+
+    def wide_halves(self, got):
+        return got
+
+    def wide_whole(self, got):
+        return jnp.stack(jnp.split(got, 2, axis=1))
+
+    def square_slots(self, feeds):
+        return slots_of([[] if slot is None else feeds[slot] for slot in self.slots], self.owners, D)
+
+    def square_to_owners(self, slots, beside):
+        return self.to_owners(slots), beside
 
     def to_rows(self, whole):
         blocks = whole.reshape(self.row_shards, -1, whole.shape[1])
@@ -372,28 +555,30 @@
         ring = [value] + [self.shift(value, by) for by in range(1, 4)]
         return place(ring, [(z - by) % 4 for by in range(4)])
 
-    def gather_weights(self, chunks):
+    def gather_weights(self, first, second, modulate, attend):
         x, y, z, c = [lax.axis_index(axis) for axis in "xyzc"]
-        spread = []
-        for chunk in chunks:
+        slots = [(z - by) % 4 for by in range(4)]
+
+        def ring_of(chunk, *others):
             piece = self.own_rows(chunk)
-            if spread:
-                piece = tie(piece, *spread[-1])
-            ring = [piece] + [self.shift(piece, by) for by in range(1, 4)]
-            spread.append(place_halves(ring, [(z - by) % 4 for by in range(4)]))
-        done = []
-        for left, right in spread:
-            if done:
-                left, right = lax.optimization_barrier((left, right, *done[-1]))[:2]
+            if others:
+                piece = tie(piece, *others)
+            return [piece] + [self.shift(piece, by) for by in range(1, 4)]
+
+        def one_hop(left, right):
             left_other, right_other = self.swap(left, "y"), self.swap(right, "x")
             left = place([left, left_other], [y, 1 - y])
             right = place([right, right_other], [x, 1 - x])
-            left_other, right_other = self.swap(left, "x"), self.swap(right, "y")
+            return left, right
+
+        def other_hop(left, right):
+            left, right = meet(left, right)
+            left_other, right_other = meet(self.swap(left, "x"), self.swap(right, "y"))
             left = place([left, left_other], [x, 1 - x])
             right = place([right, right_other], [y, 1 - y])
-            done.append((left, right))
-        full = []
-        for left, right in done:
+            return left, right
+
+        def by_core(left, right):
             others = self.swap(left, "c"), self.swap(right, "c")
             pair = []
             for half, other, order in ((left, others[0], (2, 1, 0)), (right, others[1], (2, 0, 1))):
@@ -406,49 +591,56 @@
                     return found
 
                 pair.append(place([half, other], [c, 1 - c], (4, 2, 2, 2), moves).reshape(D, -1))
-            full.append(pair)
-        return full
-
-    def gather_images(self, value):
-
-        def both(v, axis):
-            other = self.swap(v, axis)
-            first = lax.axis_index(axis) == 0
-            return jnp.where(first, jnp.stack([v, other]), jnp.stack([other, v]))
-
-        z = lax.axis_index("z")
-        shape = (32 * value.shape[0],) + value.shape[1:]
-        value = both(value, "y")
-        ring = jnp.stack([value] + [self.shift(value, by) for by in range(1, 4)])
-        value = jnp.take(ring, (z - jnp.arange(4)) % 4, axis=0)
-        value = both(value, "c")
-        value = both(value, "x")
-        return value.reshape(shape)
+            return pair
+
+        group = modulate[0]()
+        left, right = place_halves(ring_of(first), slots)
+        ring = ring_of(second, left, right)
+        left, right, group = meet(left, right, group)
+        left, right = one_hop(left, right)
+        modulation = modulate[1](group)
+        left, right, modulation, ring[0], ring[1], ring[3] = meet(
+            left, right, modulation, ring[0], ring[1], ring[3]
+        )
+        left, right = other_hop(left, right)
+        left, right, ring[2] = meet(left, right, ring[2])
+        done = by_core(left, right)
+        done, ring = meet(done, ring)
+        left, right = place_halves(ring, slots)
+        others = self.swap(left, "y"), self.swap(right, "x")
+        *done, left, right = meet(*done, left, right)
+        results = attend(done, modulation)
+        left_other, right_other, *results = meet(*others, *results)
+        left = place([left, left_other], [y, 1 - y])
+        right = place([right, right_other], [x, 1 - x])
+        left, right = other_hop(left, right)
+        return done, by_core(left, right), modulation, results
 
     def to_group(self, value):
         return lax.all_to_all(value, ("z", "y"), split_axis=0, concat_axis=0, tiled=True)
 
-    def halve(self, value, axis, dim):
-        here = lax.axis_index(axis)
-        take = lambda at: lax.dynamic_index_in_dim(value, at, dim, keepdims=False)
-        got = self.swap(take(1 - here), axis)
-        return (take(here).astype(F32) + got.astype(F32)).astype(BF16)
-
-    def reduce_core(self, partial):
-        k, _, cols = partial.shape
-        return self.halve(partial.reshape(k, 4, 2, 2, 2, D // 32, cols), "c", 4)
-
-    def reduce_first(self, value, route):
-        return self.halve(value, route[0], 3 if route[0] == "x" else 2)
-
-    def reduce_second(self, value, route):
-        return self.halve(value, route[1], 2)
-
-    def reduce_last(self, value):
-        z = lax.axis_index("z")
-        take = lambda at: lax.dynamic_index_in_dim(value, at, 1, keepdims=False)
-        got = [self.shift(take((z + by) % 4), by) for by in range(1, 4)]
-        total = take(z).astype(F32)
+    def halves(self):
+        return lax.axis_index("c")
+
+    def begin(self, mine, send):
+        return (mine, self.swap(send, "c"))
+
+    def step(self, state, axis, start=0, count=None):
+        mine, other = state
+        parts = mine.shape[1]
+        view = (4, 2) if (parts, axis) == (16, "y") else (parts // 2, 1)
+        keep, send = fold(
+            mine, other, lax.axis_index(axis), view, start, count or mine.shape[0]
+        )
+        return (keep, self.swap(send, axis))
+
+    def last(self, *states):
+        folded = [fold_last(mine, other, lax.axis_index("z")) for mine, other in states]
+        keep, *sends = [
+            parts[0] if len(states) == 1 else jnp.concatenate(parts, axis=0) for parts in zip(*folded)
+        ]
+        got = [self.shift(send, by) for by, send in enumerate(sends, 1)]
+        total = keep
         for part in got:
             total = total + part.astype(F32)
         return total
@@ -457,6 +649,24 @@
         return lax.dynamic_slice_in_dim(
             shard, self.group_index() * (D // 32), D // 32, dim % shard.ndim
         )
+
+    def quarters(self, piece):
+        x, c = lax.axis_index("x"), lax.axis_index("c")
+        by_x = self.swap(piece, "x")
+        by_c = self.swap(piece, "c")
+        by_both = self.swap(by_x, "c")
+        slots = []
+        for at_x, at_c in every(2, 2):
+            slots.append(jnp.where(at_x == x, 0, 1) + jnp.where(at_c == c, 0, 2))
+        return slots, [piece, by_x, by_c, by_both]
+
+    def images_begin(self, rows):
+        own = rows.reshape(-1, D)
+        return self.to_owners(jnp.broadcast_to(own[None], (16, *own.shape)))
+
+    def images_end(self, got):
+        c = lax.axis_index("c")
+        return place([got, self.swap(got, "c")], [c, 1 - c]).reshape(-1, 8, D)
 
     def complete(self, piece):
         value = self.exchange(piece, "x")
@@ -466,9 +676,40 @@
         return value.reshape(D // 8, -1)
 
     def to_owners(self, pieces):
-        cols = pieces.shape[2]
-        got = lax.all_to_all(pieces, self.chips, split_axis=0, concat_axis=0, tiled=True)
-        got = got.reshape(2, 4, 2, D // 32, cols)
+        return lax.all_to_all(pieces, self.chips, split_axis=0, concat_axis=0, tiled=True)
+
+    def wide_slots_of(self, feeds):
+        halved = []
+        for slot in self.wide_slots:
+            halved.append([] if slot is None else [feeds[slot[0]][slot[1]]])
+        return slots_of(halved, self.owners, FF // 2)
+
+    def wide_halves(self, got):
+        return got, self.swap(got, "x")
+
+    def wide_whole(self, got):
+        half = FF // 2
+        x, c = lax.axis_index("x"), lax.axis_index("c")
+        both = place(list(got), [x, 1 - x])
+        both = both.reshape(2, 2, 4, 2, D // 32, half)
+
+        def moves(slot):
+            return [
+                (part, (p, x, z, y), (p, z, y, x, slot[part]))
+                for part in range(2)
+                for p, x, z, y in every(2, 2, 4, 2)
+            ]
+
+        whole = place([both, self.swap(both, "c")], [c, 1 - c], (2, 4, 2, 2, 2), moves)
+        return whole.reshape(2, D, half)
+
+    def square_slots(self, feeds):
+        return slots_of([[] if slot is None else feeds[slot] for slot in self.slots], self.owners, D)
+
+    def square_to_owners(self, slots, beside):
+        got = self.to_owners(slots)
+        got, beside = meet(got, beside)
+        got = got.reshape(2, 4, 2, D // 32, D)
         c = lax.axis_index("c")
 
         def moves(slot):
@@ -478,8 +719,7 @@
                 for x, z, y in every(2, 4, 2)
             ]
 
-        whole = place([got, self.swap(got, "c")], [c, 1 - c], (4, 2, 2, 2), moves)
-        return whole.reshape(D, cols)
+        return place([got, self.swap(got, "c")], [c, 1 - c], (4, 2, 2, 2), moves).reshape(D, D), beside
 
     def to_rows(self, whole):
         cols = whole.shape[1]
@@ -583,8 +823,29 @@
     second_ref[0] = (normed * (1.0 + row(4)) + row(3)).astype(BF16)
 
 
+def split_rows(value, scratch, here, keep_ref, send_ref, which, cols):
+    scratch[...] = value
+    rows = keep_ref.shape[2]
+    for i in range(keep_ref.shape[1]):
+        for ref, at in ((keep_ref, here), (send_ref, 1 - here)):
+            start = pl.multiple_of((2 * i + at) * rows, 8)
+            ref[which, i, :, cols] = scratch[pl.ds(start, rows), :].astype(BF16)
+
+
 def feed_forward_kernel(
-    second_ref, branch_ref, gate_ref, up_ref, down_ref, out_ref, back_ref, grads_ref, second_t, branch_t
+    here_ref,
+    second_ref,
+    branch_ref,
+    gate_ref,
+    up_ref,
+    down_ref,
+    out_ref,
+    back_ref,
+    keep_ref,
+    send_ref,
+    second_t,
+    branch_t,
+    rows,
 ):
     step = pl.program_id(0)
 
@@ -606,9 +867,12 @@
     grad_gate = (grad_hidden * up_pre * sigmoid * (1.0 + gate_pre * (1.0 - sigmoid))).astype(BF16)
     grad_up = (grad_hidden * swish).astype(BF16)
     back_ref[...] += dot(grad_gate, gate, NT) + dot(grad_up, up, NT)
-    grads_ref[0] = dot(second_t[...], grad_gate).astype(BF16)
-    grads_ref[1] = dot(second_t[...], grad_up).astype(BF16)
-    grads_ref[2] = dot(branch_t[...], hidden).astype(BF16)
+    everything = slice(None)
+    products = ((second_t, grad_gate), (second_t, grad_up), (branch_t, hidden))
+    for which, (left, right) in enumerate(products):
+        split_rows(
+            dot(left[...], right), rows, here_ref[0], keep_ref, send_ref, which, everything
+        )
 
 
 def attention_backward_kernel(
@@ -684,6 +948,7 @@
 
 
 def projection_backward_kernel(
+    here_ref,
     grads_in_ref,
     first_ref,
     attended_ref,
@@ -694,40 +959,45 @@
     active_ref,
     query_key_ref,
     value_output_ref,
-    grads_ref,
+    keep_ref,
+    send_ref,
     input_grad_ref,
     modulation_grad_ref,
     first_t,
     first_grad,
+    rows,
 ):
     images, positions = input_ref.shape[:2]
     tokens = images * positions
     flat = lambda ref: ref[...].reshape(tokens, D)
     step = pl.program_id(0)
 
+    def product(grads):
+        split_rows(dot(first_t[...], grads), rows, here_ref[0], keep_ref, send_ref, 0, slice(None))
+
     @pl.when(step == 0)
     def _():
         first_t[...] = flat(first_ref).T
         grads = grads_in_ref[0].reshape(tokens, D)
-        grads_ref[0] = dot(first_t[...], grads).astype(BF16)
+        product(grads)
         first_grad[...] = dot(grads, query_key_ref[:, :D], NT)
 
     @pl.when(step == 1)
     def _():
         grads = grads_in_ref[0].reshape(tokens, D)
-        grads_ref[0] = dot(first_t[...], grads).astype(BF16)
+        product(grads)
         first_grad[...] += dot(grads, query_key_ref[:, D:], NT)
 
     @pl.when(step == 2)
     def _():
         grads = grads_in_ref[0].reshape(tokens, D)
-        grads_ref[0] = dot(first_t[...], grads).astype(BF16)
+        product(grads)
         first_grad[...] += dot(grads, value_output_ref[:, :D], NT)
 
     @pl.when(step == 3)
     def _():
         first_t[...] = flat(attended_ref).T
-        grads_ref[0] = dot(first_t[...], grads_in_ref[0].reshape(tokens, D)).astype(BF16)
+        product(grads_in_ref[0].reshape(tokens, D))
         for image in range(images):
             at = slice(image * positions, (image + 1) * positions)
             normed, inverse = norm_of(input_ref[image].astype(F32))
@@ -806,26 +1076,24 @@
     )
 
 
-def feed_forward(second, branch, weight):
+def feed_forward(here, second, branch, weight):
     tokens = second.shape[0]
     units = weight.shape[1] // 3
     tile = 256
     steps = units // tile
-    ins = (second, branch, weight, weight, weight)
-    in_specs = [whole(second), whole(branch)] + [
+    ins = (here.reshape(1).astype(jnp.int32), second, branch, weight, weight, weight)
+    in_specs = [pl.BlockSpec(memory_space=pltpu.SMEM), whole(second), whole(branch)] + [
         pl.BlockSpec((D, tile), lambda t, which=which: (0, which * steps + t)) for which in range(3)
     ]
     outs = (
         jax.ShapeDtypeStruct((tokens, D), F32),
         jax.ShapeDtypeStruct((tokens, D), F32),
-        jax.ShapeDtypeStruct((3, D, units), BF16),
-    )
-    out_specs = [
-        whole(outs[0]),
-        whole(outs[1]),
-        pl.BlockSpec((3, D, tile), lambda t: (0, 0, t)),
-    ]
-    scratch = [pltpu.VMEM((D, tokens), BF16), pltpu.VMEM((D, tokens), BF16)]
+        jax.ShapeDtypeStruct((3, D // 48, 24, units), BF16),
+        jax.ShapeDtypeStruct((3, D // 48, 24, units), BF16),
+    )
+    out_specs = [whole(outs[0]), whole(outs[1])]
+    out_specs += [pl.BlockSpec((3, D // 48, 24, tile), lambda t: (0, 0, 0, t))] * 2
+    scratch = [pltpu.VMEM((D, tokens), BF16), pltpu.VMEM((D, tokens), BF16), pltpu.VMEM((D, tile), F32)]
     flops = 2 * 9 * tokens * D * units
     return call(
         feed_forward_kernel, (steps,), ins, in_specs, outs, out_specs, scratch, flops, "feed_forward"
@@ -863,18 +1131,22 @@
     )
 
 
-def projection_backward(*ins):
+def projection_backward(here, *ins):
     _, images, positions, _ = ins[0].shape
     tokens = images * positions
-    in_specs = [pl.BlockSpec((1, images, positions, D), lambda k: (k, 0, 0, 0))]
+    in_specs = [pl.BlockSpec(memory_space=pltpu.SMEM)]
+    in_specs += [pl.BlockSpec((1, images, positions, D), lambda k: (k, 0, 0, 0))]
     in_specs += [whole(a) for a in ins[1:]]
+    ins = (here.reshape(1).astype(jnp.int32), *ins)
     outs = (
-        jax.ShapeDtypeStruct((4, D, D), BF16),
+        jax.ShapeDtypeStruct((4, D // 48, 24, D), BF16),
+        jax.ShapeDtypeStruct((4, D // 48, 24, D), BF16),
         jax.ShapeDtypeStruct((images, positions, D), F32),
         jax.ShapeDtypeStruct((images, 8, D), BF16),
     )
-    out_specs = [pl.BlockSpec((1, D, D), lambda k: (k, 0, 0)), whole(outs[1]), whole(outs[2])]
-    scratch = [pltpu.VMEM((D, tokens), BF16), pltpu.VMEM((tokens, D), F32)]
+    out_specs = [pl.BlockSpec((1, D // 48, 24, D), lambda k: (k, 0, 0, 0))] * 2
+    out_specs += [whole(outs[2]), whole(outs[3])]
+    scratch = [pltpu.VMEM((D, tokens), BF16), pltpu.VMEM((tokens, D), F32), pltpu.VMEM((D, D), F32)]
     return call(
         projection_backward_kernel,
         (4,),
@@ -932,56 +1204,70 @@
 
     half = FF // 2
     shrink_low = shrink_master.astype(BF16).T
-    (query_key_weight, value_output_weight), (left_weight, right_weight) = comm.gather_weights(
+    packed_attention = jnp.concatenate(
+        [projection_master[i].astype(BF16) for i in range(3)] + [output_master.astype(BF16)], axis=1
+    )
+    packed_units = jnp.concatenate(
         [
-            jnp.concatenate(
-                [projection_master[i].astype(BF16) for i in range(3)] + [output_master.astype(BF16)],
-                axis=1,
-            ),
-            jnp.concatenate(
-                [
-                    part
-                    for cols in (slice(None, half), slice(half, None))
-                    for part in (
-                        expand_master[0, :, cols].astype(BF16),
-                        expand_master[1, :, cols].astype(BF16),
-                        shrink_low[:, cols],
-                    )
-                ],
-                axis=1,
-            ),
-        ]
+            part
+            for cols in (slice(None, half), slice(half, None))
+            for part in (
+                expand_master[0, :, cols].astype(BF16),
+                expand_master[1, :, cols].astype(BF16),
+                shrink_low[:, cols],
+            )
+        ],
+        axis=1,
     )
     selector = (
         time_bins[:, None] == jnp.arange(time_table.shape[0], dtype=jnp.int32)[None, :]
     ).astype(F32)
     active = swish_value(jnp.dot(selector, time_table, precision=HIGHEST)).astype(BF16)
-    active_group = comm.to_group(
-        active.reshape(images, comm.row_shards, rows).transpose(1, 0, 2)
-    ).reshape(-1, rows)
-    partial = jnp.einsum(
-        "bd,kde->bke", active_group, modulation_master.astype(BF16), preferred_element_type=F32
-    )
-    modulation = jnp.sum(
-        comm.to_group(partial.reshape(comm.row_shards, images, 6, features)), axis=0
-    )
+
+    def group_rows():
+        return comm.to_group(active.reshape(images, comm.row_shards, rows).transpose(1, 0, 2))
+
+    def modulation_of(group):
+        partial = jnp.einsum(
+            "bd,kde->bke",
+            group.reshape(-1, rows),
+            modulation_master.astype(BF16),
+            preferred_element_type=F32,
+        )
+        return jnp.sum(
+            comm.to_group(partial.reshape(comm.row_shards, images, 6, features)), axis=0
+        )
+
     cosine, sine = rope_tables(image_shape, positions)
     lengths = image_shape[:, 0] * image_shape[:, 1]
+
+    def attend(weights, modulation):
+        return attention_forward(
+            lengths, inputs, cotangent, modulation, cosine, sine, weights[0], weights[1]
+        )
+
+    first, second, modulation, results = comm.gather_weights(
+        packed_attention, packed_units, (group_rows, modulation_of), attend
+    )
+    query_key_weight, value_output_weight = first
+    left_weight, right_weight = second
     (first_input, query, key, value, probs, attended, attention, middle, second_input, grad_branch) = (
-        attention_forward(
-            lengths, inputs, cotangent, modulation, cosine, sine, query_key_weight, value_output_weight
-        )
+        results
     )
     second_flat = second_input.reshape(tokens, D)
     branch_flat = grad_branch.reshape(tokens, D)
     shaped = lambda v: v.reshape(images, positions, D)
-    branch_left, back_left, grads = feed_forward(second_flat, branch_flat, left_weight)
-    left_sum = comm.reduce_core(grads)
-    second_flat = tie(second_flat, back_left)
-    branch_right, back_right, grads = feed_forward(second_flat, branch_flat, right_weight)
-    left_sum, grads = lax.optimization_barrier((left_sum, grads))
-    left_sum = comm.reduce_first(left_sum, "xy")
-    right_sum = comm.reduce_core(grads)
+    here = comm.halves()
+    branch_left, back_left, *grads = feed_forward(here, second_flat, branch_flat, left_weight)
+    left_sum = comm.begin(*grads)
+    second_flat, left_sum = meet(second_flat, left_sum)
+    left_sum = comm.step(left_sum, "x", 0, 2), comm.step(left_sum, "y", 2, 1)
+    branch_right, back_right, *grads = feed_forward(here, second_flat, branch_flat, right_weight)
+    back_right, left_sum, grads = meet(back_right, left_sum, grads)
+    right_sum = comm.begin(*grads)
+    back_right, left_sum, right_sum = meet(back_right, left_sum, right_sum)
+    left_sum = comm.step(left_sum[0], "y"), comm.step(left_sum[1], "x")
+    right_sum = comm.step(right_sum, "x", 0, 2), comm.step(right_sum, "y", 2, 1)
     block_output, grad_stream, grads, sums = attention_backward(
         lengths,
         shaped(branch_left),
@@ -1000,10 +1286,11 @@
         cosine,
         sine,
     )
-    left_sum, right_sum, grads = lax.optimization_barrier((left_sum, right_sum, grads))
-    left_sum = comm.reduce_second(left_sum, "xy")
-    right_sum = comm.reduce_first(right_sum, "yx")
-    grads, input_gradient, grad_modulation = projection_backward(
+    left_sum, right_sum, grads = meet(left_sum, right_sum, grads)
+    left_piece = comm.last(*left_sum)
+    right_sum = comm.step(right_sum[0], "y"), comm.step(right_sum[1], "x")
+    *grads, input_gradient, grad_modulation = projection_backward(
+        here,
         grads,
         first_input,
         attended,
@@ -1015,21 +1302,15 @@
         query_key_weight,
         value_output_weight,
     )
-    left_sum, right_sum, grads, grad_modulation = lax.optimization_barrier(
-        (left_sum, right_sum, grads, grad_modulation)
-    )
-    right_sum = comm.reduce_second(right_sum, "yx")
-    left_piece = comm.reduce_last(left_sum)
-    attention_sum = comm.reduce_core(grads)
-    left_piece, right_sum, attention_sum = lax.optimization_barrier(
-        (left_piece, right_sum, attention_sum)
-    )
-    right_piece = comm.reduce_last(right_sum)
-    first_sum = comm.reduce_first(attention_sum[:2], "xy")
-    second_sum = comm.reduce_first(attention_sum[2:], "yx")
-    first_sum, second_sum, right_piece = lax.optimization_barrier(
-        (first_sum, second_sum, right_piece)
-    )
+    left_piece, right_sum, grads, grad_modulation = meet(left_piece, right_sum, grads, grad_modulation)
+    attention_sum = comm.begin(*grads)
+    attention_sum, right_sum = meet(attention_sum, right_sum)
+    first_sum = comm.step(attention_sum, "x", 0, 2)
+    second_sum = comm.step(attention_sum, "y", 2, 2)
+    right_piece = comm.last(*right_sum)
+    gathered = comm.images_begin(grad_modulation)
+    right_piece, *kept = meet(right_piece, first_sum[0], second_sum[0])
+    first_sum, second_sum = (kept[0], *first_sum[1:]), (kept[1], *second_sum[1:])
 
     owner = comm.owner_index()
     own_expand = comm.own_rows(expand_moment)
@@ -1046,20 +1327,16 @@
         ]
         for which in range(3)
     ]
-    wide = comm.to_owners(
-        slots_of(
-            [[] if slot is None else wide_feed[slot[0]] for slot in comm.wide_slots],
-            comm.owners,
-            FF,
-        )
-    )
-    gathered = comm.gather_images(grad_modulation)
-    attention_piece = comm.reduce_last(
-        jnp.concatenate(
-            [comm.reduce_second(first_sum, "xy"), comm.reduce_second(second_sum, "yx")], axis=0
-        )
-    )
+    wide = comm.to_owners(comm.wide_slots_of(wide_feed))
+    first_sum, second_sum, gathered = meet(first_sum, second_sum, gathered)
+    gathered = comm.images_end(gathered)
     active_all = gathered[:, 6]
+    first_sum = comm.step(first_sum, "y")
+    second_sum = comm.step(second_sum, "x")
+    first_sum, second_sum, wide, gathered = meet(first_sum, second_sum, wide, gathered)
+    wide = comm.wide_halves(wide)
+    attention_piece, wide = meet(comm.last(first_sum, second_sum), wide)
+    wide = comm.wide_whole(wide)
 
     own_modulation = comm.own_rows(modulation_moment)
     own_projection = comm.own_rows(projection_moment)
@@ -1070,28 +1347,25 @@
             [((attention_piece, ((k,), 0, D)), (own_projection, ((k,), 0, D)))]
         )
     square_feed.append([((attention_piece, ((3,), 0, D)), (own_output, ((), 0, D)))])
-    square = comm.to_owners(
-        slots_of(
-            [[] if slot is None else square_feed[slot] for slot in comm.slots], comm.owners, D
-        )
-    )
-    item = jnp.array([-1 if slot is None else slot for slot in comm.slots], jnp.int32)[owner]
+    slots, wide = meet(comm.square_slots(square_feed), wide)
+    active_wide = pick([0 if slot is None else 1 for slot in comm.wide_slots], owner)
+    wide_done = newton_schulz(active_wide, wide)
+    square, wide_done = comm.square_to_owners(slots, wide_done)
+    item = pick([-1 if slot is None else slot for slot in comm.slots], owner)
     which = jnp.where((item >= 0) & (item < 6), item, 0)
     right = lax.dynamic_index_in_dim(gathered, which, 1, keepdims=False)
     right = jnp.where(item < 6, right, jnp.zeros_like(right))
-    active_wide = jnp.array([0 if slot is None else 1 for slot in comm.wide_slots], jnp.int32)[owner]
-    wide, square = lax.optimization_barrier((wide, square))
-    wide_done = newton_schulz(active_wide, wide)
     square_done = newton_schulz((item >= 0).astype(jnp.int32), square, active_all, right)
     size = FF // comm.wide_parts
-    part = jnp.array([0 if slot is None else slot[1] for slot in comm.wide_slots])[owner]
+    part = pick([0 if slot is None else slot[1] for slot in comm.wide_slots], owner)
     mine = lax.dynamic_slice_in_dim(wide_done, part * size, size, 1)
     mine = mine + jnp.pad(square_done, ((0, 0), (0, size - D)))
     back = comm.to_rows(mine)
 
-    pieces = [left_piece[i] for i in range(3)] + [right_piece[i] for i in range(3)]
-    pieces += [attention_piece[i] for i in range(4)]
-    totals_low = comm.complete(jnp.concatenate([p.astype(BF16) for p in pieces], axis=1)).astype(F32)
+    pieces = [(left_piece, (i,), half) for i in range(3)]
+    pieces += [(right_piece, (i,), half) for i in range(3)]
+    pieces += [(attention_piece, (i,), D) for i in range(4)]
+    totals_low = comm.complete(pack(pieces)).astype(F32)
     by_unit = [
         jnp.concatenate(
             [totals_low[:, (side * 3 + i) * half : (side * 3 + i + 1) * half] for side in range(2)],
@@ -1099,11 +1373,11 @@
         )
         for i in range(3)
     ]
-    wide_back = [
-        back[comm.wide_slots.index((i, p))] for i in range(3) for p in range(comm.wide_parts)
+    steps = [
+        (back, (comm.wide_slots.index((i, p)),), size) for i in range(3) for p in range(comm.wide_parts)
     ]
-    square_back = [back[comm.slots.index(i), :, :D] for i in range(10)]
-    steps = comm.complete(jnp.concatenate(wide_back + square_back, axis=1)).astype(F32)
+    steps += [(back, (comm.slots.index(i),), D) for i in range(10)]
+    updated = update(*comm.quarters(pack(steps)), masters)
     active_rows = lax.dynamic_slice_in_dim(active_all, row_index * rows, rows, 1)
     modulation_total = jnp.einsum(
         "bd,bke->kde",
@@ -1120,15 +1394,6 @@
         by_unit[2].T,
     )
     states = tuple((MOMENTUM_DECAY * moment + total for moment, total in zip(moments, totals)))
-    square_step = [steps[:, after + i * D : after + (i + 1) * D] for i in range(10)]
-    steps_all = (
-        jnp.stack(square_step[:6]),
-        jnp.stack(square_step[6:9]),
-        square_step[9],
-        jnp.stack([steps[:, :FF], steps[:, FF : 2 * FF]]) * (FF / D) ** 0.5,
-        steps[:, 2 * FF : after].T,
-    )
-    updated = tuple((master - LEARN_RATE * step for master, step in zip(masters, steps_all)))
     return (block_output, input_gradient, *totals, *updated, *states)
 
 

time: 585 us -> 450 us (0.77)
  waiting for transfers between devices: 217 us -> 166 us
  other arithmetic: 57.4 us -> 16.5 us
  local copies, waits for them, and re-layouts: 63.9 us -> 39.2 us
  starting transfers between devices: 111 us -> 90.3 us
  Pallas kernels: 118 us -> 125 us
    ppermute x18 -> x15, waiting for transfers between devices: 51.7 us -> 17.5 us  [shift(): return lax.ppermute(value, 'z', [(i, (i + by) % 4) for i in range(4)])]
    ppermute x32 -> x36, waiting for transfers between devices: 131 us -> 105 us  [swap(): return lax.ppermute(value, axis, [(0, 1), (1, 0)])]
    convert_element_type x13 -> x1, other arithmetic: 20.8 us -> 0.41 us  [local(): totals_low = comm.complete(pack(pieces)).astype(F32)]
    all_to_all x1, starting transfers between devices: 23.3 us -> 7.9 us  [to_rows(): lax.all_to_all(blocks, self.chips, split_axis=0, concat_axis=0, tiled=True)]
    dynamic_slice x10 -> x0, local copies, waits for them, and re-layouts: 14.5 us -> none  [the longest x6 11.6 us: halve(): take = lambda at: lax.dynamic_index_in_dim(value, at, dim, keepdims=False)]
    all_to_all x2 -> x3, waiting for transfers between devices: 0.01 us -> 13 us  [to_owners(): lax.all_to_all(pieces, self.chips, split_axis=0, concat_axis=0, tiled=True)]
    pallas_call x2 -> x23, Pallas kernels: 2.2 us -> 14.3 us  [the longest x12 6.27 us: fold(): pl.pallas_call(body, grid=(count,), out_shape=(out, out), in_specs=[pl.Bl...]
    all_to_all x2, starting transfers between devices: 16.6 us -> 7.27 us  [to_group(): lax.all_to_all(value, ('z', 'y'), split_axis=0, concat_axis=0, tiled=True)]
  transfers between devices with their start and end apart: 55 -> 57, of which waited for: 26 -> 26; matrix products, arithmetic and copies ran while one was open for 14% -> 6% of each run, Pallas kernels for 16% -> 19%
where the time goes in v3:
time: 450 us; the launch traced here: 445 us
  waiting for transfers between devices  166 us (37%)
  Pallas kernels  125 us (28%)
  starting transfers between devices  90.3 us (20%)
  local copies, waits for them, and re-layouts  39.2 us (9%)
  other arithmetic  16.5 us (4%)
  matrix products  5.22 us (1%)
    ppermute x36, waiting for transfers between devices, swap(): return lax.ppermute(value, axis, [(0, 1), (1, 0)])  105 us
    pallas_call x5, Pallas kernels, call(): pl.pallas_call(body, grid=grid, out_shape=outs, in_specs=in_specs, out_sp...  77.8 us
    ppermute x15, starting transfers between devices, shift(): return lax.ppermute(value, 'z', [(i, (i + by) % 4) for i in range(4)])  31.9 us
    unnamed x115, local copies, waits for them, and re-layouts  28.2 us
    ppermute x36, starting transfers between devices, swap(): return lax.ppermute(value, axis, [(0, 1), (1, 0)])  26.6 us
    ppermute x15, waiting for transfers between devices, shift(): return lax.ppermute(value, 'z', [(i, (i + by) % 4) for i in range(4)])  17.5 us
    all_to_all x3, starting transfers between devices, to_owners(): lax.all_to_all(pieces, self.chips, split_axis=0, concat_axis=0, tiled=True)  16.6 us
    pallas_call x2, Pallas kernels, newton_schulz(): pl.pallas_call(body, out_shape=jax.ShapeDtypeStruct((D, width), BF16), in...  16.6 us
  transfers between devices with their start and end apart: 57, of which 26 were waited for; matrix products, arithmetic and copies ran while one was open for 6% of the time, Pallas kernels for 19%

profile of v3, /device:TPU:0, one launch (start us, length us, event | category | flops | bytes accessed | tf_op | source)
XLA Modules:
  0.0 444.8 jit_solution(8786639237890530815)
XLA Ops:
  4.3 3.1 collective-permute-start
  7.4 2.6 collective-permute-start.1
  13.2 3.3 all-to-all-start
  20.7 3.1 all-to-all-done
  25.8 1.7 fusion
  28.5 4.0 all-to-all-start.1
  32.5 2.1 collective-permute-start.5
  34.6 1.9 collective-permute-start.6
  37.7 11.4 %all-to-all-done.1 = f32[8,2,6,768]{3,1,2,0:T(2,128)S(1)} async-done(((f32[8,2,6,768]{3,1,2,0:T(2,128)}), f32[8,2,6,768]{3,1,2,0:T(2,128)S(1)}, u32[]{:S(2)}, u32[]{:S(2)}) %all-to-all-start.1) | async-done | bytes 294944 | tf_op jit(solution)/shard_map/all_to_all | solution.py:620
  54.0 3.6 collective-permute-start.9
  57.6 9.6 %collective-permute-done.7.refs_1_ = bf16[2,4,24,1536]{3,2,1,0:T(8,128)(2,1)S(1)} collective-permute-done((bf16[2,4,24,1536]{3,2,1,0:T(8,128)(2,1)S(1)}, bf16[2,4,24,1536]{3,2,1,0:T(8,128)(2,1)S(1)}, u32[]{:S(2)}, u32[]{:S(2)}) %collective-permute-start.7) | collective-permute-done | bytes 589856 | tf_op jit(solution)/shard_map/ppermute | solution.py:544
  73.1 2.0 collective-permute-done.11.refs_1_
  82.8 2.1 fusion.9
  85.5 18.4 %attention_forward.1 = (bf16[2,256,768]{2,1,0:T(8,128)(2,1)}, bf16[2,256,768]{2,1,0:T(8,128)(2,1)}, bf16[2,256,768]{2,1,0:T(8,128)(2,1)}, bf16[2,256,768]{2,1,0:...) custom-call(s32[2]{0:T(128)} %mul.74.length_ref, ...), custom_call_target="tpu_custom_call" | custom-call | flops 2818572288 | bytes 21794824 | tf_op jit(solution)/shard_map/attention_forward/pallas_call | solution.py:1034
  107.3 25.4 %collective-permute-done.14.refs_1_ = bf16[2,4,24,3072]{3,2,1,0:T(8,128)(2,1)S(1)} collective-permute-done((bf16[2,4,24,3072]{3,2,1,0:T(8,128)(2,1)S(1)}, bf16[2,4,24,3072]{3,2,1,0:T(8,128)(2,1)S(1)}, u32[]{:S(2)}, u32[]{:S(2)}) %collective-permute-start.14) | collective-permute-done | bytes 1179680 | tf_op jit(solution)/shard_map/ppermute | solution.py:544
  133.7 4.5 %collective-permute-done.16.refs_1_ = bf16[2,2,4,24,3072]{4,3,2,1,0:T(8,128)(2,1)S(1)} collective-permute-done((bf16[2,2,4,24,3072]{4,3,2,1,0:T(8,128)(2,1)S(1)}, bf16[2,2,4,24,3072]{4,3,2,1,0:T(8,128)(2,1)S(1)}, u32[]{:S(2)}, u32[]{:S(2)}) %collective-permute-start.16) | collective-permute-done | bytes 2359328 | tf_op jit(solution)/shard_map/ppermute | solution.py:544
  139.1 2.2 copy-done.7
  141.3 14.3 %feed_forward.2 = (f32[512,768]{1,0:T(8,128)}, f32[512,768]{1,0:T(8,128)}, bf16[3,16,24,1024]{3,2,1,0:T(8,128)(2,1)}, bf16[3,16,24,1024]{3,2,1,0:T(8,128)(2,1)}) custom-call(s32[1]{0:T(128)} %bitcast.here_ref, bf16[512,768]{1,0:T(8,128)(2,1)} %bitcast.221, bf16[512,768]{1,0:T(8,128)(2,1)} %bitcast.223, bf16[768,3072]{1,0:T(8,128)(2,1)} %bitcast.173, ...), custom_call_target="tpu_custom_call" | custom-call | flops 7247757312 | bytes 23592964 | tf_op jit(solution)/shard_map/feed_forward/pallas_call | solution.py:1034
  157.0 3.5 collective-permute-done.17
  164.5 2.2 copy-done.6
  168.3 14.9 %feed_forward.3 = (f32[512,768]{1,0:T(8,128)}, f32[512,768]{1,0:T(8,128)}, bf16[3,16,24,1024]{3,2,1,0:T(8,128)(2,1)}, bf16[3,16,24,1024]{3,2,1,0:T(8,128)(2,1)}) custom-call(s32[1]{0:T(128)} %bitcast.here_ref, bf16[512,768]{1,0:T(8,128)(2,1)} %bitcast.222, bf16[512,768]{1,0:T(8,128)(2,1)} %bitcast.224, bf16[768,3072]{1,0:T(8,128)(2,1)} %bitcast.170, ...), custom_call_target="tpu_custom_call" | custom-call | flops 7247757312 | bytes 23592964 | tf_op jit(solution)/shard_map/feed_forward/pallas_call | solution.py:1034
  183.3 4.7 %collective-permute-done.21 = bf16[3,16,24,1024]{3,2,1,0:T(8,128)(2,1)S(1)} collective-permute-done((bf16[3,16,24,1024]{3,2,1,0:T(8,128)(2,1)}, bf16[3,16,24,1024]{3,2,1,0:T(8,128)(2,1)S(1)}, u32[]{:S(2)}, u32[]{:S(2)}) %collective-permute-start.21) | collective-permute-done | bytes 2359328 | tf_op jit(solution)/shard_map/ppermute | solution.py:544
  196.1 18.3 %attention_backward.1 = (bf16[2,256,768]{2,1,0:T(8,128)(2,1)}, f32[2,256,768]{2,1,0:T(8,128)}, bf16[4,2,256,768]{3,2,1,0:T(8,128)(2,1)}, f32[2,8,768]{2,1,0:T(8,128)}) custom-call(s32[2]{0:T(128)} %mul.74.length_ref, f32[2,256,768]{2,1,0:T(8,128)} %bitcast.214, f32[2,256,768]{2,1,0:T(8,128)} %bitcast.216, f32[2,256,768]{2,1,0:T(8,128)} %bitcast.215, ...), custom_call_target="tpu_custom_call" | custom-call | flops 1610612736 | bytes 27349000 | tf_op jit(solution)/shard_map/attention_backward/pallas_call | solution.py:1034
  221.4 3.0 collective-permute-start.28
  224.4 11.9 %projection_backward.1 = (bf16[4,16,24,768]{3,2,1,0:T(8,128)(2,1)}, bf16[4,16,24,768]{3,2,1,0:T(8,128)(2,1)}, f32[2,256,768]{2,1,0:T(8,128)}, bf16[2,8,768]{2,1,0:T(8,128)(2,1)}) custom-call(s32[1]{0:T(128)} %bitcast.here_ref, bf16[4,2,256,768]{3,2,1,0:T(8,128)(2,1)} %get-tuple-element.298.grads_in_ref, bf16[2,256,768]{2,1,0:T(8,128)(2,1)} %get-tuple-element.299.first_ref, ...), custom_call_target="tpu_custom_call" | custom-call | flops 4227858432 | bytes 18201604 | tf_op jit(solution)/shard_map/projection_backward/pallas_call | solution.py:1034
  239.1 3.7 all-to-all-start.2
  246.8 1.9 collective-permute-start.32
  248.7 2.5 collective-permute-start.33
  258.9 6.2 %collective-permute-done.33 = bf16[3,24,1024]{2,1,0:T(8,128)(2,1)S(1)} collective-permute-done((bf16[3,24,1024]{2,1,0:T(8,128)(2,1)S(1)}, bf16[3,24,1024]{2,1,0:T(8,128)(2,1)S(1)}, u32[]{:S(2)}, u32[]{:S(2)}) %collective-permute-start.33) | collective-permute-done | bytes 147488 | tf_op jit(solution)/shard_map/ppermute | solution.py:547
  267.0 7.4 %all-to-all-start.3 = ((bf16[16,24,1024]{2,1,0:T(8,128)(2,1)}), bf16[16,24,1024]{2,1,0:T(8,128)(2,1)S(1)}, u32[]{:S(2)}, u32[]{:S(2)}) async-start(bf16[16,24,1024]{2,1,0:T(8,128)(2,1)} %slots.2), calls=%async_computation.3 | async-start | bytes 1572864 | tf_op jit(solution)/shard_map/all_to_all | solution.py:679
  274.3 1.9 collective-permute-start.36
  277.7 20.1 %collective-permute-done.36 = bf16[2,8,24,768]{3,2,1,0:T(8,128)(2,1)S(1)} collective-permute-done((bf16[2,8,24,768]{3,2,1,0:T(8,128)(2,1)}, bf16[2,8,24,768]{3,2,1,0:T(8,128)(2,1)S(1)}, u32[]{:S(2)}, u32[]{:S(2)}) %collective-permute-start.36) | collective-permute-done | bytes 589856 | tf_op jit(solution)/shard_map/ppermute | solution.py:544
  301.2 6.4 %collective-permute-done.38.other_ref = bf16[2,4,24,768]{3,2,1,0:T(8,128)(2,1)S(1)} collective-permute-done((bf16[2,4,24,768]{3,2,1,0:T(8,128)(2,1)S(1)}, bf16[2,4,24,768]{3,2,1,0:T(8,128)(2,1)S(1)}, u32[]{:S(2)}, u32[]{:S(2)}) %collective-permute-start.38) | collective-permute-done | bytes 294944 | tf_op jit(solution)/shard_map/ppermute | solution.py:544
  311.2 2.4 collective-permute-start.41
  315.4 3.1 collective-permute-done.40
  318.4 4.4 collective-permute-done.41
  322.9 4.9 %collective-permute-done.43.refs_1_ = bf16[16,24,1024]{2,1,0:T(8,128)(2,1)S(1)} collective-permute-done((bf16[16,24,1024]{2,1,0:T(8,128)(2,1)S(1)}, bf16[16,24,1024]{2,1,0:T(8,128)(2,1)S(1)}, u32[]{:S(2)}, u32[]{:S(2)}) %collective-permute-start.43) | collective-permute-done | bytes 786464 | tf_op jit(solution)/shard_map/ppermute | solution.py:544
  333.7 8.5 %collective-permute-done.44.refs_1_ = bf16[24,9216]{1,0:T(8,128)(2,1)} collective-permute-done((bf16[24,9216]{1,0:T(8,128)(2,1)}, bf16[24,9216]{1,0:T(8,128)(2,1)}, u32[]{:S(2)}, u32[]{:S(2)}) %collective-permute-start.44) | collective-permute-done | bytes 442400 | tf_op jit(solution)/shard_map/ppermute | solution.py:544
  346.8 5.6 %all-to-all-start.4 = ((bf16[16,24,768]{2,1,0:T(8,128)(2,1)}), bf16[16,24,768]{2,1,0:T(8,128)(2,1)S(1)}, u32[]{:S(2)}, u32[]{:S(2)}) async-start(bf16[16,24,768]{2,1,0:T(8,128)(2,1)} %copy-done.14), calls=%async_computation.4 | async-start | bytes 1179648 | tf_op jit(solution)/shard_map/all_to_all | solution.py:679
  352.4 1.9 copy-done.9
  356.4 13.0 %all-to-all-done.4 = bf16[16,24,768]{2,1,0:T(8,128)(2,1)S(1)} async-done(((bf16[16,24,768]{2,1,0:T(8,128)(2,1)}), bf16[16,24,768]{2,1,0:T(8,128)(2,1)S(1)}, u32[]{:S(2)}, u32[]{:S(2)}) %all-to-all-start.4) | async-done | bytes 589856 | tf_op jit(solution)/shard_map/all_to_all | solution.py:679
  370.8 2.4 multiply_add_fusion
  375.2 16.2 %newton_schulz.3 = bf16[768,768]{1,0:T(8,128)(2,1)S(1)} custom-call(s32[1]{0:T(128)} %bitcast.101.active_ref, bf16[768,768]{1,0:T(8,128)(2,1)S(1)} %bitcast.181, bf16[64,768]{1,0:T(8,128)(2,1)S(1)} %bitcast.200, bf16[64,768]{1,0:T(8,128)(2,1)S(1)} %select_bitcast_fusion.right_ref), custom_call_target="tpu_custom_call" | custom-call | flops 18119393280 | bytes 2359296 | tf_op jit(solution)/shard_map/newton_schulz/pallas_call | solution.py:142
  392.9 7.9 %all-to-all-start.5 = ((bf16[16,24,1024]{2,1,0:T(8,128)(2,1)}), bf16[16,24,1024]{2,1,0:T(8,128)(2,1)S(1)}, u32[]{:S(2)}, u32[]{:S(2)}) async-start(bf16[16,24,1024]{2,1,0:T(8,128)(2,1)} %bitcast.212), calls=%async_computation.5 | async-start | bytes 1572864 | tf_op jit(solution)/shard_map/all_to_all | solution.py:729
  405.4 15.9 %all-to-all-done.5.refs_0_ = bf16[16,24,1024]{2,1,0:T(8,128)(2,1)S(1)} async-done(((bf16[16,24,1024]{2,1,0:T(8,128)(2,1)}), bf16[16,24,1024]{2,1,0:T(8,128)(2,1)S(1)}, u32[]{:S(2)}, u32[]{:S(2)}) %all-to-all-start.5) | async-done | bytes 786464 | tf_op jit(solution)/shard_map/all_to_all | solution.py:729
  424.2 12.6 %collective-permute-done.48.refs_1_ = bf16[24,13824]{1,0:T(8,128)(2,1)S(1)} collective-permute-done((bf16[24,13824]{1,0:T(8,128)(2,1)S(1)}, bf16[24,13824]{1,0:T(8,128)(2,1)S(1)}, u32[]{:S(2)}, u32[]{:S(2)}) %collective-permute-start.48) | collective-permute-done | bytes 663584 | tf_op jit(solution)/shard_map/ppermute | solution.py:544
  436.8 1.9 multiply_add_fusion.1
  438.8 5.7 %update.1 = (f32[6,96,768]{2,1,0:T(8,128)}, f32[3,96,768]{2,1,0:T(8,128)}, f32[96,768]{1,0:T(8,128)}, f32[2,96,2048]{2,1,0:T(8,128)}, f32[96,2048]{1,0:T(8,128)}) custom-call(s32[4]{0:T(128)S(1)} %pad_add_fusion.5.slot_ref, bf16[24,13824]{1,0:T(8,128)(2,1)S(1)} %pack.3.refs_0_, bf16[24,13824]{1,0:T(8,128)(2,1)S(1)} %collective-permute-done.48.refs_1_, ...), custom_call_target="tpu_custom_call" | custom-call | bytes 14000000 | tf_op jit(solution)/shard_map/update/pallas_call | solution.py:405
  (292 shorter events, 112.9 us)
Async XLA Ops:
  4.3 14.1 %collective-permute-start = (bf16[24,3072]{1,0:T(8,128)(2,1)S(1)}, bf16[24,3072]{1,0:T(8,128)(2,1)S(1)}, u32[]{:S(2)}, u32[]{:S(2)}) collective-permute-start(bf16[24,3072]{1,0:T(8,128)(2,1)S(1)} %fusion.17.refs_0_), channel_id=1, source_target_pairs={{0,2},{2,4},{4,6},{6,0},{1,3},{3,5},{5,7},{7,1},{8,10},{10,12},{12... | collective-permute-start | bytes 442376 | tf_op jit(solution)/shard_map/ppermute | solution.py:547
  7.4 12.3 %collective-permute-start.1 = (bf16[24,3072]{1,0:T(8,128)(2,1)S(1)}, bf16[24,3072]{1,0:T(8,128)(2,1)S(1)}, u32[]{:S(2)}, u32[]{:S(2)}) collective-permute-start(bf16[24,3072]{1,0:T(8,128)(2,1)S(1)} %fusion.17.refs_0_), channel_id=1, source_target_pairs={{0,4},{2,6},{4,0},{6,2},{1,5},{3,7},{5,1},{7,3},{8,12},{10,14},{12... | collective-permute-start | bytes 442376 | tf_op jit(solution)/shard_map/ppermute | solution.py:547
  10.0 9.7 %collective-permute-start.2 = (bf16[24,3072]{1,0:T(8,128)(2,1)S(1)}, bf16[24,3072]{1,0:T(8,128)(2,1)}, u32[]{:S(2)}, u32[]{:S(2)}) collective-permute-start(bf16[24,3072]{1,0:T(8,128)(2,1)S(1)} %fusion.17.refs_0_), channel_id=1, source_target_pairs={{0,6},{2,0},{4,2},{6,4},{1,7},{3,1},{5,3},{7,5},{8,14},{10,8},{12,... | collective-permute-start | bytes 442376 | tf_op jit(solution)/shard_map/ppermute | solution.py:547
  13.2 10.6 %all-to-all-start = ((bf16[8,2,96]{2,1,0:T(2,128)(2,1)}), bf16[8,2,96]{2,1,0:T(2,128)(2,1)S(1)}, u32[]{:S(2)}, u32[]{:S(2)}) async-start(bf16[8,2,96]{2,1,0:T(2,128)(2,1)} %bitcast.150), calls=%async_computation | async-start | bytes 8192 | tf_op jit(solution)/shard_map/all_to_all | solution.py:620
  23.8 12.7 %collective-permute-start.4 = (bf16[4,24,1536]{2,1,0:T(8,128)(2,1)S(1)}, bf16[4,24,1536]{2,1,0:T(8,128)(2,1)S(1)}, u32[]{:S(2)}, u32[]{:S(2)}) collective-permute-start(bf16[4,24,1536]{2,1,0:T(8,128)(2,1)S(1)} %get-tuple-element.207.refs_0_), channel_id=1, source_target_pairs={{0,16},{16,0},{1,17},{17,1},{2,18},{18,2},{3,19},{19,3},{4,20},{20... | collective-permute-start | bytes 884744 | tf_op jit(solution)/shard_map/ppermute | solution.py:544
  25.3 11.8 %collective-permute-start.3 = (bf16[4,24,1536]{2,1,0:T(8,128)(2,1)S(1)}, bf16[4,24,1536]{2,1,0:T(8,128)(2,1)S(1)}, u32[]{:S(2)}, u32[]{:S(2)}) collective-permute-start(bf16[4,24,1536]{2,1,0:T(8,128)(2,1)S(1)} %get-tuple-element.206.refs_0_), channel_id=1, source_target_pairs={{0,1},{1,0},{2,3},{3,2},{4,5},{5,4},{6,7},{7,6},{8,9},{9,8},{10,11... | collective-permute-start | bytes 884744 | tf_op jit(solution)/shard_map/ppermute | solution.py:544
  28.5 20.6 %all-to-all-start.1 = ((f32[8,2,6,768]{3,1,2,0:T(2,128)}), f32[8,2,6,768]{3,1,2,0:T(2,128)S(1)}, u32[]{:S(2)}, u32[]{:S(2)}) async-start(f32[8,2,6,768]{3,1,2,0:T(2,128)} %copy.53), calls=%async_computation.1 | async-start | bytes 589824 | tf_op jit(solution)/shard_map/all_to_all | solution.py:620
  32.5 17.3 %collective-permute-start.5 = (bf16[24,6144]{1,0:T(8,128)(2,1)S(1)}, bf16[24,6144]{1,0:T(8,128)(2,1)S(1)}, u32[]{:S(2)}, u32[]{:S(2)}) collective-permute-start(bf16[24,6144]{1,0:T(8,128)(2,1)S(1)} %constant_dynamic-slice_fusion.5.refs_0_), channel_id=1, source_target_pairs={{0,2},{2,4},{4,6},{6,0},{1,3},{3,5},{5,7},{7,1},{8,10},{10,12},{12... | collective-permute-start | bytes 884744 | tf_op jit(solution)/shard_map/ppermute | solution.py:547
  34.6 17.5 %collective-permute-start.6 = (bf16[24,6144]{1,0:T(8,128)(2,1)S(1)}, bf16[24,6144]{1,0:T(8,128)(2,1)S(1)}, u32[]{:S(2)}, u32[]{:S(2)}) collective-permute-start(bf16[24,6144]{1,0:T(8,128)(2,1)S(1)} %constant_dynamic-slice_fusion.5.refs_0_), channel_id=1, source_target_pairs={{0,6},{2,0},{4,2},{6,4},{1,7},{3,1},{5,3},{7,5},{8,14},{10,8},{12,... | collective-permute-start | bytes 884744 | tf_op jit(solution)/shard_map/ppermute | solution.py:547
  52.8 14.4 %collective-permute-start.7 = (bf16[2,4,24,1536]{3,2,1,0:T(8,128)(2,1)S(1)}, bf16[2,4,24,1536]{3,2,1,0:T(8,128)(2,1)S(1)}, u32[]{:S(2)}, u32[]{:S(2)}) collective-permute-start(bf16[2,4,24,1536]{3,2,1,0:T(8,128)(2,1)S(1)} %place.18.refs_0_), channel_id=1, source_target_pairs={{0,16},{16,0},{1,17},{17,1},{2,18},{18,2},{3,19},{19,3},{4,20},{20... | collective-permute-start | bytes 1769480 | tf_op jit(solution)/shard_map/ppermute | solution.py:544
  53.3 14.2 %collective-permute-start.8 = (bf16[2,4,24,1536]{3,2,1,0:T(8,128)(2,1)S(1)}, bf16[2,4,24,1536]{3,2,1,0:T(8,128)(2,1)S(1)}, u32[]{:S(2)}, u32[]{:S(2)}) collective-permute-start(bf16[2,4,24,1536]{3,2,1,0:T(8,128)(2,1)S(1)} %place.19.refs_0_), channel_id=1, source_target_pairs={{0,1},{1,0},{2,3},{3,2},{4,5},{5,4},{6,7},{7,6},{8,9},{9,8},{10,11... | collective-permute-start | bytes 1769480 | tf_op jit(solution)/shard_map/ppermute | solution.py:544
  54.0 15.7 %collective-permute-start.9 = (bf16[24,6144]{1,0:T(8,128)(2,1)S(1)}, bf16[24,6144]{1,0:T(8,128)(2,1)S(1)}, u32[]{:S(2)}, u32[]{:S(2)}) collective-permute-start(bf16[24,6144]{1,0:T(8,128)(2,1)S(1)} %constant_dynamic-slice_fusion.5.refs_0_), channel_id=1, source_target_pairs={{0,4},{2,6},{4,0},{6,2},{1,5},{3,7},{5,1},{7,3},{8,12},{10,14},{12... | collective-permute-start | bytes 884744 | tf_op jit(solution)/shard_map/ppermute | solution.py:547
  70.5 7.5 %collective-permute-start.10 = (bf16[2,2,4,24,1536]{4,3,2,1,0:T(8,128)(2,1)S(1)}, bf16[2,2,4,24,1536]{4,3,2,1,0:T(8,128)(2,1)S(1)}, u32[]{:S(2)}, u32[]{:S(2)}) collective-permute-start(bf16[2,2,4,24,1536]{4,3,2,1,0:T(8,128)(2,1)S(1)} %place.20.refs_0_), channel_id=1, source_target_pairs={{0,8},{8,0},{1,9},{9,1},{2,10},{10,2},{3,11},{11,3},{4,12},{12,4},... | collective-permute-start | bytes 3538952 | tf_op jit(solution)/shard_map/ppermute | solution.py:544
  80.7 23.2 %collective-permute-start.12 = (bf16[4,24,3072]{2,1,0:T(8,128)(2,1)S(1)}, bf16[4,24,3072]{2,1,0:T(8,128)(2,1)S(1)}, u32[]{:S(2)}, u32[]{:S(2)}) collective-permute-start(bf16[4,24,3072]{2,1,0:T(8,128)(2,1)S(1)} %get-tuple-element.245.refs_0_), channel_id=1, source_target_pairs={{0,1},{1,0},{2,3},{3,2},{4,5},{5,4},{6,7},{7,6},{8,9},{9,8},{10,11... | collective-permute-start | bytes 1769480 | tf_op jit(solution)/shard_map/ppermute | solution.py:544
  81.3 22.6 %collective-permute-start.13 = (bf16[4,24,3072]{2,1,0:T(8,128)(2,1)S(1)}, bf16[4,24,3072]{2,1,0:T(8,128)(2,1)S(1)}, u32[]{:S(2)}, u32[]{:S(2)}) collective-permute-start(bf16[4,24,3072]{2,1,0:T(8,128)(2,1)S(1)} %get-tuple-element.247.refs_0_), channel_id=1, source_target_pairs={{0,16},{16,0},{1,17},{17,1},{2,18},{18,2},{3,19},{19,3},{4,20},{20... | collective-permute-start | bytes 1769480 | tf_op jit(solution)/shard_map/ppermute | solution.py:544
  105.2 27.5 %collective-permute-start.14 = (bf16[2,4,24,3072]{3,2,1,0:T(8,128)(2,1)S(1)}, bf16[2,4,24,3072]{3,2,1,0:T(8,128)(2,1)S(1)}, u32[]{:S(2)}, u32[]{:S(2)}) collective-permute-start(bf16[2,4,24,3072]{3,2,1,0:T(8,128)(2,1)S(1)} %place.24.refs_0_), channel_id=1, source_target_pairs={{0,16},{16,0},{1,17},{17,1},{2,18},{18,2},{3,19},{19,3},{4,20},{20... | collective-permute-start | bytes 3538952 | tf_op jit(solution)/shard_map/ppermute | solution.py:544
  105.8 27.2 %collective-permute-start.15 = (bf16[2,4,24,3072]{3,2,1,0:T(8,128)(2,1)S(1)}, bf16[2,4,24,3072]{3,2,1,0:T(8,128)(2,1)S(1)}, u32[]{:S(2)}, u32[]{:S(2)}) collective-permute-start(bf16[2,4,24,3072]{3,2,1,0:T(8,128)(2,1)S(1)} %place.25.refs_0_), channel_id=1, source_target_pairs={{0,1},{1,0},{2,3},{3,2},{4,5},{5,4},{6,7},{7,6},{8,9},{9,8},{10,11... | collective-permute-start | bytes 3538952 | tf_op jit(solution)/shard_map/ppermute | solution.py:544
  160.8 22.4 %collective-permute-start.19 = (bf16[2,8,24,1024]{3,2,1,0:T(8,128)(2,1)S(1)}, bf16[2,8,24,1024]{3,2,1,0:T(8,128)(2,1)S(1)}, u32[]{:S(2)}, u32[]{:S(2)}) collective-permute-start(bf16[2,8,24,1024]{3,2,1,0:T(8,128)(2,1)S(1)} %bitcast.202), channel_id=1, source_target_pairs={{0,16},{16,0},{1,17},{17,1},{2,18},{18,2},{3,19},{19,3},{4,20},{20... | collective-permute-start | bytes 2359304 | tf_op jit(solution)/shard_map/ppermute | solution.py:544
  166.8 16.4 %collective-permute-start.20 = (bf16[1,8,24,1024]{3,2,1,0:T(8,128)(2,1)S(1)}, bf16[1,8,24,1024]{3,2,1,0:T(8,128)(2,1)S(1)}, u32[]{:S(2)}, u32[]{:S(2)}) collective-permute-start(bf16[1,8,24,1024]{3,2,1,0:T(8,128)(2,1)S(1)} %bitcast.206), channel_id=1, source_target_pairs={{0,1},{1,0},{2,3},{3,2},{4,5},{5,4},{6,7},{7,6},{8,9},{9,8},{10,11... | collective-permute-start | bytes 1179656 | tf_op jit(solution)/shard_map/ppermute | solution.py:544
  190.1 24.4 %collective-permute-start.24 = (bf16[2,8,24,1024]{3,2,1,0:T(8,128)(2,1)S(1)}, bf16[2,8,24,1024]{3,2,1,0:T(8,128)(2,1)S(1)}, u32[]{:S(2)}, u32[]{:S(2)}) collective-permute-start(bf16[2,8,24,1024]{3,2,1,0:T(8,128)(2,1)S(1)} %bitcast.201), channel_id=1, source_target_pairs={{0,16},{16,0},{1,17},{17,1},{2,18},{18,2},{3,19},{19,3},{4,20},{20... | collective-permute-start | bytes 2359304 | tf_op jit(solution)/shard_map/ppermute | solution.py:544
  192.6 21.9 %collective-permute-start.25 = (bf16[1,8,24,1024]{3,2,1,0:T(8,128)(2,1)}, bf16[1,8,24,1024]{3,2,1,0:T(8,128)(2,1)S(1)}, u32[]{:S(2)}, u32[]{:S(2)}) collective-permute-start(bf16[1,8,24,1024]{3,2,1,0:T(8,128)(2,1)} %bitcast.54), channel_id=1, source_target_pairs={{0,1},{1,0},{2,3},{3,2},{4,5},{5,4},{6,7},{7,6},{8,9},{9,8},{10,11... | collective-permute-start | bytes 1179656 | tf_op jit(solution)/shard_map/ppermute | solution.py:544
  193.9 20.6 %collective-permute-start.22 = (bf16[2,4,24,1024]{3,2,1,0:T(8,128)(2,1)}, bf16[2,4,24,1024]{3,2,1,0:T(8,128)(2,1)S(1)}, u32[]{:S(2)}, u32[]{:S(2)}) collective-permute-start(bf16[2,4,24,1024]{3,2,1,0:T(8,128)(2,1)} %bitcast.42), channel_id=1, source_target_pairs={{0,1},{1,0},{2,3},{3,2},{4,5},{5,4},{6,7},{7,6},{8,9},{9,8},{10,11... | collective-permute-start | bytes 1179656 | tf_op jit(solution)/shard_map/ppermute | solution.py:544
  195.5 19.0 %collective-permute-start.23 = (bf16[1,4,24,1024]{3,2,1,0:T(8,128)(2,1)S(1)}, bf16[1,4,24,1024]{3,2,1,0:T(8,128)(2,1)S(1)}, u32[]{:S(2)}, u32[]{:S(2)}) collective-permute-start(bf16[1,4,24,1024]{3,2,1,0:T(8,128)(2,1)S(1)} %bitcast.210), channel_id=1, source_target_pairs={{0,16},{16,0},{1,17},{17,1},{2,18},{18,2},{3,19},{19,3},{4,20},{20... | collective-permute-start | bytes 589832 | tf_op jit(solution)/shard_map/ppermute | solution.py:544
  215.3 21.1 %collective-permute-start.30 = (bf16[1,4,24,1024]{3,2,1,0:T(8,128)(2,1)S(1)}, bf16[1,4,24,1024]{3,2,1,0:T(8,128)(2,1)S(1)}, u32[]{:S(2)}, u32[]{:S(2)}) collective-permute-start(bf16[1,4,24,1024]{3,2,1,0:T(8,128)(2,1)S(1)} %bitcast.209), channel_id=1, source_target_pairs={{0,16},{16,0},{1,17},{17,1},{2,18},{18,2},{3,19},{19,3},{4,20},{20... | collective-permute-start | bytes 589832 | tf_op jit(solution)/shard_map/ppermute | solution.py:544
  217.7 19.4 %collective-permute-start.29 = (bf16[2,4,24,1024]{3,2,1,0:T(8,128)(2,1)S(1)}, bf16[2,4,24,1024]{3,2,1,0:T(8,128)(2,1)S(1)}, u32[]{:S(2)}, u32[]{:S(2)}) collective-permute-start(bf16[2,4,24,1024]{3,2,1,0:T(8,128)(2,1)S(1)} %bitcast.205), channel_id=1, source_target_pairs={{0,1},{1,0},{2,3},{3,2},{4,5},{5,4},{6,7},{7,6},{8,9},{9,8},{10,11... | collective-permute-start | bytes 1179656 | tf_op jit(solution)/shard_map/ppermute | solution.py:544
  218.4 17.8 %collective-permute-start.26 = (bf16[3,24,1024]{2,1,0:T(8,128)(2,1)S(1)}, bf16[3,24,1024]{2,1,0:T(8,128)(2,1)S(1)}, u32[]{:S(2)}, u32[]{:S(2)}) collective-permute-start(bf16[3,24,1024]{2,1,0:T(8,128)(2,1)S(1)} %pad_maximum_fusion.2), channel_id=1, source_target_pairs={{0,2},{2,4},{4,6},{6,0},{1,3},{3,5},{5,7},{7,1},{8,10},{10,12},{12... | collective-permute-start | bytes 442376 | tf_op jit(solution)/shard_map/ppermute | solution.py:547
  219.9 16.4 %collective-permute-start.27 = (bf16[3,24,1024]{2,1,0:T(8,128)(2,1)S(1)}, bf16[3,24,1024]{2,1,0:T(8,128)(2,1)S(1)}, u32[]{:S(2)}, u32[]{:S(2)}) collective-permute-start(bf16[3,24,1024]{2,1,0:T(8,128)(2,1)S(1)} %pad_maximum_fusion.3), channel_id=1, source_target_pairs={{0,4},{2,6},{4,0},{6,2},{1,5},{3,7},{5,1},{7,3},{8,12},{10,14},{12... | collective-permute-start | bytes 442376 | tf_op jit(solution)/shard_map/ppermute | solution.py:547
  221.4 14.9 %collective-permute-start.28 = (bf16[3,24,1024]{2,1,0:T(8,128)(2,1)S(1)}, bf16[3,24,1024]{2,1,0:T(8,128)(2,1)S(1)}, u32[]{:S(2)}, u32[]{:S(2)}) collective-permute-start(bf16[3,24,1024]{2,1,0:T(8,128)(2,1)S(1)} %pad_maximum_fusion.4), channel_id=1, source_target_pairs={{0,6},{2,0},{4,2},{6,4},{1,7},{3,1},{5,3},{7,5},{8,14},{10,8},{12,... | collective-permute-start | bytes 442376 | tf_op jit(solution)/shard_map/ppermute | solution.py:547
  239.1 27.9 %all-to-all-start.2 = ((bf16[16,16,768]{2,1,0:T(8,128)(2,1)}), bf16[16,16,768]{2,1,0:T(8,128)(2,1)S(1)}, u32[]{:S(2)}, u32[]{:S(2)}) async-start(bf16[16,16,768]{2,1,0:T(8,128)(2,1)} %broadcast_in_dim.41), calls=%async_computation.2 | async-start | bytes 786432 | tf_op jit(solution)/shard_map/all_to_all | solution.py:679
  246.8 12.1 %collective-permute-start.32 = (bf16[3,24,1024]{2,1,0:T(8,128)(2,1)S(1)}, bf16[3,24,1024]{2,1,0:T(8,128)(2,1)S(1)}, u32[]{:S(2)}, u32[]{:S(2)}) collective-permute-start(bf16[3,24,1024]{2,1,0:T(8,128)(2,1)S(1)} %pad_maximum_fusion.5), channel_id=1, source_target_pairs={{0,2},{2,4},{4,6},{6,0},{1,3},{3,5},{5,7},{7,1},{8,10},{10,12},{12... | collective-permute-start | bytes 442376 | tf_op jit(solution)/shard_map/ppermute | solution.py:547
  248.7 16.4 %collective-permute-start.33 = (bf16[3,24,1024]{2,1,0:T(8,128)(2,1)S(1)}, bf16[3,24,1024]{2,1,0:T(8,128)(2,1)S(1)}, u32[]{:S(2)}, u32[]{:S(2)}) collective-permute-start(bf16[3,24,1024]{2,1,0:T(8,128)(2,1)S(1)} %pad_maximum_fusion.6), channel_id=1, source_target_pairs={{0,4},{2,6},{4,0},{6,2},{1,5},{3,7},{5,1},{7,3},{8,12},{10,14},{12... | collective-permute-start | bytes 442376 | tf_op jit(solution)/shard_map/ppermute | solution.py:547
  251.2 14.0 %collective-permute-start.34 = (bf16[3,24,1024]{2,1,0:T(8,128)(2,1)S(1)}, bf16[3,24,1024]{2,1,0:T(8,128)(2,1)S(1)}, u32[]{:S(2)}, u32[]{:S(2)}) collective-permute-start(bf16[3,24,1024]{2,1,0:T(8,128)(2,1)S(1)} %pad_maximum_fusion.7), channel_id=1, source_target_pairs={{0,6},{2,0},{4,2},{6,4},{1,7},{3,1},{5,3},{7,5},{8,14},{10,8},{12,... | collective-permute-start | bytes 442376 | tf_op jit(solution)/shard_map/ppermute | solution.py:547
  267.0 42.0 %all-to-all-start.3 = ((bf16[16,24,1024]{2,1,0:T(8,128)(2,1)}), bf16[16,24,1024]{2,1,0:T(8,128)(2,1)S(1)}, u32[]{:S(2)}, u32[]{:S(2)}) async-start(bf16[16,24,1024]{2,1,0:T(8,128)(2,1)} %slots.2), calls=%async_computation.3 | async-start | bytes 1572864 | tf_op jit(solution)/shard_map/all_to_all | solution.py:679
  274.3 23.5 %collective-permute-start.36 = (bf16[2,8,24,768]{3,2,1,0:T(8,128)(2,1)}, bf16[2,8,24,768]{3,2,1,0:T(8,128)(2,1)S(1)}, u32[]{:S(2)}, u32[]{:S(2)}) collective-permute-start(bf16[2,8,24,768]{3,2,1,0:T(8,128)(2,1)} %bitcast.204), channel_id=1, source_target_pairs={{0,1},{1,0},{2,3},{3,2},{4,5},{5,4},{6,7},{7,6},{8,9},{9,8},{10,11... | collective-permute-start | bytes 1769480 | tf_op jit(solution)/shard_map/ppermute | solution.py:544
  276.3 21.6 %collective-permute-start.35 = (bf16[2,8,24,768]{3,2,1,0:T(8,128)(2,1)S(1)}, bf16[2,8,24,768]{3,2,1,0:T(8,128)(2,1)S(1)}, u32[]{:S(2)}, u32[]{:S(2)}) collective-permute-start(bf16[2,8,24,768]{3,2,1,0:T(8,128)(2,1)S(1)} %bitcast.203), channel_id=1, source_target_pairs={{0,16},{16,0},{1,17},{17,1},{2,18},{18,2},{3,19},{19,3},{4,20},{20... | collective-permute-start | bytes 1769480 | tf_op jit(solution)/shard_map/ppermute | solution.py:544
  298.1 9.5 %collective-permute-start.38 = (bf16[2,4,24,768]{3,2,1,0:T(8,128)(2,1)S(1)}, bf16[2,4,24,768]{3,2,1,0:T(8,128)(2,1)S(1)}, u32[]{:S(2)}, u32[]{:S(2)}) collective-permute-start(bf16[2,4,24,768]{3,2,1,0:T(8,128)(2,1)S(1)} %bitcast.207), channel_id=1, source_target_pairs={{0,16},{16,0},{1,17},{17,1},{2,18},{18,2},{3,19},{19,3},{4,20},{20... | collective-permute-start | bytes 884744 | tf_op jit(solution)/shard_map/ppermute | solution.py:544
  299.8 9.2 %collective-permute-start.37 = (bf16[2,4,24,768]{3,2,1,0:T(8,128)(2,1)S(1)}, bf16[2,4,24,768]{3,2,1,0:T(8,128)(2,1)S(1)}, u32[]{:S(2)}, u32[]{:S(2)}) collective-permute-start(bf16[2,4,24,768]{3,2,1,0:T(8,128)(2,1)S(1)} %bitcast.208), channel_id=1, source_target_pairs={{0,1},{1,0},{2,3},{3,2},{4,5},{5,4},{6,7},{7,6},{8,9},{9,8},{10,11... | collective-permute-start | bytes 884744 | tf_op jit(solution)/shard_map/ppermute | solution.py:544
  309.0 18.8 %collective-permute-start.43 = (bf16[16,24,1024]{2,1,0:T(8,128)(2,1)S(1)}, bf16[16,24,1024]{2,1,0:T(8,128)(2,1)S(1)}, u32[]{:S(2)}, u32[]{:S(2)}) collective-permute-start(bf16[16,24,1024]{2,1,0:T(8,128)(2,1)S(1)} %all-to-all-done.3.refs_0_), channel_id=1, source_target_pairs={{0,16},{16,0},{1,17},{17,1},{2,18},{18,2},{3,19},{19,3},{4,20},{20... | collective-permute-start | bytes 2359304 | tf_op jit(solution)/shard_map/ppermute | solution.py:544
  309.7 8.7 %collective-permute-start.40 = (bf16[4,24,768]{2,1,0:T(8,128)(2,1)S(1)}, bf16[4,24,768]{2,1,0:T(8,128)(2,1)S(1)}, u32[]{:S(2)}, u32[]{:S(2)}) collective-permute-start(bf16[4,24,768]{2,1,0:T(8,128)(2,1)S(1)} %pad_maximum_fusion.8), channel_id=1, source_target_pairs={{0,2},{2,4},{4,6},{6,0},{1,3},{3,5},{5,7},{7,1},{8,10},{10,12},{12... | collective-permute-start | bytes 442376 | tf_op jit(solution)/shard_map/ppermute | solution.py:547
  311.2 11.6 %collective-permute-start.41 = (bf16[4,24,768]{2,1,0:T(8,128)(2,1)S(1)}, bf16[4,24,768]{2,1,0:T(8,128)(2,1)S(1)}, u32[]{:S(2)}, u32[]{:S(2)}) collective-permute-start(bf16[4,24,768]{2,1,0:T(8,128)(2,1)S(1)} %pad_maximum_fusion.9), channel_id=1, source_target_pairs={{0,4},{2,6},{4,0},{6,2},{1,5},{3,7},{5,1},{7,3},{8,12},{10,14},{12... | collective-permute-start | bytes 442376 | tf_op jit(solution)/shard_map/ppermute | solution.py:547
  313.7 9.1 %collective-permute-start.42 = (bf16[4,24,768]{2,1,0:T(8,128)(2,1)S(1)}, bf16[4,24,768]{2,1,0:T(8,128)(2,1)S(1)}, u32[]{:S(2)}, u32[]{:S(2)}) collective-permute-start(bf16[4,24,768]{2,1,0:T(8,128)(2,1)S(1)} %pad_maximum_fusion.10), channel_id=1, source_target_pairs={{0,6},{2,0},{4,2},{6,4},{1,7},{3,1},{5,3},{7,5},{8,14},{10,8},{12,... | collective-permute-start | bytes 442376 | tf_op jit(solution)/shard_map/ppermute | solution.py:547
  328.4 15.1 %collective-permute-start.46 = (bf16[2,2,4,2,24,1024]{5,4,3,2,1,0:T(8,128)(2,1)S(1)}, bf16[2,2,4,2,24,1024]{5,4,3,2,1,0:T(8,128)(2,1)}, u32[]{:S(2)}, u32[]{:S(2)}) collective-permute-start(bf16[2,2,4,2,24,1024]{5,4,3,2,1,0:T(8,128)(2,1)S(1)} %bitcast.168), channel_id=1, source_target_pairs={{0,8},{8,0},{1,9},{9,1},{2,10},{10,2},{3,11},{11,3},{4,12},{12,4},... | collective-permute-start | bytes 4718600 | tf_op jit(solution)/shard_map/ppermute | solution.py:544
  329.3 12.9 %collective-permute-start.44 = (bf16[24,9216]{1,0:T(8,128)(2,1)}, bf16[24,9216]{1,0:T(8,128)(2,1)}, u32[]{:S(2)}, u32[]{:S(2)}) collective-permute-start(bf16[24,9216]{1,0:T(8,128)(2,1)} %pack.2.refs_0_), channel_id=1, source_target_pairs={{0,16},{16,0},{1,17},{17,1},{2,18},{18,2},{3,19},{19,3},{4,20},{20... | collective-permute-start | bytes 1327112 | tf_op jit(solution)/shard_map/ppermute | solution.py:544
  343.4 29.8 %collective-permute-start.45 = (bf16[2,24,9216]{2,1,0:T(8,128)(2,1)S(1)}, bf16[2,24,9216]{2,1,0:T(8,128)(2,1)}, u32[]{:S(2)}, u32[]{:S(2)}) collective-permute-start(bf16[2,24,9216]{2,1,0:T(8,128)(2,1)S(1)} %place.31.refs_0_), channel_id=1, source_target_pairs={{0,8},{8,0},{1,9},{9,1},{2,10},{10,2},{3,11},{11,3},{4,12},{12,4},... | collective-permute-start | bytes 2654216 | tf_op jit(solution)/shard_map/ppermute | solution.py:544
  346.8 22.5 %all-to-all-start.4 = ((bf16[16,24,768]{2,1,0:T(8,128)(2,1)}), bf16[16,24,768]{2,1,0:T(8,128)(2,1)S(1)}, u32[]{:S(2)}, u32[]{:S(2)}) async-start(bf16[16,24,768]{2,1,0:T(8,128)(2,1)} %copy-done.14), calls=%async_computation.4 | async-start | bytes 1179648 | tf_op jit(solution)/shard_map/all_to_all | solution.py:679
  392.9 28.4 %all-to-all-start.5 = ((bf16[16,24,1024]{2,1,0:T(8,128)(2,1)}), bf16[16,24,1024]{2,1,0:T(8,128)(2,1)S(1)}, u32[]{:S(2)}, u32[]{:S(2)}) async-start(bf16[16,24,1024]{2,1,0:T(8,128)(2,1)} %bitcast.212), calls=%async_computation.5 | async-start | bytes 1572864 | tf_op jit(solution)/shard_map/all_to_all | solution.py:729
  421.3 15.4 %collective-permute-start.48 = (bf16[24,13824]{1,0:T(8,128)(2,1)S(1)}, bf16[24,13824]{1,0:T(8,128)(2,1)S(1)}, u32[]{:S(2)}, u32[]{:S(2)}) collective-permute-start(bf16[24,13824]{1,0:T(8,128)(2,1)S(1)} %pack.3.refs_0_), channel_id=1, source_target_pairs={{0,16},{16,0},{1,17},{17,1},{2,18},{18,2},{3,19},{19,3},{4,20},{20... | collective-permute-start | bytes 1990664 | tf_op jit(solution)/shard_map/ppermute | solution.py:544
  424.2 14.6 %collective-permute-start.49 = (bf16[24,13824]{1,0:T(8,128)(2,1)S(1)}, bf16[24,13824]{1,0:T(8,128)(2,1)S(1)}, u32[]{:S(2)}, u32[]{:S(2)}) collective-permute-start(bf16[24,13824]{1,0:T(8,128)(2,1)S(1)} %pack.3.refs_0_), channel_id=1, source_target_pairs={{0,8},{8,0},{1,9},{9,1},{2,10},{10,2},{3,11},{11,3},{4,12},{12,4},... | collective-permute-start | bytes 1990664 | tf_op jit(solution)/shard_map/ppermute | solution.py:544
  (63 other events, 332.2 us)

commit v4 on v3

--- a/solution.py
+++ b/solution.py
@@ -196,28 +196,34 @@
     return flat(keep), flat(send)
 
 
-def fold_last(mine, other, here):
-    k, _, rows, cols = mine.shape
-
-    def body(here_ref, mine_ref, other_ref, keep_ref, *send_refs):
-        for by, ref in enumerate((keep_ref, *send_refs)):
+def fold_last(states, here):
+    rows, cols = states[0][0].shape[-2:]
+    counts = [mine.shape[0] for mine, _ in states]
+    k = sum(counts)
+
+    def body(here_ref, *refs):
+        ins, outs = refs[: 2 * len(states)], refs[2 * len(states) :]
+        for by, ref in enumerate(outs):
             at = lax.rem(here_ref[0] + by, 4)
-            total = mine_ref[:, at].astype(F32) + other_ref[:, at].astype(F32)
-            ref[...] = total.astype(ref.dtype)
+            start = 0
+            for i, count in enumerate(counts):
+                total = ins[2 * i][:, at].astype(F32) + ins[2 * i + 1][:, at].astype(F32)
+                ref[start : start + count] = total.astype(ref.dtype)
+                start += count
 
     vmem = pl.BlockSpec(memory_space=pltpu.VMEM)
     return pl.pallas_call(
         body,
         out_shape=(jax.ShapeDtypeStruct((k, rows, cols), F32),)
         + (jax.ShapeDtypeStruct((k, rows, cols), BF16),) * 3,
-        in_specs=[pl.BlockSpec(memory_space=pltpu.SMEM), vmem, vmem],
+        in_specs=[pl.BlockSpec(memory_space=pltpu.SMEM)] + [vmem] * (2 * len(states)),
         out_specs=(vmem,) * 4,
         compiler_params=pltpu.CompilerParams(vmem_limit_bytes=24 * 1024 * 1024),
         cost_estimate=pl.CostEstimate(
             flops=0, bytes_accessed=28 * k * rows * cols, transcendentals=0
         ),
         name="fold_last",
-    )(here.reshape(1).astype(jnp.int32), mine, other)
+    )(here.reshape(1).astype(jnp.int32), *[part for state in states for part in state])
 
 
 def place(parts, slots, lead=None, moves=None):
@@ -268,7 +274,8 @@
     )(jnp.stack(slots).astype(jnp.int32), *parts)
 
 
-def slots_of(feeds, owners, width, extra=None):
+def slots_of(feeds, owners, width, quarter, extra=None):
+    more = 0 if extra is None else extra.shape[0]
     arrays, index = [], {}
 
     def note(array):
@@ -282,11 +289,23 @@
 
     noted = [[(note(total), note(moment)) for total, moment in feed] for feed in feeds]
     rows = arrays[0].shape[-2]
-    more = 0 if extra is None else extra.shape[0]
-
-    def body(*refs):
-        out = refs[-1].at[:, :rows] if more else refs[-1]
+    for total, _ in sum(feeds, []):
+        if total is not None:
+            rows = total[0].shape[-2]
+    if all(total is None or total[0].shape[-2] == moment[0].shape[-2] for total, moment in sum(feeds, [])):
+        quarter = jnp.int32(0)
+
+    def block(array):
+        shape = (*array.shape[:-2], rows, array.shape[-1])
+        lead = (0,) * (array.ndim - 2)
+        if array.shape[-2] == rows:
+            return pl.BlockSpec(shape, lambda i, q: (*lead, 0, 0))
+        return pl.BlockSpec(shape, lambda i, q: (*lead, q[0], 0))
+
+    def body(_, *refs):
+        out = refs[-1]
         if more:
+            out = refs[-1].at[:, :rows]
             for slot in range(owners):
                 refs[-1][slot, rows:] = refs[-2][...]
 
@@ -313,18 +332,22 @@
                 out[slot, :, at : at + value.shape[1]] = value.astype(BF16)
                 at += value.shape[1]
 
-    vmem = pl.BlockSpec(memory_space=pltpu.VMEM)
     return pl.pallas_call(
         body,
         out_shape=jax.ShapeDtypeStruct((owners, rows + more, width), BF16),
-        in_specs=[vmem] * (len(arrays) + (more > 0)),
-        out_specs=vmem,
+        grid_spec=pltpu.PrefetchScalarGridSpec(
+            num_scalar_prefetch=1,
+            grid=(1,),
+            in_specs=[block(array) for array in arrays]
+            + [pl.BlockSpec((more, width), lambda i, q: (0, 0))] * (more > 0),
+            out_specs=pl.BlockSpec((owners, rows + more, width), lambda i, q: (0, 0, 0)),
+        ),
         cost_estimate=pl.CostEstimate(
             flops=0, bytes_accessed=2 * owners * rows * width, transcendentals=0
         ),
         compiler_params=pltpu.CompilerParams(vmem_limit_bytes=24 * 1024 * 1024),
         name="slots",
-    )(*arrays, *([extra] if more else []))
+    )(quarter.reshape(1).astype(jnp.int32), *arrays, *([extra] if more else []))
 
 
 def pack(parts):
@@ -473,17 +496,14 @@
     def own_rows(self, shard, dim=-2):
         return shard
 
-    def complete(self, piece):
+    def complete_begin(self, piece):
+        return piece
+
+    def complete_end(self, piece):
         return piece
 
     def quarters(self, piece):
         return [jnp.int32(0)], [piece]
-
-    def images_begin(self, rows):
-        return lax.all_gather(rows, ("dp", "fsdp"), axis=0, tiled=True)
-
-    def images_end(self, got):
-        return got
 
     def to_owners(self, pieces):
         got = lax.all_to_all(pieces, "fsdp", split_axis=0, concat_axis=0, tiled=True)
@@ -491,7 +511,10 @@
 
     def wide_slots_of(self, feeds):
         return slots_of(
-            [[] if slot is None else feeds[slot[0]] for slot in self.wide_slots], self.owners, FF
+            [[] if slot is None else feeds[slot[0]] for slot in self.wide_slots],
+            self.owners,
+            FF,
+            jnp.int32(0),
         )
 
     def wide_halves(self, got):
@@ -500,11 +523,21 @@
     def wide_whole(self, got):
         return jnp.stack(jnp.split(got, 2, axis=1))
 
-    def square_slots(self, feeds):
-        return slots_of([[] if slot is None else feeds[slot] for slot in self.slots], self.owners, D)
+    def square_slots(self, feeds, rows):
+        return (
+            slots_of(
+                [[] if slot is None else feeds[slot] for slot in self.slots],
+                self.owners,
+                D,
+                self.group_index(),
+            ),
+            rows,
+        )
 
     def square_to_owners(self, slots, beside):
-        return self.to_owners(slots), beside
+        pieces, rows = slots
+        rows = lax.all_gather(rows, ("dp", "fsdp"), axis=0, tiled=True)
+        return self.to_owners(pieces), rows, beside
 
     def to_rows(self, whole):
         blocks = whole.reshape(self.row_shards, -1, whole.shape[1])
@@ -595,25 +628,26 @@
 
         group = modulate[0]()
         left, right = place_halves(ring_of(first), slots)
+        left, right, group = meet(left, right, group)
         ring = ring_of(second, left, right)
-        left, right, group = meet(left, right, group)
         left, right = one_hop(left, right)
+        left, right, ring[0], ring[1], ring[3] = meet(left, right, ring[0], ring[1], ring[3])
+        left, right = other_hop(left, right)
         modulation = modulate[1](group)
-        left, right, modulation, ring[0], ring[1], ring[3] = meet(
-            left, right, modulation, ring[0], ring[1], ring[3]
-        )
-        left, right = other_hop(left, right)
         left, right, ring[2] = meet(left, right, ring[2])
+        second_left, second_right = place_halves(ring, slots)
+        others = self.swap(second_left, "y"), self.swap(second_right, "x")
         done = by_core(left, right)
-        done, ring = meet(done, ring)
-        left, right = place_halves(ring, slots)
-        others = self.swap(left, "y"), self.swap(right, "x")
-        *done, left, right = meet(*done, left, right)
+        done, others, modulation = meet(done, others, modulation)
+        left = place([second_left, others[0]], [y, 1 - y])
+        right = place([second_right, others[1]], [x, 1 - x])
+        left, right = meet(left, right)
+        others = self.swap(left, "x"), self.swap(right, "y")
+        done, left, right = meet(done, left, right)
         results = attend(done, modulation)
-        left_other, right_other, *results = meet(*others, *results)
-        left = place([left, left_other], [y, 1 - y])
-        right = place([right, right_other], [x, 1 - x])
-        left, right = other_hop(left, right)
+        left_other, right_other, results = meet(*others, results)
+        left = place([left, left_other], [x, 1 - x])
+        right = place([right, right_other], [y, 1 - y])
         return done, by_core(left, right), modulation, results
 
     def to_group(self, value):
@@ -635,10 +669,7 @@
         return (keep, self.swap(send, axis))
 
     def last(self, *states):
-        folded = [fold_last(mine, other, lax.axis_index("z")) for mine, other in states]
-        keep, *sends = [
-            parts[0] if len(states) == 1 else jnp.concatenate(parts, axis=0) for parts in zip(*folded)
-        ]
+        keep, *sends = fold_last(states, lax.axis_index("z"))
         got = [self.shift(send, by) for by, send in enumerate(sends, 1)]
         total = keep
         for part in got:
@@ -660,17 +691,12 @@
             slots.append(jnp.where(at_x == x, 0, 1) + jnp.where(at_c == c, 0, 2))
         return slots, [piece, by_x, by_c, by_both]
 
-    def images_begin(self, rows):
-        own = rows.reshape(-1, D)
-        return self.to_owners(jnp.broadcast_to(own[None], (16, *own.shape)))
-
-    def images_end(self, got):
-        c = lax.axis_index("c")
-        return place([got, self.swap(got, "c")], [c, 1 - c]).reshape(-1, 8, D)
-
-    def complete(self, piece):
-        value = self.exchange(piece, "x")
-        c = lax.axis_index("c")
+    def complete_begin(self, piece):
+        return piece, self.swap(piece, "x")
+
+    def complete_end(self, pair):
+        x, c = lax.axis_index("x"), lax.axis_index("c")
+        value = place(list(pair), [x, 1 - x])
         moves = lambda slot: [(part, (x,), (x, slot[part])) for part in range(2) for x in range(2)]
         value = place([value, self.swap(value, "c")], [c, 1 - c], (2, 2), moves)
         return value.reshape(D // 8, -1)
@@ -682,7 +708,7 @@
         halved = []
         for slot in self.wide_slots:
             halved.append([] if slot is None else [feeds[slot[0]][slot[1]]])
-        return slots_of(halved, self.owners, FF // 2)
+        return slots_of(halved, self.owners, FF // 2, self.group_index())
 
     def wide_halves(self, got):
         return got, self.swap(got, "x")
@@ -703,23 +729,45 @@
         whole = place([both, self.swap(both, "c")], [c, 1 - c], (2, 4, 2, 2, 2), moves)
         return whole.reshape(2, D, half)
 
-    def square_slots(self, feeds):
-        return slots_of([[] if slot is None else feeds[slot] for slot in self.slots], self.owners, D)
+    def square_slots(self, feeds, rows):
+        return slots_of(
+            [[] if slot is None else feeds[slot] for slot in self.slots],
+            self.owners,
+            D,
+            self.group_index(),
+            rows.reshape(-1, D),
+        )
 
     def square_to_owners(self, slots, beside):
+        quarter = D // 32
         got = self.to_owners(slots)
         got, beside = meet(got, beside)
-        got = got.reshape(2, 4, 2, D // 32, D)
-        c = lax.axis_index("c")
-
-        def moves(slot):
-            return [
-                (part, (x, z, y), (z, y, x, slot[part]))
-                for part in range(2)
-                for x, z, y in every(2, 4, 2)
-            ]
-
-        return place([got, self.swap(got, "c")], [c, 1 - c], (4, 2, 2, 2), moves).reshape(D, D), beside
+        other = self.swap(got, "c")
+        more = got.shape[1] - quarter
+
+        def body(c_ref, mine_ref, other_ref, whole_ref, rows_ref):
+            c = c_ref[0]
+            for ref, at in ((mine_ref, c), (other_ref, 1 - c)):
+                for chip, (x, z, y) in enumerate(every(2, 4, 2)):
+                    whole_ref[z, y, x, at] = ref[chip, :quarter]
+                    rows_ref[at, chip] = ref[chip, quarter:]
+
+        vmem = pl.BlockSpec(memory_space=pltpu.VMEM)
+        square, gathered = pl.pallas_call(
+            body,
+            out_shape=(
+                jax.ShapeDtypeStruct((4, 2, 2, 2, quarter, D), BF16),
+                jax.ShapeDtypeStruct((2, 16, more, D), BF16),
+            ),
+            in_specs=[pl.BlockSpec(memory_space=pltpu.SMEM), vmem, vmem],
+            out_specs=(vmem, vmem),
+            cost_estimate=pl.CostEstimate(
+                flops=0, bytes_accessed=8 * got.size, transcendentals=0
+            ),
+            compiler_params=pltpu.CompilerParams(vmem_limit_bytes=24 * 1024 * 1024),
+            name="place_square",
+        )(lax.axis_index("c").reshape(1).astype(jnp.int32), got, other)
+        return square.reshape(D, D), gathered.reshape(-1, 8, D), beside
 
     def to_rows(self, whole):
         cols = whole.shape[1]
@@ -1260,14 +1308,11 @@
     here = comm.halves()
     branch_left, back_left, *grads = feed_forward(here, second_flat, branch_flat, left_weight)
     left_sum = comm.begin(*grads)
-    second_flat, left_sum = meet(second_flat, left_sum)
-    left_sum = comm.step(left_sum, "x", 0, 2), comm.step(left_sum, "y", 2, 1)
+    second_flat = tie(second_flat, back_left)
     branch_right, back_right, *grads = feed_forward(here, second_flat, branch_flat, right_weight)
     back_right, left_sum, grads = meet(back_right, left_sum, grads)
+    left_sum = comm.step(left_sum, "x", 0, 2), comm.step(left_sum, "y", 2, 1)
     right_sum = comm.begin(*grads)
-    back_right, left_sum, right_sum = meet(back_right, left_sum, right_sum)
-    left_sum = comm.step(left_sum[0], "y"), comm.step(left_sum[1], "x")
-    right_sum = comm.step(right_sum, "x", 0, 2), comm.step(right_sum, "y", 2, 1)
     block_output, grad_stream, grads, sums = attention_backward(
         lengths,
         shaped(branch_left),
@@ -1287,8 +1332,8 @@
         sine,
     )
     left_sum, right_sum, grads = meet(left_sum, right_sum, grads)
-    left_piece = comm.last(*left_sum)
-    right_sum = comm.step(right_sum[0], "y"), comm.step(right_sum[1], "x")
+    left_sum = comm.step(left_sum[0], "y"), comm.step(left_sum[1], "x")
+    right_sum = comm.step(right_sum, "x", 0, 2), comm.step(right_sum, "y", 2, 1)
     *grads, input_gradient, grad_modulation = projection_backward(
         here,
         grads,
@@ -1302,19 +1347,18 @@
         query_key_weight,
         value_output_weight,
     )
-    left_piece, right_sum, grads, grad_modulation = meet(left_piece, right_sum, grads, grad_modulation)
+    left_sum, right_sum, grads, grad_modulation = meet(left_sum, right_sum, grads, grad_modulation)
     attention_sum = comm.begin(*grads)
-    attention_sum, right_sum = meet(attention_sum, right_sum)
+    right_sum = comm.step(right_sum[0], "y"), comm.step(right_sum[1], "x")
+    left_piece = comm.last(*left_sum)
+    attention_sum, right_sum, left_piece = meet(attention_sum, right_sum, left_piece)
+    right_piece = comm.last(*right_sum)
     first_sum = comm.step(attention_sum, "x", 0, 2)
     second_sum = comm.step(attention_sum, "y", 2, 2)
-    right_piece = comm.last(*right_sum)
-    gathered = comm.images_begin(grad_modulation)
-    right_piece, *kept = meet(right_piece, first_sum[0], second_sum[0])
-    first_sum, second_sum = (kept[0], *first_sum[1:]), (kept[1], *second_sum[1:])
+    first_sum, second_sum, right_piece = meet(first_sum, second_sum, right_piece)
 
     owner = comm.owner_index()
-    own_expand = comm.own_rows(expand_moment)
-    own_shrink = comm.own_rows(shrink_moment.T)
+    own_expand, own_shrink = expand_moment, shrink_moment.T
     wide_feed = [
         [
             (
@@ -1328,29 +1372,31 @@
         for which in range(3)
     ]
     wide = comm.to_owners(comm.wide_slots_of(wide_feed))
-    first_sum, second_sum, gathered = meet(first_sum, second_sum, gathered)
-    gathered = comm.images_end(gathered)
-    active_all = gathered[:, 6]
     first_sum = comm.step(first_sum, "y")
     second_sum = comm.step(second_sum, "x")
-    first_sum, second_sum, wide, gathered = meet(first_sum, second_sum, wide, gathered)
+    first_sum, second_sum, wide = meet(first_sum, second_sum, wide)
     wide = comm.wide_halves(wide)
     attention_piece, wide = meet(comm.last(first_sum, second_sum), wide)
-    wide = comm.wide_whole(wide)
-
-    own_modulation = comm.own_rows(modulation_moment)
-    own_projection = comm.own_rows(projection_moment)
-    own_output = comm.own_rows(output_moment)
+    own_modulation, own_projection, own_output = modulation_moment, projection_moment, output_moment
     square_feed = [[(None, (own_modulation, ((k,), 0, D)))] for k in range(6)]
     for k in range(3):
         square_feed.append(
             [((attention_piece, ((k,), 0, D)), (own_projection, ((k,), 0, D)))]
         )
     square_feed.append([((attention_piece, ((3,), 0, D)), (own_output, ((), 0, D)))])
-    slots, wide = meet(comm.square_slots(square_feed), wide)
+    slots = comm.square_slots(square_feed, grad_modulation)
+    wide = comm.wide_whole(wide)
     active_wide = pick([0 if slot is None else 1 for slot in comm.wide_slots], owner)
     wide_done = newton_schulz(active_wide, wide)
-    square, wide_done = comm.square_to_owners(slots, wide_done)
+    slots, left_piece, right_piece, attention_piece = meet(
+        slots, left_piece, right_piece, attention_piece
+    )
+    pieces = [(left_piece, (i,), half) for i in range(3)]
+    pieces += [(right_piece, (i,), half) for i in range(3)]
+    pieces += [(attention_piece, (i,), D) for i in range(4)]
+    totals_low = comm.complete_begin(pack(pieces))
+    square, gathered, (wide_done, totals_low) = comm.square_to_owners(slots, (wide_done, totals_low))
+    active_all = gathered[:, 6]
     item = pick([-1 if slot is None else slot for slot in comm.slots], owner)
     which = jnp.where((item >= 0) & (item < 6), item, 0)
     right = lax.dynamic_index_in_dim(gathered, which, 1, keepdims=False)
@@ -1362,10 +1408,7 @@
     mine = mine + jnp.pad(square_done, ((0, 0), (0, size - D)))
     back = comm.to_rows(mine)
 
-    pieces = [(left_piece, (i,), half) for i in range(3)]
-    pieces += [(right_piece, (i,), half) for i in range(3)]
-    pieces += [(attention_piece, (i,), D) for i in range(4)]
-    totals_low = comm.complete(pack(pieces)).astype(F32)
+    totals_low = comm.complete_end(totals_low).astype(F32)
     by_unit = [
         jnp.concatenate(
             [totals_low[:, (side * 3 + i) * half : (side * 3 + i + 1) * half] for side in range(2)],

time: 450 us -> 416 us (0.924)
  waiting for transfers between devices: 166 us -> 143 us
  starting transfers between devices: 90.3 us -> 76.3 us
  Pallas kernels: 125 us -> 131 us
  local copies, waits for them, and re-layouts: 39.2 us -> 33.7 us
  other arithmetic: 16.5 us -> 21.1 us
    ppermute x36 -> x35, waiting for transfers between devices: 105 us -> 66.3 us  [swap(): return lax.ppermute(value, axis, [(0, 1), (1, 0)])]
    ppermute x15, waiting for transfers between devices: 17.5 us -> 30.1 us  [shift(): return lax.ppermute(value, 'z', [(i, (i + by) % 4) for i in range(4)])]
    ppermute x15, starting transfers between devices: 31.9 us -> 24.9 us  [shift(): return lax.ppermute(value, 'z', [(i, (i + by) % 4) for i in range(4)])]
    all_to_all x3 -> x2, starting transfers between devices: 16.6 us -> 9.83 us  [to_owners(): lax.all_to_all(pieces, self.chips, split_axis=0, concat_axis=0, tiled=True)]
    all_to_all x3 -> x2, waiting for transfers between devices: 13 us -> 18.3 us  [to_owners(): lax.all_to_all(pieces, self.chips, split_axis=0, concat_axis=0, tiled=True)]
    dynamic_slice x6 -> x1, local copies, waits for them, and re-layouts: 5.03 us -> 0.03 us  [own_rows(): lax.dynamic_slice_in_dim(shard, self.group_index() * (D // 32), D // 32,...]
    ppermute x36 -> x35, starting transfers between devices: 26.6 us -> 29.6 us  [swap(): return lax.ppermute(value, axis, [(0, 1), (1, 0)])]
    pallas_call x18 -> x16, Pallas kernels: 14.9 us -> 16.4 us  [place(): pl.pallas_call(body, out_shape=jax.ShapeDtypeStruct((*lead, *parts[0].sha...]
  transfers between devices with their start and end apart: 57 -> 55, of which waited for: 26 -> 30; matrix products, arithmetic and copies ran while one was open for 6% -> 6% of each run, Pallas kernels for 19% -> 24%
where the time goes in v4:
time: 416 us; the launch traced here: 411 us
  waiting for transfers between devices  143 us (34%)
  Pallas kernels  131 us (31%)
  starting transfers between devices  76.3 us (18%)
  local copies, waits for them, and re-layouts  33.7 us (8%)
  other arithmetic  21.1 us (5%)
    pallas_call x5, Pallas kernels, call(): pl.pallas_call(body, grid=grid, out_shape=outs, in_specs=in_specs, out_sp...  78.1 us
    ppermute x35, waiting for transfers between devices, swap(): return lax.ppermute(value, axis, [(0, 1), (1, 0)])  66.3 us
    ppermute x15, waiting for transfers between devices, shift(): return lax.ppermute(value, 'z', [(i, (i + by) % 4) for i in range(4)])  30.1 us
    ppermute x35, starting transfers between devices, swap(): return lax.ppermute(value, axis, [(0, 1), (1, 0)])  29.6 us
    unnamed x145, local copies, waits for them, and re-layouts  28.2 us
    ppermute x15, starting transfers between devices, shift(): return lax.ppermute(value, 'z', [(i, (i + by) % 4) for i in range(4)])  24.9 us
    all_to_all x2, waiting for transfers between devices, to_owners(): lax.all_to_all(pieces, self.chips, split_axis=0, concat_axis=0, tiled=True)  18.3 us
    pallas_call x2, Pallas kernels, newton_schulz(): pl.pallas_call(body, out_shape=jax.ShapeDtypeStruct((D, width), BF16), in...  16.6 us
  transfers between devices with their start and end apart: 55, of which 30 were waited for; matrix products, arithmetic and copies ran while one was open for 6% of the time, Pallas kernels for 24%

profile of v4, /device:TPU:0, one launch (start us, length us, event | category | flops | bytes accessed | tf_op | source)
XLA Modules:
  0.0 410.7 jit_solution(17203185812383059369)
XLA Ops:
  4.3 3.1 collective-permute-start
  7.4 2.6 collective-permute-start.1
  13.2 3.3 all-to-all-start
  20.7 3.1 all-to-all-done
  27.6 2.1 collective-permute-start.6
  29.7 2.6 collective-permute-done.4.refs_1_
  34.2 3.4 collective-permute-done.5.refs_1_
  38.3 3.6 collective-permute-done.6.refs_3_
  45.3 12.5 %collective-permute-done.7.refs_1_ = bf16[2,4,24,1536]{3,2,1,0:T(8,128)(2,1)S(1)} collective-permute-done((bf16[2,4,24,1536]{3,2,1,0:T(8,128)(2,1)S(1)}, bf16[2,4,24,1536]{3,2,1,0:T(8,128)(2,1)S(1)}, u32[]{:S(2)}, u32[]{:S(2)}) %collective-permute-start.7) | collective-permute-done | bytes 589856 | tf_op jit(solution)/shard_map/ppermute | solution.py:577
  65.9 4.4 %all-to-all-start.1 = ((f32[8,2,6,768]{3,1,2,0:T(2,128)}), f32[8,2,6,768]{3,1,2,0:T(2,128)}, u32[]{:S(2)}, u32[]{:S(2)}) async-start(f32[8,2,6,768]{3,1,2,0:T(2,128)} %copy.53), calls=%async_computation.1 | async-start | bytes 589824 | tf_op jit(solution)/shard_map/all_to_all | solution.py:654
  72.3 9.0 %all-to-all-done.1 = f32[8,2,6,768]{3,1,2,0:T(2,128)} async-done(((f32[8,2,6,768]{3,1,2,0:T(2,128)}), f32[8,2,6,768]{3,1,2,0:T(2,128)}, u32[]{:S(2)}, u32[]{:S(2)}) %all-to-all-start.1) | async-done | bytes 294944 | tf_op jit(solution)/shard_map/all_to_all | solution.py:654
  86.6 2.2 place.23.refs_0_
  93.5 1.8 fusion.4
  96.0 18.4 %attention_forward.1 = (bf16[2,256,768]{2,1,0:T(8,128)(2,1)}, bf16[2,256,768]{2,1,0:T(8,128)(2,1)}, bf16[2,256,768]{2,1,0:T(8,128)(2,1)}, bf16[2,256,768]{2,1,0:...) custom-call(s32[2]{0:T(128)} %mul.66.length_ref, ...), custom_call_target="tpu_custom_call" | custom-call | flops 2818572288 | bytes 21794824 | tf_op jit(solution)/shard_map/attention_forward/pallas_call | solution.py:1082
  114.4 3.0 collective-permute-done.14.refs_1_
  120.6 3.3 collective-permute-done.16.refs_1_
  124.8 2.2 copy-done.12
  127.0 14.4 %feed_forward.2 = (f32[512,768]{1,0:T(8,128)}, f32[512,768]{1,0:T(8,128)}, bf16[3,16,24,1024]{3,2,1,0:T(8,128)(2,1)}, bf16[3,16,24,1024]{3,2,1,0:T(8,128)(2,1)}) custom-call(s32[1]{0:T(128)} %bitcast.here_ref.c_ref, bf16[512,768]{1,0:T(8,128)(2,1)} %bitcast.218, bf16[512,768]{1,0:T(8,128)(2,1)} %bitcast.220, bf16[768,3072]{1,0:T(8,128)(2,1)} %bitcast.172, ...), custom_call_target="tpu_custom_call" | custom-call | flops 7247757312 | bytes 23592964 | tf_op jit(solution)/shard_map/feed_forward/pallas_call | solution.py:1082
  141.5 2.0 place.27
  143.5 2.2 copy-done.11
  145.7 15.0 %feed_forward.3 = (f32[512,768]{1,0:T(8,128)}, f32[512,768]{1,0:T(8,128)}, bf16[3,16,24,1024]{3,2,1,0:T(8,128)(2,1)}, bf16[3,16,24,1024]{3,2,1,0:T(8,128)(2,1)}) custom-call(s32[1]{0:T(128)} %bitcast.here_ref.c_ref, bf16[512,768]{1,0:T(8,128)(2,1)} %bitcast.219, bf16[512,768]{1,0:T(8,128)(2,1)} %bitcast.221, bf16[768,3072]{1,0:T(8,128)(2,1)} %bitcast.169, ...), custom_call_target="tpu_custom_call" | custom-call | flops 7247757312 | bytes 23592964 | tf_op jit(solution)/shard_map/feed_forward/pallas_call | solution.py:1082
  168.0 18.5 %attention_backward.1 = (bf16[2,256,768]{2,1,0:T(8,128)(2,1)}, f32[2,256,768]{2,1,0:T(8,128)}, bf16[4,2,256,768]{3,2,1,0:T(8,128)(2,1)}, f32[2,8,768]{2,1,0:T(8,128)}) custom-call(s32[2]{0:T(128)} %mul.66.length_ref, f32[2,256,768]{2,1,0:T(8,128)} %bitcast.212, f32[2,256,768]{2,1,0:T(8,128)} %bitcast.214, f32[2,256,768]{2,1,0:T(8,128)} %bitcast.213, ...), custom_call_target="tpu_custom_call" | custom-call | flops 1610612736 | bytes 27349000 | tf_op jit(solution)/shard_map/attention_backward/pallas_call | solution.py:1082
  194.6 11.9 %projection_backward.1 = (bf16[4,16,24,768]{3,2,1,0:T(8,128)(2,1)}, bf16[4,16,24,768]{3,2,1,0:T(8,128)(2,1)}, f32[2,256,768]{2,1,0:T(8,128)}, bf16[2,8,768]{2,1,0:T(8,128)(2,1)}) custom-call(s32[1]{0:T(128)} %bitcast.here_ref.c_ref, bf16[4,2,256,768]{3,2,1,0:T(8,128)(2,1)} %get-tuple-element.252.grads_in_ref, ...), custom_call_target="tpu_custom_call" | custom-call | flops 4227858432 | bytes 18201604 | tf_op jit(solution)/shard_map/projection_backward/pallas_call | solution.py:1082
  206.4 6.2 %collective-permute-done.23.refs_3_ = bf16[1,4,24,1024]{3,2,1,0:T(8,128)(2,1)S(1)} collective-permute-done((bf16[1,4,24,1024]{3,2,1,0:T(8,128)(2,1)S(1)}, bf16[1,4,24,1024]{3,2,1,0:T(8,128)(2,1)S(1)}, u32[]{:S(2)}, u32[]{:S(2)}) %collective-permute-start.23) | collective-permute-done | bytes 196640 | tf_op jit(solution)/shard_map/ppermute | solution.py:577
  212.9 1.8 collective-permute-start.30
  214.8 2.0 collective-permute-start.31
  223.0 3.9 collective-permute-done.30
  234.9 2.8 collective-permute-start.36
  237.7 4.0 collective-permute-done.34
  241.7 3.9 collective-permute-done.35
  247.4 5.5 %all-to-all-start.2 = ((bf16[16,24,1024]{2,1,0:T(8,128)(2,1)}), bf16[16,24,1024]{2,1,0:T(8,128)(2,1)S(1)}, u32[]{:S(2)}, u32[]{:S(2)}) async-start(bf16[16,24,1024]{2,1,0:T(8,128)(2,1)} %slots.2), calls=%async_computation.2 | async-start | bytes 1572864 | tf_op jit(solution)/shard_map/all_to_all | solution.py:705
  253.1 2.0 collective-permute-start.38
  256.7 11.7 %collective-permute-done.38.refs_3_ = bf16[2,4,24,768]{3,2,1,0:T(8,128)(2,1)S(1)} collective-permute-done((bf16[2,4,24,768]{3,2,1,0:T(8,128)(2,1)S(1)}, bf16[2,4,24,768]{3,2,1,0:T(8,128)(2,1)S(1)}, u32[]{:S(2)}, u32[]{:S(2)}) %collective-permute-start.38) | collective-permute-done | bytes 294944 | tf_op jit(solution)/shard_map/ppermute | solution.py:577
  268.9 4.1 %all-to-all-done.2.refs_0_ = bf16[16,24,1024]{2,1,0:T(8,128)(2,1)S(1)} async-done(((bf16[16,24,1024]{2,1,0:T(8,128)(2,1)}), bf16[16,24,1024]{2,1,0:T(8,128)(2,1)S(1)}, u32[]{:S(2)}, u32[]{:S(2)}) %all-to-all-start.2) | async-done | bytes 786464 | tf_op jit(solution)/shard_map/all_to_all | solution.py:705
  276.7 1.9 collective-permute-start.41
  278.6 4.8 %collective-permute-done.39 = bf16[4,24,768]{2,1,0:T(8,128)(2,1)S(1)} collective-permute-done((bf16[4,24,768]{2,1,0:T(8,128)(2,1)S(1)}, bf16[4,24,768]{2,1,0:T(8,128)(2,1)S(1)}, u32[]{:S(2)}, u32[]{:S(2)}) %collective-permute-start.39) | collective-permute-done | bytes 147488 | tf_op jit(solution)/shard_map/ppermute | solution.py:580
  283.4 3.6 collective-permute-done.40
  287.8 3.0 collective-permute-done.42.refs_1_
  299.8 4.4 %all-to-all-start.3 = ((bf16[16,40,768]{2,1,0:T(8,128)(2,1)}), bf16[16,40,768]{2,1,0:T(8,128)(2,1)}, u32[]{:S(2)}, u32[]{:S(2)}) async-start(bf16[16,40,768]{2,1,0:T(8,128)(2,1)} %copy-done.13), calls=%async_computation.3 | async-start | bytes 1966080 | tf_op jit(solution)/shard_map/all_to_all | solution.py:705
  307.9 7.1 %collective-permute-done.44.refs_1_ = bf16[24,9216]{1,0:T(8,128)(2,1)} collective-permute-done((bf16[24,9216]{1,0:T(8,128)(2,1)}, bf16[24,9216]{1,0:T(8,128)(2,1)}, u32[]{:S(2)}, u32[]{:S(2)}) %collective-permute-start.44) | collective-permute-done | bytes 442400 | tf_op jit(solution)/shard_map/ppermute | solution.py:577
  315.1 14.1 %all-to-all-done.3.mine_ref = bf16[16,40,768]{2,1,0:T(8,128)(2,1)} async-done(((bf16[16,40,768]{2,1,0:T(8,128)(2,1)}), bf16[16,40,768]{2,1,0:T(8,128)(2,1)}, u32[]{:S(2)}, u32[]{:S(2)}) %all-to-all-start.3) | async-done | bytes 983072 | tf_op jit(solution)/shard_map/all_to_all | solution.py:705
  340.6 16.2 %newton_schulz.3 = bf16[768,768]{1,0:T(8,128)(2,1)S(1)} custom-call(s32[1]{0:T(128)} %bitcast.102.active_ref, bf16[768,768]{1,0:T(8,128)(2,1)S(1)} %bitcast.200, bf16[64,768]{1,0:T(8,128)(2,1)S(1)} %bitcast.198, bf16[64,768]{1,0:T(8,128)(2,1)S(1)} %fusion.13.right_ref), custom_call_target="tpu_custom_call" | custom-call | flops 18119393280 | bytes 2359296 | tf_op jit(solution)/shard_map/newton_schulz/pallas_call | solution.py:142
  358.3 4.3 %all-to-all-start.4 = ((bf16[16,24,1024]{2,1,0:T(8,128)(2,1)}), bf16[16,24,1024]{2,1,0:T(8,128)(2,1)}, u32[]{:S(2)}, u32[]{:S(2)}) async-start(bf16[16,24,1024]{2,1,0:T(8,128)(2,1)} %bitcast.210), calls=%async_computation.4 | async-start | bytes 1572864 | tf_op jit(solution)/shard_map/all_to_all | solution.py:777
  367.9 15.8 %all-to-all-done.4.refs_0_ = bf16[16,24,1024]{2,1,0:T(8,128)(2,1)} async-done(((bf16[16,24,1024]{2,1,0:T(8,128)(2,1)}), bf16[16,24,1024]{2,1,0:T(8,128)(2,1)}, u32[]{:S(2)}, u32[]{:S(2)}) %all-to-all-start.4) | async-done | bytes 786464 | tf_op jit(solution)/shard_map/all_to_all | solution.py:777
  387.8 2.0 multiply_add_fusion.1
  389.7 11.1 %collective-permute-done.47.refs_1_ = bf16[24,13824]{1,0:T(8,128)(2,1)S(1)} collective-permute-done((bf16[24,13824]{1,0:T(8,128)(2,1)S(1)}, bf16[24,13824]{1,0:T(8,128)(2,1)S(1)}, u32[]{:S(2)}, u32[]{:S(2)}) %collective-permute-start.47) | collective-permute-done | bytes 663584 | tf_op jit(solution)/shard_map/ppermute | solution.py:577
  402.4 2.4 multiply_add_fusion
  404.8 5.7 %update.1 = (f32[6,96,768]{2,1,0:T(8,128)}, f32[3,96,768]{2,1,0:T(8,128)}, f32[96,768]{1,0:T(8,128)}, f32[2,96,2048]{2,1,0:T(8,128)}, f32[96,2048]{1,0:T(8,128)}) custom-call(s32[4]{0:T(128)S(1)} %pad_add_fusion.5.slot_ref, bf16[24,13824]{1,0:T(8,128)(2,1)S(1)} %pack.3.refs_0_, bf16[24,13824]{1,0:T(8,128)(2,1)S(1)} %collective-permute-done.47.refs_1_, ...), custom_call_target="tpu_custom_call" | custom-call | bytes 14000000 | tf_op jit(solution)/shard_map/update/pallas_call | solution.py:428
  (298 shorter events, 120.0 us)
Async XLA Ops:
  4.3 14.2 %collective-permute-start = (bf16[24,3072]{1,0:T(8,128)(2,1)S(1)}, bf16[24,3072]{1,0:T(8,128)(2,1)S(1)}, u32[]{:S(2)}, u32[]{:S(2)}) collective-permute-start(bf16[24,3072]{1,0:T(8,128)(2,1)S(1)} %fusion.12.refs_0_), channel_id=1, source_target_pairs={{0,2},{2,4},{4,6},{6,0},{1,3},{3,5},{5,7},{7,1},{8,10},{10,12},{12... | collective-permute-start | bytes 442376 | tf_op jit(solution)/shard_map/ppermute | solution.py:580
  7.4 12.3 %collective-permute-start.1 = (bf16[24,3072]{1,0:T(8,128)(2,1)S(1)}, bf16[24,3072]{1,0:T(8,128)(2,1)S(1)}, u32[]{:S(2)}, u32[]{:S(2)}) collective-permute-start(bf16[24,3072]{1,0:T(8,128)(2,1)S(1)} %fusion.12.refs_0_), channel_id=1, source_target_pairs={{0,4},{2,6},{4,0},{6,2},{1,5},{3,7},{5,1},{7,3},{8,12},{10,14},{12... | collective-permute-start | bytes 442376 | tf_op jit(solution)/shard_map/ppermute | solution.py:580
  10.0 9.7 %collective-permute-start.2 = (bf16[24,3072]{1,0:T(8,128)(2,1)S(1)}, bf16[24,3072]{1,0:T(8,128)(2,1)}, u32[]{:S(2)}, u32[]{:S(2)}) collective-permute-start(bf16[24,3072]{1,0:T(8,128)(2,1)S(1)} %fusion.12.refs_0_), channel_id=1, source_target_pairs={{0,6},{2,0},{4,2},{6,4},{1,7},{3,1},{5,3},{7,5},{8,14},{10,8},{12,... | collective-permute-start | bytes 442376 | tf_op jit(solution)/shard_map/ppermute | solution.py:580
  13.2 10.6 %all-to-all-start = ((bf16[8,2,96]{2,1,0:T(2,128)(2,1)}), bf16[8,2,96]{2,1,0:T(2,128)(2,1)S(1)}, u32[]{:S(2)}, u32[]{:S(2)}) async-start(bf16[8,2,96]{2,1,0:T(2,128)(2,1)} %bitcast.149), calls=%async_computation | async-start | bytes 8192 | tf_op jit(solution)/shard_map/all_to_all | solution.py:654
  25.8 11.7 %collective-permute-start.5 = (bf16[24,6144]{1,0:T(8,128)(2,1)S(1)}, bf16[24,6144]{1,0:T(8,128)(2,1)S(1)}, u32[]{:S(2)}, u32[]{:S(2)}) collective-permute-start(bf16[24,6144]{1,0:T(8,128)(2,1)S(1)} %constant_dynamic-slice_fusion.2.refs_0_), channel_id=1, source_target_pairs={{0,2},{2,4},{4,6},{6,0},{1,3},{3,5},{5,7},{7,1},{8,10},{10,12},{12... | collective-permute-start | bytes 884744 | tf_op jit(solution)/shard_map/ppermute | solution.py:580
  27.6 14.4 %collective-permute-start.6 = (bf16[24,6144]{1,0:T(8,128)(2,1)S(1)}, bf16[24,6144]{1,0:T(8,128)(2,1)S(1)}, u32[]{:S(2)}, u32[]{:S(2)}) collective-permute-start(bf16[24,6144]{1,0:T(8,128)(2,1)S(1)} %constant_dynamic-slice_fusion.2.refs_0_), channel_id=1, source_target_pairs={{0,6},{2,0},{4,2},{6,4},{1,7},{3,1},{5,3},{7,5},{8,14},{10,8},{12,... | collective-permute-start | bytes 884744 | tf_op jit(solution)/shard_map/ppermute | solution.py:580
  42.7 15.1 %collective-permute-start.7 = (bf16[2,4,24,1536]{3,2,1,0:T(8,128)(2,1)S(1)}, bf16[2,4,24,1536]{3,2,1,0:T(8,128)(2,1)S(1)}, u32[]{:S(2)}, u32[]{:S(2)}) collective-permute-start(bf16[2,4,24,1536]{3,2,1,0:T(8,128)(2,1)S(1)} %place.16.refs_0_), channel_id=1, source_target_pairs={{0,16},{16,0},{1,17},{17,1},{2,18},{18,2},{3,19},{19,3},{4,20},{20... | collective-permute-start | bytes 1769480 | tf_op jit(solution)/shard_map/ppermute | solution.py:577
  43.2 14.8 %collective-permute-start.8 = (bf16[2,4,24,1536]{3,2,1,0:T(8,128)(2,1)S(1)}, bf16[2,4,24,1536]{3,2,1,0:T(8,128)(2,1)S(1)}, u32[]{:S(2)}, u32[]{:S(2)}) collective-permute-start(bf16[2,4,24,1536]{3,2,1,0:T(8,128)(2,1)S(1)} %place.17.refs_0_), channel_id=1, source_target_pairs={{0,1},{1,0},{2,3},{3,2},{4,5},{5,4},{6,7},{7,6},{8,9},{9,8},{10,11... | collective-permute-start | bytes 1769480 | tf_op jit(solution)/shard_map/ppermute | solution.py:577
  43.7 15.6 %collective-permute-start.9 = (bf16[24,6144]{1,0:T(8,128)(2,1)S(1)}, bf16[24,6144]{1,0:T(8,128)(2,1)S(1)}, u32[]{:S(2)}, u32[]{:S(2)}) collective-permute-start(bf16[24,6144]{1,0:T(8,128)(2,1)S(1)} %constant_dynamic-slice_fusion.2.refs_0_), channel_id=1, source_target_pairs={{0,4},{2,6},{4,0},{6,2},{1,5},{3,7},{5,1},{7,3},{8,12},{10,14},{12... | collective-permute-start | bytes 884744 | tf_op jit(solution)/shard_map/ppermute | solution.py:580
  59.3 23.6 %collective-permute-start.11 = (bf16[2,2,4,24,1536]{4,3,2,1,0:T(8,128)(2,1)S(1)}, bf16[2,2,4,24,1536]{4,3,2,1,0:T(8,128)(2,1)}, u32[]{:S(2)}, u32[]{:S(2)}) collective-permute-start(bf16[2,2,4,24,1536]{4,3,2,1,0:T(8,128)(2,1)S(1)} %place.19.refs_0_), channel_id=1, source_target_pairs={{0,8},{8,0},{1,9},{9,1},{2,10},{10,2},{3,11},{11,3},{4,12},{12,4},... | collective-permute-start | bytes 3538952 | tf_op jit(solution)/shard_map/ppermute | solution.py:577
  59.4 26.4 %collective-permute-start.10 = (bf16[2,2,4,24,1536]{4,3,2,1,0:T(8,128)(2,1)S(1)}, bf16[2,2,4,24,1536]{4,3,2,1,0:T(8,128)(2,1)S(1)}, u32[]{:S(2)}, u32[]{:S(2)}) collective-permute-start(bf16[2,2,4,24,1536]{4,3,2,1,0:T(8,128)(2,1)S(1)} %place.18.refs_0_), channel_id=1, source_target_pairs={{0,8},{8,0},{1,9},{9,1},{2,10},{10,2},{3,11},{11,3},{4,12},{12,4},... | collective-permute-start | bytes 3538952 | tf_op jit(solution)/shard_map/ppermute | solution.py:577
  62.5 24.0 %collective-permute-start.12 = (bf16[4,24,3072]{2,1,0:T(8,128)(2,1)}, bf16[4,24,3072]{2,1,0:T(8,128)(2,1)}, u32[]{:S(2)}, u32[]{:S(2)}) collective-permute-start(bf16[4,24,3072]{2,1,0:T(8,128)(2,1)} %get-tuple-element.196.refs_0_), channel_id=1, source_target_pairs={{0,1},{1,0},{2,3},{3,2},{4,5},{5,4},{6,7},{7,6},{8,9},{9,8},{10,11... | collective-permute-start | bytes 1769480 | tf_op jit(solution)/shard_map/ppermute | solution.py:577
  63.2 23.4 %collective-permute-start.13 = (bf16[4,24,3072]{2,1,0:T(8,128)(2,1)}, bf16[4,24,3072]{2,1,0:T(8,128)(2,1)}, u32[]{:S(2)}, u32[]{:S(2)}) collective-permute-start(bf16[4,24,3072]{2,1,0:T(8,128)(2,1)} %get-tuple-element.199.refs_0_), channel_id=1, source_target_pairs={{0,16},{16,0},{1,17},{17,1},{2,18},{18,2},{3,19},{19,3},{4,20},{20... | collective-permute-start | bytes 1769480 | tf_op jit(solution)/shard_map/ppermute | solution.py:577
  65.9 15.4 %all-to-all-start.1 = ((f32[8,2,6,768]{3,1,2,0:T(2,128)}), f32[8,2,6,768]{3,1,2,0:T(2,128)}, u32[]{:S(2)}, u32[]{:S(2)}) async-start(f32[8,2,6,768]{3,1,2,0:T(2,128)} %copy.53), calls=%async_computation.1 | async-start | bytes 589824 | tf_op jit(solution)/shard_map/all_to_all | solution.py:654
  90.2 27.2 %collective-permute-start.14 = (bf16[2,4,24,3072]{3,2,1,0:T(8,128)(2,1)S(1)}, bf16[2,4,24,3072]{3,2,1,0:T(8,128)(2,1)S(1)}, u32[]{:S(2)}, u32[]{:S(2)}) collective-permute-start(bf16[2,4,24,3072]{3,2,1,0:T(8,128)(2,1)S(1)} %place.22.refs_0_), channel_id=1, source_target_pairs={{0,16},{16,0},{1,17},{17,1},{2,18},{18,2},{3,19},{19,3},{4,20},{20... | collective-permute-start | bytes 3538952 | tf_op jit(solution)/shard_map/ppermute | solution.py:577
  91.8 26.8 %collective-permute-start.15 = (bf16[2,4,24,3072]{3,2,1,0:T(8,128)(2,1)S(1)}, bf16[2,4,24,3072]{3,2,1,0:T(8,128)(2,1)S(1)}, u32[]{:S(2)}, u32[]{:S(2)}) collective-permute-start(bf16[2,4,24,3072]{3,2,1,0:T(8,128)(2,1)S(1)} %place.23.refs_0_), channel_id=1, source_target_pairs={{0,1},{1,0},{2,3},{3,2},{4,5},{5,4},{6,7},{7,6},{8,9},{9,8},{10,11... | collective-permute-start | bytes 3538952 | tf_op jit(solution)/shard_map/ppermute | solution.py:577
  120.1 21.4 %collective-permute-start.17 = (bf16[2,2,4,24,3072]{4,3,2,1,0:T(8,128)(2,1)S(1)}, bf16[2,2,4,24,3072]{4,3,2,1,0:T(8,128)(2,1)}, u32[]{:S(2)}, u32[]{:S(2)}) collective-permute-start(bf16[2,2,4,24,3072]{4,3,2,1,0:T(8,128)(2,1)S(1)} %place.26.refs_0_), channel_id=1, source_target_pairs={{0,8},{8,0},{1,9},{9,1},{2,10},{10,2},{3,11},{11,3},{4,12},{12,4},... | collective-permute-start | bytes 7077896 | tf_op jit(solution)/shard_map/ppermute | solution.py:577
  141.3 19.4 %collective-permute-start.18 = (bf16[3,16,24,1024]{3,2,1,0:T(8,128)(2,1)}, bf16[3,16,24,1024]{3,2,1,0:T(8,128)(2,1)S(1)}, u32[]{:S(2)}, u32[]{:S(2)}) collective-permute-start(bf16[3,16,24,1024]{3,2,1,0:T(8,128)(2,1)} %get-tuple-element.232), channel_id=1, source_target_pairs={{0,8},{8,0},{1,9},{9,1},{2,10},{10,2},{3,11},{11,3},{4,12},{12,4},... | collective-permute-start | bytes 7077896 | tf_op jit(solution)/shard_map/ppermute | solution.py:577
  162.2 25.9 %collective-permute-start.21 = (bf16[3,16,24,1024]{3,2,1,0:T(8,128)(2,1)}, bf16[3,16,24,1024]{3,2,1,0:T(8,128)(2,1)S(1)}, u32[]{:S(2)}, u32[]{:S(2)}) collective-permute-start(bf16[3,16,24,1024]{3,2,1,0:T(8,128)(2,1)} %get-tuple-element.250), channel_id=1, source_target_pairs={{0,8},{8,0},{1,9},{9,1},{2,10},{10,2},{3,11},{11,3},{4,12},{12,4},... | collective-permute-start | bytes 7077896 | tf_op jit(solution)/shard_map/ppermute | solution.py:577
  165.3 22.0 %collective-permute-start.19 = (bf16[2,8,24,1024]{3,2,1,0:T(8,128)(2,1)}, bf16[2,8,24,1024]{3,2,1,0:T(8,128)(2,1)S(1)}, u32[]{:S(2)}, u32[]{:S(2)}) collective-permute-start(bf16[2,8,24,1024]{3,2,1,0:T(8,128)(2,1)} %bitcast.34), channel_id=1, source_target_pairs={{0,16},{16,0},{1,17},{17,1},{2,18},{18,2},{3,19},{19,3},{4,20},{20... | collective-permute-start | bytes 2359304 | tf_op jit(solution)/shard_map/ppermute | solution.py:577
  167.4 19.1 %collective-permute-start.20 = (bf16[1,8,24,1024]{3,2,1,0:T(8,128)(2,1)}, bf16[1,8,24,1024]{3,2,1,0:T(8,128)(2,1)S(1)}, u32[]{:S(2)}, u32[]{:S(2)}) collective-permute-start(bf16[1,8,24,1024]{3,2,1,0:T(8,128)(2,1)} %bitcast.38), channel_id=1, source_target_pairs={{0,1},{1,0},{2,3},{3,2},{4,5},{5,4},{6,7},{7,6},{8,9},{9,8},{10,11... | collective-permute-start | bytes 1179656 | tf_op jit(solution)/shard_map/ppermute | solution.py:577
  189.2 23.5 %collective-permute-start.24 = (bf16[2,8,24,1024]{3,2,1,0:T(8,128)(2,1)}, bf16[2,8,24,1024]{3,2,1,0:T(8,128)(2,1)}, u32[]{:S(2)}, u32[]{:S(2)}) collective-permute-start(bf16[2,8,24,1024]{3,2,1,0:T(8,128)(2,1)} %bitcast.52), channel_id=1, source_target_pairs={{0,16},{16,0},{1,17},{17,1},{2,18},{18,2},{3,19},{19,3},{4,20},{20... | collective-permute-start | bytes 2359304 | tf_op jit(solution)/shard_map/ppermute | solution.py:577
  191.5 21.1 %collective-permute-start.25 = (bf16[1,8,24,1024]{3,2,1,0:T(8,128)(2,1)}, bf16[1,8,24,1024]{3,2,1,0:T(8,128)(2,1)S(1)}, u32[]{:S(2)}, u32[]{:S(2)}) collective-permute-start(bf16[1,8,24,1024]{3,2,1,0:T(8,128)(2,1)} %bitcast.56), channel_id=1, source_target_pairs={{0,1},{1,0},{2,3},{3,2},{4,5},{5,4},{6,7},{7,6},{8,9},{9,8},{10,11... | collective-permute-start | bytes 1179656 | tf_op jit(solution)/shard_map/ppermute | solution.py:577
  193.1 19.5 %collective-permute-start.23 = (bf16[1,4,24,1024]{3,2,1,0:T(8,128)(2,1)S(1)}, bf16[1,4,24,1024]{3,2,1,0:T(8,128)(2,1)S(1)}, u32[]{:S(2)}, u32[]{:S(2)}) collective-permute-start(bf16[1,4,24,1024]{3,2,1,0:T(8,128)(2,1)S(1)} %bitcast.207), channel_id=1, source_target_pairs={{0,16},{16,0},{1,17},{17,1},{2,18},{18,2},{3,19},{19,3},{4,20},{20... | collective-permute-start | bytes 589832 | tf_op jit(solution)/shard_map/ppermute | solution.py:577
  193.9 18.7 %collective-permute-start.22 = (bf16[2,4,24,1024]{3,2,1,0:T(8,128)(2,1)S(1)}, bf16[2,4,24,1024]{3,2,1,0:T(8,128)(2,1)S(1)}, u32[]{:S(2)}, u32[]{:S(2)}) collective-permute-start(bf16[2,4,24,1024]{3,2,1,0:T(8,128)(2,1)S(1)} %bitcast.204), channel_id=1, source_target_pairs={{0,1},{1,0},{2,3},{3,2},{4,5},{5,4},{6,7},{7,6},{8,9},{9,8},{10,11... | collective-permute-start | bytes 1179656 | tf_op jit(solution)/shard_map/ppermute | solution.py:577
  212.6 16.5 %collective-permute-start.26 = (bf16[4,16,24,768]{3,2,1,0:T(8,128)(2,1)}, bf16[4,16,24,768]{3,2,1,0:T(8,128)(2,1)S(1)}, u32[]{:S(2)}, u32[]{:S(2)}) collective-permute-start(bf16[4,16,24,768]{3,2,1,0:T(8,128)(2,1)} %get-tuple-element.276), channel_id=1, source_target_pairs={{0,8},{8,0},{1,9},{9,1},{2,10},{10,2},{3,11},{11,3},{4,12},{12,4},... | collective-permute-start | bytes 7077896 | tf_op jit(solution)/shard_map/ppermute | solution.py:577
  212.9 8.6 %collective-permute-start.29 = (bf16[3,24,1024]{2,1,0:T(8,128)(2,1)S(1)}, bf16[3,24,1024]{2,1,0:T(8,128)(2,1)S(1)}, u32[]{:S(2)}, u32[]{:S(2)}) collective-permute-start(bf16[3,24,1024]{2,1,0:T(8,128)(2,1)S(1)} %get-tuple-element.290), channel_id=1, source_target_pairs={{0,2},{2,4},{4,6},{6,0},{1,3},{3,5},{5,7},{7,1},{8,10},{10,12},{12... | collective-permute-start | bytes 442376 | tf_op jit(solution)/shard_map/ppermute | solution.py:580
  212.9 14.0 %collective-permute-start.30 = (bf16[3,24,1024]{2,1,0:T(8,128)(2,1)S(1)}, bf16[3,24,1024]{2,1,0:T(8,128)(2,1)S(1)}, u32[]{:S(2)}, u32[]{:S(2)}) collective-permute-start(bf16[3,24,1024]{2,1,0:T(8,128)(2,1)S(1)} %get-tuple-element.291), channel_id=1, source_target_pairs={{0,4},{2,6},{4,0},{6,2},{1,5},{3,7},{5,1},{7,3},{8,12},{10,14},{12... | collective-permute-start | bytes 442376 | tf_op jit(solution)/shard_map/ppermute | solution.py:580
  214.8 12.2 %collective-permute-start.31 = (bf16[3,24,1024]{2,1,0:T(8,128)(2,1)S(1)}, bf16[3,24,1024]{2,1,0:T(8,128)(2,1)S(1)}, u32[]{:S(2)}, u32[]{:S(2)}) collective-permute-start(bf16[3,24,1024]{2,1,0:T(8,128)(2,1)S(1)} %get-tuple-element.292), channel_id=1, source_target_pairs={{0,6},{2,0},{4,2},{6,4},{1,7},{3,1},{5,3},{7,5},{8,14},{10,8},{12,... | collective-permute-start | bytes 442376 | tf_op jit(solution)/shard_map/ppermute | solution.py:580
  218.1 11.0 %collective-permute-start.27 = (bf16[2,4,24,1024]{3,2,1,0:T(8,128)(2,1)S(1)}, bf16[2,4,24,1024]{3,2,1,0:T(8,128)(2,1)S(1)}, u32[]{:S(2)}, u32[]{:S(2)}) collective-permute-start(bf16[2,4,24,1024]{3,2,1,0:T(8,128)(2,1)S(1)} %bitcast.203), channel_id=1, source_target_pairs={{0,1},{1,0},{2,3},{3,2},{4,5},{5,4},{6,7},{7,6},{8,9},{9,8},{10,11... | collective-permute-start | bytes 1179656 | tf_op jit(solution)/shard_map/ppermute | solution.py:577
  229.5 16.2 %collective-permute-start.33 = (bf16[2,8,24,768]{3,2,1,0:T(8,128)(2,1)S(1)}, bf16[2,8,24,768]{3,2,1,0:T(8,128)(2,1)S(1)}, u32[]{:S(2)}, u32[]{:S(2)}) collective-permute-start(bf16[2,8,24,768]{3,2,1,0:T(8,128)(2,1)S(1)} %bitcast.201), channel_id=1, source_target_pairs={{0,1},{1,0},{2,3},{3,2},{4,5},{5,4},{6,7},{7,6},{8,9},{9,8},{10,11... | collective-permute-start | bytes 1769480 | tf_op jit(solution)/shard_map/ppermute | solution.py:577
  231.3 14.3 %collective-permute-start.32 = (bf16[2,8,24,768]{3,2,1,0:T(8,128)(2,1)S(1)}, bf16[2,8,24,768]{3,2,1,0:T(8,128)(2,1)S(1)}, u32[]{:S(2)}, u32[]{:S(2)}) collective-permute-start(bf16[2,8,24,768]{3,2,1,0:T(8,128)(2,1)S(1)} %bitcast.202), channel_id=1, source_target_pairs={{0,16},{16,0},{1,17},{17,1},{2,18},{18,2},{3,19},{19,3},{4,20},{20... | collective-permute-start | bytes 1769480 | tf_op jit(solution)/shard_map/ppermute | solution.py:577
  233.0 8.7 %collective-permute-start.34 = (bf16[3,24,1024]{2,1,0:T(8,128)(2,1)S(1)}, bf16[3,24,1024]{2,1,0:T(8,128)(2,1)S(1)}, u32[]{:S(2)}, u32[]{:S(2)}) collective-permute-start(bf16[3,24,1024]{2,1,0:T(8,128)(2,1)S(1)} %get-tuple-element.304), channel_id=1, source_target_pairs={{0,2},{2,4},{4,6},{6,0},{1,3},{3,5},{5,7},{7,1},{8,10},{10,12},{12... | collective-permute-start | bytes 442376 | tf_op jit(solution)/shard_map/ppermute | solution.py:580
  234.3 11.3 %collective-permute-start.35 = (bf16[3,24,1024]{2,1,0:T(8,128)(2,1)S(1)}, bf16[3,24,1024]{2,1,0:T(8,128)(2,1)S(1)}, u32[]{:S(2)}, u32[]{:S(2)}) collective-permute-start(bf16[3,24,1024]{2,1,0:T(8,128)(2,1)S(1)} %get-tuple-element.305), channel_id=1, source_target_pairs={{0,4},{2,6},{4,0},{6,2},{1,5},{3,7},{5,1},{7,3},{8,12},{10,14},{12... | collective-permute-start | bytes 442376 | tf_op jit(solution)/shard_map/ppermute | solution.py:580
  234.9 10.7 %collective-permute-start.36 = (bf16[3,24,1024]{2,1,0:T(8,128)(2,1)S(1)}, bf16[3,24,1024]{2,1,0:T(8,128)(2,1)S(1)}, u32[]{:S(2)}, u32[]{:S(2)}) collective-permute-start(bf16[3,24,1024]{2,1,0:T(8,128)(2,1)S(1)} %get-tuple-element.306), channel_id=1, source_target_pairs={{0,6},{2,0},{4,2},{6,4},{1,7},{3,1},{5,3},{7,5},{8,14},{10,8},{12,... | collective-permute-start | bytes 442376 | tf_op jit(solution)/shard_map/ppermute | solution.py:580
  247.4 25.7 %all-to-all-start.2 = ((bf16[16,24,1024]{2,1,0:T(8,128)(2,1)}), bf16[16,24,1024]{2,1,0:T(8,128)(2,1)S(1)}, u32[]{:S(2)}, u32[]{:S(2)}) async-start(bf16[16,24,1024]{2,1,0:T(8,128)(2,1)} %slots.2), calls=%async_computation.2 | async-start | bytes 1572864 | tf_op jit(solution)/shard_map/all_to_all | solution.py:705
  253.1 15.4 %collective-permute-start.38 = (bf16[2,4,24,768]{3,2,1,0:T(8,128)(2,1)S(1)}, bf16[2,4,24,768]{3,2,1,0:T(8,128)(2,1)S(1)}, u32[]{:S(2)}, u32[]{:S(2)}) collective-permute-start(bf16[2,4,24,768]{3,2,1,0:T(8,128)(2,1)S(1)} %bitcast.205), channel_id=1, source_target_pairs={{0,16},{16,0},{1,17},{17,1},{2,18},{18,2},{3,19},{19,3},{4,20},{20... | collective-permute-start | bytes 884744 | tf_op jit(solution)/shard_map/ppermute | solution.py:577
  255.2 13.7 %collective-permute-start.37 = (bf16[2,4,24,768]{3,2,1,0:T(8,128)(2,1)S(1)}, bf16[2,4,24,768]{3,2,1,0:T(8,128)(2,1)S(1)}, u32[]{:S(2)}, u32[]{:S(2)}) collective-permute-start(bf16[2,4,24,768]{3,2,1,0:T(8,128)(2,1)S(1)} %bitcast.206), channel_id=1, source_target_pairs={{0,1},{1,0},{2,3},{3,2},{4,5},{5,4},{6,7},{7,6},{8,9},{9,8},{10,11... | collective-permute-start | bytes 884744 | tf_op jit(solution)/shard_map/ppermute | solution.py:577
  273.1 17.7 %collective-permute-start.42 = (bf16[16,24,1024]{2,1,0:T(8,128)(2,1)S(1)}, bf16[16,24,1024]{2,1,0:T(8,128)(2,1)S(1)}, u32[]{:S(2)}, u32[]{:S(2)}) collective-permute-start(bf16[16,24,1024]{2,1,0:T(8,128)(2,1)S(1)} %all-to-all-done.2.refs_0_), channel_id=1, source_target_pairs={{0,16},{16,0},{1,17},{17,1},{2,18},{18,2},{3,19},{19,3},{4,20},{20... | collective-permute-start | bytes 2359304 | tf_op jit(solution)/shard_map/ppermute | solution.py:577
  274.7 8.7 %collective-permute-start.39 = (bf16[4,24,768]{2,1,0:T(8,128)(2,1)S(1)}, bf16[4,24,768]{2,1,0:T(8,128)(2,1)S(1)}, u32[]{:S(2)}, u32[]{:S(2)}) collective-permute-start(bf16[4,24,768]{2,1,0:T(8,128)(2,1)S(1)} %get-tuple-element.322), channel_id=1, source_target_pairs={{0,2},{2,4},{4,6},{6,0},{1,3},{3,5},{5,7},{7,1},{8,10},{10,12},{12... | collective-permute-start | bytes 442376 | tf_op jit(solution)/shard_map/ppermute | solution.py:580
  275.9 11.1 %collective-permute-start.40 = (bf16[4,24,768]{2,1,0:T(8,128)(2,1)S(1)}, bf16[4,24,768]{2,1,0:T(8,128)(2,1)S(1)}, u32[]{:S(2)}, u32[]{:S(2)}) collective-permute-start(bf16[4,24,768]{2,1,0:T(8,128)(2,1)S(1)} %get-tuple-element.323), channel_id=1, source_target_pairs={{0,4},{2,6},{4,0},{6,2},{1,5},{3,7},{5,1},{7,3},{8,12},{10,14},{12... | collective-permute-start | bytes 442376 | tf_op jit(solution)/shard_map/ppermute | solution.py:580
  276.7 10.3 %collective-permute-start.41 = (bf16[4,24,768]{2,1,0:T(8,128)(2,1)S(1)}, bf16[4,24,768]{2,1,0:T(8,128)(2,1)S(1)}, u32[]{:S(2)}, u32[]{:S(2)}) collective-permute-start(bf16[4,24,768]{2,1,0:T(8,128)(2,1)S(1)} %get-tuple-element.324), channel_id=1, source_target_pairs={{0,6},{2,0},{4,2},{6,4},{1,7},{3,1},{5,3},{7,5},{8,14},{10,8},{12,... | collective-permute-start | bytes 442376 | tf_op jit(solution)/shard_map/ppermute | solution.py:580
  292.6 11.6 %collective-permute-start.43 = (bf16[2,2,4,2,24,1024]{5,4,3,2,1,0:T(8,128)(2,1)S(1)}, bf16[2,2,4,2,24,1024]{5,4,3,2,1,0:T(8,128)(2,1)}, u32[]{:S(2)}, u32[]{:S(2)}) collective-permute-start(bf16[2,2,4,2,24,1024]{5,4,3,2,1,0:T(8,128)(2,1)S(1)} %bitcast.167), channel_id=1, source_target_pairs={{0,8},{8,0},{1,9},{9,1},{2,10},{10,2},{3,11},{11,3},{4,12},{12,4},... | collective-permute-start | bytes 4718600 | tf_op jit(solution)/shard_map/ppermute | solution.py:577
  298.0 17.0 %collective-permute-start.44 = (bf16[24,9216]{1,0:T(8,128)(2,1)}, bf16[24,9216]{1,0:T(8,128)(2,1)}, u32[]{:S(2)}, u32[]{:S(2)}) collective-permute-start(bf16[24,9216]{1,0:T(8,128)(2,1)} %pack.2.refs_0_), channel_id=1, source_target_pairs={{0,16},{16,0},{1,17},{17,1},{2,18},{18,2},{3,19},{19,3},{4,20},{20... | collective-permute-start | bytes 1327112 | tf_op jit(solution)/shard_map/ppermute | solution.py:577
  299.8 29.4 %all-to-all-start.3 = ((bf16[16,40,768]{2,1,0:T(8,128)(2,1)}), bf16[16,40,768]{2,1,0:T(8,128)(2,1)}, u32[]{:S(2)}, u32[]{:S(2)}) async-start(bf16[16,40,768]{2,1,0:T(8,128)(2,1)} %copy-done.13), calls=%async_computation.3 | async-start | bytes 1966080 | tf_op jit(solution)/shard_map/all_to_all | solution.py:705
  358.3 25.4 %all-to-all-start.4 = ((bf16[16,24,1024]{2,1,0:T(8,128)(2,1)}), bf16[16,24,1024]{2,1,0:T(8,128)(2,1)}, u32[]{:S(2)}, u32[]{:S(2)}) async-start(bf16[16,24,1024]{2,1,0:T(8,128)(2,1)} %bitcast.210), calls=%async_computation.4 | async-start | bytes 1572864 | tf_op jit(solution)/shard_map/all_to_all | solution.py:777
  385.0 15.9 %collective-permute-start.47 = (bf16[24,13824]{1,0:T(8,128)(2,1)S(1)}, bf16[24,13824]{1,0:T(8,128)(2,1)S(1)}, u32[]{:S(2)}, u32[]{:S(2)}) collective-permute-start(bf16[24,13824]{1,0:T(8,128)(2,1)S(1)} %pack.3.refs_0_), channel_id=1, source_target_pairs={{0,16},{16,0},{1,17},{17,1},{2,18},{18,2},{3,19},{19,3},{4,20},{20... | collective-permute-start | bytes 1990664 | tf_op jit(solution)/shard_map/ppermute | solution.py:577
  389.7 15.0 %collective-permute-start.48 = (bf16[24,13824]{1,0:T(8,128)(2,1)S(1)}, bf16[24,13824]{1,0:T(8,128)(2,1)S(1)}, u32[]{:S(2)}, u32[]{:S(2)}) collective-permute-start(bf16[24,13824]{1,0:T(8,128)(2,1)S(1)} %pack.3.refs_0_), channel_id=1, source_target_pairs={{0,8},{8,0},{1,9},{9,1},{2,10},{10,2},{3,11},{11,3},{4,12},{12,4},... | collective-permute-start | bytes 1990664 | tf_op jit(solution)/shard_map/ppermute | solution.py:577
  (76 other events, 416.5 us)

commit v5 on v4

--- a/solution.py
+++ b/solution.py
@@ -191,7 +191,13 @@
         compiler_params=pltpu.CompilerParams(vmem_limit_bytes=24 * 1024 * 1024),
         cost_estimate=pl.CostEstimate(flops=0, bytes_accessed=size, transcendentals=0),
         name="fold",
-    )(here.reshape(1).astype(jnp.int32), mine.reshape(shape), other.reshape(shape))
+    )(
+        here.reshape(1).astype(jnp.int32),
+        pltpu.with_memory_space_constraint(mine.reshape(shape), pltpu.HBM)
+        if before * after > 4
+        else mine.reshape(shape),
+        other.reshape(shape),
+    )
     flat = lambda v: v.reshape(count, before * after, rows, cols)
     return flat(keep), flat(send)
 
@@ -347,7 +353,16 @@
         ),
         compiler_params=pltpu.CompilerParams(vmem_limit_bytes=24 * 1024 * 1024),
         name="slots",
-    )(quarter.reshape(1).astype(jnp.int32), *arrays, *([extra] if more else []))
+    )(
+        quarter.reshape(1).astype(jnp.int32),
+        *[
+            array
+            if array.shape[-2] == rows
+            else pltpu.with_memory_space_constraint(array, pltpu.HBM)
+            for array in arrays
+        ],
+        *([extra] if more else []),
+    )
 
 
 def pack(parts):
@@ -488,6 +503,12 @@
     def step(self, state, axis, start=0, count=None):
         return (state[0][start : start + (count or state[0].shape[0])],)
 
+    def last_begin(self, *states):
+        return states
+
+    def last_end(self, states):
+        return self.last(*states)
+
     def last(self, *states):
         value = jnp.concatenate([state[0] for state in states], axis=0)
         shard = lax.psum_scatter(value, "fsdp", scatter_dimension=1, tiled=True)
@@ -669,11 +690,15 @@
         return (keep, self.swap(send, axis))
 
     def last(self, *states):
-        keep, *sends = fold_last(states, lax.axis_index("z"))
-        got = [self.shift(send, by) for by, send in enumerate(sends, 1)]
-        total = keep
-        for part in got:
-            total = total + part.astype(F32)
+        return self.last_end(self.last_begin(*states))
+
+    def last_begin(self, *states):
+        return fold_last(states, lax.axis_index("z"))
+
+    def last_end(self, folded):
+        total, *sends = folded
+        for by, send in enumerate(sends, 1):
+            total = total + self.shift(send, by).astype(F32)
         return total
 
     def own_rows(self, shard, dim=-2):
@@ -807,7 +832,7 @@
 
 
 def pair_at(pair):
-    return slice(pair * 2 * HDIM, (pair + 1) * 2 * HDIM)
+    return pl.ds(pl.multiple_of(pair * 2 * HDIM, 2 * HDIM), 2 * HDIM)
 
 
 def attention_forward_kernel(
@@ -843,10 +868,12 @@
     value_ref[0] = dot(first, value_output_ref[:, :D]).astype(BF16)
     cosine, sine = cosine_ref[0], sine_ref[0]
     keep = lanes((positions, positions), 1) < length
-    for pair in range(HEADS // 2):
+
+    @pl.loop(0, HEADS // 2)
+    def _(pair):
         at = pair_at(pair)
         query = dot(first, query_key_ref[:, at])
-        key = dot(first, query_key_ref[:, D + pair * 128 : D + (pair + 1) * 128])
+        key = dot(first, query_key_ref[:, pair_at(HEADS // 2 + pair)])
         query = (query * cosine + rotate_pair(query) * sine).astype(BF16)
         key = (key * cosine + rotate_pair(key) * sine).astype(BF16)
         query_ref[0, :, at] = query
@@ -863,6 +890,7 @@
         attended_ref[0, :, at] = dot(
             jnp.concatenate(low, axis=1), jnp.concatenate(values, axis=0)
         ).astype(BF16)
+
     attention = dot(attended_ref[0], value_output_ref[:, D:])
     attention_ref[0] = attention
     middle = stream + row(2) * attention
@@ -971,7 +999,9 @@
     grads_ref[3, 0] = grad_attention
     attended_grad[...] = dot(grad_attention, value_output_ref[:, D:], NT).astype(BF16)
     cosine, sine = cosine_ref[0], sine_ref[0]
-    for pair in range(HEADS // 2):
+
+    @pl.loop(0, HEADS // 2)
+    def _(pair):
         at = pair_at(pair)
         query, key, value = query_ref[0, :, at], key_ref[0, :, at], value_ref[0, :, at]
         attended = two_heads(attended_grad[:, at])
@@ -1129,6 +1159,7 @@
     units = weight.shape[1] // 3
     tile = 256
     steps = units // tile
+    weight = pltpu.with_memory_space_constraint(weight, pltpu.HBM)
     ins = (here.reshape(1).astype(jnp.int32), second, branch, weight, weight, weight)
     in_specs = [pl.BlockSpec(memory_space=pltpu.SMEM), whole(second), whole(branch)] + [
         pl.BlockSpec((D, tile), lambda t, which=which: (0, which * steps + t)) for which in range(3)
@@ -1352,7 +1383,8 @@
     right_sum = comm.step(right_sum[0], "y"), comm.step(right_sum[1], "x")
     left_piece = comm.last(*left_sum)
     attention_sum, right_sum, left_piece = meet(attention_sum, right_sum, left_piece)
-    right_piece = comm.last(*right_sum)
+    right_begun, attention_sum = meet(comm.last_begin(*right_sum), attention_sum)
+    right_piece = comm.last_end(right_begun)
     first_sum = comm.step(attention_sum, "x", 0, 2)
     second_sum = comm.step(attention_sum, "y", 2, 2)
     first_sum, second_sum, right_piece = meet(first_sum, second_sum, right_piece)

time: 416 us -> 407 us (0.978)
  local copies, waits for them, and re-layouts: 33.7 us -> 23.5 us
  Pallas kernels: 131 us -> 138 us
  waiting for transfers between devices: 143 us -> 137 us
    unnamed x145 -> x99, local copies, waits for them, and re-layouts: 28.2 us -> 18 us
    pallas_call x12, Pallas kernels: 6.54 us -> 13.3 us  [fold(): pl.pallas_call(body, grid=(count,), out_shape=(out, out), in_specs=[pl.Bl...]
    ppermute x35, waiting for transfers between devices: 66.3 us -> 61 us  [swap(): return lax.ppermute(value, axis, [(0, 1), (1, 0)])]
  transfers between devices with their start and end apart: 55 -> 55, of which waited for: 30 -> 30; matrix products, arithmetic and copies ran while one was open for 6% -> 6% of each run, Pallas kernels for 24% -> 26%
where the time goes in v5:
time: 407 us; the launch traced here: 402 us
  Pallas kernels  138 us (34%)
  waiting for transfers between devices  137 us (34%)
  starting transfers between devices  76.2 us (19%)
  local copies, waits for them, and re-layouts  23.5 us (6%)
  other arithmetic  20.4 us (5%)
    pallas_call x5, Pallas kernels, call(): pl.pallas_call(body, grid=grid, out_shape=outs, in_specs=in_specs, out_sp...  77.9 us
    ppermute x35, waiting for transfers between devices, swap(): return lax.ppermute(value, axis, [(0, 1), (1, 0)])  61 us
    ppermute x15, waiting for transfers between devices, shift(): return lax.ppermute(value, 'z', [(i, (i + by) % 4) for i in range(4)])  30.8 us
    ppermute x35, starting transfers between devices, swap(): return lax.ppermute(value, axis, [(0, 1), (1, 0)])  29.6 us
    ppermute x15, starting transfers between devices, shift(): return lax.ppermute(value, 'z', [(i, (i + by) % 4) for i in range(4)])  24.9 us
    unnamed x99, local copies, waits for them, and re-layouts  18 us
    all_to_all x2, waiting for transfers between devices, to_owners(): lax.all_to_all(pieces, self.chips, split_axis=0, concat_axis=0, tiled=True)  17.4 us
    pallas_call x2, Pallas kernels, newton_schulz(): pl.pallas_call(body, out_shape=jax.ShapeDtypeStruct((D, width), BF16), in...  16.4 us
  transfers between devices with their start and end apart: 55, of which 30 were waited for; matrix products, arithmetic and copies ran while one was open for 6% of the time, Pallas kernels for 26%

profile of v5, /device:TPU:0, one launch (start us, length us, event | category | flops | bytes accessed | tf_op | source)
XLA Modules:
  0.0 401.7 jit_solution(1442674917975995156)
XLA Ops:
  4.3 3.1 collective-permute-start
  7.4 2.6 collective-permute-start.1
  13.2 3.3 all-to-all-start
  20.7 3.1 all-to-all-done
  27.6 2.1 collective-permute-start.6
  29.7 2.6 collective-permute-done.4.refs_1_
  34.2 3.4 collective-permute-done.5.refs_1_
  38.3 3.6 collective-permute-done.6.refs_3_
  45.3 12.5 %collective-permute-done.7.refs_1_ = bf16[2,4,24,1536]{3,2,1,0:T(8,128)(2,1)S(1)} collective-permute-done((bf16[2,4,24,1536]{3,2,1,0:T(8,128)(2,1)S(1)}, bf16[2,4,24,1536]{3,2,1,0:T(8,128)(2,1)S(1)}, u32[]{:S(2)}, u32[]{:S(2)}) %collective-permute-start.7) | collective-permute-done | bytes 589856 | tf_op jit(solution)/shard_map/ppermute | solution.py:598
  65.9 4.2 %all-to-all-start.1 = ((f32[8,2,6,768]{3,1,2,0:T(2,128)}), f32[8,2,6,768]{3,1,2,0:T(2,128)}, u32[]{:S(2)}, u32[]{:S(2)}) async-start(f32[8,2,6,768]{3,1,2,0:T(2,128)} %copy.53), calls=%async_computation.1 | async-start | bytes 589824 | tf_op jit(solution)/shard_map/all_to_all | solution.py:675
  72.2 9.1 %all-to-all-done.1 = f32[8,2,6,768]{3,1,2,0:T(2,128)} async-done(((f32[8,2,6,768]{3,1,2,0:T(2,128)}), f32[8,2,6,768]{3,1,2,0:T(2,128)}, u32[]{:S(2)}, u32[]{:S(2)}) %all-to-all-start.1) | async-done | bytes 294944 | tf_op jit(solution)/shard_map/all_to_all | solution.py:675
  86.6 2.2 place.23.refs_0_
  96.0 20.4 %attention_forward.1 = (bf16[2,256,768]{2,1,0:T(8,128)(2,1)}, bf16[2,256,768]{2,1,0:T(8,128)(2,1)}, bf16[2,256,768]{2,1,0:T(8,128)(2,1)}, bf16[2,256,768]{2,1,0:...) custom-call(s32[2]{0:T(128)} %mul.66.length_ref, ...), custom_call_target="tpu_custom_call" | custom-call | flops 2818572288 | bytes 21794824 | tf_op jit(solution)/shard_map/attention_forward/pallas_call | solution.py:1112
  120.6 3.3 collective-permute-done.16.refs_1_
  124.7 2.1 copy-done.4
  126.9 14.4 %feed_forward.2 = (f32[512,768]{1,0:T(8,128)}, f32[512,768]{1,0:T(8,128)}, bf16[3,16,24,1024]{3,2,1,0:T(8,128)(2,1)}, bf16[3,16,24,1024]{3,2,1,0:T(8,128)(2,1)}) custom-call(s32[1]{0:T(128)} %bitcast.here_ref.c_ref, bf16[512,768]{1,0:T(8,128)(2,1)} %bitcast.218, bf16[512,768]{1,0:T(8,128)(2,1)} %bitcast.220, bf16[768,3072]{1,0:T(8,128)(2,1)} %bitcast.166, ...), custom_call_target="tpu_custom_call" | custom-call | flops 7247757312 | bytes 23592964 | tf_op jit(solution)/shard_map/feed_forward/pallas_call | solution.py:1112
  143.4 2.1 copy-done.3
  145.5 14.4 %feed_forward.3 = (f32[512,768]{1,0:T(8,128)}, f32[512,768]{1,0:T(8,128)}, bf16[3,16,24,1024]{3,2,1,0:T(8,128)(2,1)}, bf16[3,16,24,1024]{3,2,1,0:T(8,128)(2,1)}) custom-call(s32[1]{0:T(128)} %bitcast.here_ref.c_ref, bf16[512,768]{1,0:T(8,128)(2,1)} %bitcast.219, bf16[512,768]{1,0:T(8,128)(2,1)} %bitcast.221, bf16[768,3072]{1,0:T(8,128)(2,1)} %bitcast.163, ...), custom_call_target="tpu_custom_call" | custom-call | flops 7247757312 | bytes 23592964 | tf_op jit(solution)/shard_map/feed_forward/pallas_call | solution.py:1112
  160.3 2.2 fold.12
  165.6 17.1 %attention_backward.1 = (bf16[2,256,768]{2,1,0:T(8,128)(2,1)}, f32[2,256,768]{2,1,0:T(8,128)}, bf16[4,2,256,768]{3,2,1,0:T(8,128)(2,1)}, f32[2,8,768]{2,1,0:T(8,128)}) custom-call(s32[2]{0:T(128)} %mul.66.length_ref, f32[2,256,768]{2,1,0:T(8,128)} %bitcast.212, f32[2,256,768]{2,1,0:T(8,128)} %bitcast.214, f32[2,256,768]{2,1,0:T(8,128)} %bitcast.213, ...), custom_call_target="tpu_custom_call" | custom-call | flops 1610612736 | bytes 27349000 | tf_op jit(solution)/shard_map/attention_backward/pallas_call | solution.py:1112
  183.4 2.2 fold.16
  187.2 2.0 fold.17
  193.3 11.7 %projection_backward.1 = (bf16[4,16,24,768]{3,2,1,0:T(8,128)(2,1)}, bf16[4,16,24,768]{3,2,1,0:T(8,128)(2,1)}, f32[2,256,768]{2,1,0:T(8,128)}, bf16[2,8,768]{2,1,0:T(8,128)(2,1)}) custom-call(s32[1]{0:T(128)} %bitcast.here_ref.c_ref, bf16[4,2,256,768]{3,2,1,0:T(8,128)(2,1)} %get-tuple-element.258.grads_in_ref, ...), custom_call_target="tpu_custom_call" | custom-call | flops 4227858432 | bytes 18201604 | tf_op jit(solution)/shard_map/projection_backward/pallas_call | solution.py:1112
  204.9 4.2 %collective-permute-done.23.refs_3_ = bf16[1,4,24,1024]{3,2,1,0:T(8,128)(2,1)S(1)} collective-permute-done((bf16[1,4,24,1024]{3,2,1,0:T(8,128)(2,1)S(1)}, bf16[1,4,24,1024]{3,2,1,0:T(8,128)(2,1)S(1)}, u32[]{:S(2)}, u32[]{:S(2)}) %collective-permute-start.23) | collective-permute-done | bytes 196640 | tf_op jit(solution)/shard_map/ppermute | solution.py:598
  211.3 2.0 collective-permute-start.31
  215.1 2.9 collective-permute-done.29
  219.5 3.9 collective-permute-done.30
  230.6 2.4 collective-permute-start.34
  233.2 2.1 collective-permute-start.36
  235.3 4.0 collective-permute-done.34
  239.3 3.8 collective-permute-done.35
  243.2 2.4 slots.2
  245.6 6.3 %all-to-all-start.2 = ((bf16[16,24,1024]{2,1,0:T(8,128)(2,1)}), bf16[16,24,1024]{2,1,0:T(8,128)(2,1)S(1)}, u32[]{:S(2)}, u32[]{:S(2)}) async-start(bf16[16,24,1024]{2,1,0:T(8,128)(2,1)} %slots.2), calls=%async_computation.2 | async-start | bytes 1572864 | tf_op jit(solution)/shard_map/all_to_all | solution.py:730
  253.1 2.0 collective-permute-start.38
  256.9 9.9 %collective-permute-done.38.refs_3_ = bf16[2,4,24,768]{3,2,1,0:T(8,128)(2,1)S(1)} collective-permute-done((bf16[2,4,24,768]{3,2,1,0:T(8,128)(2,1)S(1)}, bf16[2,4,24,768]{3,2,1,0:T(8,128)(2,1)S(1)}, u32[]{:S(2)}, u32[]{:S(2)}) %collective-permute-start.38) | collective-permute-done | bytes 294944 | tf_op jit(solution)/shard_map/ppermute | solution.py:598
  267.7 3.7 all-to-all-done.2.refs_0_
  276.7 4.8 %collective-permute-done.39 = bf16[4,24,768]{2,1,0:T(8,128)(2,1)S(1)} collective-permute-done((bf16[4,24,768]{2,1,0:T(8,128)(2,1)S(1)}, bf16[4,24,768]{2,1,0:T(8,128)(2,1)S(1)}, u32[]{:S(2)}, u32[]{:S(2)}) %collective-permute-start.39) | collective-permute-done | bytes 147488 | tf_op jit(solution)/shard_map/ppermute | solution.py:601
  281.5 3.2 collective-permute-done.40
  284.9 3.7 collective-permute-done.42.refs_1_
  294.1 4.3 %all-to-all-start.3 = ((bf16[16,40,768]{2,1,0:T(8,128)(2,1)}), bf16[16,40,768]{2,1,0:T(8,128)(2,1)S(1)}, u32[]{:S(2)}, u32[]{:S(2)}) async-start(bf16[16,40,768]{2,1,0:T(8,128)(2,1)} %copy-done.5), calls=%async_computation.3 | async-start | bytes 1966080 | tf_op jit(solution)/shard_map/all_to_all | solution.py:730
  301.9 7.6 %collective-permute-done.44.refs_1_ = bf16[24,9216]{1,0:T(8,128)(2,1)S(1)} collective-permute-done((bf16[24,9216]{1,0:T(8,128)(2,1)}, bf16[24,9216]{1,0:T(8,128)(2,1)S(1)}, u32[]{:S(2)}, u32[]{:S(2)}) %collective-permute-start.44) | collective-permute-done | bytes 442400 | tf_op jit(solution)/shard_map/ppermute | solution.py:598
  309.5 13.7 %all-to-all-done.3.mine_ref = bf16[16,40,768]{2,1,0:T(8,128)(2,1)S(1)} async-done(((bf16[16,40,768]{2,1,0:T(8,128)(2,1)}), bf16[16,40,768]{2,1,0:T(8,128)(2,1)S(1)}, u32[]{:S(2)}, u32[]{:S(2)}) %all-to-all-start.3) | async-done | bytes 983072 | tf_op jit(solution)/shard_map/all_to_all | solution.py:730
  332.8 16.2 %newton_schulz.3 = bf16[768,768]{1,0:T(8,128)(2,1)S(1)} custom-call(s32[1]{0:T(128)} %bitcast.102.active_ref, bf16[768,768]{1,0:T(8,128)(2,1)S(1)} %bitcast.193, bf16[64,768]{1,0:T(8,128)(2,1)S(1)} %bitcast.191, bf16[64,768]{1,0:T(8,128)(2,1)S(1)} %fusion.13.right_ref), custom_call_target="tpu_custom_call" | custom-call | flops 18119393280 | bytes 2359296 | tf_op jit(solution)/shard_map/newton_schulz/pallas_call | solution.py:142
  350.5 3.6 all-to-all-start.4
  359.5 15.7 %all-to-all-done.4.refs_0_ = bf16[16,24,1024]{2,1,0:T(8,128)(2,1)S(1)} async-done(((bf16[16,24,1024]{2,1,0:T(8,128)(2,1)}), bf16[16,24,1024]{2,1,0:T(8,128)(2,1)S(1)}, u32[]{:S(2)}, u32[]{:S(2)}) %all-to-all-start.4) | async-done | bytes 786464 | tf_op jit(solution)/shard_map/all_to_all | solution.py:802
  379.9 11.1 %collective-permute-done.47.refs_1_ = bf16[24,13824]{1,0:T(8,128)(2,1)S(1)} collective-permute-done((bf16[24,13824]{1,0:T(8,128)(2,1)S(1)}, bf16[24,13824]{1,0:T(8,128)(2,1)S(1)}, u32[]{:S(2)}, u32[]{:S(2)}) %collective-permute-start.47) | collective-permute-done | bytes 663584 | tf_op jit(solution)/shard_map/ppermute | solution.py:598
  393.2 2.4 multiply_add_fusion
  395.6 5.7 %update.1 = (f32[6,96,768]{2,1,0:T(8,128)}, f32[3,96,768]{2,1,0:T(8,128)}, f32[96,768]{1,0:T(8,128)}, f32[2,96,2048]{2,1,0:T(8,128)}, f32[96,2048]{1,0:T(8,128)}) custom-call(s32[4]{0:T(128)S(1)} %pad_add_fusion.5.slot_ref, bf16[24,13824]{1,0:T(8,128)(2,1)S(1)} %pack.3.refs_0_, bf16[24,13824]{1,0:T(8,128)(2,1)S(1)} %collective-permute-done.47.refs_1_, ...), custom_call_target="tpu_custom_call" | custom-call | bytes 14000000 | tf_op jit(solution)/shard_map/update/pallas_call | solution.py:443
  (252 shorter events, 114.2 us)
Async XLA Ops:
  4.3 14.2 %collective-permute-start = (bf16[24,3072]{1,0:T(8,128)(2,1)S(1)}, bf16[24,3072]{1,0:T(8,128)(2,1)S(1)}, u32[]{:S(2)}, u32[]{:S(2)}) collective-permute-start(bf16[24,3072]{1,0:T(8,128)(2,1)S(1)} %fusion.12.refs_0_), channel_id=1, source_target_pairs={{0,2},{2,4},{4,6},{6,0},{1,3},{3,5},{5,7},{7,1},{8,10},{10,12},{12... | collective-permute-start | bytes 442376 | tf_op jit(solution)/shard_map/ppermute | solution.py:601
  7.4 12.3 %collective-permute-start.1 = (bf16[24,3072]{1,0:T(8,128)(2,1)S(1)}, bf16[24,3072]{1,0:T(8,128)(2,1)S(1)}, u32[]{:S(2)}, u32[]{:S(2)}) collective-permute-start(bf16[24,3072]{1,0:T(8,128)(2,1)S(1)} %fusion.12.refs_0_), channel_id=1, source_target_pairs={{0,4},{2,6},{4,0},{6,2},{1,5},{3,7},{5,1},{7,3},{8,12},{10,14},{12... | collective-permute-start | bytes 442376 | tf_op jit(solution)/shard_map/ppermute | solution.py:601
  10.0 9.7 %collective-permute-start.2 = (bf16[24,3072]{1,0:T(8,128)(2,1)S(1)}, bf16[24,3072]{1,0:T(8,128)(2,1)}, u32[]{:S(2)}, u32[]{:S(2)}) collective-permute-start(bf16[24,3072]{1,0:T(8,128)(2,1)S(1)} %fusion.12.refs_0_), channel_id=1, source_target_pairs={{0,6},{2,0},{4,2},{6,4},{1,7},{3,1},{5,3},{7,5},{8,14},{10,8},{12,... | collective-permute-start | bytes 442376 | tf_op jit(solution)/shard_map/ppermute | solution.py:601
  13.2 10.6 %all-to-all-start = ((bf16[8,2,96]{2,1,0:T(2,128)(2,1)}), bf16[8,2,96]{2,1,0:T(2,128)(2,1)S(1)}, u32[]{:S(2)}, u32[]{:S(2)}) async-start(bf16[8,2,96]{2,1,0:T(2,128)(2,1)} %bitcast.149), calls=%async_computation | async-start | bytes 8192 | tf_op jit(solution)/shard_map/all_to_all | solution.py:675
  25.8 11.7 %collective-permute-start.5 = (bf16[24,6144]{1,0:T(8,128)(2,1)S(1)}, bf16[24,6144]{1,0:T(8,128)(2,1)S(1)}, u32[]{:S(2)}, u32[]{:S(2)}) collective-permute-start(bf16[24,6144]{1,0:T(8,128)(2,1)S(1)} %constant_dynamic-slice_fusion.2.refs_0_), channel_id=1, source_target_pairs={{0,2},{2,4},{4,6},{6,0},{1,3},{3,5},{5,7},{7,1},{8,10},{10,12},{12... | collective-permute-start | bytes 884744 | tf_op jit(solution)/shard_map/ppermute | solution.py:601
  27.6 14.4 %collective-permute-start.6 = (bf16[24,6144]{1,0:T(8,128)(2,1)S(1)}, bf16[24,6144]{1,0:T(8,128)(2,1)S(1)}, u32[]{:S(2)}, u32[]{:S(2)}) collective-permute-start(bf16[24,6144]{1,0:T(8,128)(2,1)S(1)} %constant_dynamic-slice_fusion.2.refs_0_), channel_id=1, source_target_pairs={{0,6},{2,0},{4,2},{6,4},{1,7},{3,1},{5,3},{7,5},{8,14},{10,8},{12,... | collective-permute-start | bytes 884744 | tf_op jit(solution)/shard_map/ppermute | solution.py:601
  42.7 15.1 %collective-permute-start.7 = (bf16[2,4,24,1536]{3,2,1,0:T(8,128)(2,1)S(1)}, bf16[2,4,24,1536]{3,2,1,0:T(8,128)(2,1)S(1)}, u32[]{:S(2)}, u32[]{:S(2)}) collective-permute-start(bf16[2,4,24,1536]{3,2,1,0:T(8,128)(2,1)S(1)} %place.16.refs_0_), channel_id=1, source_target_pairs={{0,16},{16,0},{1,17},{17,1},{2,18},{18,2},{3,19},{19,3},{4,20},{20... | collective-permute-start | bytes 1769480 | tf_op jit(solution)/shard_map/ppermute | solution.py:598
  43.2 14.8 %collective-permute-start.8 = (bf16[2,4,24,1536]{3,2,1,0:T(8,128)(2,1)S(1)}, bf16[2,4,24,1536]{3,2,1,0:T(8,128)(2,1)S(1)}, u32[]{:S(2)}, u32[]{:S(2)}) collective-permute-start(bf16[2,4,24,1536]{3,2,1,0:T(8,128)(2,1)S(1)} %place.17.refs_0_), channel_id=1, source_target_pairs={{0,1},{1,0},{2,3},{3,2},{4,5},{5,4},{6,7},{7,6},{8,9},{9,8},{10,11... | collective-permute-start | bytes 1769480 | tf_op jit(solution)/shard_map/ppermute | solution.py:598
  43.7 15.6 %collective-permute-start.9 = (bf16[24,6144]{1,0:T(8,128)(2,1)S(1)}, bf16[24,6144]{1,0:T(8,128)(2,1)S(1)}, u32[]{:S(2)}, u32[]{:S(2)}) collective-permute-start(bf16[24,6144]{1,0:T(8,128)(2,1)S(1)} %constant_dynamic-slice_fusion.2.refs_0_), channel_id=1, source_target_pairs={{0,4},{2,6},{4,0},{6,2},{1,5},{3,7},{5,1},{7,3},{8,12},{10,14},{12... | collective-permute-start | bytes 884744 | tf_op jit(solution)/shard_map/ppermute | solution.py:601
  59.3 23.6 %collective-permute-start.11 = (bf16[2,2,4,24,1536]{4,3,2,1,0:T(8,128)(2,1)S(1)}, bf16[2,2,4,24,1536]{4,3,2,1,0:T(8,128)(2,1)}, u32[]{:S(2)}, u32[]{:S(2)}) collective-permute-start(bf16[2,2,4,24,1536]{4,3,2,1,0:T(8,128)(2,1)S(1)} %place.19.refs_0_), channel_id=1, source_target_pairs={{0,8},{8,0},{1,9},{9,1},{2,10},{10,2},{3,11},{11,3},{4,12},{12,4},... | collective-permute-start | bytes 3538952 | tf_op jit(solution)/shard_map/ppermute | solution.py:598
  59.4 26.4 %collective-permute-start.10 = (bf16[2,2,4,24,1536]{4,3,2,1,0:T(8,128)(2,1)S(1)}, bf16[2,2,4,24,1536]{4,3,2,1,0:T(8,128)(2,1)S(1)}, u32[]{:S(2)}, u32[]{:S(2)}) collective-permute-start(bf16[2,2,4,24,1536]{4,3,2,1,0:T(8,128)(2,1)S(1)} %place.18.refs_0_), channel_id=1, source_target_pairs={{0,8},{8,0},{1,9},{9,1},{2,10},{10,2},{3,11},{11,3},{4,12},{12,4},... | collective-permute-start | bytes 3538952 | tf_op jit(solution)/shard_map/ppermute | solution.py:598
  62.5 24.0 %collective-permute-start.12 = (bf16[4,24,3072]{2,1,0:T(8,128)(2,1)}, bf16[4,24,3072]{2,1,0:T(8,128)(2,1)}, u32[]{:S(2)}, u32[]{:S(2)}) collective-permute-start(bf16[4,24,3072]{2,1,0:T(8,128)(2,1)} %get-tuple-element.202.refs_0_), channel_id=1, source_target_pairs={{0,1},{1,0},{2,3},{3,2},{4,5},{5,4},{6,7},{7,6},{8,9},{9,8},{10,11... | collective-permute-start | bytes 1769480 | tf_op jit(solution)/shard_map/ppermute | solution.py:598
  63.2 23.3 %collective-permute-start.13 = (bf16[4,24,3072]{2,1,0:T(8,128)(2,1)}, bf16[4,24,3072]{2,1,0:T(8,128)(2,1)}, u32[]{:S(2)}, u32[]{:S(2)}) collective-permute-start(bf16[4,24,3072]{2,1,0:T(8,128)(2,1)} %get-tuple-element.205.refs_0_), channel_id=1, source_target_pairs={{0,16},{16,0},{1,17},{17,1},{2,18},{18,2},{3,19},{19,3},{4,20},{20... | collective-permute-start | bytes 1769480 | tf_op jit(solution)/shard_map/ppermute | solution.py:598
  65.9 15.4 %all-to-all-start.1 = ((f32[8,2,6,768]{3,1,2,0:T(2,128)}), f32[8,2,6,768]{3,1,2,0:T(2,128)}, u32[]{:S(2)}, u32[]{:S(2)}) async-start(f32[8,2,6,768]{3,1,2,0:T(2,128)} %copy.53), calls=%async_computation.1 | async-start | bytes 589824 | tf_op jit(solution)/shard_map/all_to_all | solution.py:675
  90.2 27.2 %collective-permute-start.14 = (bf16[2,4,24,3072]{3,2,1,0:T(8,128)(2,1)S(1)}, bf16[2,4,24,3072]{3,2,1,0:T(8,128)(2,1)S(1)}, u32[]{:S(2)}, u32[]{:S(2)}) collective-permute-start(bf16[2,4,24,3072]{3,2,1,0:T(8,128)(2,1)S(1)} %place.22.refs_0_), channel_id=1, source_target_pairs={{0,16},{16,0},{1,17},{17,1},{2,18},{18,2},{3,19},{19,3},{4,20},{20... | collective-permute-start | bytes 3538952 | tf_op jit(solution)/shard_map/ppermute | solution.py:598
  91.7 26.8 %collective-permute-start.15 = (bf16[2,4,24,3072]{3,2,1,0:T(8,128)(2,1)S(1)}, bf16[2,4,24,3072]{3,2,1,0:T(8,128)(2,1)S(1)}, u32[]{:S(2)}, u32[]{:S(2)}) collective-permute-start(bf16[2,4,24,3072]{3,2,1,0:T(8,128)(2,1)S(1)} %place.23.refs_0_), channel_id=1, source_target_pairs={{0,1},{1,0},{2,3},{3,2},{4,5},{5,4},{6,7},{7,6},{8,9},{9,8},{10,11... | collective-permute-start | bytes 3538952 | tf_op jit(solution)/shard_map/ppermute | solution.py:598
  120.1 21.3 %collective-permute-start.17 = (bf16[2,2,4,24,3072]{4,3,2,1,0:T(8,128)(2,1)S(1)}, bf16[2,2,4,24,3072]{4,3,2,1,0:T(8,128)(2,1)}, u32[]{:S(2)}, u32[]{:S(2)}) collective-permute-start(bf16[2,2,4,24,3072]{4,3,2,1,0:T(8,128)(2,1)S(1)} %place.26.refs_0_), channel_id=1, source_target_pairs={{0,8},{8,0},{1,9},{9,1},{2,10},{10,2},{3,11},{11,3},{4,12},{12,4},... | collective-permute-start | bytes 7077896 | tf_op jit(solution)/shard_map/ppermute | solution.py:598
  141.2 18.6 %collective-permute-start.18 = (bf16[3,16,24,1024]{3,2,1,0:T(8,128)(2,1)}, bf16[3,16,24,1024]{3,2,1,0:T(8,128)(2,1)S(1)}, u32[]{:S(2)}, u32[]{:S(2)}) collective-permute-start(bf16[3,16,24,1024]{3,2,1,0:T(8,128)(2,1)} %get-tuple-element.238), channel_id=1, source_target_pairs={{0,8},{8,0},{1,9},{9,1},{2,10},{10,2},{3,11},{11,3},{4,12},{12,4},... | collective-permute-start | bytes 7077896 | tf_op jit(solution)/shard_map/ppermute | solution.py:598
  159.9 23.6 %collective-permute-start.21 = (bf16[3,16,24,1024]{3,2,1,0:T(8,128)(2,1)}, bf16[3,16,24,1024]{3,2,1,0:T(8,128)(2,1)S(1)}, u32[]{:S(2)}, u32[]{:S(2)}) collective-permute-start(bf16[3,16,24,1024]{3,2,1,0:T(8,128)(2,1)} %get-tuple-element.256), channel_id=1, source_target_pairs={{0,8},{8,0},{1,9},{9,1},{2,10},{10,2},{3,11},{11,3},{4,12},{12,4},... | collective-permute-start | bytes 7077896 | tf_op jit(solution)/shard_map/ppermute | solution.py:598
  162.5 20.9 %collective-permute-start.19 = (bf16[2,8,24,1024]{3,2,1,0:T(8,128)(2,1)}, bf16[2,8,24,1024]{3,2,1,0:T(8,128)(2,1)}, u32[]{:S(2)}, u32[]{:S(2)}) collective-permute-start(bf16[2,8,24,1024]{3,2,1,0:T(8,128)(2,1)} %bitcast.34), channel_id=1, source_target_pairs={{0,16},{16,0},{1,17},{17,1},{2,18},{18,2},{3,19},{19,3},{4,20},{20... | collective-permute-start | bytes 2359304 | tf_op jit(solution)/shard_map/ppermute | solution.py:598
  165.1 17.6 %collective-permute-start.20 = (bf16[1,8,24,1024]{3,2,1,0:T(8,128)(2,1)}, bf16[1,8,24,1024]{3,2,1,0:T(8,128)(2,1)S(1)}, u32[]{:S(2)}, u32[]{:S(2)}) collective-permute-start(bf16[1,8,24,1024]{3,2,1,0:T(8,128)(2,1)} %bitcast.38), channel_id=1, source_target_pairs={{0,1},{1,0},{2,3},{3,2},{4,5},{5,4},{6,7},{7,6},{8,9},{9,8},{10,11... | collective-permute-start | bytes 1179656 | tf_op jit(solution)/shard_map/ppermute | solution.py:598
  185.7 23.5 %collective-permute-start.24 = (bf16[2,8,24,1024]{3,2,1,0:T(8,128)(2,1)}, bf16[2,8,24,1024]{3,2,1,0:T(8,128)(2,1)S(1)}, u32[]{:S(2)}, u32[]{:S(2)}) collective-permute-start(bf16[2,8,24,1024]{3,2,1,0:T(8,128)(2,1)} %bitcast.52), channel_id=1, source_target_pairs={{0,16},{16,0},{1,17},{17,1},{2,18},{18,2},{3,19},{19,3},{4,20},{20... | collective-permute-start | bytes 2359304 | tf_op jit(solution)/shard_map/ppermute | solution.py:598
  189.2 19.9 %collective-permute-start.25 = (bf16[1,8,24,1024]{3,2,1,0:T(8,128)(2,1)}, bf16[1,8,24,1024]{3,2,1,0:T(8,128)(2,1)S(1)}, u32[]{:S(2)}, u32[]{:S(2)}) collective-permute-start(bf16[1,8,24,1024]{3,2,1,0:T(8,128)(2,1)} %bitcast.56), channel_id=1, source_target_pairs={{0,1},{1,0},{2,3},{3,2},{4,5},{5,4},{6,7},{7,6},{8,9},{9,8},{10,11... | collective-permute-start | bytes 1179656 | tf_op jit(solution)/shard_map/ppermute | solution.py:598
  190.8 18.3 %collective-permute-start.23 = (bf16[1,4,24,1024]{3,2,1,0:T(8,128)(2,1)S(1)}, bf16[1,4,24,1024]{3,2,1,0:T(8,128)(2,1)S(1)}, u32[]{:S(2)}, u32[]{:S(2)}) collective-permute-start(bf16[1,4,24,1024]{3,2,1,0:T(8,128)(2,1)S(1)} %bitcast.200), channel_id=1, source_target_pairs={{0,16},{16,0},{1,17},{17,1},{2,18},{18,2},{3,19},{19,3},{4,20},{20... | collective-permute-start | bytes 589832 | tf_op jit(solution)/shard_map/ppermute | solution.py:598
  192.6 16.5 %collective-permute-start.22 = (bf16[2,4,24,1024]{3,2,1,0:T(8,128)(2,1)S(1)}, bf16[2,4,24,1024]{3,2,1,0:T(8,128)(2,1)S(1)}, u32[]{:S(2)}, u32[]{:S(2)}) collective-permute-start(bf16[2,4,24,1024]{3,2,1,0:T(8,128)(2,1)S(1)} %bitcast.197), channel_id=1, source_target_pairs={{0,1},{1,0},{2,3},{3,2},{4,5},{5,4},{6,7},{7,6},{8,9},{9,8},{10,11... | collective-permute-start | bytes 1179656 | tf_op jit(solution)/shard_map/ppermute | solution.py:598
  209.1 15.3 %collective-permute-start.26 = (bf16[4,16,24,768]{3,2,1,0:T(8,128)(2,1)}, bf16[4,16,24,768]{3,2,1,0:T(8,128)(2,1)S(1)}, u32[]{:S(2)}, u32[]{:S(2)}) collective-permute-start(bf16[4,16,24,768]{3,2,1,0:T(8,128)(2,1)} %get-tuple-element.282), channel_id=1, source_target_pairs={{0,8},{8,0},{1,9},{9,1},{2,10},{10,2},{3,11},{11,3},{4,12},{12,4},... | collective-permute-start | bytes 7077896 | tf_op jit(solution)/shard_map/ppermute | solution.py:598
  209.4 8.6 %collective-permute-start.29 = (bf16[3,24,1024]{2,1,0:T(8,128)(2,1)S(1)}, bf16[3,24,1024]{2,1,0:T(8,128)(2,1)S(1)}, u32[]{:S(2)}, u32[]{:S(2)}) collective-permute-start(bf16[3,24,1024]{2,1,0:T(8,128)(2,1)S(1)} %get-tuple-element.296), channel_id=1, source_target_pairs={{0,2},{2,4},{4,6},{6,0},{1,3},{3,5},{5,7},{7,1},{8,10},{10,12},{12... | collective-permute-start | bytes 442376 | tf_op jit(solution)/shard_map/ppermute | solution.py:601
  209.4 14.0 %collective-permute-start.30 = (bf16[3,24,1024]{2,1,0:T(8,128)(2,1)S(1)}, bf16[3,24,1024]{2,1,0:T(8,128)(2,1)S(1)}, u32[]{:S(2)}, u32[]{:S(2)}) collective-permute-start(bf16[3,24,1024]{2,1,0:T(8,128)(2,1)S(1)} %get-tuple-element.297), channel_id=1, source_target_pairs={{0,4},{2,6},{4,0},{6,2},{1,5},{3,7},{5,1},{7,3},{8,12},{10,14},{12... | collective-permute-start | bytes 442376 | tf_op jit(solution)/shard_map/ppermute | solution.py:601
  211.3 12.2 %collective-permute-start.31 = (bf16[3,24,1024]{2,1,0:T(8,128)(2,1)S(1)}, bf16[3,24,1024]{2,1,0:T(8,128)(2,1)S(1)}, u32[]{:S(2)}, u32[]{:S(2)}) collective-permute-start(bf16[3,24,1024]{2,1,0:T(8,128)(2,1)S(1)} %get-tuple-element.298), channel_id=1, source_target_pairs={{0,6},{2,0},{4,2},{6,4},{1,7},{3,1},{5,3},{7,5},{8,14},{10,8},{12,... | collective-permute-start | bytes 442376 | tf_op jit(solution)/shard_map/ppermute | solution.py:601
  213.5 11.0 %collective-permute-start.27 = (bf16[2,4,24,1024]{3,2,1,0:T(8,128)(2,1)S(1)}, bf16[2,4,24,1024]{3,2,1,0:T(8,128)(2,1)S(1)}, u32[]{:S(2)}, u32[]{:S(2)}) collective-permute-start(bf16[2,4,24,1024]{3,2,1,0:T(8,128)(2,1)S(1)} %bitcast.196), channel_id=1, source_target_pairs={{0,1},{1,0},{2,3},{3,2},{4,5},{5,4},{6,7},{7,6},{8,9},{9,8},{10,11... | collective-permute-start | bytes 1179656 | tf_op jit(solution)/shard_map/ppermute | solution.py:598
  226.1 17.1 %collective-permute-start.33 = (bf16[2,8,24,768]{3,2,1,0:T(8,128)(2,1)S(1)}, bf16[2,8,24,768]{3,2,1,0:T(8,128)(2,1)S(1)}, u32[]{:S(2)}, u32[]{:S(2)}) collective-permute-start(bf16[2,8,24,768]{3,2,1,0:T(8,128)(2,1)S(1)} %bitcast.194), channel_id=1, source_target_pairs={{0,1},{1,0},{2,3},{3,2},{4,5},{5,4},{6,7},{7,6},{8,9},{9,8},{10,11... | collective-permute-start | bytes 1769480 | tf_op jit(solution)/shard_map/ppermute | solution.py:598
  229.0 14.1 %collective-permute-start.32 = (bf16[2,8,24,768]{3,2,1,0:T(8,128)(2,1)S(1)}, bf16[2,8,24,768]{3,2,1,0:T(8,128)(2,1)S(1)}, u32[]{:S(2)}, u32[]{:S(2)}) collective-permute-start(bf16[2,8,24,768]{3,2,1,0:T(8,128)(2,1)S(1)} %bitcast.195), channel_id=1, source_target_pairs={{0,16},{16,0},{1,17},{17,1},{2,18},{18,2},{3,19},{19,3},{4,20},{20... | collective-permute-start | bytes 1769480 | tf_op jit(solution)/shard_map/ppermute | solution.py:598
  230.6 8.7 %collective-permute-start.34 = (bf16[3,24,1024]{2,1,0:T(8,128)(2,1)S(1)}, bf16[3,24,1024]{2,1,0:T(8,128)(2,1)S(1)}, u32[]{:S(2)}, u32[]{:S(2)}) collective-permute-start(bf16[3,24,1024]{2,1,0:T(8,128)(2,1)S(1)} %get-tuple-element.316), channel_id=1, source_target_pairs={{0,2},{2,4},{4,6},{6,0},{1,3},{3,5},{5,7},{7,1},{8,10},{10,12},{12... | collective-permute-start | bytes 442376 | tf_op jit(solution)/shard_map/ppermute | solution.py:601
  232.9 10.1 %collective-permute-start.35 = (bf16[3,24,1024]{2,1,0:T(8,128)(2,1)S(1)}, bf16[3,24,1024]{2,1,0:T(8,128)(2,1)S(1)}, u32[]{:S(2)}, u32[]{:S(2)}) collective-permute-start(bf16[3,24,1024]{2,1,0:T(8,128)(2,1)S(1)} %get-tuple-element.317), channel_id=1, source_target_pairs={{0,4},{2,6},{4,0},{6,2},{1,5},{3,7},{5,1},{7,3},{8,12},{10,14},{12... | collective-permute-start | bytes 442376 | tf_op jit(solution)/shard_map/ppermute | solution.py:601
  233.2 9.8 %collective-permute-start.36 = (bf16[3,24,1024]{2,1,0:T(8,128)(2,1)S(1)}, bf16[3,24,1024]{2,1,0:T(8,128)(2,1)S(1)}, u32[]{:S(2)}, u32[]{:S(2)}) collective-permute-start(bf16[3,24,1024]{2,1,0:T(8,128)(2,1)S(1)} %get-tuple-element.318), channel_id=1, source_target_pairs={{0,6},{2,0},{4,2},{6,4},{1,7},{3,1},{5,3},{7,5},{8,14},{10,8},{12,... | collective-permute-start | bytes 442376 | tf_op jit(solution)/shard_map/ppermute | solution.py:601
  245.6 25.7 %all-to-all-start.2 = ((bf16[16,24,1024]{2,1,0:T(8,128)(2,1)}), bf16[16,24,1024]{2,1,0:T(8,128)(2,1)S(1)}, u32[]{:S(2)}, u32[]{:S(2)}) async-start(bf16[16,24,1024]{2,1,0:T(8,128)(2,1)} %slots.2), calls=%async_computation.2 | async-start | bytes 1572864 | tf_op jit(solution)/shard_map/all_to_all | solution.py:730
  253.1 13.6 %collective-permute-start.38 = (bf16[2,4,24,768]{3,2,1,0:T(8,128)(2,1)S(1)}, bf16[2,4,24,768]{3,2,1,0:T(8,128)(2,1)S(1)}, u32[]{:S(2)}, u32[]{:S(2)}) collective-permute-start(bf16[2,4,24,768]{3,2,1,0:T(8,128)(2,1)S(1)} %bitcast.198), channel_id=1, source_target_pairs={{0,16},{16,0},{1,17},{17,1},{2,18},{18,2},{3,19},{19,3},{4,20},{20... | collective-permute-start | bytes 884744 | tf_op jit(solution)/shard_map/ppermute | solution.py:598
  255.3 12.4 %collective-permute-start.37 = (bf16[2,4,24,768]{3,2,1,0:T(8,128)(2,1)S(1)}, bf16[2,4,24,768]{3,2,1,0:T(8,128)(2,1)S(1)}, u32[]{:S(2)}, u32[]{:S(2)}) collective-permute-start(bf16[2,4,24,768]{3,2,1,0:T(8,128)(2,1)S(1)} %bitcast.199), channel_id=1, source_target_pairs={{0,1},{1,0},{2,3},{3,2},{4,5},{5,4},{6,7},{7,6},{8,9},{9,8},{10,11... | collective-permute-start | bytes 884744 | tf_op jit(solution)/shard_map/ppermute | solution.py:598
  271.4 17.2 %collective-permute-start.42 = (bf16[16,24,1024]{2,1,0:T(8,128)(2,1)S(1)}, bf16[16,24,1024]{2,1,0:T(8,128)(2,1)S(1)}, u32[]{:S(2)}, u32[]{:S(2)}) collective-permute-start(bf16[16,24,1024]{2,1,0:T(8,128)(2,1)S(1)} %all-to-all-done.2.refs_0_), channel_id=1, source_target_pairs={{0,16},{16,0},{1,17},{17,1},{2,18},{18,2},{3,19},{19,3},{4,20},{20... | collective-permute-start | bytes 2359304 | tf_op jit(solution)/shard_map/ppermute | solution.py:598
  272.9 8.7 %collective-permute-start.39 = (bf16[4,24,768]{2,1,0:T(8,128)(2,1)S(1)}, bf16[4,24,768]{2,1,0:T(8,128)(2,1)S(1)}, u32[]{:S(2)}, u32[]{:S(2)}) collective-permute-start(bf16[4,24,768]{2,1,0:T(8,128)(2,1)S(1)} %get-tuple-element.334), channel_id=1, source_target_pairs={{0,2},{2,4},{4,6},{6,0},{1,3},{3,5},{5,7},{7,1},{8,10},{10,12},{12... | collective-permute-start | bytes 442376 | tf_op jit(solution)/shard_map/ppermute | solution.py:601
  274.0 10.8 %collective-permute-start.40 = (bf16[4,24,768]{2,1,0:T(8,128)(2,1)S(1)}, bf16[4,24,768]{2,1,0:T(8,128)(2,1)S(1)}, u32[]{:S(2)}, u32[]{:S(2)}) collective-permute-start(bf16[4,24,768]{2,1,0:T(8,128)(2,1)S(1)} %get-tuple-element.335), channel_id=1, source_target_pairs={{0,4},{2,6},{4,0},{6,2},{1,5},{3,7},{5,1},{7,3},{8,12},{10,14},{12... | collective-permute-start | bytes 442376 | tf_op jit(solution)/shard_map/ppermute | solution.py:601
  274.9 9.9 %collective-permute-start.41 = (bf16[4,24,768]{2,1,0:T(8,128)(2,1)S(1)}, bf16[4,24,768]{2,1,0:T(8,128)(2,1)S(1)}, u32[]{:S(2)}, u32[]{:S(2)}) collective-permute-start(bf16[4,24,768]{2,1,0:T(8,128)(2,1)S(1)} %get-tuple-element.336), channel_id=1, source_target_pairs={{0,6},{2,0},{4,2},{6,4},{1,7},{3,1},{5,3},{7,5},{8,14},{10,8},{12,... | collective-permute-start | bytes 442376 | tf_op jit(solution)/shard_map/ppermute | solution.py:601
  289.2 9.2 %collective-permute-start.43 = (bf16[2,2,4,2,24,1024]{5,4,3,2,1,0:T(8,128)(2,1)S(1)}, bf16[2,2,4,2,24,1024]{5,4,3,2,1,0:T(8,128)(2,1)}, u32[]{:S(2)}, u32[]{:S(2)}) collective-permute-start(bf16[2,2,4,2,24,1024]{5,4,3,2,1,0:T(8,128)(2,1)S(1)} %bitcast.161), channel_id=1, source_target_pairs={{0,8},{8,0},{1,9},{9,1},{2,10},{10,2},{3,11},{11,3},{4,12},{12,4},... | collective-permute-start | bytes 4718600 | tf_op jit(solution)/shard_map/ppermute | solution.py:598
  292.4 17.2 %collective-permute-start.44 = (bf16[24,9216]{1,0:T(8,128)(2,1)}, bf16[24,9216]{1,0:T(8,128)(2,1)S(1)}, u32[]{:S(2)}, u32[]{:S(2)}) collective-permute-start(bf16[24,9216]{1,0:T(8,128)(2,1)} %pack.2.refs_0_), channel_id=1, source_target_pairs={{0,16},{16,0},{1,17},{17,1},{2,18},{18,2},{3,19},{19,3},{4,20},{20... | collective-permute-start | bytes 1327112 | tf_op jit(solution)/shard_map/ppermute | solution.py:598
  294.1 29.1 %all-to-all-start.3 = ((bf16[16,40,768]{2,1,0:T(8,128)(2,1)}), bf16[16,40,768]{2,1,0:T(8,128)(2,1)S(1)}, u32[]{:S(2)}, u32[]{:S(2)}) async-start(bf16[16,40,768]{2,1,0:T(8,128)(2,1)} %copy-done.5), calls=%async_computation.3 | async-start | bytes 1966080 | tf_op jit(solution)/shard_map/all_to_all | solution.py:730
  350.5 24.6 %all-to-all-start.4 = ((bf16[16,24,1024]{2,1,0:T(8,128)(2,1)}), bf16[16,24,1024]{2,1,0:T(8,128)(2,1)S(1)}, u32[]{:S(2)}, u32[]{:S(2)}) async-start(bf16[16,24,1024]{2,1,0:T(8,128)(2,1)} %bitcast.209), calls=%async_computation.4 | async-start | bytes 1572864 | tf_op jit(solution)/shard_map/all_to_all | solution.py:802
  375.2 15.8 %collective-permute-start.47 = (bf16[24,13824]{1,0:T(8,128)(2,1)S(1)}, bf16[24,13824]{1,0:T(8,128)(2,1)S(1)}, u32[]{:S(2)}, u32[]{:S(2)}) collective-permute-start(bf16[24,13824]{1,0:T(8,128)(2,1)S(1)} %pack.3.refs_0_), channel_id=1, source_target_pairs={{0,16},{16,0},{1,17},{17,1},{2,18},{18,2},{3,19},{19,3},{4,20},{20... | collective-permute-start | bytes 1990664 | tf_op jit(solution)/shard_map/ppermute | solution.py:598
  379.9 15.6 %collective-permute-start.48 = (bf16[24,13824]{1,0:T(8,128)(2,1)S(1)}, bf16[24,13824]{1,0:T(8,128)(2,1)S(1)}, u32[]{:S(2)}, u32[]{:S(2)}) collective-permute-start(bf16[24,13824]{1,0:T(8,128)(2,1)S(1)} %pack.3.refs_0_), channel_id=1, source_target_pairs={{0,8},{8,0},{1,9},{9,1},{2,10},{10,2},{3,11},{11,3},{4,12},{12,4},... | collective-permute-start | bytes 1990664 | tf_op jit(solution)/shard_map/ppermute | solution.py:598
  (53 other events, 285.0 us)

commit v6 on v5

--- a/solution.py
+++ b/solution.py
@@ -1438,6 +1438,7 @@
     part = pick([0 if slot is None else slot[1] for slot in comm.wide_slots], owner)
     mine = lax.dynamic_slice_in_dim(wide_done, part * size, size, 1)
     mine = mine + jnp.pad(square_done, ((0, 0), (0, size - D)))
+    mine, totals_low = meet(mine, totals_low)
     back = comm.to_rows(mine)
 
     totals_low = comm.complete_end(totals_low).astype(F32)

time: 407 us -> 402 us (0.988)
    unnamed x99 -> x85, local copies, waits for them, and re-layouts: 18 us -> 13.4 us
  transfers between devices with their start and end apart: 55 -> 55, of which waited for: 30 -> 31; matrix products, arithmetic and copies ran while one was open for 6% -> 7% of each run, Pallas kernels for 26% -> 26%
where the time goes in v6:
time: 402 us; the launch traced here: 397 us
  Pallas kernels  138 us (34%)
  waiting for transfers between devices  135 us (34%)
  starting transfers between devices  75.8 us (19%)
  other arithmetic  20.2 us (5%)
  local copies, waits for them, and re-layouts  20.1 us (5%)
  matrix products  5.23 us (1%)
    pallas_call x5, Pallas kernels, call(): pl.pallas_call(body, grid=grid, out_shape=outs, in_specs=in_specs, out_sp...  77.9 us
    ppermute x35, waiting for transfers between devices, swap(): return lax.ppermute(value, axis, [(0, 1), (1, 0)])  63.6 us
    ppermute x15, waiting for transfers between devices, shift(): return lax.ppermute(value, 'z', [(i, (i + by) % 4) for i in range(4)])  30.9 us
    ppermute x35, starting transfers between devices, swap(): return lax.ppermute(value, axis, [(0, 1), (1, 0)])  29.2 us
    ppermute x15, starting transfers between devices, shift(): return lax.ppermute(value, 'z', [(i, (i + by) % 4) for i in range(4)])  24.9 us
    all_to_all x2, waiting for transfers between devices, to_owners(): lax.all_to_all(pieces, self.chips, split_axis=0, concat_axis=0, tiled=True)  16.6 us
    pallas_call x2, Pallas kernels, newton_schulz(): pl.pallas_call(body, out_shape=jax.ShapeDtypeStruct((D, width), BF16), in...  16.4 us
    pallas_call x16, Pallas kernels, place(): pl.pallas_call(body, out_shape=jax.ShapeDtypeStruct((*lead, *parts[0].sha...  16.3 us
  transfers between devices with their start and end apart: 55, of which 31 were waited for; matrix products, arithmetic and copies ran while one was open for 7% of the time, Pallas kernels for 26%

profile of v6, /device:TPU:0, one launch (start us, length us, event | category | flops | bytes accessed | tf_op | source)
XLA Modules:
  0.0 396.9 jit_solution(13549856564741725818)
XLA Ops:
  4.3 3.1 collective-permute-start
  7.4 2.6 collective-permute-start.1
  13.2 3.3 all-to-all-start
  20.7 3.1 all-to-all-done
  27.6 2.1 collective-permute-start.6
  29.7 2.6 collective-permute-done.4.refs_1_
  34.2 3.4 collective-permute-done.5.refs_1_
  38.3 3.6 collective-permute-done.6.refs_3_
  45.3 12.5 %collective-permute-done.7.refs_1_ = bf16[2,4,24,1536]{3,2,1,0:T(8,128)(2,1)S(1)} collective-permute-done((bf16[2,4,24,1536]{3,2,1,0:T(8,128)(2,1)S(1)}, bf16[2,4,24,1536]{3,2,1,0:T(8,128)(2,1)S(1)}, u32[]{:S(2)}, u32[]{:S(2)}) %collective-permute-start.7) | collective-permute-done | bytes 589856 | tf_op jit(solution)/shard_map/ppermute | solution.py:598
  65.9 4.2 %all-to-all-start.1 = ((f32[8,2,6,768]{3,1,2,0:T(2,128)}), f32[8,2,6,768]{3,1,2,0:T(2,128)}, u32[]{:S(2)}, u32[]{:S(2)}) async-start(f32[8,2,6,768]{3,1,2,0:T(2,128)} %copy.53), calls=%async_computation.1 | async-start | bytes 589824 | tf_op jit(solution)/shard_map/all_to_all | solution.py:675
  72.2 9.1 %all-to-all-done.1 = f32[8,2,6,768]{3,1,2,0:T(2,128)} async-done(((f32[8,2,6,768]{3,1,2,0:T(2,128)}), f32[8,2,6,768]{3,1,2,0:T(2,128)}, u32[]{:S(2)}, u32[]{:S(2)}) %all-to-all-start.1) | async-done | bytes 294944 | tf_op jit(solution)/shard_map/all_to_all | solution.py:675
  86.6 2.2 place.23.refs_0_
  95.9 20.4 %attention_forward.1 = (bf16[2,256,768]{2,1,0:T(8,128)(2,1)}, bf16[2,256,768]{2,1,0:T(8,128)(2,1)}, bf16[2,256,768]{2,1,0:T(8,128)(2,1)}, bf16[2,256,768]{2,1,0:...) custom-call(s32[2]{0:T(128)} %mul.66.length_ref, ...), custom_call_target="tpu_custom_call" | custom-call | flops 2818572288 | bytes 21794824 | tf_op jit(solution)/shard_map/attention_forward/pallas_call | solution.py:1112
  120.6 3.3 collective-permute-done.16.refs_1_
  124.7 2.1 copy-done.4
  126.9 14.4 %feed_forward.2 = (f32[512,768]{1,0:T(8,128)}, f32[512,768]{1,0:T(8,128)}, bf16[3,16,24,1024]{3,2,1,0:T(8,128)(2,1)}, bf16[3,16,24,1024]{3,2,1,0:T(8,128)(2,1)}) custom-call(s32[1]{0:T(128)} %bitcast.here_ref.c_ref, bf16[512,768]{1,0:T(8,128)(2,1)} %bitcast.218, bf16[512,768]{1,0:T(8,128)(2,1)} %bitcast.220, bf16[768,3072]{1,0:T(8,128)(2,1)} %bitcast.166, ...), custom_call_target="tpu_custom_call" | custom-call | flops 7247757312 | bytes 23592964 | tf_op jit(solution)/shard_map/feed_forward/pallas_call | solution.py:1112
  143.4 2.1 copy-done.3
  145.5 14.4 %feed_forward.3 = (f32[512,768]{1,0:T(8,128)}, f32[512,768]{1,0:T(8,128)}, bf16[3,16,24,1024]{3,2,1,0:T(8,128)(2,1)}, bf16[3,16,24,1024]{3,2,1,0:T(8,128)(2,1)}) custom-call(s32[1]{0:T(128)} %bitcast.here_ref.c_ref, bf16[512,768]{1,0:T(8,128)(2,1)} %bitcast.219, bf16[512,768]{1,0:T(8,128)(2,1)} %bitcast.221, bf16[768,3072]{1,0:T(8,128)(2,1)} %bitcast.163, ...), custom_call_target="tpu_custom_call" | custom-call | flops 7247757312 | bytes 23592964 | tf_op jit(solution)/shard_map/feed_forward/pallas_call | solution.py:1112
  160.3 2.2 fold.12
  165.6 17.1 %attention_backward.1 = (bf16[2,256,768]{2,1,0:T(8,128)(2,1)}, f32[2,256,768]{2,1,0:T(8,128)}, bf16[4,2,256,768]{3,2,1,0:T(8,128)(2,1)}, f32[2,8,768]{2,1,0:T(8,128)}) custom-call(s32[2]{0:T(128)} %mul.66.length_ref, f32[2,256,768]{2,1,0:T(8,128)} %bitcast.212, f32[2,256,768]{2,1,0:T(8,128)} %bitcast.214, f32[2,256,768]{2,1,0:T(8,128)} %bitcast.213, ...), custom_call_target="tpu_custom_call" | custom-call | flops 1610612736 | bytes 27349000 | tf_op jit(solution)/shard_map/attention_backward/pallas_call | solution.py:1112
  183.5 2.2 fold.16
  187.2 2.0 fold.17
  193.3 11.7 %projection_backward.1 = (bf16[4,16,24,768]{3,2,1,0:T(8,128)(2,1)}, bf16[4,16,24,768]{3,2,1,0:T(8,128)(2,1)}, f32[2,256,768]{2,1,0:T(8,128)}, bf16[2,8,768]{2,1,0:T(8,128)(2,1)}) custom-call(s32[1]{0:T(128)} %bitcast.here_ref.c_ref, bf16[4,2,256,768]{3,2,1,0:T(8,128)(2,1)} %get-tuple-element.261.grads_in_ref, ...), custom_call_target="tpu_custom_call" | custom-call | flops 4227858432 | bytes 18201604 | tf_op jit(solution)/shard_map/projection_backward/pallas_call | solution.py:1112
  205.0 4.2 %collective-permute-done.23.refs_3_ = bf16[1,4,24,1024]{3,2,1,0:T(8,128)(2,1)S(1)} collective-permute-done((bf16[1,4,24,1024]{3,2,1,0:T(8,128)(2,1)S(1)}, bf16[1,4,24,1024]{3,2,1,0:T(8,128)(2,1)S(1)}, u32[]{:S(2)}, u32[]{:S(2)}) %collective-permute-start.23) | collective-permute-done | bytes 196640 | tf_op jit(solution)/shard_map/ppermute | solution.py:598
  215.1 2.9 collective-permute-done.29
  219.5 3.9 collective-permute-done.30
  230.6 2.4 collective-permute-start.34
  233.2 2.1 collective-permute-start.36
  235.3 4.0 collective-permute-done.34
  239.3 3.8 collective-permute-done.35
  243.2 2.4 slots.2
  245.6 6.3 %all-to-all-start.2 = ((bf16[16,24,1024]{2,1,0:T(8,128)(2,1)}), bf16[16,24,1024]{2,1,0:T(8,128)(2,1)S(1)}, u32[]{:S(2)}, u32[]{:S(2)}) async-start(bf16[16,24,1024]{2,1,0:T(8,128)(2,1)} %slots.2), calls=%async_computation.2 | async-start | bytes 1572864 | tf_op jit(solution)/shard_map/all_to_all | solution.py:730
  256.9 9.9 %collective-permute-done.38.refs_3_ = bf16[2,4,24,768]{3,2,1,0:T(8,128)(2,1)S(1)} collective-permute-done((bf16[2,4,24,768]{3,2,1,0:T(8,128)(2,1)S(1)}, bf16[2,4,24,768]{3,2,1,0:T(8,128)(2,1)S(1)}, u32[]{:S(2)}, u32[]{:S(2)}) %collective-permute-start.38) | collective-permute-done | bytes 294944 | tf_op jit(solution)/shard_map/ppermute | solution.py:598
  267.7 3.7 all-to-all-done.2.refs_0_
  276.7 4.8 %collective-permute-done.39 = bf16[4,24,768]{2,1,0:T(8,128)(2,1)S(1)} collective-permute-done((bf16[4,24,768]{2,1,0:T(8,128)(2,1)S(1)}, bf16[4,24,768]{2,1,0:T(8,128)(2,1)S(1)}, u32[]{:S(2)}, u32[]{:S(2)}) %collective-permute-start.39) | collective-permute-done | bytes 147488 | tf_op jit(solution)/shard_map/ppermute | solution.py:601
  281.6 3.2 collective-permute-done.40
  284.9 3.7 collective-permute-done.42.refs_1_
  289.4 2.2 slots.3
  294.1 4.3 %all-to-all-start.3 = ((bf16[16,40,768]{2,1,0:T(8,128)(2,1)}), bf16[16,40,768]{2,1,0:T(8,128)(2,1)S(1)}, u32[]{:S(2)}, u32[]{:S(2)}) async-start(bf16[16,40,768]{2,1,0:T(8,128)(2,1)} %slots.3), calls=%async_computation.3 | async-start | bytes 1966080 | tf_op jit(solution)/shard_map/all_to_all | solution.py:730
  301.9 7.6 %collective-permute-done.44.refs_1_ = bf16[24,9216]{1,0:T(8,128)(2,1)S(1)} collective-permute-done((bf16[24,9216]{1,0:T(8,128)(2,1)}, bf16[24,9216]{1,0:T(8,128)(2,1)S(1)}, u32[]{:S(2)}, u32[]{:S(2)}) %collective-permute-start.44) | collective-permute-done | bytes 442400 | tf_op jit(solution)/shard_map/ppermute | solution.py:598
  310.3 13.0 %all-to-all-done.3.mine_ref = bf16[16,40,768]{2,1,0:T(8,128)(2,1)S(1)} async-done(((bf16[16,40,768]{2,1,0:T(8,128)(2,1)}), bf16[16,40,768]{2,1,0:T(8,128)(2,1)S(1)}, u32[]{:S(2)}, u32[]{:S(2)}) %all-to-all-start.3) | async-done | bytes 983072 | tf_op jit(solution)/shard_map/all_to_all | solution.py:730
  323.3 2.6 collective-permute-done.45.other_ref
  326.4 16.2 %newton_schulz.3 = bf16[768,768]{1,0:T(8,128)(2,1)S(1)} custom-call(s32[1]{0:T(128)} %bitcast.90.active_ref, bf16[768,768]{1,0:T(8,128)(2,1)S(1)} %bitcast.193, bf16[64,768]{1,0:T(8,128)(2,1)S(1)} %bitcast.191, bf16[64,768]{1,0:T(8,128)(2,1)S(1)} %fusion.13.right_ref), custom_call_target="tpu_custom_call" | custom-call | flops 18119393280 | bytes 2359296 | tf_op jit(solution)/shard_map/newton_schulz/pallas_call | solution.py:142
  347.8 3.6 all-to-all-start.4
  351.4 3.9 multiply_add_fusion
  360.7 11.8 %all-to-all-done.4.refs_0_ = bf16[16,24,1024]{2,1,0:T(8,128)(2,1)S(1)} async-done(((bf16[16,24,1024]{2,1,0:T(8,128)(2,1)}), bf16[16,24,1024]{2,1,0:T(8,128)(2,1)S(1)}, u32[]{:S(2)}, u32[]{:S(2)}) %all-to-all-start.4) | async-done | bytes 786464 | tf_op jit(solution)/shard_map/all_to_all | solution.py:802
  376.5 12.1 %collective-permute-done.47.refs_1_ = bf16[24,13824]{1,0:T(8,128)(2,1)S(1)} collective-permute-done((bf16[24,13824]{1,0:T(8,128)(2,1)S(1)}, bf16[24,13824]{1,0:T(8,128)(2,1)S(1)}, u32[]{:S(2)}, u32[]{:S(2)}) %collective-permute-start.47) | collective-permute-done | bytes 663584 | tf_op jit(solution)/shard_map/ppermute | solution.py:598
  390.7 5.7 %update.1 = (f32[6,96,768]{2,1,0:T(8,128)}, f32[3,96,768]{2,1,0:T(8,128)}, f32[96,768]{1,0:T(8,128)}, f32[2,96,2048]{2,1,0:T(8,128)}, f32[96,2048]{1,0:T(8,128)}) custom-call(s32[4]{0:T(128)S(1)} %pad_add_fusion.5.slot_ref, bf16[24,13824]{1,0:T(8,128)(2,1)S(1)} %pack.3.refs_0_, bf16[24,13824]{1,0:T(8,128)(2,1)S(1)} %collective-permute-done.47.refs_1_, ...), custom_call_target="tpu_custom_call" | custom-call | bytes 14000000 | tf_op jit(solution)/shard_map/update/pallas_call | solution.py:443
  (238 shorter events, 110.7 us)
Async XLA Ops:
  4.3 14.2 %collective-permute-start = (bf16[24,3072]{1,0:T(8,128)(2,1)S(1)}, bf16[24,3072]{1,0:T(8,128)(2,1)S(1)}, u32[]{:S(2)}, u32[]{:S(2)}) collective-permute-start(bf16[24,3072]{1,0:T(8,128)(2,1)S(1)} %fusion.12.refs_0_), channel_id=1, source_target_pairs={{0,2},{2,4},{4,6},{6,0},{1,3},{3,5},{5,7},{7,1},{8,10},{10,12},{12... | collective-permute-start | bytes 442376 | tf_op jit(solution)/shard_map/ppermute | solution.py:601
  7.4 12.3 %collective-permute-start.1 = (bf16[24,3072]{1,0:T(8,128)(2,1)S(1)}, bf16[24,3072]{1,0:T(8,128)(2,1)S(1)}, u32[]{:S(2)}, u32[]{:S(2)}) collective-permute-start(bf16[24,3072]{1,0:T(8,128)(2,1)S(1)} %fusion.12.refs_0_), channel_id=1, source_target_pairs={{0,4},{2,6},{4,0},{6,2},{1,5},{3,7},{5,1},{7,3},{8,12},{10,14},{12... | collective-permute-start | bytes 442376 | tf_op jit(solution)/shard_map/ppermute | solution.py:601
  10.0 9.7 %collective-permute-start.2 = (bf16[24,3072]{1,0:T(8,128)(2,1)S(1)}, bf16[24,3072]{1,0:T(8,128)(2,1)}, u32[]{:S(2)}, u32[]{:S(2)}) collective-permute-start(bf16[24,3072]{1,0:T(8,128)(2,1)S(1)} %fusion.12.refs_0_), channel_id=1, source_target_pairs={{0,6},{2,0},{4,2},{6,4},{1,7},{3,1},{5,3},{7,5},{8,14},{10,8},{12,... | collective-permute-start | bytes 442376 | tf_op jit(solution)/shard_map/ppermute | solution.py:601
  13.2 10.6 %all-to-all-start = ((bf16[8,2,96]{2,1,0:T(2,128)(2,1)}), bf16[8,2,96]{2,1,0:T(2,128)(2,1)S(1)}, u32[]{:S(2)}, u32[]{:S(2)}) async-start(bf16[8,2,96]{2,1,0:T(2,128)(2,1)} %bitcast.149), calls=%async_computation | async-start | bytes 8192 | tf_op jit(solution)/shard_map/all_to_all | solution.py:675
  25.8 11.7 %collective-permute-start.5 = (bf16[24,6144]{1,0:T(8,128)(2,1)S(1)}, bf16[24,6144]{1,0:T(8,128)(2,1)S(1)}, u32[]{:S(2)}, u32[]{:S(2)}) collective-permute-start(bf16[24,6144]{1,0:T(8,128)(2,1)S(1)} %constant_dynamic-slice_fusion.2.refs_0_), channel_id=1, source_target_pairs={{0,2},{2,4},{4,6},{6,0},{1,3},{3,5},{5,7},{7,1},{8,10},{10,12},{12... | collective-permute-start | bytes 884744 | tf_op jit(solution)/shard_map/ppermute | solution.py:601
  27.6 14.4 %collective-permute-start.6 = (bf16[24,6144]{1,0:T(8,128)(2,1)S(1)}, bf16[24,6144]{1,0:T(8,128)(2,1)S(1)}, u32[]{:S(2)}, u32[]{:S(2)}) collective-permute-start(bf16[24,6144]{1,0:T(8,128)(2,1)S(1)} %constant_dynamic-slice_fusion.2.refs_0_), channel_id=1, source_target_pairs={{0,6},{2,0},{4,2},{6,4},{1,7},{3,1},{5,3},{7,5},{8,14},{10,8},{12,... | collective-permute-start | bytes 884744 | tf_op jit(solution)/shard_map/ppermute | solution.py:601
  42.7 15.1 %collective-permute-start.7 = (bf16[2,4,24,1536]{3,2,1,0:T(8,128)(2,1)S(1)}, bf16[2,4,24,1536]{3,2,1,0:T(8,128)(2,1)S(1)}, u32[]{:S(2)}, u32[]{:S(2)}) collective-permute-start(bf16[2,4,24,1536]{3,2,1,0:T(8,128)(2,1)S(1)} %place.16.refs_0_), channel_id=1, source_target_pairs={{0,16},{16,0},{1,17},{17,1},{2,18},{18,2},{3,19},{19,3},{4,20},{20... | collective-permute-start | bytes 1769480 | tf_op jit(solution)/shard_map/ppermute | solution.py:598
  43.2 14.8 %collective-permute-start.8 = (bf16[2,4,24,1536]{3,2,1,0:T(8,128)(2,1)S(1)}, bf16[2,4,24,1536]{3,2,1,0:T(8,128)(2,1)S(1)}, u32[]{:S(2)}, u32[]{:S(2)}) collective-permute-start(bf16[2,4,24,1536]{3,2,1,0:T(8,128)(2,1)S(1)} %place.17.refs_0_), channel_id=1, source_target_pairs={{0,1},{1,0},{2,3},{3,2},{4,5},{5,4},{6,7},{7,6},{8,9},{9,8},{10,11... | collective-permute-start | bytes 1769480 | tf_op jit(solution)/shard_map/ppermute | solution.py:598
  43.7 15.6 %collective-permute-start.9 = (bf16[24,6144]{1,0:T(8,128)(2,1)S(1)}, bf16[24,6144]{1,0:T(8,128)(2,1)S(1)}, u32[]{:S(2)}, u32[]{:S(2)}) collective-permute-start(bf16[24,6144]{1,0:T(8,128)(2,1)S(1)} %constant_dynamic-slice_fusion.2.refs_0_), channel_id=1, source_target_pairs={{0,4},{2,6},{4,0},{6,2},{1,5},{3,7},{5,1},{7,3},{8,12},{10,14},{12... | collective-permute-start | bytes 884744 | tf_op jit(solution)/shard_map/ppermute | solution.py:601
  59.3 23.6 %collective-permute-start.11 = (bf16[2,2,4,24,1536]{4,3,2,1,0:T(8,128)(2,1)S(1)}, bf16[2,2,4,24,1536]{4,3,2,1,0:T(8,128)(2,1)}, u32[]{:S(2)}, u32[]{:S(2)}) collective-permute-start(bf16[2,2,4,24,1536]{4,3,2,1,0:T(8,128)(2,1)S(1)} %place.19.refs_0_), channel_id=1, source_target_pairs={{0,8},{8,0},{1,9},{9,1},{2,10},{10,2},{3,11},{11,3},{4,12},{12,4},... | collective-permute-start | bytes 3538952 | tf_op jit(solution)/shard_map/ppermute | solution.py:598
  59.4 26.4 %collective-permute-start.10 = (bf16[2,2,4,24,1536]{4,3,2,1,0:T(8,128)(2,1)S(1)}, bf16[2,2,4,24,1536]{4,3,2,1,0:T(8,128)(2,1)S(1)}, u32[]{:S(2)}, u32[]{:S(2)}) collective-permute-start(bf16[2,2,4,24,1536]{4,3,2,1,0:T(8,128)(2,1)S(1)} %place.18.refs_0_), channel_id=1, source_target_pairs={{0,8},{8,0},{1,9},{9,1},{2,10},{10,2},{3,11},{11,3},{4,12},{12,4},... | collective-permute-start | bytes 3538952 | tf_op jit(solution)/shard_map/ppermute | solution.py:598
  62.5 24.0 %collective-permute-start.12 = (bf16[4,24,3072]{2,1,0:T(8,128)(2,1)}, bf16[4,24,3072]{2,1,0:T(8,128)(2,1)}, u32[]{:S(2)}, u32[]{:S(2)}) collective-permute-start(bf16[4,24,3072]{2,1,0:T(8,128)(2,1)} %get-tuple-element.205.refs_0_), channel_id=1, source_target_pairs={{0,1},{1,0},{2,3},{3,2},{4,5},{5,4},{6,7},{7,6},{8,9},{9,8},{10,11... | collective-permute-start | bytes 1769480 | tf_op jit(solution)/shard_map/ppermute | solution.py:598
  63.2 23.3 %collective-permute-start.13 = (bf16[4,24,3072]{2,1,0:T(8,128)(2,1)}, bf16[4,24,3072]{2,1,0:T(8,128)(2,1)}, u32[]{:S(2)}, u32[]{:S(2)}) collective-permute-start(bf16[4,24,3072]{2,1,0:T(8,128)(2,1)} %get-tuple-element.208.refs_0_), channel_id=1, source_target_pairs={{0,16},{16,0},{1,17},{17,1},{2,18},{18,2},{3,19},{19,3},{4,20},{20... | collective-permute-start | bytes 1769480 | tf_op jit(solution)/shard_map/ppermute | solution.py:598
  65.9 15.4 %all-to-all-start.1 = ((f32[8,2,6,768]{3,1,2,0:T(2,128)}), f32[8,2,6,768]{3,1,2,0:T(2,128)}, u32[]{:S(2)}, u32[]{:S(2)}) async-start(f32[8,2,6,768]{3,1,2,0:T(2,128)} %copy.53), calls=%async_computation.1 | async-start | bytes 589824 | tf_op jit(solution)/shard_map/all_to_all | solution.py:675
  90.2 27.2 %collective-permute-start.14 = (bf16[2,4,24,3072]{3,2,1,0:T(8,128)(2,1)S(1)}, bf16[2,4,24,3072]{3,2,1,0:T(8,128)(2,1)S(1)}, u32[]{:S(2)}, u32[]{:S(2)}) collective-permute-start(bf16[2,4,24,3072]{3,2,1,0:T(8,128)(2,1)S(1)} %place.22.refs_0_), channel_id=1, source_target_pairs={{0,16},{16,0},{1,17},{17,1},{2,18},{18,2},{3,19},{19,3},{4,20},{20... | collective-permute-start | bytes 3538952 | tf_op jit(solution)/shard_map/ppermute | solution.py:598
  91.7 26.8 %collective-permute-start.15 = (bf16[2,4,24,3072]{3,2,1,0:T(8,128)(2,1)S(1)}, bf16[2,4,24,3072]{3,2,1,0:T(8,128)(2,1)S(1)}, u32[]{:S(2)}, u32[]{:S(2)}) collective-permute-start(bf16[2,4,24,3072]{3,2,1,0:T(8,128)(2,1)S(1)} %place.23.refs_0_), channel_id=1, source_target_pairs={{0,1},{1,0},{2,3},{3,2},{4,5},{5,4},{6,7},{7,6},{8,9},{9,8},{10,11... | collective-permute-start | bytes 3538952 | tf_op jit(solution)/shard_map/ppermute | solution.py:598
  120.1 21.3 %collective-permute-start.17 = (bf16[2,2,4,24,3072]{4,3,2,1,0:T(8,128)(2,1)S(1)}, bf16[2,2,4,24,3072]{4,3,2,1,0:T(8,128)(2,1)}, u32[]{:S(2)}, u32[]{:S(2)}) collective-permute-start(bf16[2,2,4,24,3072]{4,3,2,1,0:T(8,128)(2,1)S(1)} %place.26.refs_0_), channel_id=1, source_target_pairs={{0,8},{8,0},{1,9},{9,1},{2,10},{10,2},{3,11},{11,3},{4,12},{12,4},... | collective-permute-start | bytes 7077896 | tf_op jit(solution)/shard_map/ppermute | solution.py:598
  141.3 18.6 %collective-permute-start.18 = (bf16[3,16,24,1024]{3,2,1,0:T(8,128)(2,1)}, bf16[3,16,24,1024]{3,2,1,0:T(8,128)(2,1)S(1)}, u32[]{:S(2)}, u32[]{:S(2)}) collective-permute-start(bf16[3,16,24,1024]{3,2,1,0:T(8,128)(2,1)} %get-tuple-element.241), channel_id=1, source_target_pairs={{0,8},{8,0},{1,9},{9,1},{2,10},{10,2},{3,11},{11,3},{4,12},{12,4},... | collective-permute-start | bytes 7077896 | tf_op jit(solution)/shard_map/ppermute | solution.py:598
  159.9 23.6 %collective-permute-start.21 = (bf16[3,16,24,1024]{3,2,1,0:T(8,128)(2,1)}, bf16[3,16,24,1024]{3,2,1,0:T(8,128)(2,1)S(1)}, u32[]{:S(2)}, u32[]{:S(2)}) collective-permute-start(bf16[3,16,24,1024]{3,2,1,0:T(8,128)(2,1)} %get-tuple-element.259), channel_id=1, source_target_pairs={{0,8},{8,0},{1,9},{9,1},{2,10},{10,2},{3,11},{11,3},{4,12},{12,4},... | collective-permute-start | bytes 7077896 | tf_op jit(solution)/shard_map/ppermute | solution.py:598
  162.5 20.9 %collective-permute-start.19 = (bf16[2,8,24,1024]{3,2,1,0:T(8,128)(2,1)}, bf16[2,8,24,1024]{3,2,1,0:T(8,128)(2,1)}, u32[]{:S(2)}, u32[]{:S(2)}) collective-permute-start(bf16[2,8,24,1024]{3,2,1,0:T(8,128)(2,1)} %bitcast.34), channel_id=1, source_target_pairs={{0,16},{16,0},{1,17},{17,1},{2,18},{18,2},{3,19},{19,3},{4,20},{20... | collective-permute-start | bytes 2359304 | tf_op jit(solution)/shard_map/ppermute | solution.py:598
  165.1 17.6 %collective-permute-start.20 = (bf16[1,8,24,1024]{3,2,1,0:T(8,128)(2,1)}, bf16[1,8,24,1024]{3,2,1,0:T(8,128)(2,1)S(1)}, u32[]{:S(2)}, u32[]{:S(2)}) collective-permute-start(bf16[1,8,24,1024]{3,2,1,0:T(8,128)(2,1)} %bitcast.38), channel_id=1, source_target_pairs={{0,1},{1,0},{2,3},{3,2},{4,5},{5,4},{6,7},{7,6},{8,9},{9,8},{10,11... | collective-permute-start | bytes 1179656 | tf_op jit(solution)/shard_map/ppermute | solution.py:598
  185.7 23.5 %collective-permute-start.24 = (bf16[2,8,24,1024]{3,2,1,0:T(8,128)(2,1)}, bf16[2,8,24,1024]{3,2,1,0:T(8,128)(2,1)S(1)}, u32[]{:S(2)}, u32[]{:S(2)}) collective-permute-start(bf16[2,8,24,1024]{3,2,1,0:T(8,128)(2,1)} %bitcast.52), channel_id=1, source_target_pairs={{0,16},{16,0},{1,17},{17,1},{2,18},{18,2},{3,19},{19,3},{4,20},{20... | collective-permute-start | bytes 2359304 | tf_op jit(solution)/shard_map/ppermute | solution.py:598
  189.2 19.9 %collective-permute-start.25 = (bf16[1,8,24,1024]{3,2,1,0:T(8,128)(2,1)}, bf16[1,8,24,1024]{3,2,1,0:T(8,128)(2,1)S(1)}, u32[]{:S(2)}, u32[]{:S(2)}) collective-permute-start(bf16[1,8,24,1024]{3,2,1,0:T(8,128)(2,1)} %bitcast.56), channel_id=1, source_target_pairs={{0,1},{1,0},{2,3},{3,2},{4,5},{5,4},{6,7},{7,6},{8,9},{9,8},{10,11... | collective-permute-start | bytes 1179656 | tf_op jit(solution)/shard_map/ppermute | solution.py:598
  190.8 18.3 %collective-permute-start.23 = (bf16[1,4,24,1024]{3,2,1,0:T(8,128)(2,1)S(1)}, bf16[1,4,24,1024]{3,2,1,0:T(8,128)(2,1)S(1)}, u32[]{:S(2)}, u32[]{:S(2)}) collective-permute-start(bf16[1,4,24,1024]{3,2,1,0:T(8,128)(2,1)S(1)} %bitcast.200), channel_id=1, source_target_pairs={{0,16},{16,0},{1,17},{17,1},{2,18},{18,2},{3,19},{19,3},{4,20},{20... | collective-permute-start | bytes 589832 | tf_op jit(solution)/shard_map/ppermute | solution.py:598
  192.6 16.5 %collective-permute-start.22 = (bf16[2,4,24,1024]{3,2,1,0:T(8,128)(2,1)S(1)}, bf16[2,4,24,1024]{3,2,1,0:T(8,128)(2,1)S(1)}, u32[]{:S(2)}, u32[]{:S(2)}) collective-permute-start(bf16[2,4,24,1024]{3,2,1,0:T(8,128)(2,1)S(1)} %bitcast.197), channel_id=1, source_target_pairs={{0,1},{1,0},{2,3},{3,2},{4,5},{5,4},{6,7},{7,6},{8,9},{9,8},{10,11... | collective-permute-start | bytes 1179656 | tf_op jit(solution)/shard_map/ppermute | solution.py:598
  209.2 15.3 %collective-permute-start.26 = (bf16[4,16,24,768]{3,2,1,0:T(8,128)(2,1)}, bf16[4,16,24,768]{3,2,1,0:T(8,128)(2,1)S(1)}, u32[]{:S(2)}, u32[]{:S(2)}) collective-permute-start(bf16[4,16,24,768]{3,2,1,0:T(8,128)(2,1)} %get-tuple-element.285), channel_id=1, source_target_pairs={{0,8},{8,0},{1,9},{9,1},{2,10},{10,2},{3,11},{11,3},{4,12},{12,4},... | collective-permute-start | bytes 7077896 | tf_op jit(solution)/shard_map/ppermute | solution.py:598
  209.5 14.0 %collective-permute-start.30 = (bf16[3,24,1024]{2,1,0:T(8,128)(2,1)S(1)}, bf16[3,24,1024]{2,1,0:T(8,128)(2,1)S(1)}, u32[]{:S(2)}, u32[]{:S(2)}) collective-permute-start(bf16[3,24,1024]{2,1,0:T(8,128)(2,1)S(1)} %get-tuple-element.300), channel_id=1, source_target_pairs={{0,4},{2,6},{4,0},{6,2},{1,5},{3,7},{5,1},{7,3},{8,12},{10,14},{12... | collective-permute-start | bytes 442376 | tf_op jit(solution)/shard_map/ppermute | solution.py:601
  211.3 12.2 %collective-permute-start.31 = (bf16[3,24,1024]{2,1,0:T(8,128)(2,1)S(1)}, bf16[3,24,1024]{2,1,0:T(8,128)(2,1)S(1)}, u32[]{:S(2)}, u32[]{:S(2)}) collective-permute-start(bf16[3,24,1024]{2,1,0:T(8,128)(2,1)S(1)} %get-tuple-element.301), channel_id=1, source_target_pairs={{0,6},{2,0},{4,2},{6,4},{1,7},{3,1},{5,3},{7,5},{8,14},{10,8},{12,... | collective-permute-start | bytes 442376 | tf_op jit(solution)/shard_map/ppermute | solution.py:601
  213.5 11.0 %collective-permute-start.27 = (bf16[2,4,24,1024]{3,2,1,0:T(8,128)(2,1)S(1)}, bf16[2,4,24,1024]{3,2,1,0:T(8,128)(2,1)S(1)}, u32[]{:S(2)}, u32[]{:S(2)}) collective-permute-start(bf16[2,4,24,1024]{3,2,1,0:T(8,128)(2,1)S(1)} %bitcast.196), channel_id=1, source_target_pairs={{0,1},{1,0},{2,3},{3,2},{4,5},{5,4},{6,7},{7,6},{8,9},{9,8},{10,11... | collective-permute-start | bytes 1179656 | tf_op jit(solution)/shard_map/ppermute | solution.py:598
  226.1 17.1 %collective-permute-start.33 = (bf16[2,8,24,768]{3,2,1,0:T(8,128)(2,1)S(1)}, bf16[2,8,24,768]{3,2,1,0:T(8,128)(2,1)S(1)}, u32[]{:S(2)}, u32[]{:S(2)}) collective-permute-start(bf16[2,8,24,768]{3,2,1,0:T(8,128)(2,1)S(1)} %bitcast.194), channel_id=1, source_target_pairs={{0,1},{1,0},{2,3},{3,2},{4,5},{5,4},{6,7},{7,6},{8,9},{9,8},{10,11... | collective-permute-start | bytes 1769480 | tf_op jit(solution)/shard_map/ppermute | solution.py:598
  229.0 14.1 %collective-permute-start.32 = (bf16[2,8,24,768]{3,2,1,0:T(8,128)(2,1)S(1)}, bf16[2,8,24,768]{3,2,1,0:T(8,128)(2,1)S(1)}, u32[]{:S(2)}, u32[]{:S(2)}) collective-permute-start(bf16[2,8,24,768]{3,2,1,0:T(8,128)(2,1)S(1)} %bitcast.195), channel_id=1, source_target_pairs={{0,16},{16,0},{1,17},{17,1},{2,18},{18,2},{3,19},{19,3},{4,20},{20... | collective-permute-start | bytes 1769480 | tf_op jit(solution)/shard_map/ppermute | solution.py:598
  230.6 8.7 %collective-permute-start.34 = (bf16[3,24,1024]{2,1,0:T(8,128)(2,1)S(1)}, bf16[3,24,1024]{2,1,0:T(8,128)(2,1)S(1)}, u32[]{:S(2)}, u32[]{:S(2)}) collective-permute-start(bf16[3,24,1024]{2,1,0:T(8,128)(2,1)S(1)} %get-tuple-element.319), channel_id=1, source_target_pairs={{0,2},{2,4},{4,6},{6,0},{1,3},{3,5},{5,7},{7,1},{8,10},{10,12},{12... | collective-permute-start | bytes 442376 | tf_op jit(solution)/shard_map/ppermute | solution.py:601
  232.9 10.1 %collective-permute-start.35 = (bf16[3,24,1024]{2,1,0:T(8,128)(2,1)S(1)}, bf16[3,24,1024]{2,1,0:T(8,128)(2,1)S(1)}, u32[]{:S(2)}, u32[]{:S(2)}) collective-permute-start(bf16[3,24,1024]{2,1,0:T(8,128)(2,1)S(1)} %get-tuple-element.320), channel_id=1, source_target_pairs={{0,4},{2,6},{4,0},{6,2},{1,5},{3,7},{5,1},{7,3},{8,12},{10,14},{12... | collective-permute-start | bytes 442376 | tf_op jit(solution)/shard_map/ppermute | solution.py:601
  233.2 9.8 %collective-permute-start.36 = (bf16[3,24,1024]{2,1,0:T(8,128)(2,1)S(1)}, bf16[3,24,1024]{2,1,0:T(8,128)(2,1)S(1)}, u32[]{:S(2)}, u32[]{:S(2)}) collective-permute-start(bf16[3,24,1024]{2,1,0:T(8,128)(2,1)S(1)} %get-tuple-element.321), channel_id=1, source_target_pairs={{0,6},{2,0},{4,2},{6,4},{1,7},{3,1},{5,3},{7,5},{8,14},{10,8},{12,... | collective-permute-start | bytes 442376 | tf_op jit(solution)/shard_map/ppermute | solution.py:601
  245.6 25.7 %all-to-all-start.2 = ((bf16[16,24,1024]{2,1,0:T(8,128)(2,1)}), bf16[16,24,1024]{2,1,0:T(8,128)(2,1)S(1)}, u32[]{:S(2)}, u32[]{:S(2)}) async-start(bf16[16,24,1024]{2,1,0:T(8,128)(2,1)} %slots.2), calls=%async_computation.2 | async-start | bytes 1572864 | tf_op jit(solution)/shard_map/all_to_all | solution.py:730
  253.2 13.6 %collective-permute-start.38 = (bf16[2,4,24,768]{3,2,1,0:T(8,128)(2,1)S(1)}, bf16[2,4,24,768]{3,2,1,0:T(8,128)(2,1)S(1)}, u32[]{:S(2)}, u32[]{:S(2)}) collective-permute-start(bf16[2,4,24,768]{3,2,1,0:T(8,128)(2,1)S(1)} %bitcast.198), channel_id=1, source_target_pairs={{0,16},{16,0},{1,17},{17,1},{2,18},{18,2},{3,19},{19,3},{4,20},{20... | collective-permute-start | bytes 884744 | tf_op jit(solution)/shard_map/ppermute | solution.py:598
  255.3 12.4 %collective-permute-start.37 = (bf16[2,4,24,768]{3,2,1,0:T(8,128)(2,1)S(1)}, bf16[2,4,24,768]{3,2,1,0:T(8,128)(2,1)S(1)}, u32[]{:S(2)}, u32[]{:S(2)}) collective-permute-start(bf16[2,4,24,768]{3,2,1,0:T(8,128)(2,1)S(1)} %bitcast.199), channel_id=1, source_target_pairs={{0,1},{1,0},{2,3},{3,2},{4,5},{5,4},{6,7},{7,6},{8,9},{9,8},{10,11... | collective-permute-start | bytes 884744 | tf_op jit(solution)/shard_map/ppermute | solution.py:598
  271.4 17.2 %collective-permute-start.42 = (bf16[16,24,1024]{2,1,0:T(8,128)(2,1)S(1)}, bf16[16,24,1024]{2,1,0:T(8,128)(2,1)S(1)}, u32[]{:S(2)}, u32[]{:S(2)}) collective-permute-start(bf16[16,24,1024]{2,1,0:T(8,128)(2,1)S(1)} %all-to-all-done.2.refs_0_), channel_id=1, source_target_pairs={{0,16},{16,0},{1,17},{17,1},{2,18},{18,2},{3,19},{19,3},{4,20},{20... | collective-permute-start | bytes 2359304 | tf_op jit(solution)/shard_map/ppermute | solution.py:598
  272.9 8.7 %collective-permute-start.39 = (bf16[4,24,768]{2,1,0:T(8,128)(2,1)S(1)}, bf16[4,24,768]{2,1,0:T(8,128)(2,1)S(1)}, u32[]{:S(2)}, u32[]{:S(2)}) collective-permute-start(bf16[4,24,768]{2,1,0:T(8,128)(2,1)S(1)} %get-tuple-element.337), channel_id=1, source_target_pairs={{0,2},{2,4},{4,6},{6,0},{1,3},{3,5},{5,7},{7,1},{8,10},{10,12},{12... | collective-permute-start | bytes 442376 | tf_op jit(solution)/shard_map/ppermute | solution.py:601
  274.0 10.8 %collective-permute-start.40 = (bf16[4,24,768]{2,1,0:T(8,128)(2,1)S(1)}, bf16[4,24,768]{2,1,0:T(8,128)(2,1)S(1)}, u32[]{:S(2)}, u32[]{:S(2)}) collective-permute-start(bf16[4,24,768]{2,1,0:T(8,128)(2,1)S(1)} %get-tuple-element.338), channel_id=1, source_target_pairs={{0,4},{2,6},{4,0},{6,2},{1,5},{3,7},{5,1},{7,3},{8,12},{10,14},{12... | collective-permute-start | bytes 442376 | tf_op jit(solution)/shard_map/ppermute | solution.py:601
  274.9 9.9 %collective-permute-start.41 = (bf16[4,24,768]{2,1,0:T(8,128)(2,1)S(1)}, bf16[4,24,768]{2,1,0:T(8,128)(2,1)S(1)}, u32[]{:S(2)}, u32[]{:S(2)}) collective-permute-start(bf16[4,24,768]{2,1,0:T(8,128)(2,1)S(1)} %get-tuple-element.339), channel_id=1, source_target_pairs={{0,6},{2,0},{4,2},{6,4},{1,7},{3,1},{5,3},{7,5},{8,14},{10,8},{12,... | collective-permute-start | bytes 442376 | tf_op jit(solution)/shard_map/ppermute | solution.py:601
  289.2 9.2 %collective-permute-start.43 = (bf16[2,2,4,2,24,1024]{5,4,3,2,1,0:T(8,128)(2,1)S(1)}, bf16[2,2,4,2,24,1024]{5,4,3,2,1,0:T(8,128)(2,1)}, u32[]{:S(2)}, u32[]{:S(2)}) collective-permute-start(bf16[2,2,4,2,24,1024]{5,4,3,2,1,0:T(8,128)(2,1)S(1)} %bitcast.161), channel_id=1, source_target_pairs={{0,8},{8,0},{1,9},{9,1},{2,10},{10,2},{3,11},{11,3},{4,12},{12,4},... | collective-permute-start | bytes 4718600 | tf_op jit(solution)/shard_map/ppermute | solution.py:598
  292.4 17.2 %collective-permute-start.44 = (bf16[24,9216]{1,0:T(8,128)(2,1)}, bf16[24,9216]{1,0:T(8,128)(2,1)S(1)}, u32[]{:S(2)}, u32[]{:S(2)}) collective-permute-start(bf16[24,9216]{1,0:T(8,128)(2,1)} %pack.2.refs_0_), channel_id=1, source_target_pairs={{0,16},{16,0},{1,17},{17,1},{2,18},{18,2},{3,19},{19,3},{4,20},{20... | collective-permute-start | bytes 1327112 | tf_op jit(solution)/shard_map/ppermute | solution.py:598
  294.1 29.1 %all-to-all-start.3 = ((bf16[16,40,768]{2,1,0:T(8,128)(2,1)}), bf16[16,40,768]{2,1,0:T(8,128)(2,1)S(1)}, u32[]{:S(2)}, u32[]{:S(2)}) async-start(bf16[16,40,768]{2,1,0:T(8,128)(2,1)} %slots.3), calls=%async_computation.3 | async-start | bytes 1966080 | tf_op jit(solution)/shard_map/all_to_all | solution.py:730
  345.4 9.9 %collective-permute-start.46 = (bf16[2,24,9216]{2,1,0:T(8,128)(2,1)S(1)}, bf16[2,24,9216]{2,1,0:T(8,128)(2,1)S(1)}, u32[]{:S(2)}, u32[]{:S(2)}) collective-permute-start(bf16[2,24,9216]{2,1,0:T(8,128)(2,1)S(1)} %place.30.refs_0_), channel_id=1, source_target_pairs={{0,8},{8,0},{1,9},{9,1},{2,10},{10,2},{3,11},{11,3},{4,12},{12,4},... | collective-permute-start | bytes 2654216 | tf_op jit(solution)/shard_map/ppermute | solution.py:598
  347.8 24.7 %all-to-all-start.4 = ((bf16[16,24,1024]{2,1,0:T(8,128)(2,1)}), bf16[16,24,1024]{2,1,0:T(8,128)(2,1)S(1)}, u32[]{:S(2)}, u32[]{:S(2)}) async-start(bf16[16,24,1024]{2,1,0:T(8,128)(2,1)} %bitcast.209), calls=%async_computation.4 | async-start | bytes 1572864 | tf_op jit(solution)/shard_map/all_to_all | solution.py:802
  372.6 16.0 %collective-permute-start.47 = (bf16[24,13824]{1,0:T(8,128)(2,1)S(1)}, bf16[24,13824]{1,0:T(8,128)(2,1)S(1)}, u32[]{:S(2)}, u32[]{:S(2)}) collective-permute-start(bf16[24,13824]{1,0:T(8,128)(2,1)S(1)} %pack.3.refs_0_), channel_id=1, source_target_pairs={{0,16},{16,0},{1,17},{17,1},{2,18},{18,2},{3,19},{19,3},{4,20},{20... | collective-permute-start | bytes 1990664 | tf_op jit(solution)/shard_map/ppermute | solution.py:598
  376.5 14.1 %collective-permute-start.48 = (bf16[24,13824]{1,0:T(8,128)(2,1)S(1)}, bf16[24,13824]{1,0:T(8,128)(2,1)S(1)}, u32[]{:S(2)}, u32[]{:S(2)}) collective-permute-start(bf16[24,13824]{1,0:T(8,128)(2,1)S(1)} %pack.3.refs_0_), channel_id=1, source_target_pairs={{0,8},{8,0},{1,9},{9,1},{2,10},{10,2},{3,11},{11,3},{4,12},{12,4},... | collective-permute-start | bytes 1990664 | tf_op jit(solution)/shard_map/ppermute | solution.py:598
  (46 other events, 232.9 us)

commit v7 on v6

--- a/solution.py
+++ b/solution.py
@@ -151,7 +151,7 @@
             pltpu.VMEM((D, D), BF16),
             pltpu.VMEM((D, D), BF16),
         ],
-        compiler_params=pltpu.CompilerParams(vmem_limit_bytes=40 * 1024 * 1024),
+        compiler_params=pltpu.CompilerParams(vmem_limit_bytes=32 * 1024 * 1024),
         cost_estimate=pl.CostEstimate(
             flops=NS_ITERS * 4 * D * D * (width + D), bytes_accessed=4 * D * width, transcendentals=0
         ),
@@ -1096,7 +1096,7 @@
             ).astype(BF16)
 
 
-BIG_VMEM = 58 * 1024 * 1024
+BIG_VMEM = 36 * 1024 * 1024
 
 
 def whole(array):

time: 402 us -> 396 us (0.985)
  Pallas kernels: 138 us -> 121 us
  waiting for transfers between devices: 135 us -> 148 us
    pallas_call x5, Pallas kernels: 77.9 us -> 65.4 us  [call(): pl.pallas_call(body, grid=grid, out_shape=outs, in_specs=in_specs, out_sp...]
    ppermute x35, waiting for transfers between devices: 63.6 us -> 74.5 us  [swap(): return lax.ppermute(value, axis, [(0, 1), (1, 0)])]
    unnamed x85 -> x137, local copies, waits for them, and re-layouts: 13.4 us -> 16 us
  transfers between devices with their start and end apart: 55 -> 55, of which waited for: 31 -> 33; matrix products, arithmetic and copies ran while one was open for 7% -> 6% of each run, Pallas kernels for 26% -> 23%
where the time goes in v7:
time: 396 us; the launch traced here: 391 us
  waiting for transfers between devices  148 us (37%)
  Pallas kernels  121 us (31%)
  starting transfers between devices  73.8 us (19%)
  local copies, waits for them, and re-layouts  22 us (6%)
  other arithmetic  18.8 us (5%)
  matrix products  5.23 us (1%)
    ppermute x35, waiting for transfers between devices, swap(): return lax.ppermute(value, axis, [(0, 1), (1, 0)])  74.5 us
    pallas_call x5, Pallas kernels, call(): pl.pallas_call(body, grid=grid, out_shape=outs, in_specs=in_specs, out_sp...  65.4 us
    ppermute x15, waiting for transfers between devices, shift(): return lax.ppermute(value, 'z', [(i, (i + by) % 4) for i in range(4)])  32.5 us
    ppermute x35, starting transfers between devices, swap(): return lax.ppermute(value, axis, [(0, 1), (1, 0)])  25.5 us
    ppermute x15, starting transfers between devices, shift(): return lax.ppermute(value, 'z', [(i, (i + by) % 4) for i in range(4)])  25.2 us
    all_to_all x2, waiting for transfers between devices, to_owners(): lax.all_to_all(pieces, self.chips, split_axis=0, concat_axis=0, tiled=True)  16.7 us
    pallas_call x2, Pallas kernels, newton_schulz(): pl.pallas_call(body, out_shape=jax.ShapeDtypeStruct((D, width), BF16), in...  16.4 us
    unnamed x137, local copies, waits for them, and re-layouts  16 us
  transfers between devices with their start and end apart: 55, of which 33 were waited for; matrix products, arithmetic and copies ran while one was open for 6% of the time, Pallas kernels for 23%

profile of v7, /device:TPU:0, one launch (start us, length us, event | category | flops | bytes accessed | tf_op | source)
XLA Modules:
  0.0 391.1 jit_solution(6083619078339858221)
XLA Ops:
  4.3 3.1 collective-permute-start
  7.4 2.6 collective-permute-start.1
  13.2 3.3 all-to-all-start
  20.7 3.1 all-to-all-done
  27.6 2.1 collective-permute-start.6
  29.7 2.6 collective-permute-done.4.refs_1_
  34.2 3.4 collective-permute-done.5.refs_1_
  38.3 3.7 collective-permute-done.6.refs_3_
  45.3 12.5 %collective-permute-done.7.refs_1_ = bf16[2,4,24,1536]{3,2,1,0:T(8,128)(2,1)S(1)} collective-permute-done((bf16[2,4,24,1536]{3,2,1,0:T(8,128)(2,1)S(1)}, bf16[2,4,24,1536]{3,2,1,0:T(8,128)(2,1)S(1)}, u32[]{:S(2)}, u32[]{:S(2)}) %collective-permute-start.7) | collective-permute-done | bytes 589856 | tf_op jit(solution)/shard_map/ppermute | solution.py:598
  65.9 4.2 %all-to-all-start.1 = ((f32[8,2,6,768]{3,1,2,0:T(2,128)}), f32[8,2,6,768]{3,1,2,0:T(2,128)}, u32[]{:S(2)}, u32[]{:S(2)}) async-start(f32[8,2,6,768]{3,1,2,0:T(2,128)} %copy.53), calls=%async_computation.1 | async-start | bytes 589824 | tf_op jit(solution)/shard_map/all_to_all | solution.py:675
  72.2 9.1 %all-to-all-done.1 = f32[8,2,6,768]{3,1,2,0:T(2,128)} async-done(((f32[8,2,6,768]{3,1,2,0:T(2,128)}), f32[8,2,6,768]{3,1,2,0:T(2,128)}, u32[]{:S(2)}, u32[]{:S(2)}) %all-to-all-start.1) | async-done | bytes 294944 | tf_op jit(solution)/shard_map/all_to_all | solution.py:675
  92.0 16.8 %attention_forward.1 = (bf16[2,256,768]{2,1,0:T(8,128)(2,1)S(1)}, bf16[2,256,768]{2,1,0:T(8,128)(2,1)S(1)}, bf16[2,256,768]{2,1,0:T(8,128)(2,1)S(1)}, bf16[2,256...) custom-call(s32[2]{0:T(128)S(1)} %mul.66.length_ref, ...), custom_call_target="tpu_custom_call" | custom-call | flops 2818572288 | bytes 21794824 | tf_op jit(solution)/shard_map/attention_forward/pallas_call | solution.py:1112
  111.5 3.8 collective-permute-done.14.refs_1_
  118.6 3.2 collective-permute-done.16.refs_1_
  122.7 2.2 copy-done.6
  124.9 13.5 %feed_forward.2 = (f32[512,768]{1,0:T(8,128)S(1)}, f32[512,768]{1,0:T(8,128)S(1)}, bf16[3,16,24,1024]{3,2,1,0:T(8,128)(2,1)S(1)}, bf16[3,16,24,1024]{3,2,1,0:T(8,128)(2,1)}) custom-call(s32[1]{0:T(128)} %bitcast.here_ref.c_ref, bf16[512,768]{1,0:T(8,128)(2,1)S(1)} %bitcast.217, bf16[512,768]{1,0:T(8,128)(2,1)S(1)} %bitcast.219, bf16[768,3072]{1,0:T(8,128)(2,1)} %bitcast.172, ...), custom_call_target="tpu_custom_call" | custom-call | flops 7247757312 | bytes 23592964 | tf_op jit(solution)/shard_map/feed_forward/pallas_call | solution.py:1112
  140.8 2.1 copy-done.5
  142.9 13.5 %feed_forward.3 = (f32[512,768]{1,0:T(8,128)S(1)}, f32[512,768]{1,0:T(8,128)S(1)}, bf16[3,16,24,1024]{3,2,1,0:T(8,128)(2,1)S(1)}, bf16[3,16,24,1024]{3,2,1,0:T(8,128)(2,1)}) custom-call(s32[1]{0:T(128)} %bitcast.here_ref.c_ref, bf16[512,768]{1,0:T(8,128)(2,1)S(1)} %bitcast.218, bf16[512,768]{1,0:T(8,128)(2,1)S(1)} %bitcast.220, bf16[768,3072]{1,0:T(8,128)(2,1)} %bitcast.169, ...), custom_call_target="tpu_custom_call" | custom-call | flops 7247757312 | bytes 23592964 | tf_op jit(solution)/shard_map/feed_forward/pallas_call | solution.py:1112
  156.6 2.5 fold.12
  162.3 14.1 %attention_backward.1 = (bf16[2,256,768]{2,1,0:T(8,128)(2,1)}, f32[2,256,768]{2,1,0:T(8,128)S(1)}, bf16[4,2,256,768]{3,2,1,0:T(8,128)(2,1)}, f32[2,8,768]{2,1,0:T(8,128)S(1)}) custom-call(s32[2]{0:T(128)S(1)} %mul.66.length_ref, f32[2,256,768]{2,1,0:T(8,128)S(1)} %bitcast.178, f32[2,256,768]{2,1,0:T(8,128)S(1)} %bitcast.180, f32[2,256,768]{2,1,0:T(8,128)S(1)} %bitcast.179, ...), custom_call_target="tpu_custom_call" | custom-call | flops 1610612736 | bytes 27349000 | tf_op jit(solution)/shard_map/attention_backward/pallas_call | solution.py:1112
  176.4 2.3 collective-permute-done.19
  186.5 7.5 %projection_backward.1 = (bf16[4,16,24,768]{3,2,1,0:T(8,128)(2,1)S(1)}, bf16[4,16,24,768]{3,2,1,0:T(8,128)(2,1)S(1)}, f32[2,256,768]{2,1,0:T(8,128)}, bf16[2,8,768]{2,1,0:T(8,128)(2,1)S(1)}) custom-call(s32[1]{0:T(128)} %bitcast.here_ref.c_ref, bf16[4,2,256,768]{3,2,1,0:T(8,128)(2,1)S(1)} %copy-done.35, bf16[2,256,768]{2,1,0:T(8,128)(2,1)S(1)} %copy-done.44, ...), custom_call_target="tpu_custom_call" | custom-call | flops 4227858432 | bytes 18201604 | tf_op jit(solution)/shard_map/projection_backward/pallas_call | solution.py:1112
  194.0 9.3 %collective-permute-done.23.refs_3_ = bf16[1,4,24,1024]{3,2,1,0:T(8,128)(2,1)S(1)} collective-permute-done((bf16[1,4,24,1024]{3,2,1,0:T(8,128)(2,1)S(1)}, bf16[1,4,24,1024]{3,2,1,0:T(8,128)(2,1)S(1)}, u32[]{:S(2)}, u32[]{:S(2)}) %collective-permute-start.23) | collective-permute-done | bytes 196640 | tf_op jit(solution)/shard_map/ppermute | solution.py:598
  204.8 2.6 collective-permute-start.31
  208.3 3.8 collective-permute-done.29
  212.7 4.9 %collective-permute-done.30 = bf16[3,24,1024]{2,1,0:T(8,128)(2,1)S(1)} collective-permute-done((bf16[3,24,1024]{2,1,0:T(8,128)(2,1)S(1)}, bf16[3,24,1024]{2,1,0:T(8,128)(2,1)S(1)}, u32[]{:S(2)}, u32[]{:S(2)}) %collective-permute-start.30) | collective-permute-done | bytes 147488 | tf_op jit(solution)/shard_map/ppermute | solution.py:601
  222.8 2.4 collective-permute-start.34
  225.4 2.1 collective-permute-start.36
  227.5 4.0 %collective-permute-done.34 = bf16[3,24,1024]{2,1,0:T(8,128)(2,1)S(1)} collective-permute-done((bf16[3,24,1024]{2,1,0:T(8,128)(2,1)S(1)}, bf16[3,24,1024]{2,1,0:T(8,128)(2,1)S(1)}, u32[]{:S(2)}, u32[]{:S(2)}) %collective-permute-start.34) | collective-permute-done | bytes 147488 | tf_op jit(solution)/shard_map/ppermute | solution.py:601
  231.5 3.8 collective-permute-done.35
  236.3 2.2 slots.2
  238.5 7.4 %all-to-all-start.2 = ((bf16[16,24,1024]{2,1,0:T(8,128)(2,1)}), bf16[16,24,1024]{2,1,0:T(8,128)(2,1)S(1)}, u32[]{:S(2)}, u32[]{:S(2)}) async-start(bf16[16,24,1024]{2,1,0:T(8,128)(2,1)} %slots.2), calls=%async_computation.2 | async-start | bytes 1572864 | tf_op jit(solution)/shard_map/all_to_all | solution.py:730
  250.9 9.9 %collective-permute-done.38.refs_3_ = bf16[2,4,24,768]{3,2,1,0:T(8,128)(2,1)S(1)} collective-permute-done((bf16[2,4,24,768]{3,2,1,0:T(8,128)(2,1)S(1)}, bf16[2,4,24,768]{3,2,1,0:T(8,128)(2,1)S(1)}, u32[]{:S(2)}, u32[]{:S(2)}) %collective-permute-start.38) | collective-permute-done | bytes 294944 | tf_op jit(solution)/shard_map/ppermute | solution.py:598
  261.8 3.7 all-to-all-done.2.refs_0_
  271.0 4.6 %collective-permute-done.39 = bf16[4,24,768]{2,1,0:T(8,128)(2,1)S(1)} collective-permute-done((bf16[4,24,768]{2,1,0:T(8,128)(2,1)S(1)}, bf16[4,24,768]{2,1,0:T(8,128)(2,1)S(1)}, u32[]{:S(2)}, u32[]{:S(2)}) %collective-permute-start.39) | collective-permute-done | bytes 147488 | tf_op jit(solution)/shard_map/ppermute | solution.py:601
  275.6 3.2 collective-permute-done.40
  279.0 3.7 collective-permute-done.42.refs_1_
  283.4 2.2 slots.3
  288.2 4.3 %all-to-all-start.3 = ((bf16[16,40,768]{2,1,0:T(8,128)(2,1)}), bf16[16,40,768]{2,1,0:T(8,128)(2,1)S(1)}, u32[]{:S(2)}, u32[]{:S(2)}) async-start(bf16[16,40,768]{2,1,0:T(8,128)(2,1)} %slots.3), calls=%async_computation.3 | async-start | bytes 1966080 | tf_op jit(solution)/shard_map/all_to_all | solution.py:730
  296.0 7.6 %collective-permute-done.44.refs_1_ = bf16[24,9216]{1,0:T(8,128)(2,1)S(1)} collective-permute-done((bf16[24,9216]{1,0:T(8,128)(2,1)}, bf16[24,9216]{1,0:T(8,128)(2,1)S(1)}, u32[]{:S(2)}, u32[]{:S(2)}) %collective-permute-start.44) | collective-permute-done | bytes 442400 | tf_op jit(solution)/shard_map/ppermute | solution.py:598
  304.3 13.0 %all-to-all-done.3.mine_ref = bf16[16,40,768]{2,1,0:T(8,128)(2,1)S(1)} async-done(((bf16[16,40,768]{2,1,0:T(8,128)(2,1)}), bf16[16,40,768]{2,1,0:T(8,128)(2,1)S(1)}, u32[]{:S(2)}, u32[]{:S(2)}) %all-to-all-start.3) | async-done | bytes 983072 | tf_op jit(solution)/shard_map/all_to_all | solution.py:730
  317.3 2.6 collective-permute-done.45.other_ref
  320.5 16.2 %newton_schulz.3 = bf16[768,768]{1,0:T(8,128)(2,1)S(1)} custom-call(s32[1]{0:T(128)} %bitcast.90.active_ref, bf16[768,768]{1,0:T(8,128)(2,1)S(1)} %bitcast.204, bf16[64,768]{1,0:T(8,128)(2,1)S(1)} %bitcast.202, bf16[64,768]{1,0:T(8,128)(2,1)S(1)} %fusion.13.right_ref), custom_call_target="tpu_custom_call" | custom-call | flops 18119393280 | bytes 2359296 | tf_op jit(solution)/shard_map/newton_schulz/pallas_call | solution.py:142
  341.9 3.9 all-to-all-start.4
  345.8 3.9 multiply_add_fusion
  355.1 11.8 %all-to-all-done.4.refs_0_ = bf16[16,24,1024]{2,1,0:T(8,128)(2,1)S(1)} async-done(((bf16[16,24,1024]{2,1,0:T(8,128)(2,1)}), bf16[16,24,1024]{2,1,0:T(8,128)(2,1)S(1)}, u32[]{:S(2)}, u32[]{:S(2)}) %all-to-all-start.4) | async-done | bytes 786464 | tf_op jit(solution)/shard_map/all_to_all | solution.py:802
  370.8 12.0 %collective-permute-done.47.refs_1_ = bf16[24,13824]{1,0:T(8,128)(2,1)S(1)} collective-permute-done((bf16[24,13824]{1,0:T(8,128)(2,1)S(1)}, bf16[24,13824]{1,0:T(8,128)(2,1)S(1)}, u32[]{:S(2)}, u32[]{:S(2)}) %collective-permute-start.47) | collective-permute-done | bytes 663584 | tf_op jit(solution)/shard_map/ppermute | solution.py:598
  384.9 5.7 %update.1 = (f32[6,96,768]{2,1,0:T(8,128)}, f32[3,96,768]{2,1,0:T(8,128)}, f32[96,768]{1,0:T(8,128)}, f32[2,96,2048]{2,1,0:T(8,128)}, f32[96,2048]{1,0:T(8,128)}) custom-call(s32[4]{0:T(128)S(1)} %pad_add_fusion.5.slot_ref, bf16[24,13824]{1,0:T(8,128)(2,1)S(1)} %pack.3.refs_0_, bf16[24,13824]{1,0:T(8,128)(2,1)S(1)} %collective-permute-done.47.refs_1_, ...), custom_call_target="tpu_custom_call" | custom-call | bytes 14000000 | tf_op jit(solution)/shard_map/update/pallas_call | solution.py:443
  (290 shorter events, 107.1 us)
Async XLA Ops:
  4.3 14.2 %collective-permute-start = (bf16[24,3072]{1,0:T(8,128)(2,1)S(1)}, bf16[24,3072]{1,0:T(8,128)(2,1)S(1)}, u32[]{:S(2)}, u32[]{:S(2)}) collective-permute-start(bf16[24,3072]{1,0:T(8,128)(2,1)S(1)} %fusion.12.refs_0_), channel_id=1, source_target_pairs={{0,2},{2,4},{4,6},{6,0},{1,3},{3,5},{5,7},{7,1},{8,10},{10,12},{12... | collective-permute-start | bytes 442376 | tf_op jit(solution)/shard_map/ppermute | solution.py:601
  7.4 12.3 %collective-permute-start.1 = (bf16[24,3072]{1,0:T(8,128)(2,1)S(1)}, bf16[24,3072]{1,0:T(8,128)(2,1)S(1)}, u32[]{:S(2)}, u32[]{:S(2)}) collective-permute-start(bf16[24,3072]{1,0:T(8,128)(2,1)S(1)} %fusion.12.refs_0_), channel_id=1, source_target_pairs={{0,4},{2,6},{4,0},{6,2},{1,5},{3,7},{5,1},{7,3},{8,12},{10,14},{12... | collective-permute-start | bytes 442376 | tf_op jit(solution)/shard_map/ppermute | solution.py:601
  10.0 9.7 %collective-permute-start.2 = (bf16[24,3072]{1,0:T(8,128)(2,1)S(1)}, bf16[24,3072]{1,0:T(8,128)(2,1)}, u32[]{:S(2)}, u32[]{:S(2)}) collective-permute-start(bf16[24,3072]{1,0:T(8,128)(2,1)S(1)} %fusion.12.refs_0_), channel_id=1, source_target_pairs={{0,6},{2,0},{4,2},{6,4},{1,7},{3,1},{5,3},{7,5},{8,14},{10,8},{12,... | collective-permute-start | bytes 442376 | tf_op jit(solution)/shard_map/ppermute | solution.py:601
  13.2 10.6 %all-to-all-start = ((bf16[8,2,96]{2,1,0:T(2,128)(2,1)}), bf16[8,2,96]{2,1,0:T(2,128)(2,1)S(1)}, u32[]{:S(2)}, u32[]{:S(2)}) async-start(bf16[8,2,96]{2,1,0:T(2,128)(2,1)} %bitcast.149), calls=%async_computation | async-start | bytes 8192 | tf_op jit(solution)/shard_map/all_to_all | solution.py:675
  25.8 11.7 %collective-permute-start.5 = (bf16[24,6144]{1,0:T(8,128)(2,1)S(1)}, bf16[24,6144]{1,0:T(8,128)(2,1)S(1)}, u32[]{:S(2)}, u32[]{:S(2)}) collective-permute-start(bf16[24,6144]{1,0:T(8,128)(2,1)S(1)} %constant_dynamic-slice_fusion.2.refs_0_), channel_id=1, source_target_pairs={{0,2},{2,4},{4,6},{6,0},{1,3},{3,5},{5,7},{7,1},{8,10},{10,12},{12... | collective-permute-start | bytes 884744 | tf_op jit(solution)/shard_map/ppermute | solution.py:601
  27.6 14.4 %collective-permute-start.6 = (bf16[24,6144]{1,0:T(8,128)(2,1)S(1)}, bf16[24,6144]{1,0:T(8,128)(2,1)S(1)}, u32[]{:S(2)}, u32[]{:S(2)}) collective-permute-start(bf16[24,6144]{1,0:T(8,128)(2,1)S(1)} %constant_dynamic-slice_fusion.2.refs_0_), channel_id=1, source_target_pairs={{0,6},{2,0},{4,2},{6,4},{1,7},{3,1},{5,3},{7,5},{8,14},{10,8},{12,... | collective-permute-start | bytes 884744 | tf_op jit(solution)/shard_map/ppermute | solution.py:601
  42.7 15.1 %collective-permute-start.7 = (bf16[2,4,24,1536]{3,2,1,0:T(8,128)(2,1)S(1)}, bf16[2,4,24,1536]{3,2,1,0:T(8,128)(2,1)S(1)}, u32[]{:S(2)}, u32[]{:S(2)}) collective-permute-start(bf16[2,4,24,1536]{3,2,1,0:T(8,128)(2,1)S(1)} %place.16.refs_0_), channel_id=1, source_target_pairs={{0,16},{16,0},{1,17},{17,1},{2,18},{18,2},{3,19},{19,3},{4,20},{20... | collective-permute-start | bytes 1769480 | tf_op jit(solution)/shard_map/ppermute | solution.py:598
  43.2 14.8 %collective-permute-start.8 = (bf16[2,4,24,1536]{3,2,1,0:T(8,128)(2,1)S(1)}, bf16[2,4,24,1536]{3,2,1,0:T(8,128)(2,1)S(1)}, u32[]{:S(2)}, u32[]{:S(2)}) collective-permute-start(bf16[2,4,24,1536]{3,2,1,0:T(8,128)(2,1)S(1)} %place.17.refs_0_), channel_id=1, source_target_pairs={{0,1},{1,0},{2,3},{3,2},{4,5},{5,4},{6,7},{7,6},{8,9},{9,8},{10,11... | collective-permute-start | bytes 1769480 | tf_op jit(solution)/shard_map/ppermute | solution.py:598
  43.7 15.6 %collective-permute-start.9 = (bf16[24,6144]{1,0:T(8,128)(2,1)S(1)}, bf16[24,6144]{1,0:T(8,128)(2,1)S(1)}, u32[]{:S(2)}, u32[]{:S(2)}) collective-permute-start(bf16[24,6144]{1,0:T(8,128)(2,1)S(1)} %constant_dynamic-slice_fusion.2.refs_0_), channel_id=1, source_target_pairs={{0,4},{2,6},{4,0},{6,2},{1,5},{3,7},{5,1},{7,3},{8,12},{10,14},{12... | collective-permute-start | bytes 884744 | tf_op jit(solution)/shard_map/ppermute | solution.py:601
  59.4 23.6 %collective-permute-start.11 = (bf16[2,2,4,24,1536]{4,3,2,1,0:T(8,128)(2,1)S(1)}, bf16[2,2,4,24,1536]{4,3,2,1,0:T(8,128)(2,1)}, u32[]{:S(2)}, u32[]{:S(2)}) collective-permute-start(bf16[2,2,4,24,1536]{4,3,2,1,0:T(8,128)(2,1)S(1)} %place.19.refs_0_), channel_id=1, source_target_pairs={{0,8},{8,0},{1,9},{9,1},{2,10},{10,2},{3,11},{11,3},{4,12},{12,4},... | collective-permute-start | bytes 3538952 | tf_op jit(solution)/shard_map/ppermute | solution.py:598
  59.4 25.0 %collective-permute-start.10 = (bf16[2,2,4,24,1536]{4,3,2,1,0:T(8,128)(2,1)S(1)}, bf16[2,2,4,24,1536]{4,3,2,1,0:T(8,128)(2,1)S(1)}, u32[]{:S(2)}, u32[]{:S(2)}) collective-permute-start(bf16[2,2,4,24,1536]{4,3,2,1,0:T(8,128)(2,1)S(1)} %place.18.refs_0_), channel_id=1, source_target_pairs={{0,8},{8,0},{1,9},{9,1},{2,10},{10,2},{3,11},{11,3},{4,12},{12,4},... | collective-permute-start | bytes 3538952 | tf_op jit(solution)/shard_map/ppermute | solution.py:598
  62.5 22.6 %collective-permute-start.12 = (bf16[4,24,3072]{2,1,0:T(8,128)(2,1)}, bf16[4,24,3072]{2,1,0:T(8,128)(2,1)}, u32[]{:S(2)}, u32[]{:S(2)}) collective-permute-start(bf16[4,24,3072]{2,1,0:T(8,128)(2,1)} %get-tuple-element.205.refs_0_), channel_id=1, source_target_pairs={{0,1},{1,0},{2,3},{3,2},{4,5},{5,4},{6,7},{7,6},{8,9},{9,8},{10,11... | collective-permute-start | bytes 1769480 | tf_op jit(solution)/shard_map/ppermute | solution.py:598
  63.2 22.0 %collective-permute-start.13 = (bf16[4,24,3072]{2,1,0:T(8,128)(2,1)}, bf16[4,24,3072]{2,1,0:T(8,128)(2,1)}, u32[]{:S(2)}, u32[]{:S(2)}) collective-permute-start(bf16[4,24,3072]{2,1,0:T(8,128)(2,1)} %get-tuple-element.208.refs_0_), channel_id=1, source_target_pairs={{0,16},{16,0},{1,17},{17,1},{2,18},{18,2},{3,19},{19,3},{4,20},{20... | collective-permute-start | bytes 1769480 | tf_op jit(solution)/shard_map/ppermute | solution.py:598
  65.9 15.4 %all-to-all-start.1 = ((f32[8,2,6,768]{3,1,2,0:T(2,128)}), f32[8,2,6,768]{3,1,2,0:T(2,128)}, u32[]{:S(2)}, u32[]{:S(2)}) async-start(f32[8,2,6,768]{3,1,2,0:T(2,128)} %copy.53), calls=%async_computation.1 | async-start | bytes 589824 | tf_op jit(solution)/shard_map/all_to_all | solution.py:675
  88.1 27.2 %collective-permute-start.14 = (bf16[2,4,24,3072]{3,2,1,0:T(8,128)(2,1)S(1)}, bf16[2,4,24,3072]{3,2,1,0:T(8,128)(2,1)S(1)}, u32[]{:S(2)}, u32[]{:S(2)}) collective-permute-start(bf16[2,4,24,3072]{3,2,1,0:T(8,128)(2,1)S(1)} %place.22.refs_0_), channel_id=1, source_target_pairs={{0,16},{16,0},{1,17},{17,1},{2,18},{18,2},{3,19},{19,3},{4,20},{20... | collective-permute-start | bytes 3538952 | tf_op jit(solution)/shard_map/ppermute | solution.py:598
  89.7 26.8 %collective-permute-start.15 = (bf16[2,4,24,3072]{3,2,1,0:T(8,128)(2,1)S(1)}, bf16[2,4,24,3072]{3,2,1,0:T(8,128)(2,1)S(1)}, u32[]{:S(2)}, u32[]{:S(2)}) collective-permute-start(bf16[2,4,24,3072]{3,2,1,0:T(8,128)(2,1)S(1)} %place.23.refs_0_), channel_id=1, source_target_pairs={{0,1},{1,0},{2,3},{3,2},{4,5},{5,4},{6,7},{7,6},{8,9},{9,8},{10,11... | collective-permute-start | bytes 3538952 | tf_op jit(solution)/shard_map/ppermute | solution.py:598
  118.0 20.5 %collective-permute-start.17 = (bf16[2,2,4,24,3072]{4,3,2,1,0:T(8,128)(2,1)S(1)}, bf16[2,2,4,24,3072]{4,3,2,1,0:T(8,128)(2,1)S(1)}, u32[]{:S(2)}, u32[]{:S(2)}) collective-permute-start(bf16[2,2,4,24,3072]{4,3,2,1,0:T(8,128)(2,1)S(1)} %place.26.refs_0_), channel_id=1, source_target_pairs={{0,8},{8,0},{1,9},{9,1},{2,10},{10,2},{3,11},{11,3},{4,12},{12,4},... | collective-permute-start | bytes 7077896 | tf_op jit(solution)/shard_map/ppermute | solution.py:598
  138.4 18.0 %collective-permute-start.18 = (bf16[3,16,24,1024]{3,2,1,0:T(8,128)(2,1)}, bf16[3,16,24,1024]{3,2,1,0:T(8,128)(2,1)S(1)}, u32[]{:S(2)}, u32[]{:S(2)}) collective-permute-start(bf16[3,16,24,1024]{3,2,1,0:T(8,128)(2,1)} %get-tuple-element.241), channel_id=1, source_target_pairs={{0,8},{8,0},{1,9},{9,1},{2,10},{10,2},{3,11},{11,3},{4,12},{12,4},... | collective-permute-start | bytes 7077896 | tf_op jit(solution)/shard_map/ppermute | solution.py:598
  156.4 22.3 %collective-permute-start.21 = (bf16[3,16,24,1024]{3,2,1,0:T(8,128)(2,1)}, bf16[3,16,24,1024]{3,2,1,0:T(8,128)(2,1)S(1)}, u32[]{:S(2)}, u32[]{:S(2)}) collective-permute-start(bf16[3,16,24,1024]{3,2,1,0:T(8,128)(2,1)} %get-tuple-element.259), channel_id=1, source_target_pairs={{0,8},{8,0},{1,9},{9,1},{2,10},{10,2},{3,11},{11,3},{4,12},{12,4},... | collective-permute-start | bytes 7077896 | tf_op jit(solution)/shard_map/ppermute | solution.py:598
  159.1 19.6 %collective-permute-start.19 = (bf16[2,8,24,1024]{3,2,1,0:T(8,128)(2,1)S(1)}, bf16[2,8,24,1024]{3,2,1,0:T(8,128)(2,1)S(1)}, u32[]{:S(2)}, u32[]{:S(2)}) collective-permute-start(bf16[2,8,24,1024]{3,2,1,0:T(8,128)(2,1)S(1)} %bitcast.206), channel_id=1, source_target_pairs={{0,16},{16,0},{1,17},{17,1},{2,18},{18,2},{3,19},{19,3},{4,20},{20... | collective-permute-start | bytes 2359304 | tf_op jit(solution)/shard_map/ppermute | solution.py:598
  161.2 15.2 %collective-permute-start.20 = (bf16[1,8,24,1024]{3,2,1,0:T(8,128)(2,1)S(1)}, bf16[1,8,24,1024]{3,2,1,0:T(8,128)(2,1)S(1)}, u32[]{:S(2)}, u32[]{:S(2)}) collective-permute-start(bf16[1,8,24,1024]{3,2,1,0:T(8,128)(2,1)S(1)} %bitcast.212), channel_id=1, source_target_pairs={{0,1},{1,0},{2,3},{3,2},{4,5},{5,4},{6,7},{7,6},{8,9},{9,8},{10,11... | collective-permute-start | bytes 1179656 | tf_op jit(solution)/shard_map/ppermute | solution.py:598
  180.3 23.0 %collective-permute-start.24 = (bf16[2,8,24,1024]{3,2,1,0:T(8,128)(2,1)S(1)}, bf16[2,8,24,1024]{3,2,1,0:T(8,128)(2,1)S(1)}, u32[]{:S(2)}, u32[]{:S(2)}) collective-permute-start(bf16[2,8,24,1024]{3,2,1,0:T(8,128)(2,1)S(1)} %bitcast.205), channel_id=1, source_target_pairs={{0,16},{16,0},{1,17},{17,1},{2,18},{18,2},{3,19},{19,3},{4,20},{20... | collective-permute-start | bytes 2359304 | tf_op jit(solution)/shard_map/ppermute | solution.py:598
  182.4 20.8 %collective-permute-start.25 = (bf16[1,8,24,1024]{3,2,1,0:T(8,128)(2,1)S(1)}, bf16[1,8,24,1024]{3,2,1,0:T(8,128)(2,1)S(1)}, u32[]{:S(2)}, u32[]{:S(2)}) collective-permute-start(bf16[1,8,24,1024]{3,2,1,0:T(8,128)(2,1)S(1)} %bitcast.209), channel_id=1, source_target_pairs={{0,1},{1,0},{2,3},{3,2},{4,5},{5,4},{6,7},{7,6},{8,9},{9,8},{10,11... | collective-permute-start | bytes 1179656 | tf_op jit(solution)/shard_map/ppermute | solution.py:598
  183.1 20.1 %collective-permute-start.23 = (bf16[1,4,24,1024]{3,2,1,0:T(8,128)(2,1)S(1)}, bf16[1,4,24,1024]{3,2,1,0:T(8,128)(2,1)S(1)}, u32[]{:S(2)}, u32[]{:S(2)}) collective-permute-start(bf16[1,4,24,1024]{3,2,1,0:T(8,128)(2,1)S(1)} %bitcast.215), channel_id=1, source_target_pairs={{0,16},{16,0},{1,17},{17,1},{2,18},{18,2},{3,19},{19,3},{4,20},{20... | collective-permute-start | bytes 589832 | tf_op jit(solution)/shard_map/ppermute | solution.py:598
  184.9 18.4 %collective-permute-start.22 = (bf16[2,4,24,1024]{3,2,1,0:T(8,128)(2,1)S(1)}, bf16[2,4,24,1024]{3,2,1,0:T(8,128)(2,1)S(1)}, u32[]{:S(2)}, u32[]{:S(2)}) collective-permute-start(bf16[2,4,24,1024]{3,2,1,0:T(8,128)(2,1)S(1)} %bitcast.211), channel_id=1, source_target_pairs={{0,1},{1,0},{2,3},{3,2},{4,5},{5,4},{6,7},{7,6},{8,9},{9,8},{10,11... | collective-permute-start | bytes 1179656 | tf_op jit(solution)/shard_map/ppermute | solution.py:598
  203.3 15.3 %collective-permute-start.26 = (bf16[4,16,24,768]{3,2,1,0:T(8,128)(2,1)S(1)}, bf16[4,16,24,768]{3,2,1,0:T(8,128)(2,1)S(1)}, u32[]{:S(2)}, u32[]{:S(2)}) collective-permute-start(bf16[4,16,24,768]{3,2,1,0:T(8,128)(2,1)S(1)} %get-tuple-element.285), channel_id=1, source_target_pairs={{0,8},{8,0},{1,9},{9,1},{2,10},{10,2},{3,11},{11,3},{4,12},{12,4},... | collective-permute-start | bytes 7077896 | tf_op jit(solution)/shard_map/ppermute | solution.py:598
  203.6 14.0 %collective-permute-start.30 = (bf16[3,24,1024]{2,1,0:T(8,128)(2,1)S(1)}, bf16[3,24,1024]{2,1,0:T(8,128)(2,1)S(1)}, u32[]{:S(2)}, u32[]{:S(2)}) collective-permute-start(bf16[3,24,1024]{2,1,0:T(8,128)(2,1)S(1)} %get-tuple-element.300), channel_id=1, source_target_pairs={{0,4},{2,6},{4,0},{6,2},{1,5},{3,7},{5,1},{7,3},{8,12},{10,14},{12... | collective-permute-start | bytes 442376 | tf_op jit(solution)/shard_map/ppermute | solution.py:601
  204.8 12.7 %collective-permute-start.31 = (bf16[3,24,1024]{2,1,0:T(8,128)(2,1)S(1)}, bf16[3,24,1024]{2,1,0:T(8,128)(2,1)S(1)}, u32[]{:S(2)}, u32[]{:S(2)}) collective-permute-start(bf16[3,24,1024]{2,1,0:T(8,128)(2,1)S(1)} %get-tuple-element.301), channel_id=1, source_target_pairs={{0,6},{2,0},{4,2},{6,4},{1,7},{3,1},{5,3},{7,5},{8,14},{10,8},{12,... | collective-permute-start | bytes 442376 | tf_op jit(solution)/shard_map/ppermute | solution.py:601
  207.6 11.0 %collective-permute-start.27 = (bf16[2,4,24,1024]{3,2,1,0:T(8,128)(2,1)S(1)}, bf16[2,4,24,1024]{3,2,1,0:T(8,128)(2,1)S(1)}, u32[]{:S(2)}, u32[]{:S(2)}) collective-permute-start(bf16[2,4,24,1024]{3,2,1,0:T(8,128)(2,1)S(1)} %bitcast.210), channel_id=1, source_target_pairs={{0,1},{1,0},{2,3},{3,2},{4,5},{5,4},{6,7},{7,6},{8,9},{9,8},{10,11... | collective-permute-start | bytes 1179656 | tf_op jit(solution)/shard_map/ppermute | solution.py:598
  220.2 15.2 %collective-permute-start.33 = (bf16[2,8,24,768]{3,2,1,0:T(8,128)(2,1)S(1)}, bf16[2,8,24,768]{3,2,1,0:T(8,128)(2,1)S(1)}, u32[]{:S(2)}, u32[]{:S(2)}) collective-permute-start(bf16[2,8,24,768]{3,2,1,0:T(8,128)(2,1)S(1)} %bitcast.207), channel_id=1, source_target_pairs={{0,1},{1,0},{2,3},{3,2},{4,5},{5,4},{6,7},{7,6},{8,9},{9,8},{10,11... | collective-permute-start | bytes 1769480 | tf_op jit(solution)/shard_map/ppermute | solution.py:598
  222.2 14.1 %collective-permute-start.32 = (bf16[2,8,24,768]{3,2,1,0:T(8,128)(2,1)S(1)}, bf16[2,8,24,768]{3,2,1,0:T(8,128)(2,1)S(1)}, u32[]{:S(2)}, u32[]{:S(2)}) collective-permute-start(bf16[2,8,24,768]{3,2,1,0:T(8,128)(2,1)S(1)} %bitcast.208), channel_id=1, source_target_pairs={{0,16},{16,0},{1,17},{17,1},{2,18},{18,2},{3,19},{19,3},{4,20},{20... | collective-permute-start | bytes 1769480 | tf_op jit(solution)/shard_map/ppermute | solution.py:598
  222.8 8.7 %collective-permute-start.34 = (bf16[3,24,1024]{2,1,0:T(8,128)(2,1)S(1)}, bf16[3,24,1024]{2,1,0:T(8,128)(2,1)S(1)}, u32[]{:S(2)}, u32[]{:S(2)}) collective-permute-start(bf16[3,24,1024]{2,1,0:T(8,128)(2,1)S(1)} %get-tuple-element.319), channel_id=1, source_target_pairs={{0,2},{2,4},{4,6},{6,0},{1,3},{3,5},{5,7},{7,1},{8,10},{10,12},{12... | collective-permute-start | bytes 442376 | tf_op jit(solution)/shard_map/ppermute | solution.py:601
  225.2 10.1 %collective-permute-start.35 = (bf16[3,24,1024]{2,1,0:T(8,128)(2,1)S(1)}, bf16[3,24,1024]{2,1,0:T(8,128)(2,1)S(1)}, u32[]{:S(2)}, u32[]{:S(2)}) collective-permute-start(bf16[3,24,1024]{2,1,0:T(8,128)(2,1)S(1)} %get-tuple-element.320), channel_id=1, source_target_pairs={{0,4},{2,6},{4,0},{6,2},{1,5},{3,7},{5,1},{7,3},{8,12},{10,14},{12... | collective-permute-start | bytes 442376 | tf_op jit(solution)/shard_map/ppermute | solution.py:601
  225.4 9.8 %collective-permute-start.36 = (bf16[3,24,1024]{2,1,0:T(8,128)(2,1)S(1)}, bf16[3,24,1024]{2,1,0:T(8,128)(2,1)S(1)}, u32[]{:S(2)}, u32[]{:S(2)}) collective-permute-start(bf16[3,24,1024]{2,1,0:T(8,128)(2,1)S(1)} %get-tuple-element.321), channel_id=1, source_target_pairs={{0,6},{2,0},{4,2},{6,4},{1,7},{3,1},{5,3},{7,5},{8,14},{10,8},{12,... | collective-permute-start | bytes 442376 | tf_op jit(solution)/shard_map/ppermute | solution.py:601
  238.5 26.9 %all-to-all-start.2 = ((bf16[16,24,1024]{2,1,0:T(8,128)(2,1)}), bf16[16,24,1024]{2,1,0:T(8,128)(2,1)S(1)}, u32[]{:S(2)}, u32[]{:S(2)}) async-start(bf16[16,24,1024]{2,1,0:T(8,128)(2,1)} %slots.2), calls=%async_computation.2 | async-start | bytes 1572864 | tf_op jit(solution)/shard_map/all_to_all | solution.py:730
  247.2 13.6 %collective-permute-start.38 = (bf16[2,4,24,768]{3,2,1,0:T(8,128)(2,1)S(1)}, bf16[2,4,24,768]{3,2,1,0:T(8,128)(2,1)S(1)}, u32[]{:S(2)}, u32[]{:S(2)}) collective-permute-start(bf16[2,4,24,768]{3,2,1,0:T(8,128)(2,1)S(1)} %bitcast.213), channel_id=1, source_target_pairs={{0,16},{16,0},{1,17},{17,1},{2,18},{18,2},{3,19},{19,3},{4,20},{20... | collective-permute-start | bytes 884744 | tf_op jit(solution)/shard_map/ppermute | solution.py:598
  249.4 12.4 %collective-permute-start.37 = (bf16[2,4,24,768]{3,2,1,0:T(8,128)(2,1)S(1)}, bf16[2,4,24,768]{3,2,1,0:T(8,128)(2,1)S(1)}, u32[]{:S(2)}, u32[]{:S(2)}) collective-permute-start(bf16[2,4,24,768]{3,2,1,0:T(8,128)(2,1)S(1)} %bitcast.214), channel_id=1, source_target_pairs={{0,1},{1,0},{2,3},{3,2},{4,5},{5,4},{6,7},{7,6},{8,9},{9,8},{10,11... | collective-permute-start | bytes 884744 | tf_op jit(solution)/shard_map/ppermute | solution.py:598
  265.4 17.2 %collective-permute-start.42 = (bf16[16,24,1024]{2,1,0:T(8,128)(2,1)S(1)}, bf16[16,24,1024]{2,1,0:T(8,128)(2,1)S(1)}, u32[]{:S(2)}, u32[]{:S(2)}) collective-permute-start(bf16[16,24,1024]{2,1,0:T(8,128)(2,1)S(1)} %all-to-all-done.2.refs_0_), channel_id=1, source_target_pairs={{0,16},{16,0},{1,17},{17,1},{2,18},{18,2},{3,19},{19,3},{4,20},{20... | collective-permute-start | bytes 2359304 | tf_op jit(solution)/shard_map/ppermute | solution.py:598
  266.9 8.7 %collective-permute-start.39 = (bf16[4,24,768]{2,1,0:T(8,128)(2,1)S(1)}, bf16[4,24,768]{2,1,0:T(8,128)(2,1)S(1)}, u32[]{:S(2)}, u32[]{:S(2)}) collective-permute-start(bf16[4,24,768]{2,1,0:T(8,128)(2,1)S(1)} %get-tuple-element.337), channel_id=1, source_target_pairs={{0,2},{2,4},{4,6},{6,0},{1,3},{3,5},{5,7},{7,1},{8,10},{10,12},{12... | collective-permute-start | bytes 442376 | tf_op jit(solution)/shard_map/ppermute | solution.py:601
  268.1 10.8 %collective-permute-start.40 = (bf16[4,24,768]{2,1,0:T(8,128)(2,1)S(1)}, bf16[4,24,768]{2,1,0:T(8,128)(2,1)S(1)}, u32[]{:S(2)}, u32[]{:S(2)}) collective-permute-start(bf16[4,24,768]{2,1,0:T(8,128)(2,1)S(1)} %get-tuple-element.338), channel_id=1, source_target_pairs={{0,4},{2,6},{4,0},{6,2},{1,5},{3,7},{5,1},{7,3},{8,12},{10,14},{12... | collective-permute-start | bytes 442376 | tf_op jit(solution)/shard_map/ppermute | solution.py:601
  269.0 9.9 %collective-permute-start.41 = (bf16[4,24,768]{2,1,0:T(8,128)(2,1)S(1)}, bf16[4,24,768]{2,1,0:T(8,128)(2,1)S(1)}, u32[]{:S(2)}, u32[]{:S(2)}) collective-permute-start(bf16[4,24,768]{2,1,0:T(8,128)(2,1)S(1)} %get-tuple-element.339), channel_id=1, source_target_pairs={{0,6},{2,0},{4,2},{6,4},{1,7},{3,1},{5,3},{7,5},{8,14},{10,8},{12,... | collective-permute-start | bytes 442376 | tf_op jit(solution)/shard_map/ppermute | solution.py:601
  283.3 9.1 %collective-permute-start.43 = (bf16[2,2,4,2,24,1024]{5,4,3,2,1,0:T(8,128)(2,1)S(1)}, bf16[2,2,4,2,24,1024]{5,4,3,2,1,0:T(8,128)(2,1)}, u32[]{:S(2)}, u32[]{:S(2)}) collective-permute-start(bf16[2,2,4,2,24,1024]{5,4,3,2,1,0:T(8,128)(2,1)S(1)} %bitcast.167), channel_id=1, source_target_pairs={{0,8},{8,0},{1,9},{9,1},{2,10},{10,2},{3,11},{11,3},{4,12},{12,4},... | collective-permute-start | bytes 4718600 | tf_op jit(solution)/shard_map/ppermute | solution.py:598
  286.4 17.2 %collective-permute-start.44 = (bf16[24,9216]{1,0:T(8,128)(2,1)}, bf16[24,9216]{1,0:T(8,128)(2,1)S(1)}, u32[]{:S(2)}, u32[]{:S(2)}) collective-permute-start(bf16[24,9216]{1,0:T(8,128)(2,1)} %pack.2.refs_0_), channel_id=1, source_target_pairs={{0,16},{16,0},{1,17},{17,1},{2,18},{18,2},{3,19},{19,3},{4,20},{20... | collective-permute-start | bytes 1327112 | tf_op jit(solution)/shard_map/ppermute | solution.py:598
  288.2 29.2 %all-to-all-start.3 = ((bf16[16,40,768]{2,1,0:T(8,128)(2,1)}), bf16[16,40,768]{2,1,0:T(8,128)(2,1)S(1)}, u32[]{:S(2)}, u32[]{:S(2)}) async-start(bf16[16,40,768]{2,1,0:T(8,128)(2,1)} %slots.3), calls=%async_computation.3 | async-start | bytes 1966080 | tf_op jit(solution)/shard_map/all_to_all | solution.py:730
  339.4 10.3 %collective-permute-start.46 = (bf16[2,24,9216]{2,1,0:T(8,128)(2,1)S(1)}, bf16[2,24,9216]{2,1,0:T(8,128)(2,1)S(1)}, u32[]{:S(2)}, u32[]{:S(2)}) collective-permute-start(bf16[2,24,9216]{2,1,0:T(8,128)(2,1)S(1)} %place.30.refs_0_), channel_id=1, source_target_pairs={{0,8},{8,0},{1,9},{9,1},{2,10},{10,2},{3,11},{11,3},{4,12},{12,4},... | collective-permute-start | bytes 2654216 | tf_op jit(solution)/shard_map/ppermute | solution.py:598
  341.9 25.0 %all-to-all-start.4 = ((bf16[16,24,1024]{2,1,0:T(8,128)(2,1)}), bf16[16,24,1024]{2,1,0:T(8,128)(2,1)S(1)}, u32[]{:S(2)}, u32[]{:S(2)}) async-start(bf16[16,24,1024]{2,1,0:T(8,128)(2,1)} %bitcast.222), calls=%async_computation.4 | async-start | bytes 1572864 | tf_op jit(solution)/shard_map/all_to_all | solution.py:802
  366.9 15.9 %collective-permute-start.47 = (bf16[24,13824]{1,0:T(8,128)(2,1)S(1)}, bf16[24,13824]{1,0:T(8,128)(2,1)S(1)}, u32[]{:S(2)}, u32[]{:S(2)}) collective-permute-start(bf16[24,13824]{1,0:T(8,128)(2,1)S(1)} %pack.3.refs_0_), channel_id=1, source_target_pairs={{0,16},{16,0},{1,17},{17,1},{2,18},{18,2},{3,19},{19,3},{4,20},{20... | collective-permute-start | bytes 1990664 | tf_op jit(solution)/shard_map/ppermute | solution.py:598
  370.8 14.0 %collective-permute-start.48 = (bf16[24,13824]{1,0:T(8,128)(2,1)S(1)}, bf16[24,13824]{1,0:T(8,128)(2,1)S(1)}, u32[]{:S(2)}, u32[]{:S(2)}) collective-permute-start(bf16[24,13824]{1,0:T(8,128)(2,1)S(1)} %pack.3.refs_0_), channel_id=1, source_target_pairs={{0,8},{8,0},{1,9},{9,1},{2,10},{10,2},{3,11},{11,3},{4,12},{12,4},... | collective-permute-start | bytes 1990664 | tf_op jit(solution)/shard_map/ppermute | solution.py:598
  (72 other events, 362.2 us)
